TPU v7x, 32 devices: a whole 2x2x4 slice. The times are simulated.
32 devices in a mesh: row: 8 (over z, x), col: 4 (over y, core).
Axes of the slice: x: 2, y: 2, z: 4, core: 2. Of those that a mesh axis runs over, the one named last changes fastest.
Arguments:
- vectors: float32 [8192, 1024], P(('row', 'col')), may hold values from -6 to 6
- rotation: float32 [1024, 1024], P(None, 'col'), may hold values from -0.1875 to 0.1875
- blocks: bfloat16 [64, 16, 128, 128], P('row'), may hold values from -0.0625 to 0.0625
- cols: int32 [64, 16], P('row'), may hold values from 0 to 15, as said below
- lists: int32 [8, 2, 4], P('row'), may hold values from 0 to 7, as said below
- counts: int32 [8], P('row'), may hold values from 4 to 8, as said below
Outputs:
- filtered: float32 [1024, 8192], P('col', 'row')
Inputs may be any that keep to these rules, and one draw needn't show every extreme that they name: `counts`: at least one group uses all 8 slots. Every entry of lists[r] is below counts[r], and lists[r, j, 0] = counts[r] - 1; entries may repeat. cols[t, 0] = 4 + t % 8, the block row itself; on valid block rows of group r every slot between 4 and 15 that names an own block row is below 4 + counts[r].
All inputs are finite; a program needn't handle non-finite values.
Results may differ from a plain program's by a relative error of at most 0.0065.
Values may be sent and summed in bfloat16 or wider, within the bound.
No kernel may reach another device: no remote copies, remote signals or barrier semaphores. Data moves between devices by JAX's collectives and lax.ppermute only.
A program may use at most 64 MiB of HBM per device.

v0:
```python
import functools

import jax
import jax.numpy as jnp
from jax import lax
from jax.experimental import pallas as pl
from jax.experimental.pallas import tpu as pltpu
from jax.sharding import PartitionSpec as P


STEPS = 10
AXES = ("row", "col")
F32, BF16 = jnp.float32, jnp.bfloat16
VMEM = pl.BlockSpec(memory_space=pltpu.VMEM)
SMEM = pl.BlockSpec(memory_space=pltpu.SMEM)
HBM = pl.BlockSpec(memory_space=pltpu.HBM)
ANY = pl.BlockSpec(memory_space=pl.ANY)


def patterns(rows, cols):
    every = [(r, c) for r in range(rows) for c in range(cols)]
    keeps = lambda r, c: r % 2 == c % 2

    def far(r, c):
        to = r + 2 if c % 2 else r - 2
        return (to, c ^ 1) if 0 <= to < rows else (r ^ 1, c)

    ways = {
        "trade": lambda r, c: (r ^ 2, c) if keeps(r, c) else (r ^ 1, c ^ 1),
        "across": lambda r, c: (r, c ^ 2),
        "near": lambda r, c: (r, c ^ 1),
        "far": far,
    }
    at = lambda place: place[0] * cols + place[1]
    pairs = {name: [(at(p), at(way(*p))) for p in every] for name, way in ways.items()}
    pairs["across"] = [(at(p), at(ways["across"](*p))) for p in every if not keeps(*p)]
    return pairs


def call(kernel, outs, in_specs, out_specs, scratch=(), aliases={}, mib=12):
    return pl.pallas_call(
        kernel,
        out_shape=outs,
        in_specs=in_specs,
        out_specs=out_specs,
        scratch_shapes=scratch,
        input_output_aliases=aliases,
        compiler_params=pltpu.CompilerParams(vmem_limit_bytes=mib << 20),
    )


def rotate_kernel(places, width, info, rotation, *refs):
    pieces, out = refs[: len(places)], refs[len(places)]
    rot = rotation[...]
    high = rot.astype(BF16)
    low = (rot - high.astype(F32)).astype(BF16)
    mine, used = info[0], info[1] * width
    for place, piece in zip(places, pieces):
        rows = piece.shape[0]
        first = pl.multiple_of((mine ^ place) * rows, rows)
        x = piece[...]
        y = jnp.dot(x, high, preferred_element_type=F32) + jnp.dot(x, low, preferred_element_type=F32)
        at = first + lax.broadcasted_iota(jnp.int32, y.shape, 0)
        out[pl.ds(first, rows), :] = jnp.where(at < used, y, 0.0).astype(BF16)


def build_kernel(step_at, direct, cap, nblk, width, meta, blocks, moved, *refs):
    near_out, far_out = refs[-7:-5]
    raw, total, near_buf, far_buf, sems = refs[-5:]
    role, keep, half, edge, used = meta[0], meta[1], meta[2], meta[3], meta[4]
    near_w = near_buf.shape[1]

    t = row_of(half, step_at, direct, cap)
    parts = 4
    piece = nblk // parts
    for flag, src in ((keep == 1, blocks.at[t]), (keep == 0, moved.at[0])):
        copies = [
            pltpu.make_async_copy(
                src.at[pl.ds(p * piece, piece)], raw.at[pl.ds(p * piece, piece)], sems.at[p]
            )
            for p in range(parts)
        ]

        @pl.when(flag)
        def _():
            for copy in copies:
                copy.start()

    total[...] = jnp.zeros_like(total)
    for copy in copies:
        copy.wait()
    for k in range(nblk):
        slot = meta[5 + t * nblk + k]
        lanes = slot_place(slot, role, cap, nblk) * width
        lanes = pl.ds(pl.multiple_of(lanes, width), width)
        total[:, lanes] = total[:, lanes] + raw[k].astype(F32)
    scale = jnp.where(t < used, 1.0, 0.0).astype(F32)
    near_buf[...] = (total[:, :near_w] * scale).astype(BF16)
    far_buf[...] = (total[:, near_w:] * jnp.where(edge == 1, 0.0, scale)).astype(BF16)
    rows = pl.ds(pl.multiple_of(t * width, width), width)
    stores = (
        pltpu.make_async_copy(near_buf, near_out.at[rows, :], sems.at[parts]),
        pltpu.make_async_copy(far_buf, far_out.at[rows, :], sems.at[parts + 1]),
    )
    for copy in stores:
        copy.start()
    for copy in stores:
        copy.wait()


def row_of(half, step, direct, cap):
    flip = half if direct else 1 - half
    return jnp.where(flip == 1, cap - 1 - step, step)


def stage_kernel(cap, half, blocks, *refs):
    outs, sems = refs[:-1], refs[-1]
    nblk = blocks.shape[1]
    piece = nblk // 4
    copies = [
        pltpu.make_async_copy(
            blocks.at[row_of(half[0], step, True, cap), pl.ds(p * piece, piece)],
            out.at[0, pl.ds(p * piece, piece)], sems.at[step, p],
        )
        for step, out in enumerate(outs) for p in range(4)
    ]
    for copy in copies:
        copy.start()
    for copy in copies:
        copy.wait()


def slot_place(slot, role, cap, slots):
    edge = (slots - cap) // 2
    first = jnp.where(slot < edge, slot + slots - edge, slot - edge)
    second = jnp.where(slot < edge, slot + cap, jnp.where(slot < edge + cap, slot - edge, slot))
    return jnp.where(role == 0, first, second)


def pick(lists, first, edge, width):
    return [pl.ds(pl.multiple_of(lists[first + i] * width, width), width) for i in range(edge)]


def pack_kernel(width, edge, lists, own, moved, field, near_send, far_send):
    @pl.when(lists[2 * edge] == 1)
    def _():
        field[...] = own[...]

    @pl.when(lists[2 * edge] == 0)
    def _():
        field[...] = moved[...]

    for first, send in ((0, near_send), (edge, far_send)):
        for i, rows in enumerate(pick(lists, first, edge, width)):
            send[i * width : (i + 1) * width, :] = field[rows, :]


def local_kernel(near_op, field, near, acc):
    rows = field.shape[0]
    acc[...] = jnp.dot(near_op[:, :rows], field[...], preferred_element_type=F32) + jnp.dot(
        near_op[:, rows:], near[...], preferred_element_type=F32
    )


def ahead_kernel(width, edge, lists, acc, far_op, far, *refs):
    rows = pick(lists, edge, edge, width)
    join = lambda ref: jnp.concatenate([ref[r, :] for r in rows], axis=0)
    total = join(acc) + jnp.dot(join(far_op), far[...], preferred_element_type=F32)
    if len(refs) > 1:
        total = 2.0 * total - join(refs[0]).astype(F32)
    refs[-1][...] = total.astype(BF16)


def finish_kernel(first, last, width, edge, lists, acc, far_op, far, *refs):
    total = acc[...] + jnp.dot(far_op[...], far[...], preferred_element_type=F32)
    if not first:
        older, refs = refs[0], refs[1:]
        total = 2.0 * total - older[...].astype(F32)
    if last:
        refs[0][...] = total.T.astype(BF16)
        return
    value, field, near_send = refs
    value[...] = total
    field[...] = total.astype(BF16)
    for i, rows in enumerate(pick(lists, 0, edge, width)):
        near_send[i * width : (i + 1) * width, :] = field[rows, :]


def body(vectors, rotation, blocks, cols, lists, counts):
    rows, columns = lax.axis_size("row"), lax.axis_size("col")
    ways = patterns(rows, columns)

    def send(x, way):
        return lax.ppermute(x, AXES, ways[way])

    r, c = lax.axis_index("row"), lax.axis_index("col")
    cap, nblk, width = blocks.shape[0], blocks.shape[1], blocks.shape[2]
    edge = lists.shape[2]
    panel = rotation.shape[1]
    height = cap * width
    slots = cap + 2 * edge
    role = c % 2
    keep = role == r % 2
    half = c // 2 % 2
    at_edge = jnp.where(role == 0, r < 2, r >= rows - 2)
    flag = lambda x: x.astype(jnp.int32)
    sds = jax.ShapeDtypeStruct

    own_meta = jnp.concatenate([counts, cols.reshape(-1), lists.reshape(-1)])
    meta = jnp.where(keep, own_meta, send(own_meta, "trade"))
    tables = meta[1 + cap * nblk :].reshape(2, edge)
    send_lists = jnp.where(role == 0, tables, tables[::-1]).reshape(-1)
    send_lists = jnp.concatenate([send_lists, flag(keep)[None]])
    info = jnp.concatenate([jnp.stack([flag(x) for x in (role, keep, half, at_edge)]), meta[: 1 + cap * nblk]])

    pieces = {0: vectors.astype(BF16)}
    bit = columns // 2
    while bit:
        for place in list(pieces):
            pieces[place ^ bit] = lax.ppermute(
                pieces[place], "col", [(k, k ^ bit) for k in range(columns)]
            )
        bit //= 2

    held = pltpu.with_memory_space_constraint(blocks, pltpu.HBM)
    relays = cap // 2 - 1
    straight = cap - relays
    row = sds((1, nblk, width, width), BF16)
    staged = call(
        functools.partial(stage_kernel, cap), (row,) * straight, [SMEM, HBM], (ANY,) * straight,
        scratch=(pltpu.SemaphoreType.DMA((straight, 4)),),
    )(flag(half)[None], held)
    moved = [(k, True, send(x, "trade")) for k, x in enumerate(staged)]
    moved[-1:-1] = [(k, False, send(moved[k][2], "across")) for k in range(relays)]

    field = call(
        functools.partial(rotate_kernel, tuple(pieces), width),
        sds((height, panel), BF16), [SMEM, VMEM] + [VMEM] * len(pieces), VMEM,
    )(jnp.stack([c.astype(jnp.int32), counts[0]]), rotation, *pieces.values())
    moved_field = send(field, "trade")

    ops = ()
    op_shapes = (sds((height, height + edge * width), BF16), sds((height, edge * width), BF16))
    for k, direct, rowk in moved:
        ops = call(
            functools.partial(build_kernel, k, direct, cap, nblk, width),
            op_shapes, [SMEM, HBM, ANY] + [ANY] * len(ops), (ANY, ANY),
            scratch=(
                pltpu.VMEM((nblk, width, width), BF16),
                pltpu.VMEM((width, slots * width), F32),
                pltpu.VMEM((width, height + edge * width), BF16),
                pltpu.VMEM((width, edge * width), BF16),
                pltpu.SemaphoreType.DMA((6,)),
            ),
            aliases={3: 0, 4: 1} if ops else {},
        )(info, held, rowk, *ops)
    near_op, far_op = ops

    sent = sds((edge * width, panel), BF16)
    wide = lambda kind: sds((height, panel), kind)
    field, near_send, far_send = call(
        functools.partial(pack_kernel, width, edge), (wide(BF16), sent, sent),
        [SMEM, VMEM, VMEM], (VMEM,) * 3,
    )(send_lists, field, moved_field)
    older, newer = (), field
    for step in range(STEPS):
        far, near = send(far_send, "far"), send(near_send, "near")
        acc = call(local_kernel, wide(F32), [VMEM] * 3, VMEM)(near_op, field, near)
        last = step == STEPS - 1
        given = (send_lists, acc, far_op, far) + older
        specs = [SMEM] + [VMEM] * (len(given) - 1)
        if not last:
            far_send = call(functools.partial(ahead_kernel, width, edge), sent, specs, VMEM)(*given)
        result = call(
            functools.partial(finish_kernel, step == 0, last, width, edge),
            sds((panel, height), BF16) if last else (wide(F32), wide(BF16), sent),
            specs, VMEM if last else (VMEM,) * 3,
        )(*given)
        if not last:
            older = (newer,)
            newer, field, near_send = result
    return jnp.where(keep, result, send(result, "trade")).astype(F32)


def solution(mesh):
    return jax.shard_map(
        body,
        mesh=mesh,
        in_specs=(
            P(("row", "col"), None),
            P(None, "col"),
            P("row", None, None, None),
            P("row", None),
            P("row", None, None),
            P("row"),
        ),
        out_specs=P("col", "row"),
        check_vma=False,
    )
```

profile of v0, /device:TPU:0, one launch (start us, length us, event | category | flops | bytes accessed | tf_op | source)
XLA Modules:
  0.0 216.0 jit_solution(2834637946862899275)
XLA Ops:
  1.4 3.1 %collective-permute-start.9 = (bf16[256,1024]{1,0:T(8,128)(2,1)S(1)}, bf16[256,1024]{1,0:T(8,128)(2,1)S(1)}, u32[]{:S(2)}, u32[]{:S(2)}) collective-permute-start(bf16[256,1024]{1,0:T(8,128)(2,1)S(1)} %convert_element_type.4.refs_0_), channel_id=1, source_target_pairs={{0,2},{1,3},{2,0},{3,1},{4,6},{5,7},{6,4},{7,5},{8,10},{9,11},{10,... | collective-permute-start | bytes 1572872 | tf_op jit(solution)/shard_map/ppermute | solution.py:220
  4.5 11.9 %collective-permute-done.9.refs_1_ = bf16[256,1024]{1,0:T(8,128)(2,1)S(1)} collective-permute-done((bf16[256,1024]{1,0:T(8,128)(2,1)S(1)}, bf16[256,1024]{1,0:T(8,128)(2,1)S(1)}, u32[]{:S(2)}, u32[]{:S(2)}) %collective-permute-start.9) | collective-permute-done | bytes 524320 | tf_op jit(solution)/shard_map/ppermute | solution.py:220
  16.4 48.9 %shard_map.64 = (bf16[1,16,128,128]{3,2,1,0:T(8,128)(2,1)}, bf16[1,16,128,128]{3,2,1,0:T(8,128)(2,1)}, bf16[1,16,128,128]{3,2,1,0:T(8,128)(2,1)}, bf16[1,16,128,...) custom-call(s32[1]{0:T(128)} %bitcast.2.half, bf16[8,16,128,128]{3,2,1,0:T(8,128)(2,1)} %blocks.17), custom_call_target="tpu_custom_call" | custom-call | tf_op jit(solution)/shard_map/pallas_call | solution.py:229
  71.1 2.5 %shard_map.73.own = bf16[1024,256]{1,0:T(8,128)(2,1)S(1)} custom-call(s32[2]{0:T(128)S(1)} %pad_add_fusion.2.info, f32[1024,256]{1,0:T(8,128)S(1)} %copy-done, bf16[256,1024]{1,0:T(8,128)(2,1)S(1)} %convert_element_type.4.refs_0_, bf16[256,1024]{1,0:T(8,128)(2,1)S(1)} %copy-done.4, bf16[256,1024]{1,0:T(8,128)(2,1)} %collective-permute-done.10.refs_2_, ...), custom_call_target="tpu_custom_call" | custom-call | tf_op jit(solution)/shard_map/pallas_call | solution.py:236
  75.9 15.8 %collective-permute-done = s32[137]{0:T(256)S(1)} collective-permute-done((s32[137]{0:T(256)S(1)}, s32[137]{0:T(256)S(1)}, u32[]{:S(2)}, u32[]{:S(2)}) %collective-permute-start) | collective-permute-done | bytes 580 | tf_op jit(solution)/shard_map/ppermute | solution.py:194
  101.8 4.4 %collective-permute-start.13 = (bf16[512,256]{1,0:T(8,128)(2,1)}, bf16[512,256]{1,0:T(8,128)(2,1)S(1)}, u32[]{:S(2)}, u32[]{:S(2)}) collective-permute-start(bf16[512,256]{1,0:T(8,128)(2,1)} %get-tuple-element.76), channel_id=1, source_target_pairs={{0,1},{1,0},{2,3},{3,2},{4,5},{5,4},{6,7},{7,6},{8,9},{9,8},{10,11... | collective-permute-start | bytes 786440 | tf_op jit(solution)/shard_map/ppermute | solution.py:194
  107.4 2.3 %shard_map.65 = (bf16[1024,1536]{1,0:T(8,128)(2,1)S(1)}, bf16[1024,512]{1,0:T(8,128)(2,1)S(1)}) custom-call(s32[133]{0:T(256)S(1)} %concatenate.11.meta, bf16[8,16,128,128]{3,2,1,0:T(8,128)(2,1)} %blocks.17, bf16[1,16,128,128]{3,2,1,0:T(8,128)(2,1)} %collective-permute-done.6.moved), custom_call_target="tpu_custom_call" | custom-call | tf_op jit(solution)/shard_map/pallas_call | solution.py:245
  109.8 2.3 %shard_map.66 = (bf16[1024,1536]{1,0:T(8,128)(2,1)S(1)}, bf16[1024,512]{1,0:T(8,128)(2,1)S(1)}) custom-call(s32[133]{0:T(256)S(1)} %concatenate.11.meta, bf16[8,16,128,128]{3,2,1,0:T(8,128)(2,1)} %blocks.17, bf16[1,16,128,128]{3,2,1,0:T(8,128)(2,1)S(1)} %collective-permute-done.4.moved, ...), custom_call_target="tpu_custom_call", output_to_operand_aliasing={{0}: (3, {}), {1}: (4, {})} | custom-call | tf_op jit(solution)/shard_map/pallas_call | solution.py:245
  112.1 2.3 %shard_map.67 = (bf16[1024,1536]{1,0:T(8,128)(2,1)S(1)}, bf16[1024,512]{1,0:T(8,128)(2,1)S(1)}) custom-call(s32[133]{0:T(256)S(1)} %concatenate.11.meta, bf16[8,16,128,128]{3,2,1,0:T(8,128)(2,1)} %blocks.17, bf16[1,16,128,128]{3,2,1,0:T(8,128)(2,1)S(1)} %collective-permute-done.2.moved, ...), custom_call_target="tpu_custom_call", output_to_operand_aliasing={{0}: (3, {}), {1}: (4, {})} | custom-call | tf_op jit(solution)/shard_map/pallas_call | solution.py:245
  114.5 2.3 %shard_map.68 = (bf16[1024,1536]{1,0:T(8,128)(2,1)S(1)}, bf16[1024,512]{1,0:T(8,128)(2,1)S(1)}) custom-call(s32[133]{0:T(256)S(1)} %concatenate.11.meta, bf16[8,16,128,128]{3,2,1,0:T(8,128)(2,1)} %blocks.17, bf16[1,16,128,128]{3,2,1,0:T(8,128)(2,1)S(1)} %collective-permute-done.8.moved, ...), custom_call_target="tpu_custom_call", output_to_operand_aliasing={{0}: (3, {}), {1}: (4, {})} | custom-call | tf_op jit(solution)/shard_map/pallas_call | solution.py:245
  116.8 2.3 %shard_map.69 = (bf16[1024,1536]{1,0:T(8,128)(2,1)S(1)}, bf16[1024,512]{1,0:T(8,128)(2,1)S(1)}) custom-call(s32[133]{0:T(256)S(1)} %concatenate.11.meta, bf16[8,16,128,128]{3,2,1,0:T(8,128)(2,1)} %blocks.17, bf16[1,16,128,128]{3,2,1,0:T(8,128)(2,1)} %collective-permute-done.7.moved, ...), custom_call_target="tpu_custom_call", output_to_operand_aliasing={{0}: (3, {}), {1}: (4, {})} | custom-call | tf_op jit(solution)/shard_map/pallas_call | solution.py:245
  119.2 2.3 %shard_map.70 = (bf16[1024,1536]{1,0:T(8,128)(2,1)S(1)}, bf16[1024,512]{1,0:T(8,128)(2,1)S(1)}) custom-call(s32[133]{0:T(256)S(1)} %concatenate.11.meta, bf16[8,16,128,128]{3,2,1,0:T(8,128)(2,1)} %blocks.17, bf16[1,16,128,128]{3,2,1,0:T(8,128)(2,1)} %collective-permute-done.5.moved, ...), custom_call_target="tpu_custom_call", output_to_operand_aliasing={{0}: (3, {}), {1}: (4, {})} | custom-call | tf_op jit(solution)/shard_map/pallas_call | solution.py:245
  121.5 2.3 %shard_map.71 = (bf16[1024,1536]{1,0:T(8,128)(2,1)S(1)}, bf16[1024,512]{1,0:T(8,128)(2,1)S(1)}) custom-call(s32[133]{0:T(256)S(1)} %concatenate.11.meta, bf16[8,16,128,128]{3,2,1,0:T(8,128)(2,1)} %blocks.17, bf16[1,16,128,128]{3,2,1,0:T(8,128)(2,1)} %collective-permute-done.3.moved, ...), custom_call_target="tpu_custom_call", output_to_operand_aliasing={{0}: (3, {}), {1}: (4, {})} | custom-call | tf_op jit(solution)/shard_map/pallas_call | solution.py:245
  123.9 2.5 %shard_map.72 = (bf16[1024,1536]{1,0:T(8,128)(2,1)S(1)}, bf16[1024,512]{1,0:T(8,128)(2,1)S(1)}) custom-call(s32[133]{0:T(256)S(1)} %concatenate.11.meta, bf16[8,16,128,128]{3,2,1,0:T(8,128)(2,1)} %blocks.17, bf16[1,16,128,128]{3,2,1,0:T(8,128)(2,1)S(1)} %collective-permute-done.1.moved, ...), custom_call_target="tpu_custom_call", output_to_operand_aliasing={{0}: (3, {}), {1}: (4, {})} | custom-call | tf_op jit(solution)/shard_map/pallas_call | solution.py:245
  132.1 3.7 %collective-permute-done.16.far = bf16[512,256]{1,0:T(8,128)(2,1)S(1)} collective-permute-done((bf16[512,256]{1,0:T(8,128)(2,1)S(1)}, bf16[512,256]{1,0:T(8,128)(2,1)S(1)}, u32[]{:S(2)}, u32[]{:S(2)}) %collective-permute-start.16) | collective-permute-done | bytes 262176 | tf_op jit(solution)/shard_map/ppermute | solution.py:194
  140.4 3.8 %collective-permute-done.18.far = bf16[512,256]{1,0:T(8,128)(2,1)S(1)} collective-permute-done((bf16[512,256]{1,0:T(8,128)(2,1)S(1)}, bf16[512,256]{1,0:T(8,128)(2,1)S(1)}, u32[]{:S(2)}, u32[]{:S(2)}) %collective-permute-start.18) | collective-permute-done | bytes 262176 | tf_op jit(solution)/shard_map/ppermute | solution.py:194
  148.9 3.8 %collective-permute-done.20.far = bf16[512,256]{1,0:T(8,128)(2,1)S(1)} collective-permute-done((bf16[512,256]{1,0:T(8,128)(2,1)S(1)}, bf16[512,256]{1,0:T(8,128)(2,1)S(1)}, u32[]{:S(2)}, u32[]{:S(2)}) %collective-permute-start.20) | collective-permute-done | bytes 262176 | tf_op jit(solution)/shard_map/ppermute | solution.py:194
  157.4 3.8 %collective-permute-done.22.far = bf16[512,256]{1,0:T(8,128)(2,1)S(1)} collective-permute-done((bf16[512,256]{1,0:T(8,128)(2,1)S(1)}, bf16[512,256]{1,0:T(8,128)(2,1)S(1)}, u32[]{:S(2)}, u32[]{:S(2)}) %collective-permute-start.22) | collective-permute-done | bytes 262176 | tf_op jit(solution)/shard_map/ppermute | solution.py:194
  165.9 3.8 %collective-permute-done.24.far = bf16[512,256]{1,0:T(8,128)(2,1)S(1)} collective-permute-done((bf16[512,256]{1,0:T(8,128)(2,1)S(1)}, bf16[512,256]{1,0:T(8,128)(2,1)S(1)}, u32[]{:S(2)}, u32[]{:S(2)}) %collective-permute-start.24) | collective-permute-done | bytes 262176 | tf_op jit(solution)/shard_map/ppermute | solution.py:194
  174.4 3.8 %collective-permute-done.26.far = bf16[512,256]{1,0:T(8,128)(2,1)S(1)} collective-permute-done((bf16[512,256]{1,0:T(8,128)(2,1)S(1)}, bf16[512,256]{1,0:T(8,128)(2,1)S(1)}, u32[]{:S(2)}, u32[]{:S(2)}) %collective-permute-start.26) | collective-permute-done | bytes 262176 | tf_op jit(solution)/shard_map/ppermute | solution.py:194
  182.9 3.8 %collective-permute-done.28.far = bf16[512,256]{1,0:T(8,128)(2,1)S(1)} collective-permute-done((bf16[512,256]{1,0:T(8,128)(2,1)S(1)}, bf16[512,256]{1,0:T(8,128)(2,1)S(1)}, u32[]{:S(2)}, u32[]{:S(2)}) %collective-permute-start.28) | collective-permute-done | bytes 262176 | tf_op jit(solution)/shard_map/ppermute | solution.py:194
  191.4 3.8 %collective-permute-done.30.far = bf16[512,256]{1,0:T(8,128)(2,1)S(1)} collective-permute-done((bf16[512,256]{1,0:T(8,128)(2,1)S(1)}, bf16[512,256]{1,0:T(8,128)(2,1)S(1)}, u32[]{:S(2)}, u32[]{:S(2)}) %collective-permute-start.30) | collective-permute-done | bytes 262176 | tf_op jit(solution)/shard_map/ppermute | solution.py:194
  200.8 3.8 %collective-permute-done.32.far = bf16[512,256]{1,0:T(8,128)(2,1)S(1)} collective-permute-done((bf16[512,256]{1,0:T(8,128)(2,1)S(1)}, bf16[512,256]{1,0:T(8,128)(2,1)S(1)}, u32[]{:S(2)}, u32[]{:S(2)}) %collective-permute-start.32) | collective-permute-done | bytes 262176 | tf_op jit(solution)/shard_map/ppermute | solution.py:194
  205.8 9.2 %collective-permute-done.33 = bf16[256,1024]{1,0:T(8,128)(2,1)S(1)} collective-permute-done((bf16[256,1024]{1,0:T(8,128)(2,1)S(1)}, bf16[256,1024]{1,0:T(8,128)(2,1)S(1)}, u32[]{:S(2)}, u32[]{:S(2)}) %collective-permute-start.33) | collective-permute-done | bytes 524320 | tf_op jit(solution)/shard_map/ppermute | solution.py:194
  (116 shorter events, 66.2 us)
Async XLA Ops:
  1.4 15.0 %collective-permute-start.9 = (bf16[256,1024]{1,0:T(8,128)(2,1)S(1)}, bf16[256,1024]{1,0:T(8,128)(2,1)S(1)}, u32[]{:S(2)}, u32[]{:S(2)}) collective-permute-start(bf16[256,1024]{1,0:T(8,128)(2,1)S(1)} %convert_element_type.4.refs_0_), channel_id=1, source_target_pairs={{0,2},{1,3},{2,0},{3,1},{4,6},{5,7},{6,4},{7,5},{8,10},{9,11},{10,... | collective-permute-start | bytes 1572872 | tf_op jit(solution)/shard_map/ppermute | solution.py:220
  4.5 65.5 %collective-permute-start.10 = (bf16[256,1024]{1,0:T(8,128)(2,1)S(1)}, bf16[256,1024]{1,0:T(8,128)(2,1)}, u32[]{:S(2)}, u32[]{:S(2)}) collective-permute-start(bf16[256,1024]{1,0:T(8,128)(2,1)S(1)} %convert_element_type.4.refs_0_), channel_id=1, source_target_pairs={{0,1},{1,0},{2,3},{3,2},{4,5},{5,4},{6,7},{7,6},{8,9},{9,8},{10,11... | collective-permute-start | bytes 1572872 | tf_op jit(solution)/shard_map/ppermute | solution.py:220
  16.4 53.6 %collective-permute-start.11 = (bf16[256,1024]{1,0:T(8,128)(2,1)S(1)}, bf16[256,1024]{1,0:T(8,128)(2,1)}, u32[]{:S(2)}, u32[]{:S(2)}) collective-permute-start(bf16[256,1024]{1,0:T(8,128)(2,1)S(1)} %collective-permute-done.9.refs_1_), channel_id=1, source_target_pairs={{0,1},{1,0},{2,3},{3,2},{4,5},{5,4},{6,7},{7,6},{8,9},{9,8},{10,11... | collective-permute-start | bytes 1572872 | tf_op jit(solution)/shard_map/ppermute | solution.py:220
  65.4 28.2 %collective-permute-start.6 = (bf16[1,16,128,128]{3,2,1,0:T(8,128)(2,1)}, bf16[1,16,128,128]{3,2,1,0:T(8,128)(2,1)}, u32[]{:S(2)}, u32[]{:S(2)}) collective-permute-start(bf16[1,16,128,128]{3,2,1,0:T(8,128)(2,1)} %get-tuple-element.58), channel_id=1, source_target_pairs={{0,8},{1,4},{2,10},{3,6},{4,1},{5,13},{6,3},{7,15},{8,0},{9,12},{1... | collective-permute-start | bytes 1572872 | tf_op jit(solution)/shard_map/ppermute | solution.py:194
  67.2 28.0 %collective-permute-start.4 = (bf16[1,16,128,128]{3,2,1,0:T(8,128)(2,1)}, bf16[1,16,128,128]{3,2,1,0:T(8,128)(2,1)S(1)}, u32[]{:S(2)}, u32[]{:S(2)}) collective-permute-start(bf16[1,16,128,128]{3,2,1,0:T(8,128)(2,1)} %get-tuple-element.57), channel_id=1, source_target_pairs={{0,8},{1,4},{2,10},{3,6},{4,1},{5,13},{6,3},{7,15},{8,0},{9,12},{1... | collective-permute-start | bytes 1572872 | tf_op jit(solution)/shard_map/ppermute | solution.py:194
  67.5 28.1 %collective-permute-start.2 = (bf16[1,16,128,128]{3,2,1,0:T(8,128)(2,1)}, bf16[1,16,128,128]{3,2,1,0:T(8,128)(2,1)S(1)}, u32[]{:S(2)}, u32[]{:S(2)}) collective-permute-start(bf16[1,16,128,128]{3,2,1,0:T(8,128)(2,1)} %get-tuple-element.56), channel_id=1, source_target_pairs={{0,8},{1,4},{2,10},{3,6},{4,1},{5,13},{6,3},{7,15},{8,0},{9,12},{1... | collective-permute-start | bytes 1572872 | tf_op jit(solution)/shard_map/ppermute | solution.py:194
  73.6 23.4 %collective-permute-start.12 = (bf16[1024,256]{1,0:T(8,128)(2,1)S(1)}, bf16[1024,256]{1,0:T(8,128)(2,1)S(1)}, u32[]{:S(2)}, u32[]{:S(2)}) collective-permute-start(bf16[1024,256]{1,0:T(8,128)(2,1)S(1)} %shard_map.73.own), channel_id=1, source_target_pairs={{0,8},{1,4},{2,10},{3,6},{4,1},{5,13},{6,3},{7,15},{8,0},{9,12},{1... | collective-permute-start | bytes 1572872 | tf_op jit(solution)/shard_map/ppermute | solution.py:194
  74.1 17.6 %collective-permute-start = (s32[137]{0:T(256)S(1)}, s32[137]{0:T(256)S(1)}, u32[]{:S(2)}, u32[]{:S(2)}) collective-permute-start(s32[137]{0:T(256)S(1)} %pad_add_fusion), channel_id=1, source_target_pairs={{0,8},{1,4},{2,10},{3,6},{4,1},{5,13},{6,3},{7,15},{8,0},{9,12},{1... | collective-permute-start | bytes 1652 | tf_op jit(solution)/shard_map/ppermute | solution.py:194
  91.7 10.1 %collective-permute-start.8 = (bf16[1,16,128,128]{3,2,1,0:T(8,128)(2,1)}, bf16[1,16,128,128]{3,2,1,0:T(8,128)(2,1)S(1)}, u32[]{:S(2)}, u32[]{:S(2)}) collective-permute-start(bf16[1,16,128,128]{3,2,1,0:T(8,128)(2,1)} %copy-done.6), channel_id=1, source_target_pairs={{0,8},{1,4},{2,10},{3,6},{4,1},{5,13},{6,3},{7,15},{8,0},{9,12},{1... | collective-permute-start | bytes 1572872 | tf_op jit(solution)/shard_map/ppermute | solution.py:194
  93.5 12.6 %collective-permute-start.7 = (bf16[1,16,128,128]{3,2,1,0:T(8,128)(2,1)}, bf16[1,16,128,128]{3,2,1,0:T(8,128)(2,1)}, u32[]{:S(2)}, u32[]{:S(2)}) collective-permute-start(bf16[1,16,128,128]{3,2,1,0:T(8,128)(2,1)} %collective-permute-done.6.moved), channel_id=1, source_target_pairs={{1,3},{3,1},{4,6},{6,4},{9,11},{11,9},{12,14},{14,12},{17,19},{19,... | collective-permute-start | bytes 1572872 | tf_op jit(solution)/shard_map/ppermute | solution.py:194
  95.3 28.6 %collective-permute-start.1 = (bf16[1,16,128,128]{3,2,1,0:T(8,128)(2,1)}, bf16[1,16,128,128]{3,2,1,0:T(8,128)(2,1)S(1)}, u32[]{:S(2)}, u32[]{:S(2)}) collective-permute-start(bf16[1,16,128,128]{3,2,1,0:T(8,128)(2,1)} %copy-done.5), channel_id=1, source_target_pairs={{0,8},{1,4},{2,10},{3,6},{4,1},{5,13},{6,3},{7,15},{8,0},{9,12},{1... | collective-permute-start | bytes 1572872 | tf_op jit(solution)/shard_map/ppermute | solution.py:194
  95.5 23.6 %collective-permute-start.5 = (bf16[1,16,128,128]{3,2,1,0:T(8,128)(2,1)S(1)}, bf16[1,16,128,128]{3,2,1,0:T(8,128)(2,1)}, u32[]{:S(2)}, u32[]{:S(2)}) collective-permute-start(bf16[1,16,128,128]{3,2,1,0:T(8,128)(2,1)S(1)} %collective-permute-done.4.moved), channel_id=1, source_target_pairs={{1,3},{3,1},{4,6},{6,4},{9,11},{11,9},{12,14},{14,12},{17,19},{19,... | collective-permute-start | bytes 1572872 | tf_op jit(solution)/shard_map/ppermute | solution.py:194
  97.8 23.7 %collective-permute-start.3 = (bf16[1,16,128,128]{3,2,1,0:T(8,128)(2,1)S(1)}, bf16[1,16,128,128]{3,2,1,0:T(8,128)(2,1)}, u32[]{:S(2)}, u32[]{:S(2)}) collective-permute-start(bf16[1,16,128,128]{3,2,1,0:T(8,128)(2,1)S(1)} %collective-permute-done.2.moved), channel_id=1, source_target_pairs={{1,3},{3,1},{4,6},{6,4},{9,11},{11,9},{12,14},{14,12},{17,19},{19,... | collective-permute-start | bytes 1572872 | tf_op jit(solution)/shard_map/ppermute | solution.py:194
  101.8 24.6 %collective-permute-start.13 = (bf16[512,256]{1,0:T(8,128)(2,1)}, bf16[512,256]{1,0:T(8,128)(2,1)S(1)}, u32[]{:S(2)}, u32[]{:S(2)}) collective-permute-start(bf16[512,256]{1,0:T(8,128)(2,1)} %get-tuple-element.76), channel_id=1, source_target_pairs={{0,1},{1,0},{2,3},{3,2},{4,5},{5,4},{6,7},{7,6},{8,9},{9,8},{10,11... | collective-permute-start | bytes 786440 | tf_op jit(solution)/shard_map/ppermute | solution.py:194
  106.2 21.2 %collective-permute-start.14 = (bf16[512,256]{1,0:T(8,128)(2,1)S(1)}, bf16[512,256]{1,0:T(8,128)(2,1)S(1)}, u32[]{:S(2)}, u32[]{:S(2)}) collective-permute-start(bf16[512,256]{1,0:T(8,128)(2,1)S(1)} %get-tuple-element.78), channel_id=1, source_target_pairs={{0,4},{1,8},{2,6},{3,10},{4,0},{5,12},{6,2},{7,14},{8,1},{9,16},{1... | collective-permute-start | bytes 786440 | tf_op jit(solution)/shard_map/ppermute | solution.py:194
  129.3 6.4 %collective-permute-start.16 = (bf16[512,256]{1,0:T(8,128)(2,1)S(1)}, bf16[512,256]{1,0:T(8,128)(2,1)S(1)}, u32[]{:S(2)}, u32[]{:S(2)}) collective-permute-start(bf16[512,256]{1,0:T(8,128)(2,1)S(1)} %shard_map.78), channel_id=1, source_target_pairs={{0,4},{1,8},{2,6},{3,10},{4,0},{5,12},{6,2},{7,14},{8,1},{9,16},{1... | collective-permute-start | bytes 786440 | tf_op jit(solution)/shard_map/ppermute | solution.py:194
  137.8 6.4 %collective-permute-start.18 = (bf16[512,256]{1,0:T(8,128)(2,1)S(1)}, bf16[512,256]{1,0:T(8,128)(2,1)S(1)}, u32[]{:S(2)}, u32[]{:S(2)}) collective-permute-start(bf16[512,256]{1,0:T(8,128)(2,1)S(1)} %shard_map.81), channel_id=1, source_target_pairs={{0,4},{1,8},{2,6},{3,10},{4,0},{5,12},{6,2},{7,14},{8,1},{9,16},{1... | collective-permute-start | bytes 786440 | tf_op jit(solution)/shard_map/ppermute | solution.py:194
  146.3 6.4 %collective-permute-start.20 = (bf16[512,256]{1,0:T(8,128)(2,1)S(1)}, bf16[512,256]{1,0:T(8,128)(2,1)S(1)}, u32[]{:S(2)}, u32[]{:S(2)}) collective-permute-start(bf16[512,256]{1,0:T(8,128)(2,1)S(1)} %shard_map.84), channel_id=1, source_target_pairs={{0,4},{1,8},{2,6},{3,10},{4,0},{5,12},{6,2},{7,14},{8,1},{9,16},{1... | collective-permute-start | bytes 786440 | tf_op jit(solution)/shard_map/ppermute | solution.py:194
  154.8 6.4 %collective-permute-start.22 = (bf16[512,256]{1,0:T(8,128)(2,1)S(1)}, bf16[512,256]{1,0:T(8,128)(2,1)S(1)}, u32[]{:S(2)}, u32[]{:S(2)}) collective-permute-start(bf16[512,256]{1,0:T(8,128)(2,1)S(1)} %shard_map.87), channel_id=1, source_target_pairs={{0,4},{1,8},{2,6},{3,10},{4,0},{5,12},{6,2},{7,14},{8,1},{9,16},{1... | collective-permute-start | bytes 786440 | tf_op jit(solution)/shard_map/ppermute | solution.py:194
  163.3 6.4 %collective-permute-start.24 = (bf16[512,256]{1,0:T(8,128)(2,1)S(1)}, bf16[512,256]{1,0:T(8,128)(2,1)S(1)}, u32[]{:S(2)}, u32[]{:S(2)}) collective-permute-start(bf16[512,256]{1,0:T(8,128)(2,1)S(1)} %shard_map.90), channel_id=1, source_target_pairs={{0,4},{1,8},{2,6},{3,10},{4,0},{5,12},{6,2},{7,14},{8,1},{9,16},{1... | collective-permute-start | bytes 786440 | tf_op jit(solution)/shard_map/ppermute | solution.py:194
  171.8 6.4 %collective-permute-start.26 = (bf16[512,256]{1,0:T(8,128)(2,1)S(1)}, bf16[512,256]{1,0:T(8,128)(2,1)S(1)}, u32[]{:S(2)}, u32[]{:S(2)}) collective-permute-start(bf16[512,256]{1,0:T(8,128)(2,1)S(1)} %shard_map.93), channel_id=1, source_target_pairs={{0,4},{1,8},{2,6},{3,10},{4,0},{5,12},{6,2},{7,14},{8,1},{9,16},{1... | collective-permute-start | bytes 786440 | tf_op jit(solution)/shard_map/ppermute | solution.py:194
  180.3 6.4 %collective-permute-start.28 = (bf16[512,256]{1,0:T(8,128)(2,1)S(1)}, bf16[512,256]{1,0:T(8,128)(2,1)S(1)}, u32[]{:S(2)}, u32[]{:S(2)}) collective-permute-start(bf16[512,256]{1,0:T(8,128)(2,1)S(1)} %shard_map.96), channel_id=1, source_target_pairs={{0,4},{1,8},{2,6},{3,10},{4,0},{5,12},{6,2},{7,14},{8,1},{9,16},{1... | collective-permute-start | bytes 786440 | tf_op jit(solution)/shard_map/ppermute | solution.py:194
  188.8 6.4 %collective-permute-start.30 = (bf16[512,256]{1,0:T(8,128)(2,1)S(1)}, bf16[512,256]{1,0:T(8,128)(2,1)S(1)}, u32[]{:S(2)}, u32[]{:S(2)}) collective-permute-start(bf16[512,256]{1,0:T(8,128)(2,1)S(1)} %shard_map.99), channel_id=1, source_target_pairs={{0,4},{1,8},{2,6},{3,10},{4,0},{5,12},{6,2},{7,14},{8,1},{9,16},{1... | collective-permute-start | bytes 786440 | tf_op jit(solution)/shard_map/ppermute | solution.py:194
  205.7 9.2 %collective-permute-start.33 = (bf16[256,1024]{1,0:T(8,128)(2,1)S(1)}, bf16[256,1024]{1,0:T(8,128)(2,1)S(1)}, u32[]{:S(2)}, u32[]{:S(2)}) collective-permute-start(bf16[256,1024]{1,0:T(8,128)(2,1)S(1)} %shard_map.103), channel_id=1, source_target_pairs={{0,8},{1,4},{2,10},{3,6},{4,1},{5,13},{6,3},{7,15},{8,0},{9,12},{1... | collective-permute-start | bytes 1572872 | tf_op jit(solution)/shard_map/ppermute | solution.py:194
  (19 other events, 284.8 us)
where the time goes:
time: 216 us
  Pallas kernels  100 us (46%)
  waiting for transfers between devices  71 us (33%)
  starting transfers between devices  37.5 us (17%)
  local copies, waits for them, and re-layouts  3.41 us (2%)
  other arithmetic  2.73 us (1%)
    ppermute x31, waiting for transfers between devices, send(): return lax.ppermute(x, AXES, ways[way])  59.1 us
    pallas_call x1, Pallas kernels, body(): call(functools.partial(stage_kernel, cap), (row,) * straight, [SMEM, HBM]...  48.9 us
    ppermute x31, starting transfers between devices, send(): return lax.ppermute(x, AXES, ways[way])  34.5 us
    pallas_call x8, Pallas kernels, body(): call(functools.partial(build_kernel, k, direct, cap, nblk, width), op_sha...  18.8 us
    ppermute x3, waiting for transfers between devices, body(): lax.ppermute(pieces[place], 'col', [(k, k ^ bit) for k in range(columns)])  11.9 us
    pallas_call x10, Pallas kernels, body(): call(functools.partial(finish_kernel, step == 0, last, width, edge), sds(...  11.2 us
    pallas_call x10, Pallas kernels, body(): acc = call(local_kernel, wide(F32), [VMEM] * 3, VMEM)(near_op, field, near)  9.76 us
    pallas_call x9, Pallas kernels, body(): call(functools.partial(ahead_kernel, width, edge), sent, specs, VMEM)  7.55 us
  transfers between devices with their start and end apart: 34, of which 12 were waited for; matrix products, arithmetic and copies ran while one was open for 0% of the time, Pallas kernels for 41%

commit v1 on v0

--- a/solution.py
+++ b/solution.py
@@ -49,12 +49,12 @@
     )
 
 
-def rotate_kernel(places, width, info, rotation, *refs):
+def rotate_kernel(places, width, flags, counts, rotation, *refs):
     pieces, out = refs[: len(places)], refs[len(places)]
     rot = rotation[...]
     high = rot.astype(BF16)
     low = (rot - high.astype(F32)).astype(BF16)
-    mine, used = info[0], info[1] * width
+    mine, used = flags[4], counts[0] * width
     for place, piece in zip(places, pieces):
         rows = piece.shape[0]
         first = pl.multiple_of((mine ^ place) * rows, rows)
@@ -64,48 +64,78 @@
         out[pl.ds(first, rows), :] = jnp.where(at < used, y, 0.0).astype(BF16)
 
 
-def build_kernel(step_at, direct, cap, nblk, width, meta, blocks, moved, *refs):
+def build_kernel(steps, cap, nblk, width, info, blocks, *refs):
+    moved, refs = refs[: len(steps)], refs[len(steps) :]
     near_out, far_out = refs[-7:-5]
     raw, total, near_buf, far_buf, sems = refs[-5:]
-    role, keep, half, edge, used = meta[0], meta[1], meta[2], meta[3], meta[4]
-    near_w = near_buf.shape[1]
-
-    t = row_of(half, step_at, direct, cap)
+    role, keep, half, edge, used = (info[i] for i in range(5))
+    near_w = near_buf.shape[2]
     parts = 4
     piece = nblk // parts
-    for flag, src in ((keep == 1, blocks.at[t]), (keep == 0, moved.at[0])):
-        copies = [
-            pltpu.make_async_copy(
-                src.at[pl.ds(p * piece, piece)], raw.at[pl.ds(p * piece, piece)], sems.at[p]
-            )
-            for p in range(parts)
+    rows = [row_of(half, step, direct, cap) for step, direct in steps]
+
+    def loads(n, src):
+        cut = lambda p: pl.ds(p * piece, piece)
+        return [
+            pltpu.make_async_copy(src.at[cut(p)], raw.at[n, cut(p)], sems.at[n, p]) for p in range(parts)
         ]
 
-        @pl.when(flag)
+    for flag in (1, 0):
+        @pl.when(keep == flag)
         def _():
-            for copy in copies:
-                copy.start()
-
-    total[...] = jnp.zeros_like(total)
-    for copy in copies:
-        copy.wait()
-    for k in range(nblk):
-        slot = meta[5 + t * nblk + k]
-        lanes = slot_place(slot, role, cap, nblk) * width
-        lanes = pl.ds(pl.multiple_of(lanes, width), width)
-        total[:, lanes] = total[:, lanes] + raw[k].astype(F32)
-    scale = jnp.where(t < used, 1.0, 0.0).astype(F32)
-    near_buf[...] = (total[:, :near_w] * scale).astype(BF16)
-    far_buf[...] = (total[:, near_w:] * jnp.where(edge == 1, 0.0, scale)).astype(BF16)
-    rows = pl.ds(pl.multiple_of(t * width, width), width)
-    stores = (
-        pltpu.make_async_copy(near_buf, near_out.at[rows, :], sems.at[parts]),
-        pltpu.make_async_copy(far_buf, far_out.at[rows, :], sems.at[parts + 1]),
-    )
-    for copy in stores:
-        copy.start()
+            for n, t in enumerate(rows):
+                for copy in loads(n, blocks.at[t] if flag else moved[n].at[0]):
+                    copy.start()
+
+    stores = []
+    for n, t in enumerate(rows):
+        total[...] = jnp.zeros_like(total)
+        for copy in loads(n, moved[n].at[0]):
+            copy.wait()
+        for k in range(nblk):
+            slot = info[5 + t * nblk + k]
+            lanes = slot_place(slot, role, cap, nblk) * width
+            lanes = pl.ds(pl.multiple_of(lanes, width), width)
+            total[:, lanes] = total[:, lanes] + raw[n, k].astype(F32)
+        scale = jnp.where(t < used, 1.0, 0.0).astype(F32)
+        near_buf[n] = (total[:, :near_w] * scale).astype(BF16)
+        far_buf[n] = (total[:, near_w:] * jnp.where(edge == 1, 0.0, scale)).astype(BF16)
+        at = pl.ds(pl.multiple_of(t * width, width), width)
+        stores.append(pltpu.make_async_copy(near_buf.at[n], near_out.at[at, :], sems.at[n, parts]))
+        stores.append(pltpu.make_async_copy(far_buf.at[n], far_out.at[at, :], sems.at[n, parts + 1]))
+        stores[-2].start()
+        stores[-1].start()
     for copy in stores:
         copy.wait()
+
+
+def gather_kernel(counts, cols, lists, out):
+    out[0] = counts[0]
+    at = 1
+    for t in range(cols.shape[0]):
+        for k in range(cols.shape[1]):
+            out[at] = cols[t, k]
+            at += 1
+    for way in range(lists.shape[1]):
+        for i in range(lists.shape[2]):
+            out[at] = lists[0, way, i]
+            at += 1
+
+
+def tables_kernel(flags, own, moved, info, send_lists):
+    keep = flags[1] == 1
+    get = lambda i: jnp.where(keep, own[i], moved[i])
+    for i in range(4):
+        info[i] = flags[i]
+    slots = info.shape[0] - 4
+    for i in range(slots):
+        info[4 + i] = get(i)
+    edge = (send_lists.shape[0] - 1) // 2
+    for i in range(edge):
+        up, down = get(slots + i), get(slots + edge + i)
+        send_lists[i] = jnp.where(flags[0] == 0, up, down)
+        send_lists[edge + i] = jnp.where(flags[0] == 0, down, up)
+    send_lists[2 * edge] = flags[1]
 
 
 def row_of(half, step, direct, cap):
@@ -113,16 +143,15 @@
     return jnp.where(flip == 1, cap - 1 - step, step)
 
 
-def stage_kernel(cap, half, blocks, *refs):
+def stage_kernel(steps, cap, flags, blocks, *refs):
     outs, sems = refs[:-1], refs[-1]
-    nblk = blocks.shape[1]
-    piece = nblk // 4
+    piece = blocks.shape[1] // 4
     copies = [
         pltpu.make_async_copy(
-            blocks.at[row_of(half[0], step, True, cap), pl.ds(p * piece, piece)],
-            out.at[0, pl.ds(p * piece, piece)], sems.at[step, p],
+            blocks.at[row_of(flags[2], step, True, cap), pl.ds(p * piece, piece)],
+            out.at[0, pl.ds(p * piece, piece)], sems.at[n, p],
         )
-        for step, out in enumerate(outs) for p in range(4)
+        for n, (step, out) in enumerate(zip(steps, outs)) for p in range(4)
     ]
     for copy in copies:
         copy.start()
@@ -206,12 +235,8 @@
     flag = lambda x: x.astype(jnp.int32)
     sds = jax.ShapeDtypeStruct
 
-    own_meta = jnp.concatenate([counts, cols.reshape(-1), lists.reshape(-1)])
-    meta = jnp.where(keep, own_meta, send(own_meta, "trade"))
-    tables = meta[1 + cap * nblk :].reshape(2, edge)
-    send_lists = jnp.where(role == 0, tables, tables[::-1]).reshape(-1)
-    send_lists = jnp.concatenate([send_lists, flag(keep)[None]])
-    info = jnp.concatenate([jnp.stack([flag(x) for x in (role, keep, half, at_edge)]), meta[: 1 + cap * nblk]])
+    ints = lambda n: sds((n,), jnp.int32)
+    flags = jnp.stack([flag(x) for x in (role, keep, half, at_edge, c)])
 
     pieces = {0: vectors.astype(BF16)}
     bit = columns // 2
@@ -226,34 +251,53 @@
     relays = cap // 2 - 1
     straight = cap - relays
     row = sds((1, nblk, width, width), BF16)
-    staged = call(
-        functools.partial(stage_kernel, cap), (row,) * straight, [SMEM, HBM], (ANY,) * straight,
-        scratch=(pltpu.SemaphoreType.DMA((straight, 4)),),
-    )(flag(half)[None], held)
-    moved = [(k, True, send(x, "trade")) for k, x in enumerate(staged)]
-    moved[-1:-1] = [(k, False, send(moved[k][2], "across")) for k in range(relays)]
+
+    def stage(*steps):
+        return call(
+            functools.partial(stage_kernel, steps, cap), (row,) * len(steps), [SMEM, HBM], (VMEM,) * len(steps),
+            scratch=(pltpu.SemaphoreType.DMA((len(steps), 4)),),
+        )(flags, held)
+
+    staged = stage(0) + stage(*range(1, straight - 1)) + stage(straight - 1)
+    direct = [send(x, "trade") for x in staged]
+    relayed = [send(x, "across") for x in direct[:relays]]
+
+    n_slots = 1 + cap * nblk
+    own = call(gather_kernel, ints(n_slots + 2 * edge), [SMEM] * 3, SMEM)(counts, cols, lists)
+    info, send_lists = call(
+        tables_kernel, (ints(4 + n_slots), ints(2 * edge + 1)), [SMEM] * 3, (SMEM, SMEM)
+    )(flags, own, send(own, "trade"))
 
     field = call(
         functools.partial(rotate_kernel, tuple(pieces), width),
-        sds((height, panel), BF16), [SMEM, VMEM] + [VMEM] * len(pieces), VMEM,
-    )(jnp.stack([c.astype(jnp.int32), counts[0]]), rotation, *pieces.values())
+        sds((height, panel), BF16), [SMEM, SMEM, VMEM] + [VMEM] * len(pieces), VMEM,
+    )(flags, counts, rotation, *pieces.values())
     moved_field = send(field, "trade")
 
     ops = ()
     op_shapes = (sds((height, height + edge * width), BF16), sds((height, edge * width), BF16))
-    for k, direct, rowk in moved:
+    arrived = {(k, True): x for k, x in enumerate(direct)}
+    arrived.update({(k, False): x for k, x in enumerate(relayed)})
+    lots = [
+        [(k, True) for k in range(straight - 1)],
+        [(k, False) for k in range(relays - 1)],
+        [(relays - 1, False)],
+        [(straight - 1, True)],
+    ]
+    for lot in lots:
+        n = len(lot)
         ops = call(
-            functools.partial(build_kernel, k, direct, cap, nblk, width),
-            op_shapes, [SMEM, HBM, ANY] + [ANY] * len(ops), (ANY, ANY),
+            functools.partial(build_kernel, tuple(lot), cap, nblk, width),
+            op_shapes, [SMEM, HBM] + [ANY] * (n + len(ops)), (ANY, ANY),
             scratch=(
-                pltpu.VMEM((nblk, width, width), BF16),
+                pltpu.VMEM((n, nblk, width, width), BF16),
                 pltpu.VMEM((width, slots * width), F32),
-                pltpu.VMEM((width, height + edge * width), BF16),
-                pltpu.VMEM((width, edge * width), BF16),
-                pltpu.SemaphoreType.DMA((6,)),
+                pltpu.VMEM((n, width, height + edge * width), BF16),
+                pltpu.VMEM((n, width, edge * width), BF16),
+                pltpu.SemaphoreType.DMA((n, 6)),
             ),
-            aliases={3: 0, 4: 1} if ops else {},
-        )(info, held, rowk, *ops)
+            aliases={2 + n: 0, 3 + n: 1} if ops else {},
+        )(info, held, *(arrived[key] for key in lot), *ops)
     near_op, far_op = ops
 
     sent = sds((edge * width, panel), BF16)

time: 216 us -> 165 us (0.76)
  Pallas kernels: 100 us -> 51.3 us
  waiting for transfers between devices: 71 us -> 81.6 us
  starting transfers between devices: 37.5 us -> 28.2 us
  local copies, waits for them, and re-layouts: 3.41 us -> 0.1 us
    pallas_call x9, Pallas kernels: 67.8 us -> 20.6 us  [the longest x4 12.6 us: body(): call(functools.partial(build_kernel, tuple(lot), cap, nblk, width), op_sh...]
    ppermute x31, waiting for transfers between devices: 59.1 us -> 69.7 us  [send(): return lax.ppermute(x, AXES, ways[way])]
    ppermute x31, starting transfers between devices: 34.5 us -> 25.2 us  [send(): return lax.ppermute(x, AXES, ways[way])]
    unnamed x18 -> x6, local copies, waits for them, and re-layouts: 2.89 us -> 0.02 us
  transfers between devices with their start and end apart: 34 -> 34, of which waited for: 12 -> 21; matrix products, arithmetic and copies ran while one was open for 0% -> 0% of each run, Pallas kernels for 41% -> 24%
where the time goes in v1:
time: 165 us
  waiting for transfers between devices  81.6 us (49%)
  Pallas kernels  51.3 us (31%)
  starting transfers between devices  28.2 us (17%)
  other arithmetic  2.34 us (1%)
    ppermute x31, waiting for transfers between devices, send(): return lax.ppermute(x, AXES, ways[way])  69.7 us
    ppermute x31, starting transfers between devices, send(): return lax.ppermute(x, AXES, ways[way])  25.2 us
    pallas_call x4, Pallas kernels, body(): call(functools.partial(build_kernel, tuple(lot), cap, nblk, width), op_sh...  12.6 us
    ppermute x3, waiting for transfers between devices, body(): lax.ppermute(pieces[place], 'col', [(k, k ^ bit) for k in range(columns)])  11.9 us
    pallas_call x10, Pallas kernels, body(): call(functools.partial(finish_kernel, step == 0, last, width, edge), sds(...  11 us
    pallas_call x10, Pallas kernels, body(): acc = call(local_kernel, wide(F32), [VMEM] * 3, VMEM)(near_op, field, near)  9.76 us
    pallas_call x9, Pallas kernels, body(): call(functools.partial(ahead_kernel, width, edge), sent, specs, VMEM)  7.52 us
    pallas_call x3, Pallas kernels, stage(): call(functools.partial(stage_kernel, steps, cap), (row,) * len(steps), [S...  5.44 us
  transfers between devices with their start and end apart: 34, of which 21 were waited for; matrix products, arithmetic and copies ran while one was open for 0% of the time, Pallas kernels for 24%

profile of v1, /device:TPU:0, one launch (start us, length us, event | category | flops | bytes accessed | tf_op | source)
XLA Modules:
  0.0 164.7 jit_solution(1520114343123907580)
XLA Ops:
  1.3 3.1 %collective-permute-start.9 = (bf16[256,1024]{1,0:T(8,128)(2,1)S(1)}, bf16[256,1024]{1,0:T(8,128)(2,1)S(1)}, u32[]{:S(2)}, u32[]{:S(2)}) collective-permute-start(bf16[256,1024]{1,0:T(8,128)(2,1)S(1)} %convert_element_type.8.refs_0_), channel_id=1, source_target_pairs={{0,2},{1,3},{2,0},{3,1},{4,6},{5,7},{6,4},{7,5},{8,10},{9,11},{10,... | collective-permute-start | bytes 1572872 | tf_op jit(solution)/shard_map/ppermute | solution.py:245
  4.4 11.9 %collective-permute-done.9.refs_1_ = bf16[256,1024]{1,0:T(8,128)(2,1)S(1)} collective-permute-done((bf16[256,1024]{1,0:T(8,128)(2,1)S(1)}, bf16[256,1024]{1,0:T(8,128)(2,1)S(1)}, u32[]{:S(2)}, u32[]{:S(2)}) %collective-permute-start.9) | collective-permute-done | bytes 524320 | tf_op jit(solution)/shard_map/ppermute | solution.py:245
  16.4 2.1 %shard_map.67 = (bf16[1,16,128,128]{3,2,1,0:T(8,128)(2,1)S(1)}, bf16[1,16,128,128]{3,2,1,0:T(8,128)(2,1)S(1)}, bf16[1,16,128,128]{3,2,1,0:T(8,128)(2,1)S(1)}) custom-call(s32[5]{0:T(128)S(1)} %stack.31.flags, bf16[8,16,128,128]{3,2,1,0:T(8,128)(2,1)} %blocks.13), custom_call_target="tpu_custom_call" | custom-call | tf_op jit(solution)/shard_map/pallas_call | solution.py:256
  18.5 1.9 %collective-permute-start.6 = (bf16[1,16,128,128]{3,2,1,0:T(8,128)(2,1)S(1)}, bf16[1,16,128,128]{3,2,1,0:T(8,128)(2,1)S(1)}, u32[]{:S(2)}, u32[]{:S(2)}) collective-permute-start(bf16[1,16,128,128]{3,2,1,0:T(8,128)(2,1)S(1)} %get-tuple-element.50), channel_id=1, source_target_pairs={{0,8},{1,4},{2,10},{3,6},{4,1},{5,13},{6,3},{7,15},{8,0},{9,12},{1... | collective-permute-start | bytes 1572872 | tf_op jit(solution)/shard_map/ppermute | solution.py:223
  24.8 1.8 %shard_map.73.own = bf16[1024,256]{1,0:T(8,128)(2,1)S(1)} custom-call(s32[5]{0:T(128)S(1)} %stack.31.flags, s32[1]{0:T(128)S(6)} %copy.19.counts, f32[1024,256]{1,0:T(8,128)S(1)} %copy-done, bf16[256,1024]{1,0:T(8,128)(2,1)S(1)} %convert_element_type.8.refs_0_, bf16[256,1024]{1,0:T(8,128)(2,1)S(1)} %collective-permute-done.9.refs_1_, ...), custom_call_target="tpu_custom_call" | custom-call | tf_op jit(solution)/shard_map/pallas_call | solution.py:271
  28.2 1.9 %collective-permute-start = (s32[137]{0:T(256)S(1)}, s32[137]{0:T(256)S(1)}, u32[]{:S(2)}, u32[]{:S(2)}) collective-permute-start(s32[137]{0:T(256)S(1)} %shard_map.64.own), channel_id=1, source_target_pairs={{0,8},{1,4},{2,10},{3,6},{4,1},{5,13},{6,3},{7,15},{8,0},{9,12},{1... | collective-permute-start | bytes 1652 | tf_op jit(solution)/shard_map/ppermute | solution.py:223
  30.1 14.6 %collective-permute-done.moved = s32[137]{0:T(256)S(1)} collective-permute-done((s32[137]{0:T(256)S(1)}, s32[137]{0:T(256)S(1)}, u32[]{:S(2)}, u32[]{:S(2)}) %collective-permute-start) | collective-permute-done | bytes 580 | tf_op jit(solution)/shard_map/ppermute | solution.py:223
  53.8 6.0 %collective-permute-start.13 = (bf16[512,256]{1,0:T(8,128)(2,1)S(1)}, bf16[512,256]{1,0:T(8,128)(2,1)S(1)}, u32[]{:S(2)}, u32[]{:S(2)}) collective-permute-start(bf16[512,256]{1,0:T(8,128)(2,1)S(1)} %get-tuple-element.60), channel_id=1, source_target_pairs={{0,1},{1,0},{2,3},{3,2},{4,5},{5,4},{6,7},{7,6},{8,9},{9,8},{10,11... | collective-permute-start | bytes 786440 | tf_op jit(solution)/shard_map/ppermute | solution.py:223
  59.9 4.6 %shard_map.69 = (bf16[1024,1536]{1,0:T(8,128)(2,1)S(1)}, bf16[1024,512]{1,0:T(8,128)(2,1)S(1)}) custom-call(s32[133]{0:T(256)S(1)} %get-tuple-element.48.info, bf16[8,16,128,128]{3,2,1,0:T(8,128)(2,1)} %blocks.13, bf16[1,16,128,128]{3,2,1,0:T(8,128)(2,1)S(1)} %collective-permute-done.4.refs_0_, bf16[1,16,128,128]{3,2,1,0:T(8,128)(2,1)S(1)} %collective-permute-done.6.refs_1_, ...), custom_call_target="tpu_custom_call" | custom-call | tf_op jit(solution)/shard_map/pallas_call | solution.py:289
  64.5 3.1 %shard_map.70 = (bf16[1024,1536]{1,0:T(8,128)(2,1)S(1)}, bf16[1024,512]{1,0:T(8,128)(2,1)S(1)}) custom-call(s32[133]{0:T(256)S(1)} %get-tuple-element.48.info, bf16[8,16,128,128]{3,2,1,0:T(8,128)(2,1)} %blocks.13, bf16[1,16,128,128]{3,2,1,0:T(8,128)(2,1)S(1)} %collective-permute-done.5.refs_0_, ...), custom_call_target="tpu_custom_call", output_to_operand_aliasing={{0}: (4, {}), {1}: (5, {})} | custom-call | tf_op jit(solution)/shard_map/pallas_call | solution.py:289
  67.7 2.3 %shard_map.71 = (bf16[1024,1536]{1,0:T(8,128)(2,1)S(1)}, bf16[1024,512]{1,0:T(8,128)(2,1)S(1)}) custom-call(s32[133]{0:T(256)S(1)} %get-tuple-element.48.info, bf16[8,16,128,128]{3,2,1,0:T(8,128)(2,1)} %blocks.13, bf16[1,16,128,128]{3,2,1,0:T(8,128)(2,1)S(1)} %collective-permute-done.3.refs_0_, ...), custom_call_target="tpu_custom_call", output_to_operand_aliasing={{0}: (3, {}), {1}: (4, {})} | custom-call | tf_op jit(solution)/shard_map/pallas_call | solution.py:289
  70.0 2.5 %shard_map.72 = (bf16[1024,1536]{1,0:T(8,128)(2,1)S(1)}, bf16[1024,512]{1,0:T(8,128)(2,1)S(1)}) custom-call(s32[133]{0:T(256)S(1)} %get-tuple-element.48.info, bf16[8,16,128,128]{3,2,1,0:T(8,128)(2,1)} %blocks.13, bf16[1,16,128,128]{3,2,1,0:T(8,128)(2,1)S(1)} %collective-permute-done.1.refs_0_, ...), custom_call_target="tpu_custom_call", output_to_operand_aliasing={{0}: (3, {}), {1}: (4, {})} | custom-call | tf_op jit(solution)/shard_map/pallas_call | solution.py:289
  74.5 3.1 %collective-permute-start.15 = (bf16[512,256]{1,0:T(8,128)(2,1)S(1)}, bf16[512,256]{1,0:T(8,128)(2,1)S(1)}, u32[]{:S(2)}, u32[]{:S(2)}) collective-permute-start(bf16[512,256]{1,0:T(8,128)(2,1)S(1)} %get-tuple-element.64), channel_id=1, source_target_pairs={{0,1},{1,0},{2,3},{3,2},{4,5},{5,4},{6,7},{7,6},{8,9},{9,8},{10,11... | collective-permute-start | bytes 786440 | tf_op jit(solution)/shard_map/ppermute | solution.py:223
  79.8 5.0 %collective-permute-done.16.far = bf16[512,256]{1,0:T(8,128)(2,1)S(1)} collective-permute-done((bf16[512,256]{1,0:T(8,128)(2,1)S(1)}, bf16[512,256]{1,0:T(8,128)(2,1)S(1)}, u32[]{:S(2)}, u32[]{:S(2)}) %collective-permute-start.16) | collective-permute-done | bytes 262176 | tf_op jit(solution)/shard_map/ppermute | solution.py:223
  88.5 4.8 %collective-permute-done.18.far = bf16[512,256]{1,0:T(8,128)(2,1)S(1)} collective-permute-done((bf16[512,256]{1,0:T(8,128)(2,1)S(1)}, bf16[512,256]{1,0:T(8,128)(2,1)S(1)}, u32[]{:S(2)}, u32[]{:S(2)}) %collective-permute-start.18) | collective-permute-done | bytes 262176 | tf_op jit(solution)/shard_map/ppermute | solution.py:223
  96.8 4.9 %collective-permute-done.20.far = bf16[512,256]{1,0:T(8,128)(2,1)S(1)} collective-permute-done((bf16[512,256]{1,0:T(8,128)(2,1)S(1)}, bf16[512,256]{1,0:T(8,128)(2,1)S(1)}, u32[]{:S(2)}, u32[]{:S(2)}) %collective-permute-start.20) | collective-permute-done | bytes 262176 | tf_op jit(solution)/shard_map/ppermute | solution.py:223
  105.3 4.9 %collective-permute-done.22.far = bf16[512,256]{1,0:T(8,128)(2,1)S(1)} collective-permute-done((bf16[512,256]{1,0:T(8,128)(2,1)S(1)}, bf16[512,256]{1,0:T(8,128)(2,1)S(1)}, u32[]{:S(2)}, u32[]{:S(2)}) %collective-permute-start.22) | collective-permute-done | bytes 262176 | tf_op jit(solution)/shard_map/ppermute | solution.py:223
  113.7 4.9 %collective-permute-done.24.far = bf16[512,256]{1,0:T(8,128)(2,1)S(1)} collective-permute-done((bf16[512,256]{1,0:T(8,128)(2,1)S(1)}, bf16[512,256]{1,0:T(8,128)(2,1)S(1)}, u32[]{:S(2)}, u32[]{:S(2)}) %collective-permute-start.24) | collective-permute-done | bytes 262176 | tf_op jit(solution)/shard_map/ppermute | solution.py:223
  122.2 4.9 %collective-permute-done.26.far = bf16[512,256]{1,0:T(8,128)(2,1)S(1)} collective-permute-done((bf16[512,256]{1,0:T(8,128)(2,1)S(1)}, bf16[512,256]{1,0:T(8,128)(2,1)S(1)}, u32[]{:S(2)}, u32[]{:S(2)}) %collective-permute-start.26) | collective-permute-done | bytes 262176 | tf_op jit(solution)/shard_map/ppermute | solution.py:223
  130.7 4.9 %collective-permute-done.28.far = bf16[512,256]{1,0:T(8,128)(2,1)S(1)} collective-permute-done((bf16[512,256]{1,0:T(8,128)(2,1)S(1)}, bf16[512,256]{1,0:T(8,128)(2,1)S(1)}, u32[]{:S(2)}, u32[]{:S(2)}) %collective-permute-start.28) | collective-permute-done | bytes 262176 | tf_op jit(solution)/shard_map/ppermute | solution.py:223
  139.1 4.9 %collective-permute-done.30.far = bf16[512,256]{1,0:T(8,128)(2,1)S(1)} collective-permute-done((bf16[512,256]{1,0:T(8,128)(2,1)S(1)}, bf16[512,256]{1,0:T(8,128)(2,1)S(1)}, u32[]{:S(2)}, u32[]{:S(2)}) %collective-permute-start.30) | collective-permute-done | bytes 262176 | tf_op jit(solution)/shard_map/ppermute | solution.py:223
  144.0 1.9 %shard_map.100 = (f32[1024,256]{1,0:T(8,128)}, bf16[1024,256]{1,0:T(8,128)(2,1)S(1)}, bf16[512,256]{1,0:T(8,128)(2,1)S(1)}) custom-call(s32[9]{0:T(128)S(1)} %get-tuple-element.47.lists, f32[1024,256]{1,0:T(8,128)S(1)} %shard_map.98.acc, bf16[1024,512]{1,0:T(8,128)(2,1)S(1)} %get-tuple-element.61.far_op, bf16[512,256]{1,0:T(8,128)(2,1)S(1)} %collective-permute-done.30.far, ...), custom_call_target="tpu_custom_call" | custom-call | tf_op jit(solution)/shard_map/pallas_call | solution.py:318
  148.5 4.9 %collective-permute-done.32.far = bf16[512,256]{1,0:T(8,128)(2,1)S(1)} collective-permute-done((bf16[512,256]{1,0:T(8,128)(2,1)S(1)}, bf16[512,256]{1,0:T(8,128)(2,1)S(1)}, u32[]{:S(2)}, u32[]{:S(2)}) %collective-permute-start.32) | collective-permute-done | bytes 262176 | tf_op jit(solution)/shard_map/ppermute | solution.py:223
  154.5 9.2 %collective-permute-done.33 = bf16[256,1024]{1,0:T(8,128)(2,1)S(1)} collective-permute-done((bf16[256,1024]{1,0:T(8,128)(2,1)S(1)}, bf16[256,1024]{1,0:T(8,128)(2,1)S(1)}, u32[]{:S(2)}, u32[]{:S(2)}) %collective-permute-start.33) | collective-permute-done | bytes 524320 | tf_op jit(solution)/shard_map/ppermute | solution.py:223
  (93 shorter events, 49.8 us)
Async XLA Ops:
  1.3 15.0 %collective-permute-start.9 = (bf16[256,1024]{1,0:T(8,128)(2,1)S(1)}, bf16[256,1024]{1,0:T(8,128)(2,1)S(1)}, u32[]{:S(2)}, u32[]{:S(2)}) collective-permute-start(bf16[256,1024]{1,0:T(8,128)(2,1)S(1)} %convert_element_type.8.refs_0_), channel_id=1, source_target_pairs={{0,2},{1,3},{2,0},{3,1},{4,6},{5,7},{6,4},{7,5},{8,10},{9,11},{10,... | collective-permute-start | bytes 1572872 | tf_op jit(solution)/shard_map/ppermute | solution.py:245
  4.4 20.4 %collective-permute-start.10 = (bf16[256,1024]{1,0:T(8,128)(2,1)S(1)}, bf16[256,1024]{1,0:T(8,128)(2,1)S(1)}, u32[]{:S(2)}, u32[]{:S(2)}) collective-permute-start(bf16[256,1024]{1,0:T(8,128)(2,1)S(1)} %convert_element_type.8.refs_0_), channel_id=1, source_target_pairs={{0,1},{1,0},{2,3},{3,2},{4,5},{5,4},{6,7},{7,6},{8,9},{9,8},{10,11... | collective-permute-start | bytes 1572872 | tf_op jit(solution)/shard_map/ppermute | solution.py:245
  16.3 8.5 %collective-permute-start.11 = (bf16[256,1024]{1,0:T(8,128)(2,1)S(1)}, bf16[256,1024]{1,0:T(8,128)(2,1)S(1)}, u32[]{:S(2)}, u32[]{:S(2)}) collective-permute-start(bf16[256,1024]{1,0:T(8,128)(2,1)S(1)} %collective-permute-done.9.refs_1_), channel_id=1, source_target_pairs={{0,1},{1,0},{2,3},{3,2},{4,5},{5,4},{6,7},{7,6},{8,9},{9,8},{10,11... | collective-permute-start | bytes 1572872 | tf_op jit(solution)/shard_map/ppermute | solution.py:245
  18.5 28.0 %collective-permute-start.6 = (bf16[1,16,128,128]{3,2,1,0:T(8,128)(2,1)S(1)}, bf16[1,16,128,128]{3,2,1,0:T(8,128)(2,1)S(1)}, u32[]{:S(2)}, u32[]{:S(2)}) collective-permute-start(bf16[1,16,128,128]{3,2,1,0:T(8,128)(2,1)S(1)} %get-tuple-element.50), channel_id=1, source_target_pairs={{0,8},{1,4},{2,10},{3,6},{4,1},{5,13},{6,3},{7,15},{8,0},{9,12},{1... | collective-permute-start | bytes 1572872 | tf_op jit(solution)/shard_map/ppermute | solution.py:223
  22.0 25.1 %collective-permute-start.4 = (bf16[1,16,128,128]{3,2,1,0:T(8,128)(2,1)S(1)}, bf16[1,16,128,128]{3,2,1,0:T(8,128)(2,1)S(1)}, u32[]{:S(2)}, u32[]{:S(2)}) collective-permute-start(bf16[1,16,128,128]{3,2,1,0:T(8,128)(2,1)S(1)} %shard_map.68), channel_id=1, source_target_pairs={{0,8},{1,4},{2,10},{3,6},{4,1},{5,13},{6,3},{7,15},{8,0},{9,12},{1... | collective-permute-start | bytes 1572872 | tf_op jit(solution)/shard_map/ppermute | solution.py:223
  22.3 25.5 %collective-permute-start.2 = (bf16[1,16,128,128]{3,2,1,0:T(8,128)(2,1)S(1)}, bf16[1,16,128,128]{3,2,1,0:T(8,128)(2,1)S(1)}, u32[]{:S(2)}, u32[]{:S(2)}) collective-permute-start(bf16[1,16,128,128]{3,2,1,0:T(8,128)(2,1)S(1)} %get-tuple-element.49), channel_id=1, source_target_pairs={{0,8},{1,4},{2,10},{3,6},{4,1},{5,13},{6,3},{7,15},{8,0},{9,12},{1... | collective-permute-start | bytes 1572872 | tf_op jit(solution)/shard_map/ppermute | solution.py:223
  26.6 23.6 %collective-permute-start.12 = (bf16[1024,256]{1,0:T(8,128)(2,1)S(1)}, bf16[1024,256]{1,0:T(8,128)(2,1)S(1)}, u32[]{:S(2)}, u32[]{:S(2)}) collective-permute-start(bf16[1024,256]{1,0:T(8,128)(2,1)S(1)} %shard_map.73.own), channel_id=1, source_target_pairs={{0,8},{1,4},{2,10},{3,6},{4,1},{5,13},{6,3},{7,15},{8,0},{9,12},{1... | collective-permute-start | bytes 1572872 | tf_op jit(solution)/shard_map/ppermute | solution.py:223
  28.2 16.4 %collective-permute-start = (s32[137]{0:T(256)S(1)}, s32[137]{0:T(256)S(1)}, u32[]{:S(2)}, u32[]{:S(2)}) collective-permute-start(s32[137]{0:T(256)S(1)} %shard_map.64.own), channel_id=1, source_target_pairs={{0,8},{1,4},{2,10},{3,6},{4,1},{5,13},{6,3},{7,15},{8,0},{9,12},{1... | collective-permute-start | bytes 1652 | tf_op jit(solution)/shard_map/ppermute | solution.py:223
  44.7 9.2 %collective-permute-start.8 = (bf16[1,16,128,128]{3,2,1,0:T(8,128)(2,1)S(1)}, bf16[1,16,128,128]{3,2,1,0:T(8,128)(2,1)S(1)}, u32[]{:S(2)}, u32[]{:S(2)}) collective-permute-start(bf16[1,16,128,128]{3,2,1,0:T(8,128)(2,1)S(1)} %get-tuple-element.51), channel_id=1, source_target_pairs={{0,8},{1,4},{2,10},{3,6},{4,1},{5,13},{6,3},{7,15},{8,0},{9,12},{1... | collective-permute-start | bytes 1572872 | tf_op jit(solution)/shard_map/ppermute | solution.py:223
  46.5 13.3 %collective-permute-start.7 = (bf16[1,16,128,128]{3,2,1,0:T(8,128)(2,1)S(1)}, bf16[1,16,128,128]{3,2,1,0:T(8,128)(2,1)S(1)}, u32[]{:S(2)}, u32[]{:S(2)}) collective-permute-start(bf16[1,16,128,128]{3,2,1,0:T(8,128)(2,1)S(1)} %collective-permute-done.6.refs_1_), channel_id=1, source_target_pairs={{1,3},{3,1},{4,6},{6,4},{9,11},{11,9},{12,14},{14,12},{17,19},{19,... | collective-permute-start | bytes 1572872 | tf_op jit(solution)/shard_map/ppermute | solution.py:223
  47.2 17.4 %collective-permute-start.5 = (bf16[1,16,128,128]{3,2,1,0:T(8,128)(2,1)S(1)}, bf16[1,16,128,128]{3,2,1,0:T(8,128)(2,1)S(1)}, u32[]{:S(2)}, u32[]{:S(2)}) collective-permute-start(bf16[1,16,128,128]{3,2,1,0:T(8,128)(2,1)S(1)} %collective-permute-done.4.refs_0_), channel_id=1, source_target_pairs={{1,3},{3,1},{4,6},{6,4},{9,11},{11,9},{12,14},{14,12},{17,19},{19,... | collective-permute-start | bytes 1572872 | tf_op jit(solution)/shard_map/ppermute | solution.py:223
  47.9 19.8 %collective-permute-start.3 = (bf16[1,16,128,128]{3,2,1,0:T(8,128)(2,1)S(1)}, bf16[1,16,128,128]{3,2,1,0:T(8,128)(2,1)S(1)}, u32[]{:S(2)}, u32[]{:S(2)}) collective-permute-start(bf16[1,16,128,128]{3,2,1,0:T(8,128)(2,1)S(1)} %collective-permute-done.2.refs_2_), channel_id=1, source_target_pairs={{1,3},{3,1},{4,6},{6,4},{9,11},{11,9},{12,14},{14,12},{17,19},{19,... | collective-permute-start | bytes 1572872 | tf_op jit(solution)/shard_map/ppermute | solution.py:223
  50.3 19.7 %collective-permute-start.1 = (bf16[1,16,128,128]{3,2,1,0:T(8,128)(2,1)S(1)}, bf16[1,16,128,128]{3,2,1,0:T(8,128)(2,1)S(1)}, u32[]{:S(2)}, u32[]{:S(2)}) collective-permute-start(bf16[1,16,128,128]{3,2,1,0:T(8,128)(2,1)S(1)} %shard_map.66), channel_id=1, source_target_pairs={{0,8},{1,4},{2,10},{3,6},{4,1},{5,13},{6,3},{7,15},{8,0},{9,12},{1... | collective-permute-start | bytes 1572872 | tf_op jit(solution)/shard_map/ppermute | solution.py:223
  53.8 18.7 %collective-permute-start.13 = (bf16[512,256]{1,0:T(8,128)(2,1)S(1)}, bf16[512,256]{1,0:T(8,128)(2,1)S(1)}, u32[]{:S(2)}, u32[]{:S(2)}) collective-permute-start(bf16[512,256]{1,0:T(8,128)(2,1)S(1)} %get-tuple-element.60), channel_id=1, source_target_pairs={{0,1},{1,0},{2,3},{3,2},{4,5},{5,4},{6,7},{7,6},{8,9},{9,8},{10,11... | collective-permute-start | bytes 786440 | tf_op jit(solution)/shard_map/ppermute | solution.py:223
  59.8 13.7 %collective-permute-start.14 = (bf16[512,256]{1,0:T(8,128)(2,1)S(1)}, bf16[512,256]{1,0:T(8,128)(2,1)S(1)}, u32[]{:S(2)}, u32[]{:S(2)}) collective-permute-start(bf16[512,256]{1,0:T(8,128)(2,1)S(1)} %get-tuple-element.62), channel_id=1, source_target_pairs={{0,4},{1,8},{2,6},{3,10},{4,0},{5,12},{6,2},{7,14},{8,1},{9,16},{1... | collective-permute-start | bytes 786440 | tf_op jit(solution)/shard_map/ppermute | solution.py:223
  78.4 6.4 %collective-permute-start.16 = (bf16[512,256]{1,0:T(8,128)(2,1)S(1)}, bf16[512,256]{1,0:T(8,128)(2,1)S(1)}, u32[]{:S(2)}, u32[]{:S(2)}) collective-permute-start(bf16[512,256]{1,0:T(8,128)(2,1)S(1)} %shard_map.78), channel_id=1, source_target_pairs={{0,4},{1,8},{2,6},{3,10},{4,0},{5,12},{6,2},{7,14},{8,1},{9,16},{1... | collective-permute-start | bytes 786440 | tf_op jit(solution)/shard_map/ppermute | solution.py:223
  86.8 6.4 %collective-permute-start.18 = (bf16[512,256]{1,0:T(8,128)(2,1)S(1)}, bf16[512,256]{1,0:T(8,128)(2,1)S(1)}, u32[]{:S(2)}, u32[]{:S(2)}) collective-permute-start(bf16[512,256]{1,0:T(8,128)(2,1)S(1)} %shard_map.81), channel_id=1, source_target_pairs={{0,4},{1,8},{2,6},{3,10},{4,0},{5,12},{6,2},{7,14},{8,1},{9,16},{1... | collective-permute-start | bytes 786440 | tf_op jit(solution)/shard_map/ppermute | solution.py:223
  95.3 6.4 %collective-permute-start.20 = (bf16[512,256]{1,0:T(8,128)(2,1)S(1)}, bf16[512,256]{1,0:T(8,128)(2,1)S(1)}, u32[]{:S(2)}, u32[]{:S(2)}) collective-permute-start(bf16[512,256]{1,0:T(8,128)(2,1)S(1)} %shard_map.84), channel_id=1, source_target_pairs={{0,4},{1,8},{2,6},{3,10},{4,0},{5,12},{6,2},{7,14},{8,1},{9,16},{1... | collective-permute-start | bytes 786440 | tf_op jit(solution)/shard_map/ppermute | solution.py:223
  103.7 6.4 %collective-permute-start.22 = (bf16[512,256]{1,0:T(8,128)(2,1)S(1)}, bf16[512,256]{1,0:T(8,128)(2,1)S(1)}, u32[]{:S(2)}, u32[]{:S(2)}) collective-permute-start(bf16[512,256]{1,0:T(8,128)(2,1)S(1)} %shard_map.87), channel_id=1, source_target_pairs={{0,4},{1,8},{2,6},{3,10},{4,0},{5,12},{6,2},{7,14},{8,1},{9,16},{1... | collective-permute-start | bytes 786440 | tf_op jit(solution)/shard_map/ppermute | solution.py:223
  112.2 6.4 %collective-permute-start.24 = (bf16[512,256]{1,0:T(8,128)(2,1)S(1)}, bf16[512,256]{1,0:T(8,128)(2,1)S(1)}, u32[]{:S(2)}, u32[]{:S(2)}) collective-permute-start(bf16[512,256]{1,0:T(8,128)(2,1)S(1)} %shard_map.90), channel_id=1, source_target_pairs={{0,4},{1,8},{2,6},{3,10},{4,0},{5,12},{6,2},{7,14},{8,1},{9,16},{1... | collective-permute-start | bytes 786440 | tf_op jit(solution)/shard_map/ppermute | solution.py:223
  120.6 6.4 %collective-permute-start.26 = (bf16[512,256]{1,0:T(8,128)(2,1)S(1)}, bf16[512,256]{1,0:T(8,128)(2,1)S(1)}, u32[]{:S(2)}, u32[]{:S(2)}) collective-permute-start(bf16[512,256]{1,0:T(8,128)(2,1)S(1)} %shard_map.93), channel_id=1, source_target_pairs={{0,4},{1,8},{2,6},{3,10},{4,0},{5,12},{6,2},{7,14},{8,1},{9,16},{1... | collective-permute-start | bytes 786440 | tf_op jit(solution)/shard_map/ppermute | solution.py:223
  129.1 6.4 %collective-permute-start.28 = (bf16[512,256]{1,0:T(8,128)(2,1)S(1)}, bf16[512,256]{1,0:T(8,128)(2,1)S(1)}, u32[]{:S(2)}, u32[]{:S(2)}) collective-permute-start(bf16[512,256]{1,0:T(8,128)(2,1)S(1)} %shard_map.96), channel_id=1, source_target_pairs={{0,4},{1,8},{2,6},{3,10},{4,0},{5,12},{6,2},{7,14},{8,1},{9,16},{1... | collective-permute-start | bytes 786440 | tf_op jit(solution)/shard_map/ppermute | solution.py:223
  137.6 6.4 %collective-permute-start.30 = (bf16[512,256]{1,0:T(8,128)(2,1)S(1)}, bf16[512,256]{1,0:T(8,128)(2,1)S(1)}, u32[]{:S(2)}, u32[]{:S(2)}) collective-permute-start(bf16[512,256]{1,0:T(8,128)(2,1)S(1)} %shard_map.99), channel_id=1, source_target_pairs={{0,4},{1,8},{2,6},{3,10},{4,0},{5,12},{6,2},{7,14},{8,1},{9,16},{1... | collective-permute-start | bytes 786440 | tf_op jit(solution)/shard_map/ppermute | solution.py:223
  154.4 9.2 %collective-permute-start.33 = (bf16[256,1024]{1,0:T(8,128)(2,1)S(1)}, bf16[256,1024]{1,0:T(8,128)(2,1)S(1)}, u32[]{:S(2)}, u32[]{:S(2)}) collective-permute-start(bf16[256,1024]{1,0:T(8,128)(2,1)S(1)} %shard_map.103), channel_id=1, source_target_pairs={{0,8},{1,4},{2,10},{3,6},{4,1},{5,13},{6,3},{7,15},{8,0},{9,12},{1... | collective-permute-start | bytes 1572872 | tf_op jit(solution)/shard_map/ppermute | solution.py:223
  (13 other events, 46.7 us)

commit v2 on v1

v2 whole, which is shorter than its diff:
```python
import functools

import jax
import jax.numpy as jnp
from jax import lax
from jax.experimental import pallas as pl
from jax.experimental.pallas import tpu as pltpu
from jax.sharding import PartitionSpec as P


STEPS = 10
AXES = ("row", "col")
F32, BF16 = jnp.float32, jnp.bfloat16
VMEM = pl.BlockSpec(memory_space=pltpu.VMEM)
SMEM = pl.BlockSpec(memory_space=pltpu.SMEM)
HBM = pl.BlockSpec(memory_space=pltpu.HBM)
ANY = pl.BlockSpec(memory_space=pl.ANY)


def patterns(rows, cols):
    every = [(r, c) for r in range(rows) for c in range(cols)]
    keeps = lambda r, c: r % 2 == c % 2

    def far(r, c):
        to = r + 2 if c % 2 else r - 2
        return (to, c ^ 1) if 0 <= to < rows else (r ^ 1, c)

    ways = {
        "trade": lambda r, c: (r ^ 2, c) if keeps(r, c) else (r ^ 1, c ^ 1),
        "across": lambda r, c: (r, c ^ 2),
        "near": lambda r, c: (r, c ^ 1),
        "far": far,
    }
    at = lambda place: place[0] * cols + place[1]
    pairs = {name: [(at(p), at(way(*p))) for p in every] for name, way in ways.items()}
    pairs["across"] = [(at(p), at(ways["across"](*p))) for p in every if not keeps(*p)]
    return pairs


def call(kernel, outs, in_specs, out_specs, scratch=(), aliases={}, mib=12):
    return pl.pallas_call(
        kernel,
        out_shape=outs,
        in_specs=in_specs,
        out_specs=out_specs,
        scratch_shapes=scratch,
        input_output_aliases=aliases,
        compiler_params=pltpu.CompilerParams(vmem_limit_bytes=mib << 20),
    )


def here():
    r, c = lax.axis_index("row"), lax.axis_index("col")
    role = lax.rem(c, 2)
    keep = role == lax.rem(r, 2)
    half = lax.rem(lax.div(c, 2), 2)
    edge = jnp.where(role == 0, r < 2, r >= lax.axis_size("row") - 2)
    return role, keep, half, edge, c


def rotate_kernel(places, width, counts, rotation, *refs):
    pieces, out = refs[: len(places)], refs[len(places)]
    rot = rotation[...]
    high = rot.astype(BF16)
    low = (rot - high.astype(F32)).astype(BF16)
    mine, used = here()[4], counts[0] * width
    for place, piece in zip(places, pieces):
        rows = piece.shape[0]
        first = pl.multiple_of((mine ^ place) * rows, rows)
        x = piece[...]
        y = jnp.dot(x, high, preferred_element_type=F32) + jnp.dot(x, low, preferred_element_type=F32)
        at = first + lax.broadcasted_iota(jnp.int32, y.shape, 0)
        out[pl.ds(first, rows), :] = jnp.where(at < used, y, 0.0).astype(BF16)


def build_kernel(steps, cap, nblk, width, info, blocks, *refs):
    moved, refs = refs[: len(steps)], refs[len(steps) :]
    near_out, far_out, raw, total, sems = refs[-5:]
    role, keep, half, at_edge, _ = here()
    slots = total.shape[0]
    near_slots = near_out.shape[1] // width
    parts = 4
    piece = nblk // parts
    rows = [row_of(half, step, direct, cap) for step, direct in steps]

    def loads(n, t):
        cut = lambda p: pl.ds(p * piece, piece)
        return [
            pltpu.make_async_copy(blocks.at[t, cut(p)], raw.at[n, cut(p)], sems.at[n, p])
            for p in range(parts)
        ]

    def add(source, t):
        total[...] = jnp.zeros_like(total)
        for k in range(nblk):
            slot = slot_place(info[1 + t * nblk + k], role, cap, slots)
            total[slot] = total[slot] + source(k).astype(F32)

    @pl.when(keep)
    def _():
        for n, t in enumerate(rows):
            for copy in loads(n, t):
                copy.start()

    for n, t in enumerate(rows):
        @pl.when(keep)
        def _():
            for copy in loads(n, t):
                copy.wait()
            add(lambda k: raw[n, k], t)

        @pl.when(jnp.logical_not(keep))
        def _():
            add(lambda k: moved[n][0, k], t)

        scale = jnp.where(t < info[0], 2.0, 0.0).astype(F32)
        far_scale = jnp.where(at_edge, 0.0, scale)
        at = pl.ds(pl.multiple_of(t * width, width), width)
        for slot in range(slots):
            near = slot < near_slots
            lane = (slot if near else slot - near_slots) * width
            value = total[slot] * (scale if near else far_scale)
            (near_out if near else far_out)[at, lane : lane + width] = value.astype(BF16)


def gather_kernel(counts, cols, lists, out):
    out[0] = counts[0]
    at = 1
    for t in range(cols.shape[0]):
        for k in range(cols.shape[1]):
            out[at] = cols[t, k]
            at += 1
    for way in range(lists.shape[1]):
        for i in range(lists.shape[2]):
            out[at] = lists[0, way, i]
            at += 1


def tables_kernel(own, moved, info, send_lists):
    role, keep = here()[:2]
    get = lambda i: jnp.where(keep, own[i], moved[i])
    slots = info.shape[0]
    for i in range(slots):
        info[i] = get(i)
    edge = send_lists.shape[0] // 2
    for i in range(edge):
        up, down = get(slots + i), get(slots + edge + i)
        send_lists[i] = jnp.where(role == 0, up, down)
        send_lists[edge + i] = jnp.where(role == 0, down, up)


def row_of(half, step, direct, cap):
    flip = half if direct else 1 - half
    return jnp.where(flip == 1, cap - 1 - step, step)


def stage_kernel(steps, cap, blocks, *refs):
    outs, sems = refs[:-1], refs[-1]
    half = here()[2]
    piece = blocks.shape[1] // 4
    copies = [
        pltpu.make_async_copy(
            blocks.at[row_of(half, step, True, cap), pl.ds(p * piece, piece)],
            out.at[0, pl.ds(p * piece, piece)], sems.at[n, p],
        )
        for n, (step, out) in enumerate(zip(steps, outs)) for p in range(4)
    ]
    for copy in copies:
        copy.start()
    for copy in copies:
        copy.wait()


def slot_place(slot, role, cap, slots):
    edge = (slots - cap) // 2
    first = jnp.where(slot < edge, slot + slots - edge, slot - edge)
    second = jnp.where(slot < edge, slot + cap, jnp.where(slot < edge + cap, slot - edge, slot))
    return jnp.where(role == 0, first, second)


def pick(lists, first, edge, width):
    return [pl.ds(pl.multiple_of(lists[first + i] * width, width), width) for i in range(edge)]


def pack_kernel(width, edge, lists, own, moved, field, near_send, far_send):
    keep = here()[1]

    @pl.when(keep)
    def _():
        field[...] = own[...]

    @pl.when(jnp.logical_not(keep))
    def _():
        field[...] = moved[...]

    for first, send in ((0, near_send), (edge, far_send)):
        for i, rows in enumerate(pick(lists, first, edge, width)):
            send[i * width : (i + 1) * width, :] = field[rows, :]


def local_kernel(width, edge, lists, near_op, field, near, *refs):
    first = len(refs) == 4
    rows = field.shape[0]
    total = jnp.dot(near_op[:, :rows], field[...], preferred_element_type=F32) + jnp.dot(
        near_op[:, rows:], near[...], preferred_element_type=F32
    )
    acc = refs[1]
    acc[...] = total if first else total - refs[0][...].astype(F32)
    for i, at in enumerate(pick(lists, edge, edge, width)):
        if len(refs) > 2:
            refs[2][i * width : (i + 1) * width, :] = acc[at, :]
        if first:
            refs[3][i * width : (i + 1) * width, :] = refs[0][at, :]


def result_of(first, acc, far_op, far):
    total = acc[...] + jnp.dot(far_op[...], far[...], preferred_element_type=F32)
    return 0.5 * total if first else total


def ahead_kernel(first, acc, far_op, far, out):
    out[...] = result_of(first, acc, far_op, far).astype(BF16)


def finish_kernel(first, width, edge, lists, acc, far_op, far, *refs):
    field, near_send = refs[-2:]
    total = result_of(first, acc, far_op, far)
    if len(refs) > 2:
        refs[0][...] = total
    field[...] = total.astype(BF16)
    for i, rows in enumerate(pick(lists, 0, edge, width)):
        near_send[i * width : (i + 1) * width, :] = field[rows, :]


def last_kernel(acc, far_op, far, out):
    out[...] = result_of(False, acc, far_op, far).T.astype(BF16)


def body(vectors, rotation, blocks, cols, lists, counts):
    rows, columns = lax.axis_size("row"), lax.axis_size("col")
    ways = patterns(rows, columns)

    def send(x, way):
        return lax.ppermute(x, AXES, ways[way])

    r, c = lax.axis_index("row"), lax.axis_index("col")
    cap, nblk, width = blocks.shape[0], blocks.shape[1], blocks.shape[2]
    edge = lists.shape[2]
    panel = rotation.shape[1]
    height = cap * width
    slots = cap + 2 * edge
    sds = jax.ShapeDtypeStruct

    ints = lambda n: sds((n,), jnp.int32)

    pieces = {0: vectors.astype(BF16)}
    bit = columns // 2
    while bit:
        for place in list(pieces):
            pieces[place ^ bit] = lax.ppermute(
                pieces[place], "col", [(k, k ^ bit) for k in range(columns)]
            )
        bit //= 2

    held = pltpu.with_memory_space_constraint(blocks, pltpu.HBM)
    relays = cap // 2 - 1
    straight = cap - relays
    row = sds((1, nblk, width, width), BF16)

    def stage(*steps):
        return call(
            functools.partial(stage_kernel, steps, cap), (row,) * len(steps), [HBM], (VMEM,) * len(steps),
            scratch=(pltpu.SemaphoreType.DMA((len(steps), 4)),),
        )(held)

    staged = stage(0) + stage(*range(1, straight))
    direct = [send(x, "trade") for x in staged]
    relayed = [send(x, "across") for x in direct[:relays]]

    n_slots = 1 + cap * nblk
    own = call(gather_kernel, ints(n_slots + 2 * edge), [SMEM] * 3, SMEM)(counts, cols, lists)
    info, send_lists = call(
        tables_kernel, (ints(n_slots), ints(2 * edge)), [SMEM] * 2, (SMEM, SMEM)
    )(own, send(own, "trade"))

    field = call(
        functools.partial(rotate_kernel, tuple(pieces), width),
        sds((height, panel), BF16), [SMEM, VMEM] + [VMEM] * len(pieces), VMEM,
    )(counts, rotation, *pieces.values())
    moved_field = send(field, "trade")

    ops = ()
    op_shapes = (sds((height, height + edge * width), BF16), sds((height, edge * width), BF16))
    arrived = {(k, True): x for k, x in enumerate(direct)}
    arrived.update({(k, False): x for k, x in enumerate(relayed)})
    keys = [(k, True) for k in range(straight - 1)]
    cut = len(keys) // 2
    lots = [keys[:cut], keys[cut:], [(k, False) for k in range(relays - 1)]]
    lots += [[(relays - 1, False)], [(straight - 1, True)]]
    for lot in lots:
        n = len(lot)
        ops = call(
            functools.partial(build_kernel, tuple(lot), cap, nblk, width),
            op_shapes, [SMEM, HBM] + [VMEM] * (n + len(ops)), (VMEM, VMEM),
            scratch=(
                pltpu.VMEM((n, nblk, width, width), BF16),
                pltpu.VMEM((slots, width, width), F32),
                pltpu.SemaphoreType.DMA((n, 4)),
            ),
            aliases={2 + n: 0, 3 + n: 1} if ops else {},
        )(info, held, *(arrived[key] for key in lot), *ops)
    near_op, far_op = ops

    sent = sds((edge * width, panel), BF16)
    wide = lambda kind: sds((height, panel), kind)
    field, near_send, far_send = call(
        functools.partial(pack_kernel, width, edge), (wide(BF16), sent, sent),
        [SMEM, VMEM, VMEM], (VMEM,) * 3,
    )(send_lists, field, moved_field)
    older, newer = (), field
    part = sds((edge * width, panel), F32)
    for step in range(STEPS):
        far, near = send(far_send, "far"), send(near_send, "near")
        first, last = step == 0, step == STEPS - 1
        extra = (far_op,) if first else older
        outs = (wide(F32),) if last else (wide(F32), part)
        if first:
            outs += (sds((edge * width, edge * width), BF16),)
        mine = call(
            functools.partial(local_kernel, width, edge), outs,
            [SMEM] + [VMEM] * 4, (VMEM,) * len(outs),
        )(send_lists, near_op, field, near, *extra)
        if first:
            far_part = mine[2]
        if last:
            result = call(last_kernel, sds((panel, height), BF16), [VMEM] * 3, VMEM)(mine[0], far_op, far)
            continue
        far_send = call(
            functools.partial(ahead_kernel, first), sent, [VMEM] * 3, VMEM
        )(mine[1], far_part, far)
        outs = (wide(BF16), sent) if step == STEPS - 2 else (wide(F32), wide(BF16), sent)
        result = call(
            functools.partial(finish_kernel, first, width, edge), outs,
            [SMEM] + [VMEM] * 3, (VMEM,) * len(outs),
        )(send_lists, mine[0], far_op, far)
        older, newer = (newer,), result[0]
        field, near_send = result[-2:]
    keep = c % 2 == r % 2
    return jnp.where(keep, result, send(result, "trade")).astype(F32)


def solution(mesh):
    return jax.shard_map(
        body,
        mesh=mesh,
        in_specs=(
            P(("row", "col"), None),
            P(None, "col"),
            P("row", None, None, None),
            P("row", None),
            P("row", None, None),
            P("row"),
        ),
        out_specs=P("col", "row"),
        check_vma=False,
    )
```

time: 165 us -> 153 us (0.927)
  waiting for transfers between devices: 81.6 us -> 68.8 us
  starting transfers between devices: 28.2 us -> 34.2 us
  Pallas kernels: 51.3 us -> 46 us
    ppermute x31, waiting for transfers between devices: 69.7 us -> 56.8 us  [send(): return lax.ppermute(x, AXES, ways[way])]
    ppermute x31, starting transfers between devices: 25.2 us -> 31.1 us  [send(): return lax.ppermute(x, AXES, ways[way])]
    pallas_call x33 -> x32, Pallas kernels: 35 us -> 31.7 us  [the longest x10 15.5 us: body(): call(functools.partial(local_kernel, width, edge), outs, [SMEM] + [VMEM]...]
    pallas_call x4 -> x5, Pallas kernels: 12.6 us -> 11.1 us  [body(): call(functools.partial(build_kernel, tuple(lot), cap, nblk, width), op_sh...]
  transfers between devices with their start and end apart: 34 -> 34, of which waited for: 21 -> 13; matrix products, arithmetic and copies ran while one was open for 0% -> 0% of each run, Pallas kernels for 24% -> 24%
where the time goes in v2:
time: 153 us
  waiting for transfers between devices  68.8 us (45%)
  Pallas kernels  46 us (30%)
  starting transfers between devices  34.2 us (22%)
  other arithmetic  2.34 us (2%)
    ppermute x31, waiting for transfers between devices, send(): return lax.ppermute(x, AXES, ways[way])  56.8 us
    ppermute x31, starting transfers between devices, send(): return lax.ppermute(x, AXES, ways[way])  31.1 us
    pallas_call x10, Pallas kernels, body(): call(functools.partial(local_kernel, width, edge), outs, [SMEM] + [VMEM]...  15.5 us
    ppermute x3, waiting for transfers between devices, body(): lax.ppermute(pieces[place], 'col', [(k, k ^ bit) for k in range(columns)])  11.9 us
    pallas_call x5, Pallas kernels, body(): call(functools.partial(build_kernel, tuple(lot), cap, nblk, width), op_sh...  11.1 us
    pallas_call x9, Pallas kernels, body(): call(functools.partial(finish_kernel, first, width, edge), outs, [SMEM] +...  8.92 us
    ppermute x3, starting transfers between devices, body(): lax.ppermute(pieces[place], 'col', [(k, k ^ bit) for k in range(columns)])  3.07 us
  transfers between devices with their start and end apart: 34, of which 13 were waited for; matrix products, arithmetic and copies ran while one was open for 0% of the time, Pallas kernels for 24%

profile of v2, /device:TPU:0, one launch (start us, length us, event | category | flops | bytes accessed | tf_op | source)
XLA Modules:
  0.0 152.5 jit_solution(16774235386348945430)
XLA Ops:
  1.3 3.1 %collective-permute-start.9 = (bf16[256,1024]{1,0:T(8,128)(2,1)S(1)}, bf16[256,1024]{1,0:T(8,128)(2,1)S(1)}, u32[]{:S(2)}, u32[]{:S(2)}) collective-permute-start(bf16[256,1024]{1,0:T(8,128)(2,1)S(1)} %convert_element_type.6.refs_0_), channel_id=1, source_target_pairs={{0,2},{1,3},{2,0},{3,1},{4,6},{5,7},{6,4},{7,5},{8,10},{9,11},{10,... | collective-permute-start | bytes 1572872 | tf_op jit(solution)/shard_map/ppermute | solution.py:260
  4.4 11.9 %collective-permute-done.9.refs_1_ = bf16[256,1024]{1,0:T(8,128)(2,1)S(1)} collective-permute-done((bf16[256,1024]{1,0:T(8,128)(2,1)S(1)}, bf16[256,1024]{1,0:T(8,128)(2,1)S(1)}, u32[]{:S(2)}, u32[]{:S(2)}) %collective-permute-start.9) | collective-permute-done | bytes 524320 | tf_op jit(solution)/shard_map/ppermute | solution.py:260
  18.1 1.9 %collective-permute-start.6 = (bf16[1,16,128,128]{3,2,1,0:T(8,128)(2,1)S(1)}, bf16[1,16,128,128]{3,2,1,0:T(8,128)(2,1)S(1)}, u32[]{:S(2)}, u32[]{:S(2)}) collective-permute-start(bf16[1,16,128,128]{3,2,1,0:T(8,128)(2,1)S(1)} %get-tuple-element.73), channel_id=1, source_target_pairs={{0,8},{1,4},{2,10},{3,6},{4,1},{5,13},{6,3},{7,15},{8,0},{9,12},{1... | collective-permute-start | bytes 1572872 | tf_op jit(solution)/shard_map/ppermute | solution.py:244
  21.4 1.8 %collective-permute-start.2 = (bf16[1,16,128,128]{3,2,1,0:T(8,128)(2,1)S(1)}, bf16[1,16,128,128]{3,2,1,0:T(8,128)(2,1)S(1)}, u32[]{:S(2)}, u32[]{:S(2)}) collective-permute-start(bf16[1,16,128,128]{3,2,1,0:T(8,128)(2,1)S(1)} %get-tuple-element.72), channel_id=1, source_target_pairs={{0,8},{1,4},{2,10},{3,6},{4,1},{5,13},{6,3},{7,15},{8,0},{9,12},{1... | collective-permute-start | bytes 1572872 | tf_op jit(solution)/shard_map/ppermute | solution.py:244
  26.7 1.8 %collective-permute-start = (s32[137]{0:T(256)S(1)}, s32[137]{0:T(256)S(1)}, u32[]{:S(2)}, u32[]{:S(2)}) collective-permute-start(s32[137]{0:T(256)S(1)} %shard_map.64.own), channel_id=1, source_target_pairs={{0,8},{1,4},{2,10},{3,6},{4,1},{5,13},{6,3},{7,15},{8,0},{9,12},{1... | collective-permute-start | bytes 1652 | tf_op jit(solution)/shard_map/ppermute | solution.py:244
  28.6 15.6 %collective-permute-done.moved = s32[137]{0:T(256)S(1)} collective-permute-done((s32[137]{0:T(256)S(1)}, s32[137]{0:T(256)S(1)}, u32[]{:S(2)}, u32[]{:S(2)}) %collective-permute-start) | collective-permute-done | bytes 580 | tf_op jit(solution)/shard_map/ppermute | solution.py:244
  44.2 1.8 %collective-permute-start.8 = (bf16[1,16,128,128]{3,2,1,0:T(8,128)(2,1)S(1)}, bf16[1,16,128,128]{3,2,1,0:T(8,128)(2,1)S(1)}, u32[]{:S(2)}, u32[]{:S(2)}) collective-permute-start(bf16[1,16,128,128]{3,2,1,0:T(8,128)(2,1)S(1)} %get-tuple-element.74), channel_id=1, source_target_pairs={{0,8},{1,4},{2,10},{3,6},{4,1},{5,13},{6,3},{7,15},{8,0},{9,12},{1... | collective-permute-start | bytes 1572872 | tf_op jit(solution)/shard_map/ppermute | solution.py:244
  50.4 3.0 %collective-permute-done.8.refs_1_ = bf16[1,16,128,128]{3,2,1,0:T(8,128)(2,1)S(1)} collective-permute-done((bf16[1,16,128,128]{3,2,1,0:T(8,128)(2,1)S(1)}, bf16[1,16,128,128]{3,2,1,0:T(8,128)(2,1)S(1)}, u32[]{:S(2)}, u32[]{:S(2)}) %collective-permute-start.8) | collective-permute-done | bytes 524320 | tf_op jit(solution)/shard_map/ppermute | solution.py:244
  53.4 4.3 %collective-permute-start.13 = (bf16[512,256]{1,0:T(8,128)(2,1)S(1)}, bf16[512,256]{1,0:T(8,128)(2,1)S(1)}, u32[]{:S(2)}, u32[]{:S(2)}) collective-permute-start(bf16[512,256]{1,0:T(8,128)(2,1)S(1)} %get-tuple-element.85), channel_id=1, source_target_pairs={{0,1},{1,0},{2,3},{3,2},{4,5},{5,4},{6,7},{7,6},{8,9},{9,8},{10,11... | collective-permute-start | bytes 786440 | tf_op jit(solution)/shard_map/ppermute | solution.py:244
  57.8 2.3 %shard_map.68 = (bf16[1024,1536]{1,0:T(8,128)(2,1)S(1)}, bf16[1024,512]{1,0:T(8,128)(2,1)S(1)}) custom-call(s32[129]{0:T(256)S(1)} %get-tuple-element.70.info, bf16[8,16,128,128]{3,2,1,0:T(8,128)(2,1)} %blocks.13, bf16[1,16,128,128]{3,2,1,0:T(8,128)(2,1)S(1)} %collective-permute-done.4.refs_0_, bf16[1,16,128,128]{3,2,1,0:T(8,128)(2,1)S(1)} %collective-permute-done.6.refs_1_), custom_call_target="tpu_custom_call" | custom-call | tf_op jit(solution)/shard_map/pallas_call | solution.py:302
  60.1 2.3 %shard_map.69 = (bf16[1024,1536]{1,0:T(8,128)(2,1)S(1)}, bf16[1024,512]{1,0:T(8,128)(2,1)S(1)}) custom-call(s32[129]{0:T(256)S(1)} %get-tuple-element.70.info, bf16[8,16,128,128]{3,2,1,0:T(8,128)(2,1)} %blocks.13, bf16[1,16,128,128]{3,2,1,0:T(8,128)(2,1)S(1)} %collective-permute-done.2.refs_0_, ...), custom_call_target="tpu_custom_call", output_to_operand_aliasing={{0}: (4, {}), {1}: (5, {})} | custom-call | tf_op jit(solution)/shard_map/pallas_call | solution.py:302
  62.5 2.3 %shard_map.70 = (bf16[1024,1536]{1,0:T(8,128)(2,1)S(1)}, bf16[1024,512]{1,0:T(8,128)(2,1)S(1)}) custom-call(s32[129]{0:T(256)S(1)} %get-tuple-element.70.info, bf16[8,16,128,128]{3,2,1,0:T(8,128)(2,1)} %blocks.13, bf16[1,16,128,128]{3,2,1,0:T(8,128)(2,1)S(1)} %collective-permute-done.5.refs_0_, ...), custom_call_target="tpu_custom_call", output_to_operand_aliasing={{0}: (4, {}), {1}: (5, {})} | custom-call | tf_op jit(solution)/shard_map/pallas_call | solution.py:302
  64.8 2.0 %shard_map.71 = (bf16[1024,1536]{1,0:T(8,128)(2,1)S(1)}, bf16[1024,512]{1,0:T(8,128)(2,1)S(1)}) custom-call(s32[129]{0:T(256)S(1)} %get-tuple-element.70.info, bf16[8,16,128,128]{3,2,1,0:T(8,128)(2,1)} %blocks.13, bf16[1,16,128,128]{3,2,1,0:T(8,128)(2,1)S(1)} %collective-permute-done.3.refs_0_, ...), custom_call_target="tpu_custom_call", output_to_operand_aliasing={{0}: (3, {}), {1}: (4, {})} | custom-call | tf_op jit(solution)/shard_map/pallas_call | solution.py:302
  66.8 2.2 %shard_map.72 = (bf16[1024,1536]{1,0:T(8,128)(2,1)S(1)}, bf16[1024,512]{1,0:T(8,128)(2,1)S(1)}) custom-call(s32[129]{0:T(256)S(1)} %get-tuple-element.70.info, bf16[8,16,128,128]{3,2,1,0:T(8,128)(2,1)} %blocks.13, bf16[1,16,128,128]{3,2,1,0:T(8,128)(2,1)S(1)} %collective-permute-done.1.refs_0_, ...), custom_call_target="tpu_custom_call", output_to_operand_aliasing={{0}: (3, {}), {1}: (4, {})} | custom-call | tf_op jit(solution)/shard_map/pallas_call | solution.py:302
  75.3 3.1 %collective-permute-done.16.far = bf16[512,256]{1,0:T(8,128)(2,1)S(1)} collective-permute-done((bf16[512,256]{1,0:T(8,128)(2,1)S(1)}, bf16[512,256]{1,0:T(8,128)(2,1)S(1)}, u32[]{:S(2)}, u32[]{:S(2)}) %collective-permute-start.16) | collective-permute-done | bytes 262176 | tf_op jit(solution)/shard_map/ppermute | solution.py:244
  83.1 3.2 %collective-permute-done.18.far = bf16[512,256]{1,0:T(8,128)(2,1)S(1)} collective-permute-done((bf16[512,256]{1,0:T(8,128)(2,1)S(1)}, bf16[512,256]{1,0:T(8,128)(2,1)S(1)}, u32[]{:S(2)}, u32[]{:S(2)}) %collective-permute-start.18) | collective-permute-done | bytes 262176 | tf_op jit(solution)/shard_map/ppermute | solution.py:244
  91.0 3.2 %collective-permute-done.20.far = bf16[512,256]{1,0:T(8,128)(2,1)S(1)} collective-permute-done((bf16[512,256]{1,0:T(8,128)(2,1)S(1)}, bf16[512,256]{1,0:T(8,128)(2,1)S(1)}, u32[]{:S(2)}, u32[]{:S(2)}) %collective-permute-start.20) | collective-permute-done | bytes 262176 | tf_op jit(solution)/shard_map/ppermute | solution.py:244
  98.9 3.2 %collective-permute-done.22.far = bf16[512,256]{1,0:T(8,128)(2,1)S(1)} collective-permute-done((bf16[512,256]{1,0:T(8,128)(2,1)S(1)}, bf16[512,256]{1,0:T(8,128)(2,1)S(1)}, u32[]{:S(2)}, u32[]{:S(2)}) %collective-permute-start.22) | collective-permute-done | bytes 262176 | tf_op jit(solution)/shard_map/ppermute | solution.py:244
  106.8 3.2 %collective-permute-done.24.far = bf16[512,256]{1,0:T(8,128)(2,1)S(1)} collective-permute-done((bf16[512,256]{1,0:T(8,128)(2,1)S(1)}, bf16[512,256]{1,0:T(8,128)(2,1)S(1)}, u32[]{:S(2)}, u32[]{:S(2)}) %collective-permute-start.24) | collective-permute-done | bytes 262176 | tf_op jit(solution)/shard_map/ppermute | solution.py:244
  114.7 3.2 %collective-permute-done.26.far = bf16[512,256]{1,0:T(8,128)(2,1)S(1)} collective-permute-done((bf16[512,256]{1,0:T(8,128)(2,1)S(1)}, bf16[512,256]{1,0:T(8,128)(2,1)S(1)}, u32[]{:S(2)}, u32[]{:S(2)}) %collective-permute-start.26) | collective-permute-done | bytes 262176 | tf_op jit(solution)/shard_map/ppermute | solution.py:244
  122.7 3.2 %collective-permute-done.28.far = bf16[512,256]{1,0:T(8,128)(2,1)S(1)} collective-permute-done((bf16[512,256]{1,0:T(8,128)(2,1)S(1)}, bf16[512,256]{1,0:T(8,128)(2,1)S(1)}, u32[]{:S(2)}, u32[]{:S(2)}) %collective-permute-start.28) | collective-permute-done | bytes 262176 | tf_op jit(solution)/shard_map/ppermute | solution.py:244
  130.6 3.2 %collective-permute-done.30.far = bf16[512,256]{1,0:T(8,128)(2,1)S(1)} collective-permute-done((bf16[512,256]{1,0:T(8,128)(2,1)S(1)}, bf16[512,256]{1,0:T(8,128)(2,1)S(1)}, u32[]{:S(2)}, u32[]{:S(2)}) %collective-permute-start.30) | collective-permute-done | bytes 262176 | tf_op jit(solution)/shard_map/ppermute | solution.py:244
  138.5 3.3 %collective-permute-done.32.far = bf16[512,256]{1,0:T(8,128)(2,1)S(1)} collective-permute-done((bf16[512,256]{1,0:T(8,128)(2,1)S(1)}, bf16[512,256]{1,0:T(8,128)(2,1)S(1)}, u32[]{:S(2)}, u32[]{:S(2)}) %collective-permute-start.32) | collective-permute-done | bytes 262176 | tf_op jit(solution)/shard_map/ppermute | solution.py:244
  142.3 9.1 %collective-permute-done.33 = bf16[256,1024]{1,0:T(8,128)(2,1)S(1)} collective-permute-done((bf16[256,1024]{1,0:T(8,128)(2,1)S(1)}, bf16[256,1024]{1,0:T(8,128)(2,1)S(1)}, u32[]{:S(2)}, u32[]{:S(2)}) %collective-permute-start.33) | collective-permute-done | bytes 524320 | tf_op jit(solution)/shard_map/ppermute | solution.py:244
  (92 shorter events, 56.9 us)
Async XLA Ops:
  1.3 15.0 %collective-permute-start.9 = (bf16[256,1024]{1,0:T(8,128)(2,1)S(1)}, bf16[256,1024]{1,0:T(8,128)(2,1)S(1)}, u32[]{:S(2)}, u32[]{:S(2)}) collective-permute-start(bf16[256,1024]{1,0:T(8,128)(2,1)S(1)} %convert_element_type.6.refs_0_), channel_id=1, source_target_pairs={{0,2},{1,3},{2,0},{3,1},{4,6},{5,7},{6,4},{7,5},{8,10},{9,11},{10,... | collective-permute-start | bytes 1572872 | tf_op jit(solution)/shard_map/ppermute | solution.py:260
  4.4 19.4 %collective-permute-start.10 = (bf16[256,1024]{1,0:T(8,128)(2,1)S(1)}, bf16[256,1024]{1,0:T(8,128)(2,1)S(1)}, u32[]{:S(2)}, u32[]{:S(2)}) collective-permute-start(bf16[256,1024]{1,0:T(8,128)(2,1)S(1)} %convert_element_type.6.refs_0_), channel_id=1, source_target_pairs={{0,1},{1,0},{2,3},{3,2},{4,5},{5,4},{6,7},{7,6},{8,9},{9,8},{10,11... | collective-permute-start | bytes 1572872 | tf_op jit(solution)/shard_map/ppermute | solution.py:260
  16.3 7.5 %collective-permute-start.11 = (bf16[256,1024]{1,0:T(8,128)(2,1)S(1)}, bf16[256,1024]{1,0:T(8,128)(2,1)S(1)}, u32[]{:S(2)}, u32[]{:S(2)}) collective-permute-start(bf16[256,1024]{1,0:T(8,128)(2,1)S(1)} %collective-permute-done.9.refs_1_), channel_id=1, source_target_pairs={{0,1},{1,0},{2,3},{3,2},{4,5},{5,4},{6,7},{7,6},{8,9},{9,8},{10,11... | collective-permute-start | bytes 1572872 | tf_op jit(solution)/shard_map/ppermute | solution.py:260
  18.1 28.0 %collective-permute-start.6 = (bf16[1,16,128,128]{3,2,1,0:T(8,128)(2,1)S(1)}, bf16[1,16,128,128]{3,2,1,0:T(8,128)(2,1)S(1)}, u32[]{:S(2)}, u32[]{:S(2)}) collective-permute-start(bf16[1,16,128,128]{3,2,1,0:T(8,128)(2,1)S(1)} %get-tuple-element.73), channel_id=1, source_target_pairs={{0,8},{1,4},{2,10},{3,6},{4,1},{5,13},{6,3},{7,15},{8,0},{9,12},{1... | collective-permute-start | bytes 1572872 | tf_op jit(solution)/shard_map/ppermute | solution.py:244
  21.1 25.7 %collective-permute-start.4 = (bf16[1,16,128,128]{3,2,1,0:T(8,128)(2,1)S(1)}, bf16[1,16,128,128]{3,2,1,0:T(8,128)(2,1)S(1)}, u32[]{:S(2)}, u32[]{:S(2)}) collective-permute-start(bf16[1,16,128,128]{3,2,1,0:T(8,128)(2,1)S(1)} %shard_map.67), channel_id=1, source_target_pairs={{0,8},{1,4},{2,10},{3,6},{4,1},{5,13},{6,3},{7,15},{8,0},{9,12},{1... | collective-permute-start | bytes 1572872 | tf_op jit(solution)/shard_map/ppermute | solution.py:244
  21.4 26.0 %collective-permute-start.2 = (bf16[1,16,128,128]{3,2,1,0:T(8,128)(2,1)S(1)}, bf16[1,16,128,128]{3,2,1,0:T(8,128)(2,1)S(1)}, u32[]{:S(2)}, u32[]{:S(2)}) collective-permute-start(bf16[1,16,128,128]{3,2,1,0:T(8,128)(2,1)S(1)} %get-tuple-element.72), channel_id=1, source_target_pairs={{0,8},{1,4},{2,10},{3,6},{4,1},{5,13},{6,3},{7,15},{8,0},{9,12},{1... | collective-permute-start | bytes 1572872 | tf_op jit(solution)/shard_map/ppermute | solution.py:244
  25.1 23.0 %collective-permute-start.12 = (bf16[1024,256]{1,0:T(8,128)(2,1)S(1)}, bf16[1024,256]{1,0:T(8,128)(2,1)S(1)}, u32[]{:S(2)}, u32[]{:S(2)}) collective-permute-start(bf16[1024,256]{1,0:T(8,128)(2,1)S(1)} %shard_map.73.own), channel_id=1, source_target_pairs={{0,8},{1,4},{2,10},{3,6},{4,1},{5,13},{6,3},{7,15},{8,0},{9,12},{1... | collective-permute-start | bytes 1572872 | tf_op jit(solution)/shard_map/ppermute | solution.py:244
  26.7 17.5 %collective-permute-start = (s32[137]{0:T(256)S(1)}, s32[137]{0:T(256)S(1)}, u32[]{:S(2)}, u32[]{:S(2)}) collective-permute-start(s32[137]{0:T(256)S(1)} %shard_map.64.own), channel_id=1, source_target_pairs={{0,8},{1,4},{2,10},{3,6},{4,1},{5,13},{6,3},{7,15},{8,0},{9,12},{1... | collective-permute-start | bytes 1652 | tf_op jit(solution)/shard_map/ppermute | solution.py:244
  44.2 9.2 %collective-permute-start.8 = (bf16[1,16,128,128]{3,2,1,0:T(8,128)(2,1)S(1)}, bf16[1,16,128,128]{3,2,1,0:T(8,128)(2,1)S(1)}, u32[]{:S(2)}, u32[]{:S(2)}) collective-permute-start(bf16[1,16,128,128]{3,2,1,0:T(8,128)(2,1)S(1)} %get-tuple-element.74), channel_id=1, source_target_pairs={{0,8},{1,4},{2,10},{3,6},{4,1},{5,13},{6,3},{7,15},{8,0},{9,12},{1... | collective-permute-start | bytes 1572872 | tf_op jit(solution)/shard_map/ppermute | solution.py:244
  46.0 11.7 %collective-permute-start.7 = (bf16[1,16,128,128]{3,2,1,0:T(8,128)(2,1)S(1)}, bf16[1,16,128,128]{3,2,1,0:T(8,128)(2,1)S(1)}, u32[]{:S(2)}, u32[]{:S(2)}) collective-permute-start(bf16[1,16,128,128]{3,2,1,0:T(8,128)(2,1)S(1)} %collective-permute-done.6.refs_1_), channel_id=1, source_target_pairs={{1,3},{3,1},{4,6},{6,4},{9,11},{11,9},{12,14},{14,12},{17,19},{19,... | collective-permute-start | bytes 1572872 | tf_op jit(solution)/shard_map/ppermute | solution.py:244
  46.7 15.7 %collective-permute-start.5 = (bf16[1,16,128,128]{3,2,1,0:T(8,128)(2,1)S(1)}, bf16[1,16,128,128]{3,2,1,0:T(8,128)(2,1)S(1)}, u32[]{:S(2)}, u32[]{:S(2)}) collective-permute-start(bf16[1,16,128,128]{3,2,1,0:T(8,128)(2,1)S(1)} %collective-permute-done.4.refs_0_), channel_id=1, source_target_pairs={{1,3},{3,1},{4,6},{6,4},{9,11},{11,9},{12,14},{14,12},{17,19},{19,... | collective-permute-start | bytes 1572872 | tf_op jit(solution)/shard_map/ppermute | solution.py:244
  47.4 17.4 %collective-permute-start.3 = (bf16[1,16,128,128]{3,2,1,0:T(8,128)(2,1)S(1)}, bf16[1,16,128,128]{3,2,1,0:T(8,128)(2,1)S(1)}, u32[]{:S(2)}, u32[]{:S(2)}) collective-permute-start(bf16[1,16,128,128]{3,2,1,0:T(8,128)(2,1)S(1)} %collective-permute-done.2.refs_0_), channel_id=1, source_target_pairs={{1,3},{3,1},{4,6},{6,4},{9,11},{11,9},{12,14},{14,12},{17,19},{19,... | collective-permute-start | bytes 1572872 | tf_op jit(solution)/shard_map/ppermute | solution.py:244
  48.1 18.7 %collective-permute-start.1 = (bf16[1,16,128,128]{3,2,1,0:T(8,128)(2,1)S(1)}, bf16[1,16,128,128]{3,2,1,0:T(8,128)(2,1)S(1)}, u32[]{:S(2)}, u32[]{:S(2)}) collective-permute-start(bf16[1,16,128,128]{3,2,1,0:T(8,128)(2,1)S(1)} %get-tuple-element.71), channel_id=1, source_target_pairs={{0,8},{1,4},{2,10},{3,6},{4,1},{5,13},{6,3},{7,15},{8,0},{9,12},{1... | collective-permute-start | bytes 1572872 | tf_op jit(solution)/shard_map/ppermute | solution.py:244
  53.4 15.6 %collective-permute-start.13 = (bf16[512,256]{1,0:T(8,128)(2,1)S(1)}, bf16[512,256]{1,0:T(8,128)(2,1)S(1)}, u32[]{:S(2)}, u32[]{:S(2)}) collective-permute-start(bf16[512,256]{1,0:T(8,128)(2,1)S(1)} %get-tuple-element.85), channel_id=1, source_target_pairs={{0,1},{1,0},{2,3},{3,2},{4,5},{5,4},{6,7},{7,6},{8,9},{9,8},{10,11... | collective-permute-start | bytes 786440 | tf_op jit(solution)/shard_map/ppermute | solution.py:244
  57.7 12.9 %collective-permute-start.14 = (bf16[512,256]{1,0:T(8,128)(2,1)S(1)}, bf16[512,256]{1,0:T(8,128)(2,1)S(1)}, u32[]{:S(2)}, u32[]{:S(2)}) collective-permute-start(bf16[512,256]{1,0:T(8,128)(2,1)S(1)} %get-tuple-element.88), channel_id=1, source_target_pairs={{0,4},{1,8},{2,6},{3,10},{4,0},{5,12},{6,2},{7,14},{8,1},{9,16},{1... | collective-permute-start | bytes 786440 | tf_op jit(solution)/shard_map/ppermute | solution.py:244
  72.0 6.4 %collective-permute-start.16 = (bf16[512,256]{1,0:T(8,128)(2,1)S(1)}, bf16[512,256]{1,0:T(8,128)(2,1)S(1)}, u32[]{:S(2)}, u32[]{:S(2)}) collective-permute-start(bf16[512,256]{1,0:T(8,128)(2,1)S(1)} %shard_map.78), channel_id=1, source_target_pairs={{0,4},{1,8},{2,6},{3,10},{4,0},{5,12},{6,2},{7,14},{8,1},{9,16},{1... | collective-permute-start | bytes 786440 | tf_op jit(solution)/shard_map/ppermute | solution.py:244
  79.9 6.4 %collective-permute-start.18 = (bf16[512,256]{1,0:T(8,128)(2,1)S(1)}, bf16[512,256]{1,0:T(8,128)(2,1)S(1)}, u32[]{:S(2)}, u32[]{:S(2)}) collective-permute-start(bf16[512,256]{1,0:T(8,128)(2,1)S(1)} %shard_map.81), channel_id=1, source_target_pairs={{0,4},{1,8},{2,6},{3,10},{4,0},{5,12},{6,2},{7,14},{8,1},{9,16},{1... | collective-permute-start | bytes 786440 | tf_op jit(solution)/shard_map/ppermute | solution.py:244
  87.8 6.4 %collective-permute-start.20 = (bf16[512,256]{1,0:T(8,128)(2,1)S(1)}, bf16[512,256]{1,0:T(8,128)(2,1)S(1)}, u32[]{:S(2)}, u32[]{:S(2)}) collective-permute-start(bf16[512,256]{1,0:T(8,128)(2,1)S(1)} %shard_map.84), channel_id=1, source_target_pairs={{0,4},{1,8},{2,6},{3,10},{4,0},{5,12},{6,2},{7,14},{8,1},{9,16},{1... | collective-permute-start | bytes 786440 | tf_op jit(solution)/shard_map/ppermute | solution.py:244
  95.7 6.4 %collective-permute-start.22 = (bf16[512,256]{1,0:T(8,128)(2,1)S(1)}, bf16[512,256]{1,0:T(8,128)(2,1)S(1)}, u32[]{:S(2)}, u32[]{:S(2)}) collective-permute-start(bf16[512,256]{1,0:T(8,128)(2,1)S(1)} %shard_map.87), channel_id=1, source_target_pairs={{0,4},{1,8},{2,6},{3,10},{4,0},{5,12},{6,2},{7,14},{8,1},{9,16},{1... | collective-permute-start | bytes 786440 | tf_op jit(solution)/shard_map/ppermute | solution.py:244
  103.6 6.4 %collective-permute-start.24 = (bf16[512,256]{1,0:T(8,128)(2,1)S(1)}, bf16[512,256]{1,0:T(8,128)(2,1)S(1)}, u32[]{:S(2)}, u32[]{:S(2)}) collective-permute-start(bf16[512,256]{1,0:T(8,128)(2,1)S(1)} %shard_map.90), channel_id=1, source_target_pairs={{0,4},{1,8},{2,6},{3,10},{4,0},{5,12},{6,2},{7,14},{8,1},{9,16},{1... | collective-permute-start | bytes 786440 | tf_op jit(solution)/shard_map/ppermute | solution.py:244
  111.5 6.4 %collective-permute-start.26 = (bf16[512,256]{1,0:T(8,128)(2,1)S(1)}, bf16[512,256]{1,0:T(8,128)(2,1)S(1)}, u32[]{:S(2)}, u32[]{:S(2)}) collective-permute-start(bf16[512,256]{1,0:T(8,128)(2,1)S(1)} %shard_map.93), channel_id=1, source_target_pairs={{0,4},{1,8},{2,6},{3,10},{4,0},{5,12},{6,2},{7,14},{8,1},{9,16},{1... | collective-permute-start | bytes 786440 | tf_op jit(solution)/shard_map/ppermute | solution.py:244
  119.4 6.4 %collective-permute-start.28 = (bf16[512,256]{1,0:T(8,128)(2,1)S(1)}, bf16[512,256]{1,0:T(8,128)(2,1)S(1)}, u32[]{:S(2)}, u32[]{:S(2)}) collective-permute-start(bf16[512,256]{1,0:T(8,128)(2,1)S(1)} %shard_map.96), channel_id=1, source_target_pairs={{0,4},{1,8},{2,6},{3,10},{4,0},{5,12},{6,2},{7,14},{8,1},{9,16},{1... | collective-permute-start | bytes 786440 | tf_op jit(solution)/shard_map/ppermute | solution.py:244
  127.4 6.4 %collective-permute-start.30 = (bf16[512,256]{1,0:T(8,128)(2,1)S(1)}, bf16[512,256]{1,0:T(8,128)(2,1)S(1)}, u32[]{:S(2)}, u32[]{:S(2)}) collective-permute-start(bf16[512,256]{1,0:T(8,128)(2,1)S(1)} %shard_map.99), channel_id=1, source_target_pairs={{0,4},{1,8},{2,6},{3,10},{4,0},{5,12},{6,2},{7,14},{8,1},{9,16},{1... | collective-permute-start | bytes 786440 | tf_op jit(solution)/shard_map/ppermute | solution.py:244
  142.2 9.2 %collective-permute-start.33 = (bf16[256,1024]{1,0:T(8,128)(2,1)S(1)}, bf16[256,1024]{1,0:T(8,128)(2,1)S(1)}, u32[]{:S(2)}, u32[]{:S(2)}) collective-permute-start(bf16[256,1024]{1,0:T(8,128)(2,1)S(1)} %shard_map.103), channel_id=1, source_target_pairs={{0,8},{1,4},{2,10},{3,6},{4,1},{5,13},{6,3},{7,15},{8,0},{9,12},{1... | collective-permute-start | bytes 1572872 | tf_op jit(solution)/shard_map/ppermute | solution.py:244
  (13 other events, 46.2 us)

commit v3 on v2

--- a/solution.py
+++ b/solution.py
@@ -9,6 +9,7 @@
 
 
 STEPS = 10
+PLAIN = 2
 AXES = ("row", "col")
 F32, BF16 = jnp.float32, jnp.bfloat16
 VMEM = pl.BlockSpec(memory_space=pltpu.VMEM)
@@ -198,42 +199,76 @@
             send[i * width : (i + 1) * width, :] = field[rows, :]
 
 
-def local_kernel(width, edge, lists, near_op, field, near, *refs):
-    first = len(refs) == 4
+def fetch(lists, table, sem):
+    return pltpu.make_async_copy(lists, table, sem)
+
+
+def local_kernel(width, edge, less, gives, lists, near_op, field, near, *refs):
+    table, sem = refs[-2:]
+    refs = list(refs[:-2])
+    copy = fetch(lists, table, sem)
+    copy.start()
     rows = field.shape[0]
+    older = refs.pop(0) if less else None
+    far_op = refs.pop(0) if gives == "both" else None
+    acc = refs.pop(0)
     total = jnp.dot(near_op[:, :rows], field[...], preferred_element_type=F32) + jnp.dot(
         near_op[:, rows:], near[...], preferred_element_type=F32
     )
-    acc = refs[1]
-    acc[...] = total if first else total - refs[0][...].astype(F32)
-    for i, at in enumerate(pick(lists, edge, edge, width)):
-        if len(refs) > 2:
-            refs[2][i * width : (i + 1) * width, :] = acc[at, :]
-        if first:
-            refs[3][i * width : (i + 1) * width, :] = refs[0][at, :]
+    acc[...] = total - older[...].astype(F32) if less else total
+    copy.wait()
+    if not gives:
+        return
+    part = refs.pop(0)
+    for i, at in enumerate(pick(table, edge, edge, width)):
+        part[i * width : (i + 1) * width, :] = acc[at, :].astype(part.dtype)
+        if gives == "both":
+            half, place = divmod(i, edge // 2)
+            refs[half][place * width : (place + 1) * width, :] = far_op[at, :]
 
 
 def result_of(first, acc, far_op, far):
-    total = acc[...] + jnp.dot(far_op[...], far[...], preferred_element_type=F32)
+    total = acc[...] + jnp.dot(far_op[...], far, preferred_element_type=F32)
     return 0.5 * total if first else total
 
 
-def ahead_kernel(first, acc, far_op, far, out):
-    out[...] = result_of(first, acc, far_op, far).astype(BF16)
-
-
-def finish_kernel(first, width, edge, lists, acc, far_op, far, *refs):
-    field, near_send = refs[-2:]
+def ahead_kernel(first, acc, low, high, far, out):
+    far_op = jnp.concatenate([low[...], high[...]], axis=0)
+    total = acc[...] + jnp.dot(far_op, far[...], preferred_element_type=F32)
+    out[...] = (0.5 * total if first else total).astype(BF16)
+
+
+def far_rows(part, low, high, sent):
+    op = jnp.concatenate([low[...], high[...]], axis=0)
+    total = part[...].astype(F32) + jnp.dot(op, sent[...], preferred_element_type=F32)
+    return total.astype(BF16)
+
+
+def finish_kernel(first, apart, wants, width, edge, lists, acc, far_op, *refs):
+    table, sem = refs[-2:]
+    refs = list(refs[:-2])
+    copy = fetch(lists, table, sem)
+    copy.start()
+    if apart:
+        far = far_rows(*refs[:4])
+        refs = refs[4:]
+    else:
+        far = refs.pop(0)[...]
     total = result_of(first, acc, far_op, far)
-    if len(refs) > 2:
-        refs[0][...] = total
+    value, part = wants
+    if value:
+        refs.pop(0)[...] = total
+    field, near_send = refs[:2]
     field[...] = total.astype(BF16)
-    for i, rows in enumerate(pick(lists, 0, edge, width)):
-        near_send[i * width : (i + 1) * width, :] = field[rows, :]
-
-
-def last_kernel(acc, far_op, far, out):
-    out[...] = result_of(False, acc, far_op, far).T.astype(BF16)
+    copy.wait()
+    sends = [(0, near_send)] + ([(edge, refs[2])] if part else [])
+    for begin, send in sends:
+        for i, rows in enumerate(pick(table, begin, edge, width)):
+            send[i * width : (i + 1) * width, :] = field[rows, :]
+
+
+def last_kernel(acc, far_op, part, low, high, sent, out):
+    out[...] = result_of(False, acc, far_op, far_rows(part, low, high, sent)).T.astype(BF16)
 
 
 def body(vectors, rotation, blocks, cols, lists, counts):
@@ -318,33 +353,55 @@
         [SMEM, VMEM, VMEM], (VMEM,) * 3,
     )(send_lists, field, moved_field)
     older, newer = (), field
-    part = sds((edge * width, panel), F32)
+    part = lambda kind: sds((edge * width, panel), kind)
+    square = sds((edge // 2 * width, edge * width), BF16)
+    table = (pltpu.SMEM((2 * edge,), jnp.int32), pltpu.SemaphoreType.DMA)
+    lists_at = pltpu.with_memory_space_constraint(send_lists, pltpu.HBM)
+    moved_part, sent_rows, theirs = None, {}, []
     for step in range(STEPS):
-        far, near = send(far_send, "far"), send(near_send, "near")
+        plain = step <= PLAIN
         first, last = step == 0, step == STEPS - 1
-        extra = (far_op,) if first else older
-        outs = (wide(F32),) if last else (wide(F32), part)
+        near = send(near_send, "near")
+        if plain:
+            far = send(far_send, "far")
+            sent_rows[step] = far_send
+        if 0 < step <= 2:
+            theirs.append(send(far_part[step - 1], "far"))
+        gives = "both" if first else "" if last else "one"
+        kind = F32 if step < PLAIN else BF16
+        outs = (wide(F32),) + ((part(kind),) if gives else ()) + ((square,) * 2 if first else ())
+        given = (lists_at, near_op, field, near) + older + ((far_op,) if first else ())
+        mine = call(
+            functools.partial(local_kernel, width, edge, not first, gives), outs,
+            [HBM] + [VMEM] * (len(given) - 1), (VMEM,) * len(outs), scratch=table,
+        )(*given)
+        acc = mine[0]
         if first:
-            outs += (sds((edge * width, edge * width), BF16),)
-        mine = call(
-            functools.partial(local_kernel, width, edge), outs,
-            [SMEM] + [VMEM] * 4, (VMEM,) * len(outs),
-        )(send_lists, near_op, field, near, *extra)
-        if first:
-            far_part = mine[2]
+            far_part = mine[2:]
+        arrived_part, moved_part = moved_part, None
+        if PLAIN <= step and not last:
+            moved_part = send(mine[1], "far")
         if last:
-            result = call(last_kernel, sds((panel, height), BF16), [VMEM] * 3, VMEM)(mine[0], far_op, far)
+            result = call(last_kernel, sds((panel, height), BF16), [VMEM] * 6, VMEM)(
+                acc, far_op, arrived_part, *theirs, sent_rows[step - 1]
+            )
             continue
-        far_send = call(
-            functools.partial(ahead_kernel, first), sent, [VMEM] * 3, VMEM
-        )(mine[1], far_part, far)
-        outs = (wide(BF16), sent) if step == STEPS - 2 else (wide(F32), wide(BF16), sent)
+        if step < PLAIN:
+            far_send = call(
+                functools.partial(ahead_kernel, first), sent, [VMEM] * 4, VMEM
+            )(mine[1], *far_part, far)
+        wants = (step < STEPS - 2, PLAIN <= step < STEPS - 2)
+        outs = ((wide(F32),) if wants[0] else ()) + (wide(BF16), sent) + ((sent,) if wants[1] else ())
+        given = (far,) if plain else (arrived_part, *theirs, sent_rows[step - 1])
         result = call(
-            functools.partial(finish_kernel, first, width, edge), outs,
-            [SMEM] + [VMEM] * 3, (VMEM,) * len(outs),
-        )(send_lists, mine[0], far_op, far)
-        older, newer = (newer,), result[0]
-        field, near_send = result[-2:]
+            functools.partial(finish_kernel, first, not plain, wants, width, edge), outs,
+            [HBM] + [VMEM] * (2 + len(given)), (VMEM,) * len(outs), scratch=table,
+        )(lists_at, acc, far_op, *given)
+        result = list(result)
+        older, newer = (newer,), result.pop(0) if wants[0] else None
+        field, near_send = result[:2]
+        if wants[1]:
+            sent_rows[step + 1] = result[2]
     keep = c % 2 == r % 2
     return jnp.where(keep, result, send(result, "trade")).astype(F32)
 

time: 153 us -> 156 us (1.020)
  waiting for transfers between devices: 68.8 us -> 76.9 us
  Pallas kernels: 46 us -> 39.3 us
    ppermute x31 -> x33, waiting for transfers between devices: 56.8 us -> 65 us  [send(): return lax.ppermute(x, AXES, ways[way])]
    pallas_call x29 -> x22, Pallas kernels: 27.5 us -> 20.8 us  [the longest x10 10.7 us: body(): call(functools.partial(local_kernel, width, edge, not first, gives), outs...]
    ppermute x31 -> x33, starting transfers between devices: 31.1 us -> 32.6 us  [send(): return lax.ppermute(x, AXES, ways[way])]
  transfers between devices with their start and end apart: 34 -> 36, of which waited for: 13 -> 15; matrix products, arithmetic and copies ran while one was open for 0% -> 0% of each run, Pallas kernels for 24% -> 19%
where the time goes in v3:
time: 156 us; the launch traced here: 155 us
  waiting for transfers between devices  76.9 us (49%)
  Pallas kernels  39.3 us (25%)
  starting transfers between devices  35.7 us (23%)
  other arithmetic  2.34 us (2%)
    ppermute x33, waiting for transfers between devices, send(): return lax.ppermute(x, AXES, ways[way])  65 us
    ppermute x33, starting transfers between devices, send(): return lax.ppermute(x, AXES, ways[way])  32.6 us
    ppermute x3, waiting for transfers between devices, body(): lax.ppermute(pieces[place], 'col', [(k, k ^ bit) for k in range(columns)])  11.9 us
    pallas_call x5, Pallas kernels, body(): call(functools.partial(build_kernel, tuple(lot), cap, nblk, width), op_sh...  11.1 us
    pallas_call x10, Pallas kernels, body(): call(functools.partial(local_kernel, width, edge, not first, gives), outs...  10.7 us
    pallas_call x9, Pallas kernels, body(): call(functools.partial(finish_kernel, first, not plain, wants, width, edg...  8.56 us
  transfers between devices with their start and end apart: 36, of which 15 were waited for; matrix products, arithmetic and copies ran while one was open for 0% of the time, Pallas kernels for 19%

profile of v3, /device:TPU:0, one launch (start us, length us, event | category | flops | bytes accessed | tf_op | source)
XLA Modules:
  0.0 155.4 jit_solution(14178917955847437436)
XLA Ops:
  1.3 3.1 %collective-permute-start.9 = (bf16[256,1024]{1,0:T(8,128)(2,1)S(1)}, bf16[256,1024]{1,0:T(8,128)(2,1)S(1)}, u32[]{:S(2)}, u32[]{:S(2)}) collective-permute-start(bf16[256,1024]{1,0:T(8,128)(2,1)S(1)} %convert_element_type.6.refs_0_), channel_id=1, source_target_pairs={{0,2},{1,3},{2,0},{3,1},{4,6},{5,7},{6,4},{7,5},{8,10},{9,11},{10,... | collective-permute-start | bytes 1572872 | tf_op jit(solution)/shard_map/ppermute | solution.py:295
  4.4 11.9 %collective-permute-done.9.refs_1_ = bf16[256,1024]{1,0:T(8,128)(2,1)S(1)} collective-permute-done((bf16[256,1024]{1,0:T(8,128)(2,1)S(1)}, bf16[256,1024]{1,0:T(8,128)(2,1)S(1)}, u32[]{:S(2)}, u32[]{:S(2)}) %collective-permute-start.9) | collective-permute-done | bytes 524320 | tf_op jit(solution)/shard_map/ppermute | solution.py:295
  18.1 1.9 %collective-permute-start.6 = (bf16[1,16,128,128]{3,2,1,0:T(8,128)(2,1)S(1)}, bf16[1,16,128,128]{3,2,1,0:T(8,128)(2,1)S(1)}, u32[]{:S(2)}, u32[]{:S(2)}) collective-permute-start(bf16[1,16,128,128]{3,2,1,0:T(8,128)(2,1)S(1)} %get-tuple-element.80), channel_id=1, source_target_pairs={{0,8},{1,4},{2,10},{3,6},{4,1},{5,13},{6,3},{7,15},{8,0},{9,12},{1... | collective-permute-start | bytes 1572872 | tf_op jit(solution)/shard_map/ppermute | solution.py:279
  26.7 1.8 %collective-permute-start = (s32[137]{0:T(256)S(1)}, s32[137]{0:T(256)S(1)}, u32[]{:S(2)}, u32[]{:S(2)}) collective-permute-start(s32[137]{0:T(256)S(1)} %shard_map.64.own), channel_id=1, source_target_pairs={{0,8},{1,4},{2,10},{3,6},{4,1},{5,13},{6,3},{7,15},{8,0},{9,12},{1... | collective-permute-start | bytes 1652 | tf_op jit(solution)/shard_map/ppermute | solution.py:279
  28.6 15.6 %collective-permute-done.moved = s32[137]{0:T(256)S(1)} collective-permute-done((s32[137]{0:T(256)S(1)}, s32[137]{0:T(256)S(1)}, u32[]{:S(2)}, u32[]{:S(2)}) %collective-permute-start) | collective-permute-done | bytes 580 | tf_op jit(solution)/shard_map/ppermute | solution.py:279
  44.2 1.8 %collective-permute-start.8 = (bf16[1,16,128,128]{3,2,1,0:T(8,128)(2,1)S(1)}, bf16[1,16,128,128]{3,2,1,0:T(8,128)(2,1)S(1)}, u32[]{:S(2)}, u32[]{:S(2)}) collective-permute-start(bf16[1,16,128,128]{3,2,1,0:T(8,128)(2,1)S(1)} %get-tuple-element.81), channel_id=1, source_target_pairs={{0,8},{1,4},{2,10},{3,6},{4,1},{5,13},{6,3},{7,15},{8,0},{9,12},{1... | collective-permute-start | bytes 1572872 | tf_op jit(solution)/shard_map/ppermute | solution.py:279
  50.4 3.0 %collective-permute-done.8.refs_1_ = bf16[1,16,128,128]{3,2,1,0:T(8,128)(2,1)S(1)} collective-permute-done((bf16[1,16,128,128]{3,2,1,0:T(8,128)(2,1)S(1)}, bf16[1,16,128,128]{3,2,1,0:T(8,128)(2,1)S(1)}, u32[]{:S(2)}, u32[]{:S(2)}) %collective-permute-start.8) | collective-permute-done | bytes 524320 | tf_op jit(solution)/shard_map/ppermute | solution.py:279
  53.4 4.3 %collective-permute-start.13 = (bf16[512,256]{1,0:T(8,128)(2,1)S(1)}, bf16[512,256]{1,0:T(8,128)(2,1)S(1)}, u32[]{:S(2)}, u32[]{:S(2)}) collective-permute-start(bf16[512,256]{1,0:T(8,128)(2,1)S(1)} %get-tuple-element.92), channel_id=1, source_target_pairs={{0,1},{1,0},{2,3},{3,2},{4,5},{5,4},{6,7},{7,6},{8,9},{9,8},{10,11... | collective-permute-start | bytes 786440 | tf_op jit(solution)/shard_map/ppermute | solution.py:279
  57.8 2.3 %shard_map.68 = (bf16[1024,1536]{1,0:T(8,128)(2,1)S(1)}, bf16[1024,512]{1,0:T(8,128)(2,1)S(1)}) custom-call(s32[129]{0:T(256)S(1)} %get-tuple-element.77.info, bf16[8,16,128,128]{3,2,1,0:T(8,128)(2,1)} %blocks.13, bf16[1,16,128,128]{3,2,1,0:T(8,128)(2,1)S(1)} %collective-permute-done.4.refs_0_, bf16[1,16,128,128]{3,2,1,0:T(8,128)(2,1)S(1)} %collective-permute-done.6.refs_1_), custom_call_target="tpu_custom_call" | custom-call | tf_op jit(solution)/shard_map/pallas_call | solution.py:337
  60.1 2.3 %shard_map.69 = (bf16[1024,1536]{1,0:T(8,128)(2,1)S(1)}, bf16[1024,512]{1,0:T(8,128)(2,1)S(1)}) custom-call(s32[129]{0:T(256)S(1)} %get-tuple-element.77.info, bf16[8,16,128,128]{3,2,1,0:T(8,128)(2,1)} %blocks.13, bf16[1,16,128,128]{3,2,1,0:T(8,128)(2,1)S(1)} %collective-permute-done.2.refs_0_, ...), custom_call_target="tpu_custom_call", output_to_operand_aliasing={{0}: (4, {}), {1}: (5, {})} | custom-call | tf_op jit(solution)/shard_map/pallas_call | solution.py:337
  62.5 2.3 %shard_map.70 = (bf16[1024,1536]{1,0:T(8,128)(2,1)S(1)}, bf16[1024,512]{1,0:T(8,128)(2,1)S(1)}) custom-call(s32[129]{0:T(256)S(1)} %get-tuple-element.77.info, bf16[8,16,128,128]{3,2,1,0:T(8,128)(2,1)} %blocks.13, bf16[1,16,128,128]{3,2,1,0:T(8,128)(2,1)S(1)} %collective-permute-done.5.refs_0_, ...), custom_call_target="tpu_custom_call", output_to_operand_aliasing={{0}: (4, {}), {1}: (5, {})} | custom-call | tf_op jit(solution)/shard_map/pallas_call | solution.py:337
  64.8 2.0 %shard_map.71 = (bf16[1024,1536]{1,0:T(8,128)(2,1)S(1)}, bf16[1024,512]{1,0:T(8,128)(2,1)S(1)}) custom-call(s32[129]{0:T(256)S(1)} %get-tuple-element.77.info, bf16[8,16,128,128]{3,2,1,0:T(8,128)(2,1)} %blocks.13, bf16[1,16,128,128]{3,2,1,0:T(8,128)(2,1)S(1)} %collective-permute-done.3.refs_0_, ...), custom_call_target="tpu_custom_call", output_to_operand_aliasing={{0}: (3, {}), {1}: (4, {})} | custom-call | tf_op jit(solution)/shard_map/pallas_call | solution.py:337
  66.8 2.2 %shard_map.72 = (bf16[1024,1536]{1,0:T(8,128)(2,1)S(1)}, bf16[1024,512]{1,0:T(8,128)(2,1)S(1)}) custom-call(s32[129]{0:T(256)S(1)} %get-tuple-element.77.info, bf16[8,16,128,128]{3,2,1,0:T(8,128)(2,1)} %blocks.13, bf16[1,16,128,128]{3,2,1,0:T(8,128)(2,1)S(1)} %collective-permute-done.1.refs_0_, ...), custom_call_target="tpu_custom_call", output_to_operand_aliasing={{0}: (3, {}), {1}: (4, {})} | custom-call | tf_op jit(solution)/shard_map/pallas_call | solution.py:337
  74.1 3.7 %collective-permute-done.16.refs_0_.far = bf16[512,256]{1,0:T(8,128)(2,1)S(1)} collective-permute-done((bf16[512,256]{1,0:T(8,128)(2,1)S(1)}, bf16[512,256]{1,0:T(8,128)(2,1)S(1)}, u32[]{:S(2)}, u32[]{:S(2)}) %collective-permute-start.16) | collective-permute-done | bytes 262176 | tf_op jit(solution)/shard_map/ppermute | solution.py:279
  81.9 3.8 %collective-permute-done.18.refs_0_ = bf16[512,256]{1,0:T(8,128)(2,1)S(1)} collective-permute-done((bf16[512,256]{1,0:T(8,128)(2,1)S(1)}, bf16[512,256]{1,0:T(8,128)(2,1)S(1)}, u32[]{:S(2)}, u32[]{:S(2)}) %collective-permute-start.18) | collective-permute-done | bytes 262176 | tf_op jit(solution)/shard_map/ppermute | solution.py:279
  93.0 2.8 %collective-permute-done.22.refs_2_.high = bf16[256,512]{1,0:T(8,128)(2,1)S(1)} collective-permute-done((bf16[256,512]{1,0:T(8,128)(2,1)S(1)}, bf16[256,512]{1,0:T(8,128)(2,1)S(1)}, u32[]{:S(2)}, u32[]{:S(2)}) %collective-permute-start.22) | collective-permute-done | bytes 262176 | tf_op jit(solution)/shard_map/ppermute | solution.py:279
  95.8 2.8 %collective-permute-done.20.refs_0_ = bf16[512,256]{1,0:T(8,128)(2,1)S(1)} collective-permute-done((bf16[512,256]{1,0:T(8,128)(2,1)S(1)}, bf16[512,256]{1,0:T(8,128)(2,1)S(1)}, u32[]{:S(2)}, u32[]{:S(2)}) %collective-permute-start.20) | collective-permute-done | bytes 262176 | tf_op jit(solution)/shard_map/ppermute | solution.py:279
  102.3 3.8 %collective-permute-done.24.refs_0_ = bf16[512,256]{1,0:T(8,128)(2,1)S(1)} collective-permute-done((bf16[512,256]{1,0:T(8,128)(2,1)S(1)}, bf16[512,256]{1,0:T(8,128)(2,1)S(1)}, u32[]{:S(2)}, u32[]{:S(2)}) %collective-permute-start.24) | collective-permute-done | bytes 262176 | tf_op jit(solution)/shard_map/ppermute | solution.py:279
  109.8 3.8 %collective-permute-done.26.refs_0_ = bf16[512,256]{1,0:T(8,128)(2,1)S(1)} collective-permute-done((bf16[512,256]{1,0:T(8,128)(2,1)S(1)}, bf16[512,256]{1,0:T(8,128)(2,1)S(1)}, u32[]{:S(2)}, u32[]{:S(2)}) %collective-permute-start.26) | collective-permute-done | bytes 262176 | tf_op jit(solution)/shard_map/ppermute | solution.py:279
  117.3 3.8 %collective-permute-done.28.refs_0_ = bf16[512,256]{1,0:T(8,128)(2,1)S(1)} collective-permute-done((bf16[512,256]{1,0:T(8,128)(2,1)S(1)}, bf16[512,256]{1,0:T(8,128)(2,1)S(1)}, u32[]{:S(2)}, u32[]{:S(2)}) %collective-permute-start.28) | collective-permute-done | bytes 262176 | tf_op jit(solution)/shard_map/ppermute | solution.py:279
  124.8 3.8 %collective-permute-done.30.refs_0_ = bf16[512,256]{1,0:T(8,128)(2,1)S(1)} collective-permute-done((bf16[512,256]{1,0:T(8,128)(2,1)S(1)}, bf16[512,256]{1,0:T(8,128)(2,1)S(1)}, u32[]{:S(2)}, u32[]{:S(2)}) %collective-permute-start.30) | collective-permute-done | bytes 262176 | tf_op jit(solution)/shard_map/ppermute | solution.py:279
  132.6 3.6 %collective-permute-done.32.refs_0_ = bf16[512,256]{1,0:T(8,128)(2,1)S(1)} collective-permute-done((bf16[512,256]{1,0:T(8,128)(2,1)S(1)}, bf16[512,256]{1,0:T(8,128)(2,1)S(1)}, u32[]{:S(2)}, u32[]{:S(2)}) %collective-permute-start.32) | collective-permute-done | bytes 262176 | tf_op jit(solution)/shard_map/ppermute | solution.py:279
  140.3 3.8 %collective-permute-done.34.part = bf16[512,256]{1,0:T(8,128)(2,1)S(1)} collective-permute-done((bf16[512,256]{1,0:T(8,128)(2,1)S(1)}, bf16[512,256]{1,0:T(8,128)(2,1)S(1)}, u32[]{:S(2)}, u32[]{:S(2)}) %collective-permute-start.34) | collective-permute-done | bytes 262176 | tf_op jit(solution)/shard_map/ppermute | solution.py:279
  145.2 9.1 %collective-permute-done.35 = bf16[256,1024]{1,0:T(8,128)(2,1)S(1)} collective-permute-done((bf16[256,1024]{1,0:T(8,128)(2,1)S(1)}, bf16[256,1024]{1,0:T(8,128)(2,1)S(1)}, u32[]{:S(2)}, u32[]{:S(2)}) %collective-permute-start.35) | collective-permute-done | bytes 524320 | tf_op jit(solution)/shard_map/ppermute | solution.py:279
  (91 shorter events, 55.1 us)
Async XLA Ops:
  1.3 15.0 %collective-permute-start.9 = (bf16[256,1024]{1,0:T(8,128)(2,1)S(1)}, bf16[256,1024]{1,0:T(8,128)(2,1)S(1)}, u32[]{:S(2)}, u32[]{:S(2)}) collective-permute-start(bf16[256,1024]{1,0:T(8,128)(2,1)S(1)} %convert_element_type.6.refs_0_), channel_id=1, source_target_pairs={{0,2},{1,3},{2,0},{3,1},{4,6},{5,7},{6,4},{7,5},{8,10},{9,11},{10,... | collective-permute-start | bytes 1572872 | tf_op jit(solution)/shard_map/ppermute | solution.py:295
  4.4 19.4 %collective-permute-start.10 = (bf16[256,1024]{1,0:T(8,128)(2,1)S(1)}, bf16[256,1024]{1,0:T(8,128)(2,1)S(1)}, u32[]{:S(2)}, u32[]{:S(2)}) collective-permute-start(bf16[256,1024]{1,0:T(8,128)(2,1)S(1)} %convert_element_type.6.refs_0_), channel_id=1, source_target_pairs={{0,1},{1,0},{2,3},{3,2},{4,5},{5,4},{6,7},{7,6},{8,9},{9,8},{10,11... | collective-permute-start | bytes 1572872 | tf_op jit(solution)/shard_map/ppermute | solution.py:295
  16.3 7.5 %collective-permute-start.11 = (bf16[256,1024]{1,0:T(8,128)(2,1)S(1)}, bf16[256,1024]{1,0:T(8,128)(2,1)S(1)}, u32[]{:S(2)}, u32[]{:S(2)}) collective-permute-start(bf16[256,1024]{1,0:T(8,128)(2,1)S(1)} %collective-permute-done.9.refs_1_), channel_id=1, source_target_pairs={{0,1},{1,0},{2,3},{3,2},{4,5},{5,4},{6,7},{7,6},{8,9},{9,8},{10,11... | collective-permute-start | bytes 1572872 | tf_op jit(solution)/shard_map/ppermute | solution.py:295
  18.1 28.0 %collective-permute-start.6 = (bf16[1,16,128,128]{3,2,1,0:T(8,128)(2,1)S(1)}, bf16[1,16,128,128]{3,2,1,0:T(8,128)(2,1)S(1)}, u32[]{:S(2)}, u32[]{:S(2)}) collective-permute-start(bf16[1,16,128,128]{3,2,1,0:T(8,128)(2,1)S(1)} %get-tuple-element.80), channel_id=1, source_target_pairs={{0,8},{1,4},{2,10},{3,6},{4,1},{5,13},{6,3},{7,15},{8,0},{9,12},{1... | collective-permute-start | bytes 1572872 | tf_op jit(solution)/shard_map/ppermute | solution.py:279
  21.1 25.7 %collective-permute-start.4 = (bf16[1,16,128,128]{3,2,1,0:T(8,128)(2,1)S(1)}, bf16[1,16,128,128]{3,2,1,0:T(8,128)(2,1)S(1)}, u32[]{:S(2)}, u32[]{:S(2)}) collective-permute-start(bf16[1,16,128,128]{3,2,1,0:T(8,128)(2,1)S(1)} %shard_map.67), channel_id=1, source_target_pairs={{0,8},{1,4},{2,10},{3,6},{4,1},{5,13},{6,3},{7,15},{8,0},{9,12},{1... | collective-permute-start | bytes 1572872 | tf_op jit(solution)/shard_map/ppermute | solution.py:279
  21.4 26.0 %collective-permute-start.2 = (bf16[1,16,128,128]{3,2,1,0:T(8,128)(2,1)S(1)}, bf16[1,16,128,128]{3,2,1,0:T(8,128)(2,1)S(1)}, u32[]{:S(2)}, u32[]{:S(2)}) collective-permute-start(bf16[1,16,128,128]{3,2,1,0:T(8,128)(2,1)S(1)} %get-tuple-element.79), channel_id=1, source_target_pairs={{0,8},{1,4},{2,10},{3,6},{4,1},{5,13},{6,3},{7,15},{8,0},{9,12},{1... | collective-permute-start | bytes 1572872 | tf_op jit(solution)/shard_map/ppermute | solution.py:279
  25.1 23.0 %collective-permute-start.12 = (bf16[1024,256]{1,0:T(8,128)(2,1)S(1)}, bf16[1024,256]{1,0:T(8,128)(2,1)S(1)}, u32[]{:S(2)}, u32[]{:S(2)}) collective-permute-start(bf16[1024,256]{1,0:T(8,128)(2,1)S(1)} %shard_map.73.own), channel_id=1, source_target_pairs={{0,8},{1,4},{2,10},{3,6},{4,1},{5,13},{6,3},{7,15},{8,0},{9,12},{1... | collective-permute-start | bytes 1572872 | tf_op jit(solution)/shard_map/ppermute | solution.py:279
  26.7 17.5 %collective-permute-start = (s32[137]{0:T(256)S(1)}, s32[137]{0:T(256)S(1)}, u32[]{:S(2)}, u32[]{:S(2)}) collective-permute-start(s32[137]{0:T(256)S(1)} %shard_map.64.own), channel_id=1, source_target_pairs={{0,8},{1,4},{2,10},{3,6},{4,1},{5,13},{6,3},{7,15},{8,0},{9,12},{1... | collective-permute-start | bytes 1652 | tf_op jit(solution)/shard_map/ppermute | solution.py:279
  44.2 9.2 %collective-permute-start.8 = (bf16[1,16,128,128]{3,2,1,0:T(8,128)(2,1)S(1)}, bf16[1,16,128,128]{3,2,1,0:T(8,128)(2,1)S(1)}, u32[]{:S(2)}, u32[]{:S(2)}) collective-permute-start(bf16[1,16,128,128]{3,2,1,0:T(8,128)(2,1)S(1)} %get-tuple-element.81), channel_id=1, source_target_pairs={{0,8},{1,4},{2,10},{3,6},{4,1},{5,13},{6,3},{7,15},{8,0},{9,12},{1... | collective-permute-start | bytes 1572872 | tf_op jit(solution)/shard_map/ppermute | solution.py:279
  46.0 11.7 %collective-permute-start.7 = (bf16[1,16,128,128]{3,2,1,0:T(8,128)(2,1)S(1)}, bf16[1,16,128,128]{3,2,1,0:T(8,128)(2,1)S(1)}, u32[]{:S(2)}, u32[]{:S(2)}) collective-permute-start(bf16[1,16,128,128]{3,2,1,0:T(8,128)(2,1)S(1)} %collective-permute-done.6.refs_1_), channel_id=1, source_target_pairs={{1,3},{3,1},{4,6},{6,4},{9,11},{11,9},{12,14},{14,12},{17,19},{19,... | collective-permute-start | bytes 1572872 | tf_op jit(solution)/shard_map/ppermute | solution.py:279
  46.7 15.7 %collective-permute-start.5 = (bf16[1,16,128,128]{3,2,1,0:T(8,128)(2,1)S(1)}, bf16[1,16,128,128]{3,2,1,0:T(8,128)(2,1)S(1)}, u32[]{:S(2)}, u32[]{:S(2)}) collective-permute-start(bf16[1,16,128,128]{3,2,1,0:T(8,128)(2,1)S(1)} %collective-permute-done.4.refs_0_), channel_id=1, source_target_pairs={{1,3},{3,1},{4,6},{6,4},{9,11},{11,9},{12,14},{14,12},{17,19},{19,... | collective-permute-start | bytes 1572872 | tf_op jit(solution)/shard_map/ppermute | solution.py:279
  47.4 17.4 %collective-permute-start.3 = (bf16[1,16,128,128]{3,2,1,0:T(8,128)(2,1)S(1)}, bf16[1,16,128,128]{3,2,1,0:T(8,128)(2,1)S(1)}, u32[]{:S(2)}, u32[]{:S(2)}) collective-permute-start(bf16[1,16,128,128]{3,2,1,0:T(8,128)(2,1)S(1)} %collective-permute-done.2.refs_0_), channel_id=1, source_target_pairs={{1,3},{3,1},{4,6},{6,4},{9,11},{11,9},{12,14},{14,12},{17,19},{19,... | collective-permute-start | bytes 1572872 | tf_op jit(solution)/shard_map/ppermute | solution.py:279
  48.1 18.7 %collective-permute-start.1 = (bf16[1,16,128,128]{3,2,1,0:T(8,128)(2,1)S(1)}, bf16[1,16,128,128]{3,2,1,0:T(8,128)(2,1)S(1)}, u32[]{:S(2)}, u32[]{:S(2)}) collective-permute-start(bf16[1,16,128,128]{3,2,1,0:T(8,128)(2,1)S(1)} %get-tuple-element.78), channel_id=1, source_target_pairs={{0,8},{1,4},{2,10},{3,6},{4,1},{5,13},{6,3},{7,15},{8,0},{9,12},{1... | collective-permute-start | bytes 1572872 | tf_op jit(solution)/shard_map/ppermute | solution.py:279
  53.4 15.6 %collective-permute-start.13 = (bf16[512,256]{1,0:T(8,128)(2,1)S(1)}, bf16[512,256]{1,0:T(8,128)(2,1)S(1)}, u32[]{:S(2)}, u32[]{:S(2)}) collective-permute-start(bf16[512,256]{1,0:T(8,128)(2,1)S(1)} %get-tuple-element.92), channel_id=1, source_target_pairs={{0,1},{1,0},{2,3},{3,2},{4,5},{5,4},{6,7},{7,6},{8,9},{9,8},{10,11... | collective-permute-start | bytes 786440 | tf_op jit(solution)/shard_map/ppermute | solution.py:279
  57.7 12.5 %collective-permute-start.14 = (bf16[512,256]{1,0:T(8,128)(2,1)S(1)}, bf16[512,256]{1,0:T(8,128)(2,1)S(1)}, u32[]{:S(2)}, u32[]{:S(2)}) collective-permute-start(bf16[512,256]{1,0:T(8,128)(2,1)S(1)} %get-tuple-element.95), channel_id=1, source_target_pairs={{0,4},{1,8},{2,6},{3,10},{4,0},{5,12},{6,2},{7,14},{8,1},{9,16},{1... | collective-permute-start | bytes 786440 | tf_op jit(solution)/shard_map/ppermute | solution.py:279
  71.3 6.4 %collective-permute-start.16 = (bf16[512,256]{1,0:T(8,128)(2,1)S(1)}, bf16[512,256]{1,0:T(8,128)(2,1)S(1)}, u32[]{:S(2)}, u32[]{:S(2)}) collective-permute-start(bf16[512,256]{1,0:T(8,128)(2,1)S(1)} %shard_map.78), channel_id=1, source_target_pairs={{0,4},{1,8},{2,6},{3,10},{4,0},{5,12},{6,2},{7,14},{8,1},{9,16},{1... | collective-permute-start | bytes 786440 | tf_op jit(solution)/shard_map/ppermute | solution.py:279
  79.3 6.4 %collective-permute-start.18 = (bf16[512,256]{1,0:T(8,128)(2,1)S(1)}, bf16[512,256]{1,0:T(8,128)(2,1)S(1)}, u32[]{:S(2)}, u32[]{:S(2)}) collective-permute-start(bf16[512,256]{1,0:T(8,128)(2,1)S(1)} %shard_map.81.refs_3_), channel_id=1, source_target_pairs={{0,4},{1,8},{2,6},{3,10},{4,0},{5,12},{6,2},{7,14},{8,1},{9,16},{1... | collective-permute-start | bytes 786440 | tf_op jit(solution)/shard_map/ppermute | solution.py:279
  86.6 6.4 %collective-permute-start.21 = (bf16[256,512]{1,0:T(8,128)(2,1)S(1)}, bf16[256,512]{1,0:T(8,128)(2,1)S(1)}, u32[]{:S(2)}, u32[]{:S(2)}) collective-permute-start(bf16[256,512]{1,0:T(8,128)(2,1)S(1)} %get-tuple-element.100.low), channel_id=1, source_target_pairs={{0,4},{1,8},{2,6},{3,10},{4,0},{5,12},{6,2},{7,14},{8,1},{9,16},{1... | collective-permute-start | bytes 786440 | tf_op jit(solution)/shard_map/ppermute | solution.py:279
  88.2 7.6 %collective-permute-start.22 = (bf16[256,512]{1,0:T(8,128)(2,1)S(1)}, bf16[256,512]{1,0:T(8,128)(2,1)S(1)}, u32[]{:S(2)}, u32[]{:S(2)}) collective-permute-start(bf16[256,512]{1,0:T(8,128)(2,1)S(1)} %get-tuple-element.101.high), channel_id=1, source_target_pairs={{0,4},{1,8},{2,6},{3,10},{4,0},{5,12},{6,2},{7,14},{8,1},{9,16},{1... | collective-permute-start | bytes 786440 | tf_op jit(solution)/shard_map/ppermute | solution.py:279
  88.6 10.0 %collective-permute-start.20 = (bf16[512,256]{1,0:T(8,128)(2,1)S(1)}, bf16[512,256]{1,0:T(8,128)(2,1)S(1)}, u32[]{:S(2)}, u32[]{:S(2)}) collective-permute-start(bf16[512,256]{1,0:T(8,128)(2,1)S(1)} %get-tuple-element.111), channel_id=1, source_target_pairs={{0,4},{1,8},{2,6},{3,10},{4,0},{5,12},{6,2},{7,14},{8,1},{9,16},{1... | collective-permute-start | bytes 786440 | tf_op jit(solution)/shard_map/ppermute | solution.py:279
  99.7 6.4 %collective-permute-start.24 = (bf16[512,256]{1,0:T(8,128)(2,1)S(1)}, bf16[512,256]{1,0:T(8,128)(2,1)S(1)}, u32[]{:S(2)}, u32[]{:S(2)}) collective-permute-start(bf16[512,256]{1,0:T(8,128)(2,1)S(1)} %get-tuple-element.116), channel_id=1, source_target_pairs={{0,4},{1,8},{2,6},{3,10},{4,0},{5,12},{6,2},{7,14},{8,1},{9,16},{1... | collective-permute-start | bytes 786440 | tf_op jit(solution)/shard_map/ppermute | solution.py:279
  107.2 6.4 %collective-permute-start.26 = (bf16[512,256]{1,0:T(8,128)(2,1)S(1)}, bf16[512,256]{1,0:T(8,128)(2,1)S(1)}, u32[]{:S(2)}, u32[]{:S(2)}) collective-permute-start(bf16[512,256]{1,0:T(8,128)(2,1)S(1)} %get-tuple-element.122), channel_id=1, source_target_pairs={{0,4},{1,8},{2,6},{3,10},{4,0},{5,12},{6,2},{7,14},{8,1},{9,16},{1... | collective-permute-start | bytes 786440 | tf_op jit(solution)/shard_map/ppermute | solution.py:279
  114.7 6.4 %collective-permute-start.28 = (bf16[512,256]{1,0:T(8,128)(2,1)S(1)}, bf16[512,256]{1,0:T(8,128)(2,1)S(1)}, u32[]{:S(2)}, u32[]{:S(2)}) collective-permute-start(bf16[512,256]{1,0:T(8,128)(2,1)S(1)} %get-tuple-element.128), channel_id=1, source_target_pairs={{0,4},{1,8},{2,6},{3,10},{4,0},{5,12},{6,2},{7,14},{8,1},{9,16},{1... | collective-permute-start | bytes 786440 | tf_op jit(solution)/shard_map/ppermute | solution.py:279
  145.1 9.2 %collective-permute-start.35 = (bf16[256,1024]{1,0:T(8,128)(2,1)S(1)}, bf16[256,1024]{1,0:T(8,128)(2,1)S(1)}, u32[]{:S(2)}, u32[]{:S(2)}) collective-permute-start(bf16[256,1024]{1,0:T(8,128)(2,1)S(1)} %shard_map.96), channel_id=1, source_target_pairs={{0,8},{1,4},{2,10},{3,6},{4,1},{5,13},{6,3},{7,15},{8,0},{9,12},{1... | collective-permute-start | bytes 1572872 | tf_op jit(solution)/shard_map/ppermute | solution.py:279
  (16 other events, 68.6 us)

commit v4 on v3

--- a/solution.py
+++ b/solution.py
@@ -74,46 +74,22 @@
         out[pl.ds(first, rows), :] = jnp.where(at < used, y, 0.0).astype(BF16)
 
 
-def build_kernel(steps, cap, nblk, width, info, blocks, *refs):
-    moved, refs = refs[: len(steps)], refs[len(steps) :]
+def build_kernel(lot, held, cap, nblk, width, info, blocks, *refs):
+    count = sum(pieces for _, _, pieces in lot)
+    moved, refs = list(refs[:count]), refs[count:]
     near_out, far_out, raw, total, sems = refs[-5:]
     role, keep, half, at_edge, _ = here()
     slots = total.shape[0]
     near_slots = near_out.shape[1] // width
     parts = 4
     piece = nblk // parts
-    rows = [row_of(half, step, direct, cap) for step, direct in steps]
-
-    def loads(n, t):
-        cut = lambda p: pl.ds(p * piece, piece)
-        return [
-            pltpu.make_async_copy(blocks.at[t, cut(p)], raw.at[n, cut(p)], sems.at[n, p])
-            for p in range(parts)
-        ]
-
-    def add(source, t):
+    place = lambda step, direct: row_of(half, step, direct, cap)
+
+    def build(source, t):
         total[...] = jnp.zeros_like(total)
         for k in range(nblk):
             slot = slot_place(info[1 + t * nblk + k], role, cap, slots)
             total[slot] = total[slot] + source(k).astype(F32)
-
-    @pl.when(keep)
-    def _():
-        for n, t in enumerate(rows):
-            for copy in loads(n, t):
-                copy.start()
-
-    for n, t in enumerate(rows):
-        @pl.when(keep)
-        def _():
-            for copy in loads(n, t):
-                copy.wait()
-            add(lambda k: raw[n, k], t)
-
-        @pl.when(jnp.logical_not(keep))
-        def _():
-            add(lambda k: moved[n][0, k], t)
-
         scale = jnp.where(t < info[0], 2.0, 0.0).astype(F32)
         far_scale = jnp.where(at_edge, 0.0, scale)
         at = pl.ds(pl.multiple_of(t * width, width), width)
@@ -122,6 +98,38 @@
             lane = (slot if near else slot - near_slots) * width
             value = total[slot] * (scale if near else far_scale)
             (near_out if near else far_out)[at, lane : lane + width] = value.astype(BF16)
+
+    def loads(n, t):
+        cut = lambda p: pl.ds(p * piece, piece)
+        return [
+            pltpu.make_async_copy(blocks.at[t, cut(p)], raw.at[n, cut(p)], sems.at[n, p])
+            for p in range(parts)
+        ]
+
+    if held:
+        @pl.when(keep)
+        def _():
+            for n, row in enumerate(held):
+                for copy in loads(n, place(*row)):
+                    copy.start()
+
+            def one(n, carry):
+                steps = sum(jnp.where(n == at, step, 0) for at, (step, _) in enumerate(held))
+                direct = sum(jnp.where(n == at, int(direct), 0) for at, (_, direct) in enumerate(held))
+                t = place(steps, direct)
+                for copy in loads(n, t):
+                    copy.wait()
+                build(lambda k: raw[n, k], t)
+                return carry
+
+            lax.fori_loop(0, len(held), one, 0)
+
+    @pl.when(jnp.logical_not(keep))
+    def _():
+        for step, direct, pieces in lot:
+            arrays = [moved.pop(0) for _ in range(pieces)]
+            each = nblk // pieces
+            build(lambda k: arrays[k // each][0, k % each], place(step, direct))
 
 
 def gather_kernel(counts, cols, lists, out):
@@ -151,21 +159,23 @@
 
 
 def row_of(half, step, direct, cap):
-    flip = half if direct else 1 - half
+    flip = jnp.where(direct == 1, half, 1 - half)
     return jnp.where(flip == 1, cap - 1 - step, step)
 
 
-def stage_kernel(steps, cap, blocks, *refs):
+def stage_kernel(cuts, cap, blocks, *refs):
     outs, sems = refs[:-1], refs[-1]
     half = here()[2]
-    piece = blocks.shape[1] // 4
-    copies = [
-        pltpu.make_async_copy(
-            blocks.at[row_of(half, step, True, cap), pl.ds(p * piece, piece)],
-            out.at[0, pl.ds(p * piece, piece)], sems.at[n, p],
-        )
-        for n, (step, out) in enumerate(zip(steps, outs)) for p in range(4)
-    ]
+    copies = []
+    for n, ((step, first, count), out) in enumerate(zip(cuts, outs)):
+        piece = count // 2
+        for p in range(2):
+            copies.append(
+                pltpu.make_async_copy(
+                    blocks.at[row_of(half, step, 1, cap), pl.ds(first + p * piece, piece)],
+                    out.at[0, pl.ds(p * piece, piece)], sems.at[n, p],
+                )
+            )
     for copy in copies:
         copy.start()
     for copy in copies:
@@ -267,8 +277,28 @@
             send[i * width : (i + 1) * width, :] = field[rows, :]
 
 
-def last_kernel(acc, far_op, part, low, high, sent, out):
-    out[...] = result_of(False, acc, far_op, far_rows(part, low, high, sent)).T.astype(BF16)
+def last_kernel(begin, acc, far_op, part, low, high, sent, out):
+    rows = pl.ds(begin, out.shape[1])
+    far = far_rows(part, low, high, sent)
+    total = acc[rows, :] + jnp.dot(far_op[rows, :], far, preferred_element_type=F32)
+    out[...] = total.T.astype(BF16)
+
+
+def merge_kernel(begin, own, moved, *refs):
+    out, wide, sem = refs[-3:]
+    keep = here()[1]
+
+    @pl.when(keep)
+    def _():
+        wide[...] = own[...].astype(F32)
+
+    @pl.when(jnp.logical_not(keep))
+    def _():
+        wide[...] = moved[...].astype(F32)
+
+    copy = pltpu.make_async_copy(wide, out.at[:, pl.ds(begin, wide.shape[1])], sem)
+    copy.start()
+    copy.wait()
 
 
 def body(vectors, rotation, blocks, cols, lists, counts):
@@ -278,7 +308,6 @@
     def send(x, way):
         return lax.ppermute(x, AXES, ways[way])
 
-    r, c = lax.axis_index("row"), lax.axis_index("col")
     cap, nblk, width = blocks.shape[0], blocks.shape[1], blocks.shape[2]
     edge = lists.shape[2]
     panel = rotation.shape[1]
@@ -298,19 +327,22 @@
         bit //= 2
 
     held = pltpu.with_memory_space_constraint(blocks, pltpu.HBM)
-    relays = cap // 2 - 1
-    straight = cap - relays
-    row = sds((1, nblk, width, width), BF16)
-
-    def stage(*steps):
+    middle, part_blocks = cap // 2, nblk // 2
+    block_rows = lambda count: sds((1, count, width, width), BF16)
+
+    def stage(*cuts):
         return call(
-            functools.partial(stage_kernel, steps, cap), (row,) * len(steps), [HBM], (VMEM,) * len(steps),
-            scratch=(pltpu.SemaphoreType.DMA((len(steps), 4)),),
+            functools.partial(stage_kernel, cuts, cap), tuple(block_rows(cut[2]) for cut in cuts),
+            [HBM], (VMEM,) * len(cuts), scratch=(pltpu.SemaphoreType.DMA((len(cuts), 2)),),
         )(held)
 
-    staged = stage(0) + stage(*range(1, straight))
+    staged = stage((0, 0, nblk))
+    staged += stage(
+        *((k, 0, nblk) for k in range(1, middle - 1)),
+        (middle - 1, part_blocks, part_blocks), (middle - 1, 0, part_blocks), (middle, 0, part_blocks),
+    )
     direct = [send(x, "trade") for x in staged]
-    relayed = [send(x, "across") for x in direct[:relays]]
+    relayed = [send(x, "across") for x in direct[:middle]]
 
     n_slots = 1 + cap * nblk
     own = call(gather_kernel, ints(n_slots + 2 * edge), [SMEM] * 3, SMEM)(counts, cols, lists)
@@ -326,24 +358,30 @@
 
     ops = ()
     op_shapes = (sds((height, height + edge * width), BF16), sds((height, edge * width), BF16))
-    arrived = {(k, True): x for k, x in enumerate(direct)}
-    arrived.update({(k, False): x for k, x in enumerate(relayed)})
-    keys = [(k, True) for k in range(straight - 1)]
-    cut = len(keys) // 2
-    lots = [keys[:cut], keys[cut:], [(k, False) for k in range(relays - 1)]]
-    lots += [[(relays - 1, False)], [(straight - 1, True)]]
-    for lot in lots:
-        n = len(lot)
+    low, high, extra = direct[middle], direct[middle - 1], direct[middle + 1]
+    cut = middle // 2
+    lots = [
+        [(k, 1, (direct[k],)) for k in range(cut)],
+        [(k, 1, (direct[k],)) for k in range(cut, middle - 1)] + [(middle - 1, 1, (low, high))],
+        [(k, 0, (relayed[k],)) for k in range(middle - 2)],
+        [(middle - 2, 0, (relayed[middle - 2],))],
+        [(middle, 1, (extra, relayed[middle - 1]))],
+    ]
+    whole = [[row[:2] for row in lot] for lot in lots]
+    holds = [whole[0], sum(whole[1:], []), [], [], []]
+    for lot, hold in zip(lots, holds):
+        given = [x for row in lot for x in row[2]]
+        n = len(given)
         ops = call(
-            functools.partial(build_kernel, tuple(lot), cap, nblk, width),
+            functools.partial(build_kernel, [(*row[:2], len(row[2])) for row in lot], hold, cap, nblk, width),
             op_shapes, [SMEM, HBM] + [VMEM] * (n + len(ops)), (VMEM, VMEM),
             scratch=(
-                pltpu.VMEM((n, nblk, width, width), BF16),
+                pltpu.VMEM((max(1, len(hold)), nblk, width, width), BF16),
                 pltpu.VMEM((slots, width, width), F32),
-                pltpu.SemaphoreType.DMA((n, 4)),
+                pltpu.SemaphoreType.DMA((max(1, len(hold)), 4)),
             ),
-            aliases={2 + n: 0, 3 + n: 1} if ops else {},
-        )(info, held, *(arrived[key] for key in lot), *ops)
+            aliases={2 + n: 0, 3 + n: 1} if ops else {}, mib=20,
+        )(info, held, *given, *ops)
     near_op, far_op = ops
 
     sent = sds((edge * width, panel), BF16)
@@ -382,14 +420,27 @@
         if PLAIN <= step and not last:
             moved_part = send(mine[1], "far")
         if last:
-            result = call(last_kernel, sds((panel, height), BF16), [VMEM] * 6, VMEM)(
-                acc, far_op, arrived_part, *theirs, sent_rows[step - 1]
-            )
-            continue
+            cut = height // 2
+            ends = [
+                call(
+                    functools.partial(last_kernel, begin), sds((panel, cut), BF16), [VMEM] * 6, VMEM
+                )(acc, far_op, arrived_part, *theirs, sent_rows[step - 1])
+                for begin in (0, cut)
+            ]
+            backs = [send(x, "trade") for x in ends]
+            out = ()
+            for at, (own, back) in enumerate(zip(ends, backs)):
+                out = (
+                    call(
+                        functools.partial(merge_kernel, at * cut), sds((panel, height), F32),
+                        [VMEM] * 2 + [HBM] * len(out), HBM,
+                        scratch=(pltpu.VMEM((panel, cut), F32), pltpu.SemaphoreType.DMA),
+                        aliases={2: 0} if out else {},
+                    )(own, back, *out),
+                )
+            return out[0]
         if step < PLAIN:
-            far_send = call(
-                functools.partial(ahead_kernel, first), sent, [VMEM] * 4, VMEM
-            )(mine[1], *far_part, far)
+            far_send = call(functools.partial(ahead_kernel, first), sent, [VMEM] * 4, VMEM)(mine[1], *far_part, far)
         wants = (step < STEPS - 2, PLAIN <= step < STEPS - 2)
         outs = ((wide(F32),) if wants[0] else ()) + (wide(BF16), sent) + ((sent,) if wants[1] else ())
         given = (far,) if plain else (arrived_part, *theirs, sent_rows[step - 1])
@@ -402,8 +453,6 @@
         field, near_send = result[:2]
         if wants[1]:
             sent_rows[step + 1] = result[2]
-    keep = c % 2 == r % 2
-    return jnp.where(keep, result, send(result, "trade")).astype(F32)
 
 
 def solution(mesh):

time: 156 us -> 153 us (0.981)
  waiting for transfers between devices: 76.9 us -> 70.6 us
  starting transfers between devices: 35.7 us -> 41.6 us
    ppermute x33 -> x36, waiting for transfers between devices: 65 us -> 58.7 us  [send(): return lax.ppermute(x, AXES, ways[way])]
    ppermute x33 -> x36, starting transfers between devices: 32.6 us -> 38.5 us  [send(): return lax.ppermute(x, AXES, ways[way])]
    pallas_call x8 -> x11, Pallas kernels: 14.9 us -> 13.8 us  [the longest x5 8.01 us: body(): call(functools.partial(build_kernel, [(*row[:2], len(row[2])) for row in...]
  transfers between devices with their start and end apart: 36 -> 39, of which waited for: 15 -> 16; matrix products, arithmetic and copies ran while one was open for 0% -> 0% of each run, Pallas kernels for 19% -> 18%
where the time goes in v4:
time: 153 us
  waiting for transfers between devices  70.6 us (46%)
  starting transfers between devices  41.6 us (27%)
  Pallas kernels  38.2 us (25%)
    ppermute x36, waiting for transfers between devices, send(): return lax.ppermute(x, AXES, ways[way])  58.7 us
    ppermute x36, starting transfers between devices, send(): return lax.ppermute(x, AXES, ways[way])  38.5 us
    ppermute x3, waiting for transfers between devices, body(): lax.ppermute(pieces[place], 'col', [(k, k ^ bit) for k in range(columns)])  11.9 us
    pallas_call x10, Pallas kernels, body(): call(functools.partial(local_kernel, width, edge, not first, gives), outs...  10.7 us
    pallas_call x9, Pallas kernels, body(): call(functools.partial(finish_kernel, first, not plain, wants, width, edg...  8.61 us
    pallas_call x5, Pallas kernels, body(): call(functools.partial(build_kernel, [(*row[:2], len(row[2])) for row in...  8.01 us
    ppermute x3, starting transfers between devices, body(): lax.ppermute(pieces[place], 'col', [(k, k ^ bit) for k in range(columns)])  3.07 us
  transfers between devices with their start and end apart: 39, of which 16 were waited for; matrix products, arithmetic and copies ran while one was open for 0% of the time, Pallas kernels for 18%

profile of v4, /device:TPU:0, one launch (start us, length us, event | category | flops | bytes accessed | tf_op | source)
XLA Modules:
  0.0 153.1 jit_solution(662742330573434849)
XLA Ops:
  1.3 3.1 %collective-permute-start.11 = (bf16[256,1024]{1,0:T(8,128)(2,1)S(1)}, bf16[256,1024]{1,0:T(8,128)(2,1)S(1)}, u32[]{:S(2)}, u32[]{:S(2)}) collective-permute-start(bf16[256,1024]{1,0:T(8,128)(2,1)S(1)} %convert_element_type.3.refs_0_), channel_id=1, source_target_pairs={{0,2},{1,3},{2,0},{3,1},{4,6},{5,7},{6,4},{7,5},{8,10},{9,11},{10,... | collective-permute-start | bytes 1572872 | tf_op jit(solution)/shard_map/ppermute | solution.py:324
  4.4 11.9 %collective-permute-done.11.refs_1_ = bf16[256,1024]{1,0:T(8,128)(2,1)S(1)} collective-permute-done((bf16[256,1024]{1,0:T(8,128)(2,1)S(1)}, bf16[256,1024]{1,0:T(8,128)(2,1)S(1)}, u32[]{:S(2)}, u32[]{:S(2)}) %collective-permute-start.11) | collective-permute-done | bytes 524320 | tf_op jit(solution)/shard_map/ppermute | solution.py:324
  17.8 1.9 %collective-permute-start.8 = (bf16[1,16,128,128]{3,2,1,0:T(8,128)(2,1)S(1)}, bf16[1,16,128,128]{3,2,1,0:T(8,128)(2,1)S(1)}, u32[]{:S(2)}, u32[]{:S(2)}) collective-permute-start(bf16[1,16,128,128]{3,2,1,0:T(8,128)(2,1)S(1)} %get-tuple-element.82), channel_id=1, source_target_pairs={{0,8},{1,4},{2,10},{3,6},{4,1},{5,13},{6,3},{7,15},{8,0},{9,12},{1... | collective-permute-start | bytes 1572872 | tf_op jit(solution)/shard_map/ppermute | solution.py:309
  25.1 1.8 %collective-permute-start.2 = (bf16[1,8,128,128]{3,2,1,0:T(8,128)(2,1)S(1)}, bf16[1,8,128,128]{3,2,1,0:T(8,128)(2,1)S(1)}, u32[]{:S(2)}, u32[]{:S(2)}) collective-permute-start(bf16[1,8,128,128]{3,2,1,0:T(8,128)(2,1)S(1)} %get-tuple-element.80), channel_id=1, source_target_pairs={{0,8},{1,4},{2,10},{3,6},{4,1},{5,13},{6,3},{7,15},{8,0},{9,12},{1... | collective-permute-start | bytes 786440 | tf_op jit(solution)/shard_map/ppermute | solution.py:309
  28.2 10.2 %collective-permute-done.moved = s32[137]{0:T(256)S(1)} collective-permute-done((s32[137]{0:T(256)S(1)}, s32[137]{0:T(256)S(1)}, u32[]{:S(2)}, u32[]{:S(2)}) %collective-permute-start) | collective-permute-done | bytes 580 | tf_op jit(solution)/shard_map/ppermute | solution.py:309
  38.4 1.8 %collective-permute-start.14 = (bf16[1024,256]{1,0:T(8,128)(2,1)S(1)}, bf16[1024,256]{1,0:T(8,128)(2,1)S(1)}, u32[]{:S(2)}, u32[]{:S(2)}) collective-permute-start(bf16[1024,256]{1,0:T(8,128)(2,1)S(1)} %shard_map.73.own), channel_id=1, source_target_pairs={{0,8},{1,4},{2,10},{3,6},{4,1},{5,13},{6,3},{7,15},{8,0},{9,12},{1... | collective-permute-start | bytes 1572872 | tf_op jit(solution)/shard_map/ppermute | solution.py:309
  44.3 6.1 %collective-permute-done.10.refs_1_ = bf16[1,8,128,128]{3,2,1,0:T(8,128)(2,1)S(1)} collective-permute-done((bf16[1,8,128,128]{3,2,1,0:T(8,128)(2,1)S(1)}, bf16[1,8,128,128]{3,2,1,0:T(8,128)(2,1)S(1)}, u32[]{:S(2)}, u32[]{:S(2)}) %collective-permute-start.10) | collective-permute-done | bytes 262176 | tf_op jit(solution)/shard_map/ppermute | solution.py:309
  50.4 1.8 %collective-permute-start.1 = (bf16[1,8,128,128]{3,2,1,0:T(8,128)(2,1)S(1)}, bf16[1,8,128,128]{3,2,1,0:T(8,128)(2,1)S(1)}, u32[]{:S(2)}, u32[]{:S(2)}) collective-permute-start(bf16[1,8,128,128]{3,2,1,0:T(8,128)(2,1)S(1)} %get-tuple-element.79), channel_id=1, source_target_pairs={{0,8},{1,4},{2,10},{3,6},{4,1},{5,13},{6,3},{7,15},{8,0},{9,12},{1... | collective-permute-start | bytes 786440 | tf_op jit(solution)/shard_map/ppermute | solution.py:309
  53.5 4.9 %collective-permute-start.15 = (bf16[512,256]{1,0:T(8,128)(2,1)S(1)}, bf16[512,256]{1,0:T(8,128)(2,1)S(1)}, u32[]{:S(2)}, u32[]{:S(2)}) collective-permute-start(bf16[512,256]{1,0:T(8,128)(2,1)S(1)} %get-tuple-element.94), channel_id=1, source_target_pairs={{0,1},{1,0},{2,3},{3,2},{4,5},{5,4},{6,7},{7,6},{8,9},{9,8},{10,11... | collective-permute-start | bytes 786440 | tf_op jit(solution)/shard_map/ppermute | solution.py:309
  58.8 2.3 %shard_map.68 = (bf16[1024,1536]{1,0:T(8,128)(2,1)S(1)}, bf16[1024,512]{1,0:T(8,128)(2,1)S(1)}) custom-call(s32[129]{0:T(256)S(1)} %get-tuple-element.78.info, bf16[8,16,128,128]{3,2,1,0:T(8,128)(2,1)} %blocks.13, bf16[1,16,128,128]{3,2,1,0:T(8,128)(2,1)S(1)} %collective-permute-done.6.refs_0_, bf16[1,16,128,128]{3,2,1,0:T(8,128)(2,1)S(1)} %collective-permute-done.8.refs_1_), custom_call_target="tpu_custom_call" | custom-call | tf_op jit(solution)/shard_map/pallas_call | solution.py:375
  61.2 3.7 %shard_map.69 = (bf16[1024,1536]{1,0:T(8,128)(2,1)S(1)}, bf16[1024,512]{1,0:T(8,128)(2,1)S(1)}) custom-call(s32[129]{0:T(256)S(1)} %get-tuple-element.78.info, bf16[8,16,128,128]{3,2,1,0:T(8,128)(2,1)} %blocks.13, bf16[1,16,128,128]{3,2,1,0:T(8,128)(2,1)S(1)} %collective-permute-done.4.refs_0_, ...), custom_call_target="tpu_custom_call", output_to_operand_aliasing={{0}: (5, {}), {1}: (6, {})} | custom-call | tf_op jit(solution)/shard_map/pallas_call | solution.py:375
  72.0 3.6 %collective-permute-done.18.refs_0_.far = bf16[512,256]{1,0:T(8,128)(2,1)S(1)} collective-permute-done((bf16[512,256]{1,0:T(8,128)(2,1)S(1)}, bf16[512,256]{1,0:T(8,128)(2,1)S(1)}, u32[]{:S(2)}, u32[]{:S(2)}) %collective-permute-start.18) | collective-permute-done | bytes 262176 | tf_op jit(solution)/shard_map/ppermute | solution.py:309
  79.9 3.8 %collective-permute-done.20.refs_0_ = bf16[512,256]{1,0:T(8,128)(2,1)S(1)} collective-permute-done((bf16[512,256]{1,0:T(8,128)(2,1)S(1)}, bf16[512,256]{1,0:T(8,128)(2,1)S(1)}, u32[]{:S(2)}, u32[]{:S(2)}) %collective-permute-start.20) | collective-permute-done | bytes 262176 | tf_op jit(solution)/shard_map/ppermute | solution.py:309
  90.9 2.8 %collective-permute-done.24.refs_2_.high = bf16[256,512]{1,0:T(8,128)(2,1)S(1)} collective-permute-done((bf16[256,512]{1,0:T(8,128)(2,1)S(1)}, bf16[256,512]{1,0:T(8,128)(2,1)S(1)}, u32[]{:S(2)}, u32[]{:S(2)}) %collective-permute-start.24) | collective-permute-done | bytes 262176 | tf_op jit(solution)/shard_map/ppermute | solution.py:309
  93.7 2.8 %collective-permute-done.22.refs_0_ = bf16[512,256]{1,0:T(8,128)(2,1)S(1)} collective-permute-done((bf16[512,256]{1,0:T(8,128)(2,1)S(1)}, bf16[512,256]{1,0:T(8,128)(2,1)S(1)}, u32[]{:S(2)}, u32[]{:S(2)}) %collective-permute-start.22) | collective-permute-done | bytes 262176 | tf_op jit(solution)/shard_map/ppermute | solution.py:309
  100.3 3.7 %collective-permute-done.26.refs_0_ = bf16[512,256]{1,0:T(8,128)(2,1)S(1)} collective-permute-done((bf16[512,256]{1,0:T(8,128)(2,1)S(1)}, bf16[512,256]{1,0:T(8,128)(2,1)S(1)}, u32[]{:S(2)}, u32[]{:S(2)}) %collective-permute-start.26) | collective-permute-done | bytes 262176 | tf_op jit(solution)/shard_map/ppermute | solution.py:309
  107.8 3.7 %collective-permute-done.28.refs_0_ = bf16[512,256]{1,0:T(8,128)(2,1)S(1)} collective-permute-done((bf16[512,256]{1,0:T(8,128)(2,1)S(1)}, bf16[512,256]{1,0:T(8,128)(2,1)S(1)}, u32[]{:S(2)}, u32[]{:S(2)}) %collective-permute-start.28) | collective-permute-done | bytes 262176 | tf_op jit(solution)/shard_map/ppermute | solution.py:309
  115.3 3.7 %collective-permute-done.30.refs_0_ = bf16[512,256]{1,0:T(8,128)(2,1)S(1)} collective-permute-done((bf16[512,256]{1,0:T(8,128)(2,1)S(1)}, bf16[512,256]{1,0:T(8,128)(2,1)S(1)}, u32[]{:S(2)}, u32[]{:S(2)}) %collective-permute-start.30) | collective-permute-done | bytes 262176 | tf_op jit(solution)/shard_map/ppermute | solution.py:309
  122.8 3.7 %collective-permute-done.32.refs_0_ = bf16[512,256]{1,0:T(8,128)(2,1)S(1)} collective-permute-done((bf16[512,256]{1,0:T(8,128)(2,1)S(1)}, bf16[512,256]{1,0:T(8,128)(2,1)S(1)}, u32[]{:S(2)}, u32[]{:S(2)}) %collective-permute-start.32) | collective-permute-done | bytes 262176 | tf_op jit(solution)/shard_map/ppermute | solution.py:309
  130.5 3.5 %collective-permute-done.34.refs_0_ = bf16[512,256]{1,0:T(8,128)(2,1)S(1)} collective-permute-done((bf16[512,256]{1,0:T(8,128)(2,1)S(1)}, bf16[512,256]{1,0:T(8,128)(2,1)S(1)}, u32[]{:S(2)}, u32[]{:S(2)}) %collective-permute-start.34) | collective-permute-done | bytes 262176 | tf_op jit(solution)/shard_map/ppermute | solution.py:309
  138.3 3.8 %collective-permute-done.36.part = bf16[512,256]{1,0:T(8,128)(2,1)S(1)} collective-permute-done((bf16[512,256]{1,0:T(8,128)(2,1)S(1)}, bf16[512,256]{1,0:T(8,128)(2,1)S(1)}, u32[]{:S(2)}, u32[]{:S(2)}) %collective-permute-start.36) | collective-permute-done | bytes 262176 | tf_op jit(solution)/shard_map/ppermute | solution.py:309
  143.8 2.1 %collective-permute-start.37 = (bf16[256,512]{1,0:T(8,128)(2,1)S(1)}, bf16[256,512]{1,0:T(8,128)(2,1)S(1)}, u32[]{:S(2)}, u32[]{:S(2)}) collective-permute-start(bf16[256,512]{1,0:T(8,128)(2,1)S(1)} %shard_map.96.own), channel_id=1, source_target_pairs={{0,8},{1,4},{2,10},{3,6},{4,1},{5,13},{6,3},{7,15},{8,0},{9,12},{1... | collective-permute-start | bytes 786440 | tf_op jit(solution)/shard_map/ppermute | solution.py:309
  145.8 3.5 %collective-permute-done.38.moved = bf16[256,512]{1,0:T(8,128)(2,1)S(1)} collective-permute-done((bf16[256,512]{1,0:T(8,128)(2,1)S(1)}, bf16[256,512]{1,0:T(8,128)(2,1)S(1)}, u32[]{:S(2)}, u32[]{:S(2)}) %collective-permute-start.38) | collective-permute-done | bytes 262176 | tf_op jit(solution)/shard_map/ppermute | solution.py:309
  150.1 2.0 %collective-permute-done.37.moved = bf16[256,512]{1,0:T(8,128)(2,1)S(1)} collective-permute-done((bf16[256,512]{1,0:T(8,128)(2,1)S(1)}, bf16[256,512]{1,0:T(8,128)(2,1)S(1)}, u32[]{:S(2)}, u32[]{:S(2)}) %collective-permute-start.37) | collective-permute-done | bytes 262176 | tf_op jit(solution)/shard_map/ppermute | solution.py:309
  (99 shorter events, 59.7 us)
Async XLA Ops:
  1.3 15.0 %collective-permute-start.11 = (bf16[256,1024]{1,0:T(8,128)(2,1)S(1)}, bf16[256,1024]{1,0:T(8,128)(2,1)S(1)}, u32[]{:S(2)}, u32[]{:S(2)}) collective-permute-start(bf16[256,1024]{1,0:T(8,128)(2,1)S(1)} %convert_element_type.3.refs_0_), channel_id=1, source_target_pairs={{0,2},{1,3},{2,0},{3,1},{4,6},{5,7},{6,4},{7,5},{8,10},{9,11},{10,... | collective-permute-start | bytes 1572872 | tf_op jit(solution)/shard_map/ppermute | solution.py:324
  4.4 20.4 %collective-permute-start.12 = (bf16[256,1024]{1,0:T(8,128)(2,1)S(1)}, bf16[256,1024]{1,0:T(8,128)(2,1)S(1)}, u32[]{:S(2)}, u32[]{:S(2)}) collective-permute-start(bf16[256,1024]{1,0:T(8,128)(2,1)S(1)} %convert_element_type.3.refs_0_), channel_id=1, source_target_pairs={{0,1},{1,0},{2,3},{3,2},{4,5},{5,4},{6,7},{7,6},{8,9},{9,8},{10,11... | collective-permute-start | bytes 1572872 | tf_op jit(solution)/shard_map/ppermute | solution.py:324
  16.3 8.9 %collective-permute-start.13 = (bf16[256,1024]{1,0:T(8,128)(2,1)S(1)}, bf16[256,1024]{1,0:T(8,128)(2,1)S(1)}, u32[]{:S(2)}, u32[]{:S(2)}) collective-permute-start(bf16[256,1024]{1,0:T(8,128)(2,1)S(1)} %collective-permute-done.11.refs_1_), channel_id=1, source_target_pairs={{0,1},{1,0},{2,3},{3,2},{4,5},{5,4},{6,7},{7,6},{8,9},{9,8},{10,11... | collective-permute-start | bytes 1572872 | tf_op jit(solution)/shard_map/ppermute | solution.py:324
  17.8 22.3 %collective-permute-start.8 = (bf16[1,16,128,128]{3,2,1,0:T(8,128)(2,1)S(1)}, bf16[1,16,128,128]{3,2,1,0:T(8,128)(2,1)S(1)}, u32[]{:S(2)}, u32[]{:S(2)}) collective-permute-start(bf16[1,16,128,128]{3,2,1,0:T(8,128)(2,1)S(1)} %get-tuple-element.82), channel_id=1, source_target_pairs={{0,8},{1,4},{2,10},{3,6},{4,1},{5,13},{6,3},{7,15},{8,0},{9,12},{1... | collective-permute-start | bytes 1572872 | tf_op jit(solution)/shard_map/ppermute | solution.py:309
  20.8 20.1 %collective-permute-start.6 = (bf16[1,16,128,128]{3,2,1,0:T(8,128)(2,1)S(1)}, bf16[1,16,128,128]{3,2,1,0:T(8,128)(2,1)S(1)}, u32[]{:S(2)}, u32[]{:S(2)}) collective-permute-start(bf16[1,16,128,128]{3,2,1,0:T(8,128)(2,1)S(1)} %shard_map.67), channel_id=1, source_target_pairs={{0,8},{1,4},{2,10},{3,6},{4,1},{5,13},{6,3},{7,15},{8,0},{9,12},{1... | collective-permute-start | bytes 1572872 | tf_op jit(solution)/shard_map/ppermute | solution.py:309
  21.1 20.5 %collective-permute-start.4 = (bf16[1,16,128,128]{3,2,1,0:T(8,128)(2,1)S(1)}, bf16[1,16,128,128]{3,2,1,0:T(8,128)(2,1)S(1)}, u32[]{:S(2)}, u32[]{:S(2)}) collective-permute-start(bf16[1,16,128,128]{3,2,1,0:T(8,128)(2,1)S(1)} %get-tuple-element.81), channel_id=1, source_target_pairs={{0,8},{1,4},{2,10},{3,6},{4,1},{5,13},{6,3},{7,15},{8,0},{9,12},{1... | collective-permute-start | bytes 1572872 | tf_op jit(solution)/shard_map/ppermute | solution.py:309
  24.8 13.6 %collective-permute-start = (s32[137]{0:T(256)S(1)}, s32[137]{0:T(256)S(1)}, u32[]{:S(2)}, u32[]{:S(2)}) collective-permute-start(s32[137]{0:T(256)S(1)} %shard_map.64.own), channel_id=1, source_target_pairs={{0,8},{1,4},{2,10},{3,6},{4,1},{5,13},{6,3},{7,15},{8,0},{9,12},{1... | collective-permute-start | bytes 1652 | tf_op jit(solution)/shard_map/ppermute | solution.py:309
  25.1 17.1 %collective-permute-start.2 = (bf16[1,8,128,128]{3,2,1,0:T(8,128)(2,1)S(1)}, bf16[1,8,128,128]{3,2,1,0:T(8,128)(2,1)S(1)}, u32[]{:S(2)}, u32[]{:S(2)}) collective-permute-start(bf16[1,8,128,128]{3,2,1,0:T(8,128)(2,1)S(1)} %get-tuple-element.80), channel_id=1, source_target_pairs={{0,8},{1,4},{2,10},{3,6},{4,1},{5,13},{6,3},{7,15},{8,0},{9,12},{1... | collective-permute-start | bytes 786440 | tf_op jit(solution)/shard_map/ppermute | solution.py:309
  38.4 13.8 %collective-permute-start.14 = (bf16[1024,256]{1,0:T(8,128)(2,1)S(1)}, bf16[1024,256]{1,0:T(8,128)(2,1)S(1)}, u32[]{:S(2)}, u32[]{:S(2)}) collective-permute-start(bf16[1024,256]{1,0:T(8,128)(2,1)S(1)} %shard_map.73.own), channel_id=1, source_target_pairs={{0,8},{1,4},{2,10},{3,6},{4,1},{5,13},{6,3},{7,15},{8,0},{9,12},{1... | collective-permute-start | bytes 1572872 | tf_op jit(solution)/shard_map/ppermute | solution.py:309
  40.2 13.3 %collective-permute-start.9 = (bf16[1,16,128,128]{3,2,1,0:T(8,128)(2,1)S(1)}, bf16[1,16,128,128]{3,2,1,0:T(8,128)(2,1)S(1)}, u32[]{:S(2)}, u32[]{:S(2)}) collective-permute-start(bf16[1,16,128,128]{3,2,1,0:T(8,128)(2,1)S(1)} %collective-permute-done.8.refs_1_), channel_id=1, source_target_pairs={{1,3},{3,1},{4,6},{6,4},{9,11},{11,9},{12,14},{14,12},{17,19},{19,... | collective-permute-start | bytes 1572872 | tf_op jit(solution)/shard_map/ppermute | solution.py:309
  40.9 17.5 %collective-permute-start.7 = (bf16[1,16,128,128]{3,2,1,0:T(8,128)(2,1)S(1)}, bf16[1,16,128,128]{3,2,1,0:T(8,128)(2,1)S(1)}, u32[]{:S(2)}, u32[]{:S(2)}) collective-permute-start(bf16[1,16,128,128]{3,2,1,0:T(8,128)(2,1)S(1)} %collective-permute-done.6.refs_0_), channel_id=1, source_target_pairs={{1,3},{3,1},{4,6},{6,4},{9,11},{11,9},{12,14},{14,12},{17,19},{19,... | collective-permute-start | bytes 1572872 | tf_op jit(solution)/shard_map/ppermute | solution.py:309
  41.6 23.9 %collective-permute-start.5 = (bf16[1,16,128,128]{3,2,1,0:T(8,128)(2,1)S(1)}, bf16[1,16,128,128]{3,2,1,0:T(8,128)(2,1)S(1)}, u32[]{:S(2)}, u32[]{:S(2)}) collective-permute-start(bf16[1,16,128,128]{3,2,1,0:T(8,128)(2,1)S(1)} %collective-permute-done.4.refs_0_), channel_id=1, source_target_pairs={{1,3},{3,1},{4,6},{6,4},{9,11},{11,9},{12,14},{14,12},{17,19},{19,... | collective-permute-start | bytes 1572872 | tf_op jit(solution)/shard_map/ppermute | solution.py:309
  42.3 8.1 %collective-permute-start.10 = (bf16[1,8,128,128]{3,2,1,0:T(8,128)(2,1)S(1)}, bf16[1,8,128,128]{3,2,1,0:T(8,128)(2,1)S(1)}, u32[]{:S(2)}, u32[]{:S(2)}) collective-permute-start(bf16[1,8,128,128]{3,2,1,0:T(8,128)(2,1)S(1)} %get-tuple-element.83), channel_id=1, source_target_pairs={{0,8},{1,4},{2,10},{3,6},{4,1},{5,13},{6,3},{7,15},{8,0},{9,12},{1... | collective-permute-start | bytes 786440 | tf_op jit(solution)/shard_map/ppermute | solution.py:309
  50.4 15.7 %collective-permute-start.1 = (bf16[1,8,128,128]{3,2,1,0:T(8,128)(2,1)S(1)}, bf16[1,8,128,128]{3,2,1,0:T(8,128)(2,1)S(1)}, u32[]{:S(2)}, u32[]{:S(2)}) collective-permute-start(bf16[1,8,128,128]{3,2,1,0:T(8,128)(2,1)S(1)} %get-tuple-element.79), channel_id=1, source_target_pairs={{0,8},{1,4},{2,10},{3,6},{4,1},{5,13},{6,3},{7,15},{8,0},{9,12},{1... | collective-permute-start | bytes 786440 | tf_op jit(solution)/shard_map/ppermute | solution.py:309
  52.2 13.9 %collective-permute-start.3 = (bf16[1,8,128,128]{3,2,1,0:T(8,128)(2,1)S(1)}, bf16[1,8,128,128]{3,2,1,0:T(8,128)(2,1)S(1)}, u32[]{:S(2)}, u32[]{:S(2)}) collective-permute-start(bf16[1,8,128,128]{3,2,1,0:T(8,128)(2,1)S(1)} %collective-permute-done.2.refs_2_), channel_id=1, source_target_pairs={{1,3},{3,1},{4,6},{6,4},{9,11},{11,9},{12,14},{14,12},{17,19},{19,... | collective-permute-start | bytes 786440 | tf_op jit(solution)/shard_map/ppermute | solution.py:309
  53.5 13.4 %collective-permute-start.15 = (bf16[512,256]{1,0:T(8,128)(2,1)S(1)}, bf16[512,256]{1,0:T(8,128)(2,1)S(1)}, u32[]{:S(2)}, u32[]{:S(2)}) collective-permute-start(bf16[512,256]{1,0:T(8,128)(2,1)S(1)} %get-tuple-element.94), channel_id=1, source_target_pairs={{0,1},{1,0},{2,3},{3,2},{4,5},{5,4},{6,7},{7,6},{8,9},{9,8},{10,11... | collective-permute-start | bytes 786440 | tf_op jit(solution)/shard_map/ppermute | solution.py:309
  58.3 9.8 %collective-permute-start.16 = (bf16[512,256]{1,0:T(8,128)(2,1)S(1)}, bf16[512,256]{1,0:T(8,128)(2,1)S(1)}, u32[]{:S(2)}, u32[]{:S(2)}) collective-permute-start(bf16[512,256]{1,0:T(8,128)(2,1)S(1)} %get-tuple-element.97), channel_id=1, source_target_pairs={{0,4},{1,8},{2,6},{3,10},{4,0},{5,12},{6,2},{7,14},{8,1},{9,16},{1... | collective-permute-start | bytes 786440 | tf_op jit(solution)/shard_map/ppermute | solution.py:309
  69.2 6.4 %collective-permute-start.18 = (bf16[512,256]{1,0:T(8,128)(2,1)S(1)}, bf16[512,256]{1,0:T(8,128)(2,1)S(1)}, u32[]{:S(2)}, u32[]{:S(2)}) collective-permute-start(bf16[512,256]{1,0:T(8,128)(2,1)S(1)} %shard_map.78), channel_id=1, source_target_pairs={{0,4},{1,8},{2,6},{3,10},{4,0},{5,12},{6,2},{7,14},{8,1},{9,16},{1... | collective-permute-start | bytes 786440 | tf_op jit(solution)/shard_map/ppermute | solution.py:309
  77.2 6.4 %collective-permute-start.20 = (bf16[512,256]{1,0:T(8,128)(2,1)S(1)}, bf16[512,256]{1,0:T(8,128)(2,1)S(1)}, u32[]{:S(2)}, u32[]{:S(2)}) collective-permute-start(bf16[512,256]{1,0:T(8,128)(2,1)S(1)} %shard_map.81.refs_3_), channel_id=1, source_target_pairs={{0,4},{1,8},{2,6},{3,10},{4,0},{5,12},{6,2},{7,14},{8,1},{9,16},{1... | collective-permute-start | bytes 786440 | tf_op jit(solution)/shard_map/ppermute | solution.py:309
  86.1 7.6 %collective-permute-start.24 = (bf16[256,512]{1,0:T(8,128)(2,1)S(1)}, bf16[256,512]{1,0:T(8,128)(2,1)S(1)}, u32[]{:S(2)}, u32[]{:S(2)}) collective-permute-start(bf16[256,512]{1,0:T(8,128)(2,1)S(1)} %get-tuple-element.103.high), channel_id=1, source_target_pairs={{0,4},{1,8},{2,6},{3,10},{4,0},{5,12},{6,2},{7,14},{8,1},{9,16},{1... | collective-permute-start | bytes 786440 | tf_op jit(solution)/shard_map/ppermute | solution.py:309
  86.6 10.0 %collective-permute-start.22 = (bf16[512,256]{1,0:T(8,128)(2,1)S(1)}, bf16[512,256]{1,0:T(8,128)(2,1)S(1)}, u32[]{:S(2)}, u32[]{:S(2)}) collective-permute-start(bf16[512,256]{1,0:T(8,128)(2,1)S(1)} %get-tuple-element.113), channel_id=1, source_target_pairs={{0,4},{1,8},{2,6},{3,10},{4,0},{5,12},{6,2},{7,14},{8,1},{9,16},{1... | collective-permute-start | bytes 786440 | tf_op jit(solution)/shard_map/ppermute | solution.py:309
  112.7 6.4 %collective-permute-start.30 = (bf16[512,256]{1,0:T(8,128)(2,1)S(1)}, bf16[512,256]{1,0:T(8,128)(2,1)S(1)}, u32[]{:S(2)}, u32[]{:S(2)}) collective-permute-start(bf16[512,256]{1,0:T(8,128)(2,1)S(1)} %get-tuple-element.130), channel_id=1, source_target_pairs={{0,4},{1,8},{2,6},{3,10},{4,0},{5,12},{6,2},{7,14},{8,1},{9,16},{1... | collective-permute-start | bytes 786440 | tf_op jit(solution)/shard_map/ppermute | solution.py:309
  142.9 6.4 %collective-permute-start.38 = (bf16[256,512]{1,0:T(8,128)(2,1)S(1)}, bf16[256,512]{1,0:T(8,128)(2,1)S(1)}, u32[]{:S(2)}, u32[]{:S(2)}) collective-permute-start(bf16[256,512]{1,0:T(8,128)(2,1)S(1)} %shard_map.97.own), channel_id=1, source_target_pairs={{0,8},{1,4},{2,10},{3,6},{4,1},{5,13},{6,3},{7,15},{8,0},{9,12},{1... | collective-permute-start | bytes 786440 | tf_op jit(solution)/shard_map/ppermute | solution.py:309
  143.8 8.4 %collective-permute-start.37 = (bf16[256,512]{1,0:T(8,128)(2,1)S(1)}, bf16[256,512]{1,0:T(8,128)(2,1)S(1)}, u32[]{:S(2)}, u32[]{:S(2)}) collective-permute-start(bf16[256,512]{1,0:T(8,128)(2,1)S(1)} %shard_map.96.own), channel_id=1, source_target_pairs={{0,8},{1,4},{2,10},{3,6},{4,1},{5,13},{6,3},{7,15},{8,0},{9,12},{1... | collective-permute-start | bytes 786440 | tf_op jit(solution)/shard_map/ppermute | solution.py:309
  (19 other events, 94.3 us)

commit v5 on v4

--- a/solution.py
+++ b/solution.py
@@ -362,13 +362,13 @@
     cut = middle // 2
     lots = [
         [(k, 1, (direct[k],)) for k in range(cut)],
-        [(k, 1, (direct[k],)) for k in range(cut, middle - 1)] + [(middle - 1, 1, (low, high))],
+        [(k, 1, (direct[k],)) for k in range(cut, middle - 1)],
         [(k, 0, (relayed[k],)) for k in range(middle - 2)],
-        [(middle - 2, 0, (relayed[middle - 2],))],
+        [(middle - 2, 0, (relayed[middle - 2],)), (middle - 1, 1, (low, high))],
         [(middle, 1, (extra, relayed[middle - 1]))],
     ]
-    whole = [[row[:2] for row in lot] for lot in lots]
-    holds = [whole[0], sum(whole[1:], []), [], [], []]
+    whole = sum([[row[:2] for row in lot] for lot in lots], [])
+    holds = [whole[: cap // 2], whole[cap // 2 :], [], [], []]
     for lot, hold in zip(lots, holds):
         given = [x for row in lot for x in row[2]]
         n = len(given)

time: 153 us -> 153 us (level)
  no operation moved by 1% of the time
where the time goes in v5:
time: 153 us
  waiting for transfers between devices  70.8 us (46%)
  starting transfers between devices  41.4 us (27%)
  Pallas kernels  38.3 us (25%)
    ppermute x36, waiting for transfers between devices, send(): return lax.ppermute(x, AXES, ways[way])  58.9 us
    ppermute x36, starting transfers between devices, send(): return lax.ppermute(x, AXES, ways[way])  38.4 us
    ppermute x3, waiting for transfers between devices, body(): lax.ppermute(pieces[place], 'col', [(k, k ^ bit) for k in range(columns)])  11.9 us
    pallas_call x10, Pallas kernels, body(): call(functools.partial(local_kernel, width, edge, not first, gives), outs...  10.7 us
    pallas_call x9, Pallas kernels, body(): call(functools.partial(finish_kernel, first, not plain, wants, width, edg...  8.62 us
    pallas_call x5, Pallas kernels, body(): call(functools.partial(build_kernel, [(*row[:2], len(row[2])) for row in...  8.01 us
    ppermute x3, starting transfers between devices, body(): lax.ppermute(pieces[place], 'col', [(k, k ^ bit) for k in range(columns)])  3.07 us
  transfers between devices with their start and end apart: 39, of which 16 were waited for; matrix products, arithmetic and copies ran while one was open for 0% of the time, Pallas kernels for 18%

profile of v5, /device:TPU:0, one launch (start us, length us, event | category | flops | bytes accessed | tf_op | source)
XLA Modules:
  0.0 153.1 jit_solution(4625555298491599199)
XLA Ops:
  1.3 3.1 %collective-permute-start.11 = (bf16[256,1024]{1,0:T(8,128)(2,1)S(1)}, bf16[256,1024]{1,0:T(8,128)(2,1)S(1)}, u32[]{:S(2)}, u32[]{:S(2)}) collective-permute-start(bf16[256,1024]{1,0:T(8,128)(2,1)S(1)} %convert_element_type.3.refs_0_), channel_id=1, source_target_pairs={{0,2},{1,3},{2,0},{3,1},{4,6},{5,7},{6,4},{7,5},{8,10},{9,11},{10,... | collective-permute-start | bytes 1572872 | tf_op jit(solution)/shard_map/ppermute | solution.py:324
  4.4 11.9 %collective-permute-done.11.refs_1_ = bf16[256,1024]{1,0:T(8,128)(2,1)S(1)} collective-permute-done((bf16[256,1024]{1,0:T(8,128)(2,1)S(1)}, bf16[256,1024]{1,0:T(8,128)(2,1)S(1)}, u32[]{:S(2)}, u32[]{:S(2)}) %collective-permute-start.11) | collective-permute-done | bytes 524320 | tf_op jit(solution)/shard_map/ppermute | solution.py:324
  17.8 1.9 %collective-permute-start.9 = (bf16[1,16,128,128]{3,2,1,0:T(8,128)(2,1)S(1)}, bf16[1,16,128,128]{3,2,1,0:T(8,128)(2,1)S(1)}, u32[]{:S(2)}, u32[]{:S(2)}) collective-permute-start(bf16[1,16,128,128]{3,2,1,0:T(8,128)(2,1)S(1)} %get-tuple-element.83), channel_id=1, source_target_pairs={{0,8},{1,4},{2,10},{3,6},{4,1},{5,13},{6,3},{7,15},{8,0},{9,12},{1... | collective-permute-start | bytes 1572872 | tf_op jit(solution)/shard_map/ppermute | solution.py:309
  25.1 1.8 %collective-permute-start.2 = (bf16[1,8,128,128]{3,2,1,0:T(8,128)(2,1)S(1)}, bf16[1,8,128,128]{3,2,1,0:T(8,128)(2,1)S(1)}, u32[]{:S(2)}, u32[]{:S(2)}) collective-permute-start(bf16[1,8,128,128]{3,2,1,0:T(8,128)(2,1)S(1)} %get-tuple-element.80), channel_id=1, source_target_pairs={{0,8},{1,4},{2,10},{3,6},{4,1},{5,13},{6,3},{7,15},{8,0},{9,12},{1... | collective-permute-start | bytes 786440 | tf_op jit(solution)/shard_map/ppermute | solution.py:309
  28.2 10.2 %collective-permute-done.moved = s32[137]{0:T(256)S(1)} collective-permute-done((s32[137]{0:T(256)S(1)}, s32[137]{0:T(256)S(1)}, u32[]{:S(2)}, u32[]{:S(2)}) %collective-permute-start) | collective-permute-done | bytes 580 | tf_op jit(solution)/shard_map/ppermute | solution.py:309
  38.4 1.8 %collective-permute-start.14 = (bf16[1024,256]{1,0:T(8,128)(2,1)S(1)}, bf16[1024,256]{1,0:T(8,128)(2,1)S(1)}, u32[]{:S(2)}, u32[]{:S(2)}) collective-permute-start(bf16[1024,256]{1,0:T(8,128)(2,1)S(1)} %shard_map.73.own), channel_id=1, source_target_pairs={{0,8},{1,4},{2,10},{3,6},{4,1},{5,13},{6,3},{7,15},{8,0},{9,12},{1... | collective-permute-start | bytes 1572872 | tf_op jit(solution)/shard_map/ppermute | solution.py:309
  44.3 6.1 %collective-permute-done.6.refs_1_ = bf16[1,8,128,128]{3,2,1,0:T(8,128)(2,1)S(1)} collective-permute-done((bf16[1,8,128,128]{3,2,1,0:T(8,128)(2,1)S(1)}, bf16[1,8,128,128]{3,2,1,0:T(8,128)(2,1)S(1)}, u32[]{:S(2)}, u32[]{:S(2)}) %collective-permute-start.6) | collective-permute-done | bytes 262176 | tf_op jit(solution)/shard_map/ppermute | solution.py:309
  50.4 1.8 %collective-permute-start.1 = (bf16[1,8,128,128]{3,2,1,0:T(8,128)(2,1)S(1)}, bf16[1,8,128,128]{3,2,1,0:T(8,128)(2,1)S(1)}, u32[]{:S(2)}, u32[]{:S(2)}) collective-permute-start(bf16[1,8,128,128]{3,2,1,0:T(8,128)(2,1)S(1)} %get-tuple-element.79), channel_id=1, source_target_pairs={{0,8},{1,4},{2,10},{3,6},{4,1},{5,13},{6,3},{7,15},{8,0},{9,12},{1... | collective-permute-start | bytes 786440 | tf_op jit(solution)/shard_map/ppermute | solution.py:309
  53.5 4.9 %collective-permute-start.15 = (bf16[512,256]{1,0:T(8,128)(2,1)S(1)}, bf16[512,256]{1,0:T(8,128)(2,1)S(1)}, u32[]{:S(2)}, u32[]{:S(2)}) collective-permute-start(bf16[512,256]{1,0:T(8,128)(2,1)S(1)} %get-tuple-element.94), channel_id=1, source_target_pairs={{0,1},{1,0},{2,3},{3,2},{4,5},{5,4},{6,7},{7,6},{8,9},{9,8},{10,11... | collective-permute-start | bytes 786440 | tf_op jit(solution)/shard_map/ppermute | solution.py:309
  58.8 3.0 %shard_map.68 = (bf16[1024,1536]{1,0:T(8,128)(2,1)S(1)}, bf16[1024,512]{1,0:T(8,128)(2,1)S(1)}) custom-call(s32[129]{0:T(256)S(1)} %get-tuple-element.78.info, bf16[8,16,128,128]{3,2,1,0:T(8,128)(2,1)} %blocks.13, bf16[1,16,128,128]{3,2,1,0:T(8,128)(2,1)S(1)} %collective-permute-done.7.refs_0_, bf16[1,16,128,128]{3,2,1,0:T(8,128)(2,1)S(1)} %collective-permute-done.9.refs_1_), custom_call_target="tpu_custom_call" | custom-call | tf_op jit(solution)/shard_map/pallas_call | solution.py:375
  61.8 3.0 %shard_map.69 = (bf16[1024,1536]{1,0:T(8,128)(2,1)S(1)}, bf16[1024,512]{1,0:T(8,128)(2,1)S(1)}) custom-call(s32[129]{0:T(256)S(1)} %get-tuple-element.78.info, bf16[8,16,128,128]{3,2,1,0:T(8,128)(2,1)} %blocks.13, bf16[1,16,128,128]{3,2,1,0:T(8,128)(2,1)S(1)} %collective-permute-done.4.refs_0_, ...), custom_call_target="tpu_custom_call", output_to_operand_aliasing={{0}: (3, {}), {1}: (4, {})} | custom-call | tf_op jit(solution)/shard_map/pallas_call | solution.py:375
  72.0 3.6 %collective-permute-done.18.refs_0_.far = bf16[512,256]{1,0:T(8,128)(2,1)S(1)} collective-permute-done((bf16[512,256]{1,0:T(8,128)(2,1)S(1)}, bf16[512,256]{1,0:T(8,128)(2,1)S(1)}, u32[]{:S(2)}, u32[]{:S(2)}) %collective-permute-start.18) | collective-permute-done | bytes 262176 | tf_op jit(solution)/shard_map/ppermute | solution.py:309
  79.9 3.8 %collective-permute-done.20.refs_0_ = bf16[512,256]{1,0:T(8,128)(2,1)S(1)} collective-permute-done((bf16[512,256]{1,0:T(8,128)(2,1)S(1)}, bf16[512,256]{1,0:T(8,128)(2,1)S(1)}, u32[]{:S(2)}, u32[]{:S(2)}) %collective-permute-start.20) | collective-permute-done | bytes 262176 | tf_op jit(solution)/shard_map/ppermute | solution.py:309
  90.9 2.8 %collective-permute-done.24.refs_2_.high = bf16[256,512]{1,0:T(8,128)(2,1)S(1)} collective-permute-done((bf16[256,512]{1,0:T(8,128)(2,1)S(1)}, bf16[256,512]{1,0:T(8,128)(2,1)S(1)}, u32[]{:S(2)}, u32[]{:S(2)}) %collective-permute-start.24) | collective-permute-done | bytes 262176 | tf_op jit(solution)/shard_map/ppermute | solution.py:309
  93.7 2.8 %collective-permute-done.22.refs_0_ = bf16[512,256]{1,0:T(8,128)(2,1)S(1)} collective-permute-done((bf16[512,256]{1,0:T(8,128)(2,1)S(1)}, bf16[512,256]{1,0:T(8,128)(2,1)S(1)}, u32[]{:S(2)}, u32[]{:S(2)}) %collective-permute-start.22) | collective-permute-done | bytes 262176 | tf_op jit(solution)/shard_map/ppermute | solution.py:309
  100.3 3.8 %collective-permute-done.26.refs_0_ = bf16[512,256]{1,0:T(8,128)(2,1)S(1)} collective-permute-done((bf16[512,256]{1,0:T(8,128)(2,1)S(1)}, bf16[512,256]{1,0:T(8,128)(2,1)S(1)}, u32[]{:S(2)}, u32[]{:S(2)}) %collective-permute-start.26) | collective-permute-done | bytes 262176 | tf_op jit(solution)/shard_map/ppermute | solution.py:309
  107.8 3.8 %collective-permute-done.28.refs_0_ = bf16[512,256]{1,0:T(8,128)(2,1)S(1)} collective-permute-done((bf16[512,256]{1,0:T(8,128)(2,1)S(1)}, bf16[512,256]{1,0:T(8,128)(2,1)S(1)}, u32[]{:S(2)}, u32[]{:S(2)}) %collective-permute-start.28) | collective-permute-done | bytes 262176 | tf_op jit(solution)/shard_map/ppermute | solution.py:309
  115.3 3.8 %collective-permute-done.30.refs_0_ = bf16[512,256]{1,0:T(8,128)(2,1)S(1)} collective-permute-done((bf16[512,256]{1,0:T(8,128)(2,1)S(1)}, bf16[512,256]{1,0:T(8,128)(2,1)S(1)}, u32[]{:S(2)}, u32[]{:S(2)}) %collective-permute-start.30) | collective-permute-done | bytes 262176 | tf_op jit(solution)/shard_map/ppermute | solution.py:309
  122.8 3.8 %collective-permute-done.32.refs_0_ = bf16[512,256]{1,0:T(8,128)(2,1)S(1)} collective-permute-done((bf16[512,256]{1,0:T(8,128)(2,1)S(1)}, bf16[512,256]{1,0:T(8,128)(2,1)S(1)}, u32[]{:S(2)}, u32[]{:S(2)}) %collective-permute-start.32) | collective-permute-done | bytes 262176 | tf_op jit(solution)/shard_map/ppermute | solution.py:309
  130.5 3.5 %collective-permute-done.34.refs_0_ = bf16[512,256]{1,0:T(8,128)(2,1)S(1)} collective-permute-done((bf16[512,256]{1,0:T(8,128)(2,1)S(1)}, bf16[512,256]{1,0:T(8,128)(2,1)S(1)}, u32[]{:S(2)}, u32[]{:S(2)}) %collective-permute-start.34) | collective-permute-done | bytes 262176 | tf_op jit(solution)/shard_map/ppermute | solution.py:309
  138.3 3.8 %collective-permute-done.36.part = bf16[512,256]{1,0:T(8,128)(2,1)S(1)} collective-permute-done((bf16[512,256]{1,0:T(8,128)(2,1)S(1)}, bf16[512,256]{1,0:T(8,128)(2,1)S(1)}, u32[]{:S(2)}, u32[]{:S(2)}) %collective-permute-start.36) | collective-permute-done | bytes 262176 | tf_op jit(solution)/shard_map/ppermute | solution.py:309
  143.8 2.1 %collective-permute-start.37 = (bf16[256,512]{1,0:T(8,128)(2,1)S(1)}, bf16[256,512]{1,0:T(8,128)(2,1)S(1)}, u32[]{:S(2)}, u32[]{:S(2)}) collective-permute-start(bf16[256,512]{1,0:T(8,128)(2,1)S(1)} %shard_map.96.own), channel_id=1, source_target_pairs={{0,8},{1,4},{2,10},{3,6},{4,1},{5,13},{6,3},{7,15},{8,0},{9,12},{1... | collective-permute-start | bytes 786440 | tf_op jit(solution)/shard_map/ppermute | solution.py:309
  145.9 3.5 %collective-permute-done.38.moved = bf16[256,512]{1,0:T(8,128)(2,1)S(1)} collective-permute-done((bf16[256,512]{1,0:T(8,128)(2,1)S(1)}, bf16[256,512]{1,0:T(8,128)(2,1)S(1)}, u32[]{:S(2)}, u32[]{:S(2)}) %collective-permute-start.38) | collective-permute-done | bytes 262176 | tf_op jit(solution)/shard_map/ppermute | solution.py:309
  150.2 2.0 %collective-permute-done.37.moved = bf16[256,512]{1,0:T(8,128)(2,1)S(1)} collective-permute-done((bf16[256,512]{1,0:T(8,128)(2,1)S(1)}, bf16[256,512]{1,0:T(8,128)(2,1)S(1)}, u32[]{:S(2)}, u32[]{:S(2)}) %collective-permute-start.37) | collective-permute-done | bytes 262176 | tf_op jit(solution)/shard_map/ppermute | solution.py:309
  (99 shorter events, 59.6 us)
Async XLA Ops:
  1.3 15.0 %collective-permute-start.11 = (bf16[256,1024]{1,0:T(8,128)(2,1)S(1)}, bf16[256,1024]{1,0:T(8,128)(2,1)S(1)}, u32[]{:S(2)}, u32[]{:S(2)}) collective-permute-start(bf16[256,1024]{1,0:T(8,128)(2,1)S(1)} %convert_element_type.3.refs_0_), channel_id=1, source_target_pairs={{0,2},{1,3},{2,0},{3,1},{4,6},{5,7},{6,4},{7,5},{8,10},{9,11},{10,... | collective-permute-start | bytes 1572872 | tf_op jit(solution)/shard_map/ppermute | solution.py:324
  4.4 20.4 %collective-permute-start.12 = (bf16[256,1024]{1,0:T(8,128)(2,1)S(1)}, bf16[256,1024]{1,0:T(8,128)(2,1)S(1)}, u32[]{:S(2)}, u32[]{:S(2)}) collective-permute-start(bf16[256,1024]{1,0:T(8,128)(2,1)S(1)} %convert_element_type.3.refs_0_), channel_id=1, source_target_pairs={{0,1},{1,0},{2,3},{3,2},{4,5},{5,4},{6,7},{7,6},{8,9},{9,8},{10,11... | collective-permute-start | bytes 1572872 | tf_op jit(solution)/shard_map/ppermute | solution.py:324
  16.3 8.9 %collective-permute-start.13 = (bf16[256,1024]{1,0:T(8,128)(2,1)S(1)}, bf16[256,1024]{1,0:T(8,128)(2,1)S(1)}, u32[]{:S(2)}, u32[]{:S(2)}) collective-permute-start(bf16[256,1024]{1,0:T(8,128)(2,1)S(1)} %collective-permute-done.11.refs_1_), channel_id=1, source_target_pairs={{0,1},{1,0},{2,3},{3,2},{4,5},{5,4},{6,7},{7,6},{8,9},{9,8},{10,11... | collective-permute-start | bytes 1572872 | tf_op jit(solution)/shard_map/ppermute | solution.py:324
  17.8 22.3 %collective-permute-start.9 = (bf16[1,16,128,128]{3,2,1,0:T(8,128)(2,1)S(1)}, bf16[1,16,128,128]{3,2,1,0:T(8,128)(2,1)S(1)}, u32[]{:S(2)}, u32[]{:S(2)}) collective-permute-start(bf16[1,16,128,128]{3,2,1,0:T(8,128)(2,1)S(1)} %get-tuple-element.83), channel_id=1, source_target_pairs={{0,8},{1,4},{2,10},{3,6},{4,1},{5,13},{6,3},{7,15},{8,0},{9,12},{1... | collective-permute-start | bytes 1572872 | tf_op jit(solution)/shard_map/ppermute | solution.py:309
  20.8 20.1 %collective-permute-start.7 = (bf16[1,16,128,128]{3,2,1,0:T(8,128)(2,1)S(1)}, bf16[1,16,128,128]{3,2,1,0:T(8,128)(2,1)S(1)}, u32[]{:S(2)}, u32[]{:S(2)}) collective-permute-start(bf16[1,16,128,128]{3,2,1,0:T(8,128)(2,1)S(1)} %shard_map.67), channel_id=1, source_target_pairs={{0,8},{1,4},{2,10},{3,6},{4,1},{5,13},{6,3},{7,15},{8,0},{9,12},{1... | collective-permute-start | bytes 1572872 | tf_op jit(solution)/shard_map/ppermute | solution.py:309
  21.1 20.5 %collective-permute-start.4 = (bf16[1,16,128,128]{3,2,1,0:T(8,128)(2,1)S(1)}, bf16[1,16,128,128]{3,2,1,0:T(8,128)(2,1)S(1)}, u32[]{:S(2)}, u32[]{:S(2)}) collective-permute-start(bf16[1,16,128,128]{3,2,1,0:T(8,128)(2,1)S(1)} %get-tuple-element.81), channel_id=1, source_target_pairs={{0,8},{1,4},{2,10},{3,6},{4,1},{5,13},{6,3},{7,15},{8,0},{9,12},{1... | collective-permute-start | bytes 1572872 | tf_op jit(solution)/shard_map/ppermute | solution.py:309
  24.8 13.6 %collective-permute-start = (s32[137]{0:T(256)S(1)}, s32[137]{0:T(256)S(1)}, u32[]{:S(2)}, u32[]{:S(2)}) collective-permute-start(s32[137]{0:T(256)S(1)} %shard_map.64.own), channel_id=1, source_target_pairs={{0,8},{1,4},{2,10},{3,6},{4,1},{5,13},{6,3},{7,15},{8,0},{9,12},{1... | collective-permute-start | bytes 1652 | tf_op jit(solution)/shard_map/ppermute | solution.py:309
  25.1 17.1 %collective-permute-start.2 = (bf16[1,8,128,128]{3,2,1,0:T(8,128)(2,1)S(1)}, bf16[1,8,128,128]{3,2,1,0:T(8,128)(2,1)S(1)}, u32[]{:S(2)}, u32[]{:S(2)}) collective-permute-start(bf16[1,8,128,128]{3,2,1,0:T(8,128)(2,1)S(1)} %get-tuple-element.80), channel_id=1, source_target_pairs={{0,8},{1,4},{2,10},{3,6},{4,1},{5,13},{6,3},{7,15},{8,0},{9,12},{1... | collective-permute-start | bytes 786440 | tf_op jit(solution)/shard_map/ppermute | solution.py:309
  38.4 13.8 %collective-permute-start.14 = (bf16[1024,256]{1,0:T(8,128)(2,1)S(1)}, bf16[1024,256]{1,0:T(8,128)(2,1)S(1)}, u32[]{:S(2)}, u32[]{:S(2)}) collective-permute-start(bf16[1024,256]{1,0:T(8,128)(2,1)S(1)} %shard_map.73.own), channel_id=1, source_target_pairs={{0,8},{1,4},{2,10},{3,6},{4,1},{5,13},{6,3},{7,15},{8,0},{9,12},{1... | collective-permute-start | bytes 1572872 | tf_op jit(solution)/shard_map/ppermute | solution.py:309
  40.2 13.3 %collective-permute-start.10 = (bf16[1,16,128,128]{3,2,1,0:T(8,128)(2,1)S(1)}, bf16[1,16,128,128]{3,2,1,0:T(8,128)(2,1)S(1)}, u32[]{:S(2)}, u32[]{:S(2)}) collective-permute-start(bf16[1,16,128,128]{3,2,1,0:T(8,128)(2,1)S(1)} %collective-permute-done.9.refs_1_), channel_id=1, source_target_pairs={{1,3},{3,1},{4,6},{6,4},{9,11},{11,9},{12,14},{14,12},{17,19},{19,... | collective-permute-start | bytes 1572872 | tf_op jit(solution)/shard_map/ppermute | solution.py:309
  40.9 17.5 %collective-permute-start.8 = (bf16[1,16,128,128]{3,2,1,0:T(8,128)(2,1)S(1)}, bf16[1,16,128,128]{3,2,1,0:T(8,128)(2,1)S(1)}, u32[]{:S(2)}, u32[]{:S(2)}) collective-permute-start(bf16[1,16,128,128]{3,2,1,0:T(8,128)(2,1)S(1)} %collective-permute-done.7.refs_0_), channel_id=1, source_target_pairs={{1,3},{3,1},{4,6},{6,4},{9,11},{11,9},{12,14},{14,12},{17,19},{19,... | collective-permute-start | bytes 1572872 | tf_op jit(solution)/shard_map/ppermute | solution.py:309
  41.6 23.9 %collective-permute-start.5 = (bf16[1,16,128,128]{3,2,1,0:T(8,128)(2,1)S(1)}, bf16[1,16,128,128]{3,2,1,0:T(8,128)(2,1)S(1)}, u32[]{:S(2)}, u32[]{:S(2)}) collective-permute-start(bf16[1,16,128,128]{3,2,1,0:T(8,128)(2,1)S(1)} %collective-permute-done.4.refs_0_), channel_id=1, source_target_pairs={{1,3},{3,1},{4,6},{6,4},{9,11},{11,9},{12,14},{14,12},{17,19},{19,... | collective-permute-start | bytes 1572872 | tf_op jit(solution)/shard_map/ppermute | solution.py:309
  42.3 8.1 %collective-permute-start.6 = (bf16[1,8,128,128]{3,2,1,0:T(8,128)(2,1)S(1)}, bf16[1,8,128,128]{3,2,1,0:T(8,128)(2,1)S(1)}, u32[]{:S(2)}, u32[]{:S(2)}) collective-permute-start(bf16[1,8,128,128]{3,2,1,0:T(8,128)(2,1)S(1)} %get-tuple-element.82), channel_id=1, source_target_pairs={{0,8},{1,4},{2,10},{3,6},{4,1},{5,13},{6,3},{7,15},{8,0},{9,12},{1... | collective-permute-start | bytes 786440 | tf_op jit(solution)/shard_map/ppermute | solution.py:309
  50.4 15.7 %collective-permute-start.1 = (bf16[1,8,128,128]{3,2,1,0:T(8,128)(2,1)S(1)}, bf16[1,8,128,128]{3,2,1,0:T(8,128)(2,1)S(1)}, u32[]{:S(2)}, u32[]{:S(2)}) collective-permute-start(bf16[1,8,128,128]{3,2,1,0:T(8,128)(2,1)S(1)} %get-tuple-element.79), channel_id=1, source_target_pairs={{0,8},{1,4},{2,10},{3,6},{4,1},{5,13},{6,3},{7,15},{8,0},{9,12},{1... | collective-permute-start | bytes 786440 | tf_op jit(solution)/shard_map/ppermute | solution.py:309
  52.2 13.9 %collective-permute-start.3 = (bf16[1,8,128,128]{3,2,1,0:T(8,128)(2,1)S(1)}, bf16[1,8,128,128]{3,2,1,0:T(8,128)(2,1)S(1)}, u32[]{:S(2)}, u32[]{:S(2)}) collective-permute-start(bf16[1,8,128,128]{3,2,1,0:T(8,128)(2,1)S(1)} %collective-permute-done.2.refs_2_), channel_id=1, source_target_pairs={{1,3},{3,1},{4,6},{6,4},{9,11},{11,9},{12,14},{14,12},{17,19},{19,... | collective-permute-start | bytes 786440 | tf_op jit(solution)/shard_map/ppermute | solution.py:309
  53.5 13.4 %collective-permute-start.15 = (bf16[512,256]{1,0:T(8,128)(2,1)S(1)}, bf16[512,256]{1,0:T(8,128)(2,1)S(1)}, u32[]{:S(2)}, u32[]{:S(2)}) collective-permute-start(bf16[512,256]{1,0:T(8,128)(2,1)S(1)} %get-tuple-element.94), channel_id=1, source_target_pairs={{0,1},{1,0},{2,3},{3,2},{4,5},{5,4},{6,7},{7,6},{8,9},{9,8},{10,11... | collective-permute-start | bytes 786440 | tf_op jit(solution)/shard_map/ppermute | solution.py:309
  58.3 9.8 %collective-permute-start.16 = (bf16[512,256]{1,0:T(8,128)(2,1)S(1)}, bf16[512,256]{1,0:T(8,128)(2,1)S(1)}, u32[]{:S(2)}, u32[]{:S(2)}) collective-permute-start(bf16[512,256]{1,0:T(8,128)(2,1)S(1)} %get-tuple-element.97), channel_id=1, source_target_pairs={{0,4},{1,8},{2,6},{3,10},{4,0},{5,12},{6,2},{7,14},{8,1},{9,16},{1... | collective-permute-start | bytes 786440 | tf_op jit(solution)/shard_map/ppermute | solution.py:309
  69.2 6.4 %collective-permute-start.18 = (bf16[512,256]{1,0:T(8,128)(2,1)S(1)}, bf16[512,256]{1,0:T(8,128)(2,1)S(1)}, u32[]{:S(2)}, u32[]{:S(2)}) collective-permute-start(bf16[512,256]{1,0:T(8,128)(2,1)S(1)} %shard_map.78), channel_id=1, source_target_pairs={{0,4},{1,8},{2,6},{3,10},{4,0},{5,12},{6,2},{7,14},{8,1},{9,16},{1... | collective-permute-start | bytes 786440 | tf_op jit(solution)/shard_map/ppermute | solution.py:309
  77.2 6.4 %collective-permute-start.20 = (bf16[512,256]{1,0:T(8,128)(2,1)S(1)}, bf16[512,256]{1,0:T(8,128)(2,1)S(1)}, u32[]{:S(2)}, u32[]{:S(2)}) collective-permute-start(bf16[512,256]{1,0:T(8,128)(2,1)S(1)} %shard_map.81.refs_3_), channel_id=1, source_target_pairs={{0,4},{1,8},{2,6},{3,10},{4,0},{5,12},{6,2},{7,14},{8,1},{9,16},{1... | collective-permute-start | bytes 786440 | tf_op jit(solution)/shard_map/ppermute | solution.py:309
  84.6 6.4 %collective-permute-start.23 = (bf16[256,512]{1,0:T(8,128)(2,1)S(1)}, bf16[256,512]{1,0:T(8,128)(2,1)S(1)}, u32[]{:S(2)}, u32[]{:S(2)}) collective-permute-start(bf16[256,512]{1,0:T(8,128)(2,1)S(1)} %get-tuple-element.102.low), channel_id=1, source_target_pairs={{0,4},{1,8},{2,6},{3,10},{4,0},{5,12},{6,2},{7,14},{8,1},{9,16},{1... | collective-permute-start | bytes 786440 | tf_op jit(solution)/shard_map/ppermute | solution.py:309
  86.1 7.6 %collective-permute-start.24 = (bf16[256,512]{1,0:T(8,128)(2,1)S(1)}, bf16[256,512]{1,0:T(8,128)(2,1)S(1)}, u32[]{:S(2)}, u32[]{:S(2)}) collective-permute-start(bf16[256,512]{1,0:T(8,128)(2,1)S(1)} %get-tuple-element.103.high), channel_id=1, source_target_pairs={{0,4},{1,8},{2,6},{3,10},{4,0},{5,12},{6,2},{7,14},{8,1},{9,16},{1... | collective-permute-start | bytes 786440 | tf_op jit(solution)/shard_map/ppermute | solution.py:309
  86.6 10.0 %collective-permute-start.22 = (bf16[512,256]{1,0:T(8,128)(2,1)S(1)}, bf16[512,256]{1,0:T(8,128)(2,1)S(1)}, u32[]{:S(2)}, u32[]{:S(2)}) collective-permute-start(bf16[512,256]{1,0:T(8,128)(2,1)S(1)} %get-tuple-element.113), channel_id=1, source_target_pairs={{0,4},{1,8},{2,6},{3,10},{4,0},{5,12},{6,2},{7,14},{8,1},{9,16},{1... | collective-permute-start | bytes 786440 | tf_op jit(solution)/shard_map/ppermute | solution.py:309
  142.9 6.4 %collective-permute-start.38 = (bf16[256,512]{1,0:T(8,128)(2,1)S(1)}, bf16[256,512]{1,0:T(8,128)(2,1)S(1)}, u32[]{:S(2)}, u32[]{:S(2)}) collective-permute-start(bf16[256,512]{1,0:T(8,128)(2,1)S(1)} %shard_map.97.own), channel_id=1, source_target_pairs={{0,8},{1,4},{2,10},{3,6},{4,1},{5,13},{6,3},{7,15},{8,0},{9,12},{1... | collective-permute-start | bytes 786440 | tf_op jit(solution)/shard_map/ppermute | solution.py:309
  143.8 8.4 %collective-permute-start.37 = (bf16[256,512]{1,0:T(8,128)(2,1)S(1)}, bf16[256,512]{1,0:T(8,128)(2,1)S(1)}, u32[]{:S(2)}, u32[]{:S(2)}) collective-permute-start(bf16[256,512]{1,0:T(8,128)(2,1)S(1)} %shard_map.96.own), channel_id=1, source_target_pairs={{0,8},{1,4},{2,10},{3,6},{4,1},{5,13},{6,3},{7,15},{8,0},{9,12},{1... | collective-permute-start | bytes 786440 | tf_op jit(solution)/shard_map/ppermute | solution.py:309
  (19 other events, 94.8 us)

commit v6 on v5

--- a/solution.py
+++ b/solution.py
@@ -9,7 +9,7 @@
 
 
 STEPS = 10
-PLAIN = 2
+PLAIN = 1
 AXES = ("row", "col")
 F32, BF16 = jnp.float32, jnp.bfloat16
 VMEM = pl.BlockSpec(memory_space=pltpu.VMEM)
@@ -403,8 +403,8 @@
         if plain:
             far = send(far_send, "far")
             sent_rows[step] = far_send
-        if 0 < step <= 2:
-            theirs.append(send(far_part[step - 1], "far"))
+        if step == 1:
+            theirs = [send(x, "far") for x in far_part]
         gives = "both" if first else "" if last else "one"
         kind = F32 if step < PLAIN else BF16
         outs = (wide(F32),) + ((part(kind),) if gives else ()) + ((square,) * 2 if first else ())

time: 153 us -> 153 us (level)
  no operation moved by 1% of the time
where the time goes in v6:
time: 153 us
  waiting for transfers between devices  70.2 us (46%)
  starting transfers between devices  41.9 us (27%)
  Pallas kernels  37.9 us (25%)
    ppermute x36, waiting for transfers between devices, send(): return lax.ppermute(x, AXES, ways[way])  58.3 us
    ppermute x36, starting transfers between devices, send(): return lax.ppermute(x, AXES, ways[way])  38.9 us
    ppermute x3, waiting for transfers between devices, body(): lax.ppermute(pieces[place], 'col', [(k, k ^ bit) for k in range(columns)])  11.9 us
    pallas_call x10, Pallas kernels, body(): call(functools.partial(local_kernel, width, edge, not first, gives), outs...  10.7 us
    pallas_call x9, Pallas kernels, body(): call(functools.partial(finish_kernel, first, not plain, wants, width, edg...  8.52 us
    pallas_call x5, Pallas kernels, body(): call(functools.partial(build_kernel, [(*row[:2], len(row[2])) for row in...  8.01 us
    ppermute x3, starting transfers between devices, body(): lax.ppermute(pieces[place], 'col', [(k, k ^ bit) for k in range(columns)])  3.07 us
  transfers between devices with their start and end apart: 39, of which 16 were waited for; matrix products, arithmetic and copies ran while one was open for 0% of the time, Pallas kernels for 18%

profile of v6, /device:TPU:0, one launch (start us, length us, event | category | flops | bytes accessed | tf_op | source)
XLA Modules:
  0.0 152.7 jit_solution(9797036190165799982)
XLA Ops:
  1.3 3.1 %collective-permute-start.11 = (bf16[256,1024]{1,0:T(8,128)(2,1)S(1)}, bf16[256,1024]{1,0:T(8,128)(2,1)S(1)}, u32[]{:S(2)}, u32[]{:S(2)}) collective-permute-start(bf16[256,1024]{1,0:T(8,128)(2,1)S(1)} %convert_element_type.3.refs_0_), channel_id=1, source_target_pairs={{0,2},{1,3},{2,0},{3,1},{4,6},{5,7},{6,4},{7,5},{8,10},{9,11},{10,... | collective-permute-start | bytes 1572872 | tf_op jit(solution)/shard_map/ppermute | solution.py:324
  4.4 11.9 %collective-permute-done.11.refs_1_ = bf16[256,1024]{1,0:T(8,128)(2,1)S(1)} collective-permute-done((bf16[256,1024]{1,0:T(8,128)(2,1)S(1)}, bf16[256,1024]{1,0:T(8,128)(2,1)S(1)}, u32[]{:S(2)}, u32[]{:S(2)}) %collective-permute-start.11) | collective-permute-done | bytes 524320 | tf_op jit(solution)/shard_map/ppermute | solution.py:324
  17.8 1.9 %collective-permute-start.9 = (bf16[1,16,128,128]{3,2,1,0:T(8,128)(2,1)S(1)}, bf16[1,16,128,128]{3,2,1,0:T(8,128)(2,1)S(1)}, u32[]{:S(2)}, u32[]{:S(2)}) collective-permute-start(bf16[1,16,128,128]{3,2,1,0:T(8,128)(2,1)S(1)} %get-tuple-element.84), channel_id=1, source_target_pairs={{0,8},{1,4},{2,10},{3,6},{4,1},{5,13},{6,3},{7,15},{8,0},{9,12},{1... | collective-permute-start | bytes 1572872 | tf_op jit(solution)/shard_map/ppermute | solution.py:309
  25.1 1.8 %collective-permute-start.2 = (bf16[1,8,128,128]{3,2,1,0:T(8,128)(2,1)S(1)}, bf16[1,8,128,128]{3,2,1,0:T(8,128)(2,1)S(1)}, u32[]{:S(2)}, u32[]{:S(2)}) collective-permute-start(bf16[1,8,128,128]{3,2,1,0:T(8,128)(2,1)S(1)} %get-tuple-element.81), channel_id=1, source_target_pairs={{0,8},{1,4},{2,10},{3,6},{4,1},{5,13},{6,3},{7,15},{8,0},{9,12},{1... | collective-permute-start | bytes 786440 | tf_op jit(solution)/shard_map/ppermute | solution.py:309
  28.2 10.2 %collective-permute-done.moved = s32[137]{0:T(256)S(1)} collective-permute-done((s32[137]{0:T(256)S(1)}, s32[137]{0:T(256)S(1)}, u32[]{:S(2)}, u32[]{:S(2)}) %collective-permute-start) | collective-permute-done | bytes 580 | tf_op jit(solution)/shard_map/ppermute | solution.py:309
  38.4 1.8 %collective-permute-start.14 = (bf16[1024,256]{1,0:T(8,128)(2,1)S(1)}, bf16[1024,256]{1,0:T(8,128)(2,1)S(1)}, u32[]{:S(2)}, u32[]{:S(2)}) collective-permute-start(bf16[1024,256]{1,0:T(8,128)(2,1)S(1)} %shard_map.73.own), channel_id=1, source_target_pairs={{0,8},{1,4},{2,10},{3,6},{4,1},{5,13},{6,3},{7,15},{8,0},{9,12},{1... | collective-permute-start | bytes 1572872 | tf_op jit(solution)/shard_map/ppermute | solution.py:309
  44.3 6.1 %collective-permute-done.6.refs_1_ = bf16[1,8,128,128]{3,2,1,0:T(8,128)(2,1)S(1)} collective-permute-done((bf16[1,8,128,128]{3,2,1,0:T(8,128)(2,1)S(1)}, bf16[1,8,128,128]{3,2,1,0:T(8,128)(2,1)S(1)}, u32[]{:S(2)}, u32[]{:S(2)}) %collective-permute-start.6) | collective-permute-done | bytes 262176 | tf_op jit(solution)/shard_map/ppermute | solution.py:309
  50.4 1.8 %collective-permute-start.1 = (bf16[1,8,128,128]{3,2,1,0:T(8,128)(2,1)S(1)}, bf16[1,8,128,128]{3,2,1,0:T(8,128)(2,1)S(1)}, u32[]{:S(2)}, u32[]{:S(2)}) collective-permute-start(bf16[1,8,128,128]{3,2,1,0:T(8,128)(2,1)S(1)} %get-tuple-element.80), channel_id=1, source_target_pairs={{0,8},{1,4},{2,10},{3,6},{4,1},{5,13},{6,3},{7,15},{8,0},{9,12},{1... | collective-permute-start | bytes 786440 | tf_op jit(solution)/shard_map/ppermute | solution.py:309
  53.5 4.9 %collective-permute-start.15 = (bf16[512,256]{1,0:T(8,128)(2,1)S(1)}, bf16[512,256]{1,0:T(8,128)(2,1)S(1)}, u32[]{:S(2)}, u32[]{:S(2)}) collective-permute-start(bf16[512,256]{1,0:T(8,128)(2,1)S(1)} %get-tuple-element.95), channel_id=1, source_target_pairs={{0,1},{1,0},{2,3},{3,2},{4,5},{5,4},{6,7},{7,6},{8,9},{9,8},{10,11... | collective-permute-start | bytes 786440 | tf_op jit(solution)/shard_map/ppermute | solution.py:309
  58.8 3.0 %shard_map.68 = (bf16[1024,1536]{1,0:T(8,128)(2,1)S(1)}, bf16[1024,512]{1,0:T(8,128)(2,1)S(1)}) custom-call(s32[129]{0:T(256)S(1)} %get-tuple-element.79.info, bf16[8,16,128,128]{3,2,1,0:T(8,128)(2,1)} %blocks.13, bf16[1,16,128,128]{3,2,1,0:T(8,128)(2,1)S(1)} %collective-permute-done.7.refs_0_, bf16[1,16,128,128]{3,2,1,0:T(8,128)(2,1)S(1)} %collective-permute-done.9.refs_1_), custom_call_target="tpu_custom_call" | custom-call | tf_op jit(solution)/shard_map/pallas_call | solution.py:375
  61.8 3.0 %shard_map.69 = (bf16[1024,1536]{1,0:T(8,128)(2,1)S(1)}, bf16[1024,512]{1,0:T(8,128)(2,1)S(1)}) custom-call(s32[129]{0:T(256)S(1)} %get-tuple-element.79.info, bf16[8,16,128,128]{3,2,1,0:T(8,128)(2,1)} %blocks.13, bf16[1,16,128,128]{3,2,1,0:T(8,128)(2,1)S(1)} %collective-permute-done.4.refs_0_, ...), custom_call_target="tpu_custom_call", output_to_operand_aliasing={{0}: (3, {}), {1}: (4, {})} | custom-call | tf_op jit(solution)/shard_map/pallas_call | solution.py:375
  72.0 3.7 %collective-permute-done.18.refs_0_ = bf16[512,256]{1,0:T(8,128)(2,1)S(1)} collective-permute-done((bf16[512,256]{1,0:T(8,128)(2,1)S(1)}, bf16[512,256]{1,0:T(8,128)(2,1)S(1)}, u32[]{:S(2)}, u32[]{:S(2)}) %collective-permute-start.18) | collective-permute-done | bytes 262176 | tf_op jit(solution)/shard_map/ppermute | solution.py:309
  83.0 2.8 %collective-permute-done.22.refs_2_.high = bf16[256,512]{1,0:T(8,128)(2,1)S(1)} collective-permute-done((bf16[256,512]{1,0:T(8,128)(2,1)S(1)}, bf16[256,512]{1,0:T(8,128)(2,1)S(1)}, u32[]{:S(2)}, u32[]{:S(2)}) %collective-permute-start.22) | collective-permute-done | bytes 262176 | tf_op jit(solution)/shard_map/ppermute | solution.py:309
  85.8 2.8 %collective-permute-done.20.refs_0_ = bf16[512,256]{1,0:T(8,128)(2,1)S(1)} collective-permute-done((bf16[512,256]{1,0:T(8,128)(2,1)S(1)}, bf16[512,256]{1,0:T(8,128)(2,1)S(1)}, u32[]{:S(2)}, u32[]{:S(2)}) %collective-permute-start.20) | collective-permute-done | bytes 262176 | tf_op jit(solution)/shard_map/ppermute | solution.py:309
  92.4 3.7 %collective-permute-done.24.refs_0_ = bf16[512,256]{1,0:T(8,128)(2,1)S(1)} collective-permute-done((bf16[512,256]{1,0:T(8,128)(2,1)S(1)}, bf16[512,256]{1,0:T(8,128)(2,1)S(1)}, u32[]{:S(2)}, u32[]{:S(2)}) %collective-permute-start.24) | collective-permute-done | bytes 262176 | tf_op jit(solution)/shard_map/ppermute | solution.py:309
  99.9 3.7 %collective-permute-done.26.refs_0_ = bf16[512,256]{1,0:T(8,128)(2,1)S(1)} collective-permute-done((bf16[512,256]{1,0:T(8,128)(2,1)S(1)}, bf16[512,256]{1,0:T(8,128)(2,1)S(1)}, u32[]{:S(2)}, u32[]{:S(2)}) %collective-permute-start.26) | collective-permute-done | bytes 262176 | tf_op jit(solution)/shard_map/ppermute | solution.py:309
  107.4 3.7 %collective-permute-done.28.refs_0_ = bf16[512,256]{1,0:T(8,128)(2,1)S(1)} collective-permute-done((bf16[512,256]{1,0:T(8,128)(2,1)S(1)}, bf16[512,256]{1,0:T(8,128)(2,1)S(1)}, u32[]{:S(2)}, u32[]{:S(2)}) %collective-permute-start.28) | collective-permute-done | bytes 262176 | tf_op jit(solution)/shard_map/ppermute | solution.py:309
  114.9 3.7 %collective-permute-done.30.refs_0_ = bf16[512,256]{1,0:T(8,128)(2,1)S(1)} collective-permute-done((bf16[512,256]{1,0:T(8,128)(2,1)S(1)}, bf16[512,256]{1,0:T(8,128)(2,1)S(1)}, u32[]{:S(2)}, u32[]{:S(2)}) %collective-permute-start.30) | collective-permute-done | bytes 262176 | tf_op jit(solution)/shard_map/ppermute | solution.py:309
  122.4 3.7 %collective-permute-done.32.refs_0_ = bf16[512,256]{1,0:T(8,128)(2,1)S(1)} collective-permute-done((bf16[512,256]{1,0:T(8,128)(2,1)S(1)}, bf16[512,256]{1,0:T(8,128)(2,1)S(1)}, u32[]{:S(2)}, u32[]{:S(2)}) %collective-permute-start.32) | collective-permute-done | bytes 262176 | tf_op jit(solution)/shard_map/ppermute | solution.py:309
  130.2 3.4 %collective-permute-done.34.refs_0_ = bf16[512,256]{1,0:T(8,128)(2,1)S(1)} collective-permute-done((bf16[512,256]{1,0:T(8,128)(2,1)S(1)}, bf16[512,256]{1,0:T(8,128)(2,1)S(1)}, u32[]{:S(2)}, u32[]{:S(2)}) %collective-permute-start.34) | collective-permute-done | bytes 262176 | tf_op jit(solution)/shard_map/ppermute | solution.py:309
  137.9 3.7 %collective-permute-done.36.part = bf16[512,256]{1,0:T(8,128)(2,1)S(1)} collective-permute-done((bf16[512,256]{1,0:T(8,128)(2,1)S(1)}, bf16[512,256]{1,0:T(8,128)(2,1)S(1)}, u32[]{:S(2)}, u32[]{:S(2)}) %collective-permute-start.36) | collective-permute-done | bytes 262176 | tf_op jit(solution)/shard_map/ppermute | solution.py:309
  143.3 2.1 %collective-permute-start.37 = (bf16[256,512]{1,0:T(8,128)(2,1)S(1)}, bf16[256,512]{1,0:T(8,128)(2,1)S(1)}, u32[]{:S(2)}, u32[]{:S(2)}) collective-permute-start(bf16[256,512]{1,0:T(8,128)(2,1)S(1)} %shard_map.95.own), channel_id=1, source_target_pairs={{0,8},{1,4},{2,10},{3,6},{4,1},{5,13},{6,3},{7,15},{8,0},{9,12},{1... | collective-permute-start | bytes 786440 | tf_op jit(solution)/shard_map/ppermute | solution.py:309
  145.4 3.5 %collective-permute-done.38.moved = bf16[256,512]{1,0:T(8,128)(2,1)S(1)} collective-permute-done((bf16[256,512]{1,0:T(8,128)(2,1)S(1)}, bf16[256,512]{1,0:T(8,128)(2,1)S(1)}, u32[]{:S(2)}, u32[]{:S(2)}) %collective-permute-start.38) | collective-permute-done | bytes 262176 | tf_op jit(solution)/shard_map/ppermute | solution.py:309
  149.7 2.0 %collective-permute-done.37.moved = bf16[256,512]{1,0:T(8,128)(2,1)S(1)} collective-permute-done((bf16[256,512]{1,0:T(8,128)(2,1)S(1)}, bf16[256,512]{1,0:T(8,128)(2,1)S(1)}, u32[]{:S(2)}, u32[]{:S(2)}) %collective-permute-start.37) | collective-permute-done | bytes 262176 | tf_op jit(solution)/shard_map/ppermute | solution.py:309
  (98 shorter events, 59.6 us)
Async XLA Ops:
  1.3 15.0 %collective-permute-start.11 = (bf16[256,1024]{1,0:T(8,128)(2,1)S(1)}, bf16[256,1024]{1,0:T(8,128)(2,1)S(1)}, u32[]{:S(2)}, u32[]{:S(2)}) collective-permute-start(bf16[256,1024]{1,0:T(8,128)(2,1)S(1)} %convert_element_type.3.refs_0_), channel_id=1, source_target_pairs={{0,2},{1,3},{2,0},{3,1},{4,6},{5,7},{6,4},{7,5},{8,10},{9,11},{10,... | collective-permute-start | bytes 1572872 | tf_op jit(solution)/shard_map/ppermute | solution.py:324
  4.4 20.4 %collective-permute-start.12 = (bf16[256,1024]{1,0:T(8,128)(2,1)S(1)}, bf16[256,1024]{1,0:T(8,128)(2,1)S(1)}, u32[]{:S(2)}, u32[]{:S(2)}) collective-permute-start(bf16[256,1024]{1,0:T(8,128)(2,1)S(1)} %convert_element_type.3.refs_0_), channel_id=1, source_target_pairs={{0,1},{1,0},{2,3},{3,2},{4,5},{5,4},{6,7},{7,6},{8,9},{9,8},{10,11... | collective-permute-start | bytes 1572872 | tf_op jit(solution)/shard_map/ppermute | solution.py:324
  16.3 8.9 %collective-permute-start.13 = (bf16[256,1024]{1,0:T(8,128)(2,1)S(1)}, bf16[256,1024]{1,0:T(8,128)(2,1)S(1)}, u32[]{:S(2)}, u32[]{:S(2)}) collective-permute-start(bf16[256,1024]{1,0:T(8,128)(2,1)S(1)} %collective-permute-done.11.refs_1_), channel_id=1, source_target_pairs={{0,1},{1,0},{2,3},{3,2},{4,5},{5,4},{6,7},{7,6},{8,9},{9,8},{10,11... | collective-permute-start | bytes 1572872 | tf_op jit(solution)/shard_map/ppermute | solution.py:324
  17.8 22.3 %collective-permute-start.9 = (bf16[1,16,128,128]{3,2,1,0:T(8,128)(2,1)S(1)}, bf16[1,16,128,128]{3,2,1,0:T(8,128)(2,1)S(1)}, u32[]{:S(2)}, u32[]{:S(2)}) collective-permute-start(bf16[1,16,128,128]{3,2,1,0:T(8,128)(2,1)S(1)} %get-tuple-element.84), channel_id=1, source_target_pairs={{0,8},{1,4},{2,10},{3,6},{4,1},{5,13},{6,3},{7,15},{8,0},{9,12},{1... | collective-permute-start | bytes 1572872 | tf_op jit(solution)/shard_map/ppermute | solution.py:309
  20.8 20.1 %collective-permute-start.7 = (bf16[1,16,128,128]{3,2,1,0:T(8,128)(2,1)S(1)}, bf16[1,16,128,128]{3,2,1,0:T(8,128)(2,1)S(1)}, u32[]{:S(2)}, u32[]{:S(2)}) collective-permute-start(bf16[1,16,128,128]{3,2,1,0:T(8,128)(2,1)S(1)} %shard_map.67), channel_id=1, source_target_pairs={{0,8},{1,4},{2,10},{3,6},{4,1},{5,13},{6,3},{7,15},{8,0},{9,12},{1... | collective-permute-start | bytes 1572872 | tf_op jit(solution)/shard_map/ppermute | solution.py:309
  21.1 20.5 %collective-permute-start.4 = (bf16[1,16,128,128]{3,2,1,0:T(8,128)(2,1)S(1)}, bf16[1,16,128,128]{3,2,1,0:T(8,128)(2,1)S(1)}, u32[]{:S(2)}, u32[]{:S(2)}) collective-permute-start(bf16[1,16,128,128]{3,2,1,0:T(8,128)(2,1)S(1)} %get-tuple-element.82), channel_id=1, source_target_pairs={{0,8},{1,4},{2,10},{3,6},{4,1},{5,13},{6,3},{7,15},{8,0},{9,12},{1... | collective-permute-start | bytes 1572872 | tf_op jit(solution)/shard_map/ppermute | solution.py:309
  24.8 13.6 %collective-permute-start = (s32[137]{0:T(256)S(1)}, s32[137]{0:T(256)S(1)}, u32[]{:S(2)}, u32[]{:S(2)}) collective-permute-start(s32[137]{0:T(256)S(1)} %shard_map.64.own), channel_id=1, source_target_pairs={{0,8},{1,4},{2,10},{3,6},{4,1},{5,13},{6,3},{7,15},{8,0},{9,12},{1... | collective-permute-start | bytes 1652 | tf_op jit(solution)/shard_map/ppermute | solution.py:309
  25.1 17.1 %collective-permute-start.2 = (bf16[1,8,128,128]{3,2,1,0:T(8,128)(2,1)S(1)}, bf16[1,8,128,128]{3,2,1,0:T(8,128)(2,1)S(1)}, u32[]{:S(2)}, u32[]{:S(2)}) collective-permute-start(bf16[1,8,128,128]{3,2,1,0:T(8,128)(2,1)S(1)} %get-tuple-element.81), channel_id=1, source_target_pairs={{0,8},{1,4},{2,10},{3,6},{4,1},{5,13},{6,3},{7,15},{8,0},{9,12},{1... | collective-permute-start | bytes 786440 | tf_op jit(solution)/shard_map/ppermute | solution.py:309
  38.4 13.8 %collective-permute-start.14 = (bf16[1024,256]{1,0:T(8,128)(2,1)S(1)}, bf16[1024,256]{1,0:T(8,128)(2,1)S(1)}, u32[]{:S(2)}, u32[]{:S(2)}) collective-permute-start(bf16[1024,256]{1,0:T(8,128)(2,1)S(1)} %shard_map.73.own), channel_id=1, source_target_pairs={{0,8},{1,4},{2,10},{3,6},{4,1},{5,13},{6,3},{7,15},{8,0},{9,12},{1... | collective-permute-start | bytes 1572872 | tf_op jit(solution)/shard_map/ppermute | solution.py:309
  40.2 13.3 %collective-permute-start.10 = (bf16[1,16,128,128]{3,2,1,0:T(8,128)(2,1)S(1)}, bf16[1,16,128,128]{3,2,1,0:T(8,128)(2,1)S(1)}, u32[]{:S(2)}, u32[]{:S(2)}) collective-permute-start(bf16[1,16,128,128]{3,2,1,0:T(8,128)(2,1)S(1)} %collective-permute-done.9.refs_1_), channel_id=1, source_target_pairs={{1,3},{3,1},{4,6},{6,4},{9,11},{11,9},{12,14},{14,12},{17,19},{19,... | collective-permute-start | bytes 1572872 | tf_op jit(solution)/shard_map/ppermute | solution.py:309
  40.9 17.5 %collective-permute-start.8 = (bf16[1,16,128,128]{3,2,1,0:T(8,128)(2,1)S(1)}, bf16[1,16,128,128]{3,2,1,0:T(8,128)(2,1)S(1)}, u32[]{:S(2)}, u32[]{:S(2)}) collective-permute-start(bf16[1,16,128,128]{3,2,1,0:T(8,128)(2,1)S(1)} %collective-permute-done.7.refs_0_), channel_id=1, source_target_pairs={{1,3},{3,1},{4,6},{6,4},{9,11},{11,9},{12,14},{14,12},{17,19},{19,... | collective-permute-start | bytes 1572872 | tf_op jit(solution)/shard_map/ppermute | solution.py:309
  41.6 23.9 %collective-permute-start.5 = (bf16[1,16,128,128]{3,2,1,0:T(8,128)(2,1)S(1)}, bf16[1,16,128,128]{3,2,1,0:T(8,128)(2,1)S(1)}, u32[]{:S(2)}, u32[]{:S(2)}) collective-permute-start(bf16[1,16,128,128]{3,2,1,0:T(8,128)(2,1)S(1)} %collective-permute-done.4.refs_0_), channel_id=1, source_target_pairs={{1,3},{3,1},{4,6},{6,4},{9,11},{11,9},{12,14},{14,12},{17,19},{19,... | collective-permute-start | bytes 1572872 | tf_op jit(solution)/shard_map/ppermute | solution.py:309
  42.3 8.1 %collective-permute-start.6 = (bf16[1,8,128,128]{3,2,1,0:T(8,128)(2,1)S(1)}, bf16[1,8,128,128]{3,2,1,0:T(8,128)(2,1)S(1)}, u32[]{:S(2)}, u32[]{:S(2)}) collective-permute-start(bf16[1,8,128,128]{3,2,1,0:T(8,128)(2,1)S(1)} %get-tuple-element.83), channel_id=1, source_target_pairs={{0,8},{1,4},{2,10},{3,6},{4,1},{5,13},{6,3},{7,15},{8,0},{9,12},{1... | collective-permute-start | bytes 786440 | tf_op jit(solution)/shard_map/ppermute | solution.py:309
  50.4 15.7 %collective-permute-start.1 = (bf16[1,8,128,128]{3,2,1,0:T(8,128)(2,1)S(1)}, bf16[1,8,128,128]{3,2,1,0:T(8,128)(2,1)S(1)}, u32[]{:S(2)}, u32[]{:S(2)}) collective-permute-start(bf16[1,8,128,128]{3,2,1,0:T(8,128)(2,1)S(1)} %get-tuple-element.80), channel_id=1, source_target_pairs={{0,8},{1,4},{2,10},{3,6},{4,1},{5,13},{6,3},{7,15},{8,0},{9,12},{1... | collective-permute-start | bytes 786440 | tf_op jit(solution)/shard_map/ppermute | solution.py:309
  52.2 13.9 %collective-permute-start.3 = (bf16[1,8,128,128]{3,2,1,0:T(8,128)(2,1)S(1)}, bf16[1,8,128,128]{3,2,1,0:T(8,128)(2,1)S(1)}, u32[]{:S(2)}, u32[]{:S(2)}) collective-permute-start(bf16[1,8,128,128]{3,2,1,0:T(8,128)(2,1)S(1)} %collective-permute-done.2.refs_2_), channel_id=1, source_target_pairs={{1,3},{3,1},{4,6},{6,4},{9,11},{11,9},{12,14},{14,12},{17,19},{19,... | collective-permute-start | bytes 786440 | tf_op jit(solution)/shard_map/ppermute | solution.py:309
  53.5 13.4 %collective-permute-start.15 = (bf16[512,256]{1,0:T(8,128)(2,1)S(1)}, bf16[512,256]{1,0:T(8,128)(2,1)S(1)}, u32[]{:S(2)}, u32[]{:S(2)}) collective-permute-start(bf16[512,256]{1,0:T(8,128)(2,1)S(1)} %get-tuple-element.95), channel_id=1, source_target_pairs={{0,1},{1,0},{2,3},{3,2},{4,5},{5,4},{6,7},{7,6},{8,9},{9,8},{10,11... | collective-permute-start | bytes 786440 | tf_op jit(solution)/shard_map/ppermute | solution.py:309
  58.3 9.8 %collective-permute-start.16 = (bf16[512,256]{1,0:T(8,128)(2,1)S(1)}, bf16[512,256]{1,0:T(8,128)(2,1)S(1)}, u32[]{:S(2)}, u32[]{:S(2)}) collective-permute-start(bf16[512,256]{1,0:T(8,128)(2,1)S(1)} %get-tuple-element.98), channel_id=1, source_target_pairs={{0,4},{1,8},{2,6},{3,10},{4,0},{5,12},{6,2},{7,14},{8,1},{9,16},{1... | collective-permute-start | bytes 786440 | tf_op jit(solution)/shard_map/ppermute | solution.py:309
  69.2 6.4 %collective-permute-start.18 = (bf16[512,256]{1,0:T(8,128)(2,1)S(1)}, bf16[512,256]{1,0:T(8,128)(2,1)S(1)}, u32[]{:S(2)}, u32[]{:S(2)}) collective-permute-start(bf16[512,256]{1,0:T(8,128)(2,1)S(1)} %shard_map.78.refs_3_), channel_id=1, source_target_pairs={{0,4},{1,8},{2,6},{3,10},{4,0},{5,12},{6,2},{7,14},{8,1},{9,16},{1... | collective-permute-start | bytes 786440 | tf_op jit(solution)/shard_map/ppermute | solution.py:309
  78.2 7.5 %collective-permute-start.22 = (bf16[256,512]{1,0:T(8,128)(2,1)S(1)}, bf16[256,512]{1,0:T(8,128)(2,1)S(1)}, u32[]{:S(2)}, u32[]{:S(2)}) collective-permute-start(bf16[256,512]{1,0:T(8,128)(2,1)S(1)} %get-tuple-element.104.high), channel_id=1, source_target_pairs={{0,4},{1,8},{2,6},{3,10},{4,0},{5,12},{6,2},{7,14},{8,1},{9,16},{1... | collective-permute-start | bytes 786440 | tf_op jit(solution)/shard_map/ppermute | solution.py:309
  78.6 10.0 %collective-permute-start.20 = (bf16[512,256]{1,0:T(8,128)(2,1)S(1)}, bf16[512,256]{1,0:T(8,128)(2,1)S(1)}, u32[]{:S(2)}, u32[]{:S(2)}) collective-permute-start(bf16[512,256]{1,0:T(8,128)(2,1)S(1)} %get-tuple-element.109), channel_id=1, source_target_pairs={{0,4},{1,8},{2,6},{3,10},{4,0},{5,12},{6,2},{7,14},{8,1},{9,16},{1... | collective-permute-start | bytes 786440 | tf_op jit(solution)/shard_map/ppermute | solution.py:309
  89.7 6.4 %collective-permute-start.24 = (bf16[512,256]{1,0:T(8,128)(2,1)S(1)}, bf16[512,256]{1,0:T(8,128)(2,1)S(1)}, u32[]{:S(2)}, u32[]{:S(2)}) collective-permute-start(bf16[512,256]{1,0:T(8,128)(2,1)S(1)} %get-tuple-element.114), channel_id=1, source_target_pairs={{0,4},{1,8},{2,6},{3,10},{4,0},{5,12},{6,2},{7,14},{8,1},{9,16},{1... | collective-permute-start | bytes 786440 | tf_op jit(solution)/shard_map/ppermute | solution.py:309
  97.2 6.4 %collective-permute-start.26 = (bf16[512,256]{1,0:T(8,128)(2,1)S(1)}, bf16[512,256]{1,0:T(8,128)(2,1)S(1)}, u32[]{:S(2)}, u32[]{:S(2)}) collective-permute-start(bf16[512,256]{1,0:T(8,128)(2,1)S(1)} %get-tuple-element.120), channel_id=1, source_target_pairs={{0,4},{1,8},{2,6},{3,10},{4,0},{5,12},{6,2},{7,14},{8,1},{9,16},{1... | collective-permute-start | bytes 786440 | tf_op jit(solution)/shard_map/ppermute | solution.py:309
  142.4 6.4 %collective-permute-start.38 = (bf16[256,512]{1,0:T(8,128)(2,1)S(1)}, bf16[256,512]{1,0:T(8,128)(2,1)S(1)}, u32[]{:S(2)}, u32[]{:S(2)}) collective-permute-start(bf16[256,512]{1,0:T(8,128)(2,1)S(1)} %shard_map.96.own), channel_id=1, source_target_pairs={{0,8},{1,4},{2,10},{3,6},{4,1},{5,13},{6,3},{7,15},{8,0},{9,12},{1... | collective-permute-start | bytes 786440 | tf_op jit(solution)/shard_map/ppermute | solution.py:309
  143.3 8.4 %collective-permute-start.37 = (bf16[256,512]{1,0:T(8,128)(2,1)S(1)}, bf16[256,512]{1,0:T(8,128)(2,1)S(1)}, u32[]{:S(2)}, u32[]{:S(2)}) collective-permute-start(bf16[256,512]{1,0:T(8,128)(2,1)S(1)} %shard_map.95.own), channel_id=1, source_target_pairs={{0,8},{1,4},{2,10},{3,6},{4,1},{5,13},{6,3},{7,15},{8,0},{9,12},{1... | collective-permute-start | bytes 786440 | tf_op jit(solution)/shard_map/ppermute | solution.py:309
  (19 other events, 95.0 us)

commit v7 on v5

--- a/solution.py
+++ b/solution.py
@@ -229,12 +229,17 @@
     copy.wait()
     if not gives:
         return
-    part = refs.pop(0)
-    for i, at in enumerate(pick(table, edge, edge, width)):
-        part[i * width : (i + 1) * width, :] = acc[at, :].astype(part.dtype)
-        if gives == "both":
+    part, near_part = refs[:2]
+    ats = pick(table, edge, edge, width), pick(table, 0, edge, width)
+    for out, places in zip((part, near_part), ats):
+        for i, at in enumerate(places):
+            out[i * width : (i + 1) * width, :] = acc[at, :].astype(out.dtype)
+    if gives == "both":
+        for i, at in enumerate(ats[0]):
             half, place = divmod(i, edge // 2)
-            refs[half][place * width : (place + 1) * width, :] = far_op[at, :]
+            refs[2 + half][place * width : (place + 1) * width, :] = far_op[at, :]
+        for i, at in enumerate(ats[1]):
+            refs[4][i * width : (i + 1) * width, :] = far_op[at, :]
 
 
 def result_of(first, acc, far_op, far):
@@ -254,27 +259,31 @@
     return total.astype(BF16)
 
 
-def finish_kernel(first, apart, wants, width, edge, lists, acc, far_op, *refs):
+def near_kernel(first, apart, acc, far_op, *refs):
+    if apart:
+        far = far_rows(*refs[:4])
+        refs[5][...] = far
+        out = refs[4]
+    else:
+        far, out = refs[0][...], refs[1]
+    out[...] = result_of(first, acc, far_op, far).astype(BF16)
+
+
+def finish_kernel(first, wants, width, edge, lists, acc, far_op, far, *refs):
     table, sem = refs[-2:]
     refs = list(refs[:-2])
     copy = fetch(lists, table, sem)
     copy.start()
-    if apart:
-        far = far_rows(*refs[:4])
-        refs = refs[4:]
-    else:
-        far = refs.pop(0)[...]
-    total = result_of(first, acc, far_op, far)
+    total = result_of(first, acc, far_op, far[...])
     value, part = wants
     if value:
         refs.pop(0)[...] = total
-    field, near_send = refs[:2]
+    field = refs[0]
     field[...] = total.astype(BF16)
     copy.wait()
-    sends = [(0, near_send)] + ([(edge, refs[2])] if part else [])
-    for begin, send in sends:
-        for i, rows in enumerate(pick(table, begin, edge, width)):
-            send[i * width : (i + 1) * width, :] = field[rows, :]
+    if part:
+        for i, rows in enumerate(pick(table, edge, edge, width)):
+            refs[1][i * width : (i + 1) * width, :] = field[rows, :]
 
 
 def last_kernel(begin, acc, far_op, part, low, high, sent, out):
@@ -407,7 +416,8 @@
             theirs.append(send(far_part[step - 1], "far"))
         gives = "both" if first else "" if last else "one"
         kind = F32 if step < PLAIN else BF16
-        outs = (wide(F32),) + ((part(kind),) if gives else ()) + ((square,) * 2 if first else ())
+        outs = (wide(F32),) + ((part(kind), part(F32)) if gives else ())
+        outs += (square, square, sds((edge * width, edge * width), BF16)) if first else ()
         given = (lists_at, near_op, field, near) + older + ((far_op,) if first else ())
         mine = call(
             functools.partial(local_kernel, width, edge, not first, gives), outs,
@@ -415,7 +425,7 @@
         )(*given)
         acc = mine[0]
         if first:
-            far_part = mine[2:]
+            far_part, near_far = mine[3:5], mine[5]
         arrived_part, moved_part = moved_part, None
         if PLAIN <= step and not last:
             moved_part = send(mine[1], "far")
@@ -440,19 +450,28 @@
                 )
             return out[0]
         if step < PLAIN:
-            far_send = call(functools.partial(ahead_kernel, first), sent, [VMEM] * 4, VMEM)(mine[1], *far_part, far)
+            far_send = call(
+                functools.partial(ahead_kernel, first), sent, [VMEM] * 4, VMEM
+            )(mine[1], *far_part, far)
+        given = (far,) if plain else (arrived_part, *theirs, sent_rows[step - 1])
+        outs = (sent,) if plain else (sent, sent)
+        ready = call(
+            functools.partial(near_kernel, first, not plain), outs,
+            [VMEM] * (2 + len(given)), (VMEM,) * len(outs),
+        )(mine[2], near_far, *given)
+        near_send = ready[0]
+        far = far if plain else ready[1]
         wants = (step < STEPS - 2, PLAIN <= step < STEPS - 2)
-        outs = ((wide(F32),) if wants[0] else ()) + (wide(BF16), sent) + ((sent,) if wants[1] else ())
-        given = (far,) if plain else (arrived_part, *theirs, sent_rows[step - 1])
+        outs = ((wide(F32),) if wants[0] else ()) + (wide(BF16),) + ((sent,) if wants[1] else ())
         result = call(
-            functools.partial(finish_kernel, first, not plain, wants, width, edge), outs,
-            [HBM] + [VMEM] * (2 + len(given)), (VMEM,) * len(outs), scratch=table,
-        )(lists_at, acc, far_op, *given)
+            functools.partial(finish_kernel, first, wants, width, edge), outs,
+            [HBM] + [VMEM] * 3, (VMEM,) * len(outs), scratch=table,
+        )(lists_at, acc, far_op, far)
         result = list(result)
         older, newer = (newer,), result.pop(0) if wants[0] else None
-        field, near_send = result[:2]
+        field = result[0]
         if wants[1]:
-            sent_rows[step + 1] = result[2]
+            sent_rows[step + 1] = result[1]
 
 
 def solution(mesh):

time: 153 us -> 150 us (0.980)
  waiting for transfers between devices: 70.8 us -> 58.3 us
  Pallas kernels: 38.3 us -> 47.4 us
    ppermute x36, waiting for transfers between devices: 58.9 us -> 46.3 us  [send(): return lax.ppermute(x, AXES, ways[way])]
    pallas_call x9 -> x18, Pallas kernels: 8.62 us -> 13.9 us  [the longest x9 8.57 us: body(): call(functools.partial(finish_kernel, first, wants, width, edge), outs, [...]
    pallas_call x10, Pallas kernels: 10.7 us -> 14.6 us  [body(): call(functools.partial(local_kernel, width, edge, not first, gives), outs...]
  transfers between devices with their start and end apart: 39 -> 39, of which waited for: 16 -> 16; matrix products, arithmetic and copies ran while one was open for 0% -> 0% of each run, Pallas kernels for 18% -> 27%
where the time goes in v7:
time: 150 us
  waiting for transfers between devices  58.3 us (39%)
  Pallas kernels  47.4 us (32%)
  starting transfers between devices  41.3 us (28%)
    ppermute x36, waiting for transfers between devices, send(): return lax.ppermute(x, AXES, ways[way])  46.3 us
    ppermute x36, starting transfers between devices, send(): return lax.ppermute(x, AXES, ways[way])  38.3 us
    pallas_call x10, Pallas kernels, body(): call(functools.partial(local_kernel, width, edge, not first, gives), outs...  14.6 us
    ppermute x3, waiting for transfers between devices, body(): lax.ppermute(pieces[place], 'col', [(k, k ^ bit) for k in range(columns)])  11.9 us
    pallas_call x9, Pallas kernels, body(): call(functools.partial(finish_kernel, first, wants, width, edge), outs, [...  8.57 us
    pallas_call x5, Pallas kernels, body(): call(functools.partial(build_kernel, [(*row[:2], len(row[2])) for row in...  8.01 us
    pallas_call x9, Pallas kernels, body(): call(functools.partial(near_kernel, first, not plain), outs, [VMEM] * (2...  5.31 us
    ppermute x3, starting transfers between devices, body(): lax.ppermute(pieces[place], 'col', [(k, k ^ bit) for k in range(columns)])  3.07 us
  transfers between devices with their start and end apart: 39, of which 16 were waited for; matrix products, arithmetic and copies ran while one was open for 0% of the time, Pallas kernels for 27%

profile of v7, /device:TPU:0, one launch (start us, length us, event | category | flops | bytes accessed | tf_op | source)
XLA Modules:
  0.0 149.8 jit_solution(17055064875661776297)
XLA Ops:
  1.3 3.1 %collective-permute-start.11 = (bf16[256,1024]{1,0:T(8,128)(2,1)S(1)}, bf16[256,1024]{1,0:T(8,128)(2,1)S(1)}, u32[]{:S(2)}, u32[]{:S(2)}) collective-permute-start(bf16[256,1024]{1,0:T(8,128)(2,1)S(1)} %convert_element_type.3.refs_0_), channel_id=1, source_target_pairs={{0,2},{1,3},{2,0},{3,1},{4,6},{5,7},{6,4},{7,5},{8,10},{9,11},{10,... | collective-permute-start | bytes 1572872 | tf_op jit(solution)/shard_map/ppermute | solution.py:333
  4.4 11.9 %collective-permute-done.11.refs_1_ = bf16[256,1024]{1,0:T(8,128)(2,1)S(1)} collective-permute-done((bf16[256,1024]{1,0:T(8,128)(2,1)S(1)}, bf16[256,1024]{1,0:T(8,128)(2,1)S(1)}, u32[]{:S(2)}, u32[]{:S(2)}) %collective-permute-start.11) | collective-permute-done | bytes 524320 | tf_op jit(solution)/shard_map/ppermute | solution.py:333
  17.8 1.9 %collective-permute-start.9 = (bf16[1,16,128,128]{3,2,1,0:T(8,128)(2,1)S(1)}, bf16[1,16,128,128]{3,2,1,0:T(8,128)(2,1)S(1)}, u32[]{:S(2)}, u32[]{:S(2)}) collective-permute-start(bf16[1,16,128,128]{3,2,1,0:T(8,128)(2,1)S(1)} %get-tuple-element.95), channel_id=1, source_target_pairs={{0,8},{1,4},{2,10},{3,6},{4,1},{5,13},{6,3},{7,15},{8,0},{9,12},{1... | collective-permute-start | bytes 1572872 | tf_op jit(solution)/shard_map/ppermute | solution.py:318
  28.2 10.2 %collective-permute-done.moved = s32[137]{0:T(256)S(1)} collective-permute-done((s32[137]{0:T(256)S(1)}, s32[137]{0:T(256)S(1)}, u32[]{:S(2)}, u32[]{:S(2)}) %collective-permute-start) | collective-permute-done | bytes 580 | tf_op jit(solution)/shard_map/ppermute | solution.py:318
  38.4 1.8 %collective-permute-start.14 = (bf16[1024,256]{1,0:T(8,128)(2,1)S(1)}, bf16[1024,256]{1,0:T(8,128)(2,1)S(1)}, u32[]{:S(2)}, u32[]{:S(2)}) collective-permute-start(bf16[1024,256]{1,0:T(8,128)(2,1)S(1)} %shard_map.73.own), channel_id=1, source_target_pairs={{0,8},{1,4},{2,10},{3,6},{4,1},{5,13},{6,3},{7,15},{8,0},{9,12},{1... | collective-permute-start | bytes 1572872 | tf_op jit(solution)/shard_map/ppermute | solution.py:318
  44.3 6.1 %collective-permute-done.6.refs_1_ = bf16[1,8,128,128]{3,2,1,0:T(8,128)(2,1)S(1)} collective-permute-done((bf16[1,8,128,128]{3,2,1,0:T(8,128)(2,1)S(1)}, bf16[1,8,128,128]{3,2,1,0:T(8,128)(2,1)S(1)}, u32[]{:S(2)}, u32[]{:S(2)}) %collective-permute-start.6) | collective-permute-done | bytes 262176 | tf_op jit(solution)/shard_map/ppermute | solution.py:318
  50.4 1.8 %collective-permute-start.1 = (bf16[1,8,128,128]{3,2,1,0:T(8,128)(2,1)S(1)}, bf16[1,8,128,128]{3,2,1,0:T(8,128)(2,1)S(1)}, u32[]{:S(2)}, u32[]{:S(2)}) collective-permute-start(bf16[1,8,128,128]{3,2,1,0:T(8,128)(2,1)S(1)} %get-tuple-element.91), channel_id=1, source_target_pairs={{0,8},{1,4},{2,10},{3,6},{4,1},{5,13},{6,3},{7,15},{8,0},{9,12},{1... | collective-permute-start | bytes 786440 | tf_op jit(solution)/shard_map/ppermute | solution.py:318
  53.5 4.9 %collective-permute-start.15 = (bf16[512,256]{1,0:T(8,128)(2,1)S(1)}, bf16[512,256]{1,0:T(8,128)(2,1)S(1)}, u32[]{:S(2)}, u32[]{:S(2)}) collective-permute-start(bf16[512,256]{1,0:T(8,128)(2,1)S(1)} %get-tuple-element.106), channel_id=1, source_target_pairs={{0,1},{1,0},{2,3},{3,2},{4,5},{5,4},{6,7},{7,6},{8,9},{9,8},{10,11... | collective-permute-start | bytes 786440 | tf_op jit(solution)/shard_map/ppermute | solution.py:318
  58.8 3.0 %shard_map.68 = (bf16[1024,1536]{1,0:T(8,128)(2,1)S(1)}, bf16[1024,512]{1,0:T(8,128)(2,1)S(1)}) custom-call(s32[129]{0:T(256)S(1)} %get-tuple-element.90.info, bf16[8,16,128,128]{3,2,1,0:T(8,128)(2,1)} %blocks.13, bf16[1,16,128,128]{3,2,1,0:T(8,128)(2,1)S(1)} %collective-permute-done.7.refs_0_, bf16[1,16,128,128]{3,2,1,0:T(8,128)(2,1)S(1)} %collective-permute-done.9.refs_1_), custom_call_target="tpu_custom_call" | custom-call | tf_op jit(solution)/shard_map/pallas_call | solution.py:384
  61.8 3.0 %shard_map.69 = (bf16[1024,1536]{1,0:T(8,128)(2,1)S(1)}, bf16[1024,512]{1,0:T(8,128)(2,1)S(1)}) custom-call(s32[129]{0:T(256)S(1)} %get-tuple-element.90.info, bf16[8,16,128,128]{3,2,1,0:T(8,128)(2,1)} %blocks.13, bf16[1,16,128,128]{3,2,1,0:T(8,128)(2,1)S(1)} %collective-permute-done.4.refs_0_, ...), custom_call_target="tpu_custom_call", output_to_operand_aliasing={{0}: (3, {}), {1}: (4, {})} | custom-call | tf_op jit(solution)/shard_map/pallas_call | solution.py:384
  72.3 2.9 %collective-permute-done.18.far.refs_0_ = bf16[512,256]{1,0:T(8,128)(2,1)S(1)} collective-permute-done((bf16[512,256]{1,0:T(8,128)(2,1)S(1)}, bf16[512,256]{1,0:T(8,128)(2,1)S(1)}, u32[]{:S(2)}, u32[]{:S(2)}) %collective-permute-start.18) | collective-permute-done | bytes 262176 | tf_op jit(solution)/shard_map/ppermute | solution.py:318
  79.9 2.5 %collective-permute-done.20.far.refs_0_ = bf16[512,256]{1,0:T(8,128)(2,1)S(1)} collective-permute-done((bf16[512,256]{1,0:T(8,128)(2,1)S(1)}, bf16[512,256]{1,0:T(8,128)(2,1)S(1)}, u32[]{:S(2)}, u32[]{:S(2)}) %collective-permute-start.20) | collective-permute-done | bytes 262176 | tf_op jit(solution)/shard_map/ppermute | solution.py:318
  89.3 2.8 %collective-permute-done.24.refs_2_.high = bf16[256,512]{1,0:T(8,128)(2,1)S(1)} collective-permute-done((bf16[256,512]{1,0:T(8,128)(2,1)S(1)}, bf16[256,512]{1,0:T(8,128)(2,1)S(1)}, u32[]{:S(2)}, u32[]{:S(2)}) %collective-permute-start.24) | collective-permute-done | bytes 262176 | tf_op jit(solution)/shard_map/ppermute | solution.py:318
  92.1 2.8 %collective-permute-done.22.refs_0_ = bf16[512,256]{1,0:T(8,128)(2,1)S(1)} collective-permute-done((bf16[512,256]{1,0:T(8,128)(2,1)S(1)}, bf16[512,256]{1,0:T(8,128)(2,1)S(1)}, u32[]{:S(2)}, u32[]{:S(2)}) %collective-permute-start.22) | collective-permute-done | bytes 262176 | tf_op jit(solution)/shard_map/ppermute | solution.py:318
  100.0 2.2 %collective-permute-done.26.refs_0_ = bf16[512,256]{1,0:T(8,128)(2,1)S(1)} collective-permute-done((bf16[512,256]{1,0:T(8,128)(2,1)S(1)}, bf16[512,256]{1,0:T(8,128)(2,1)S(1)}, u32[]{:S(2)}, u32[]{:S(2)}) %collective-permute-start.26) | collective-permute-done | bytes 262176 | tf_op jit(solution)/shard_map/ppermute | solution.py:318
  107.3 2.2 %collective-permute-done.28.refs_0_ = bf16[512,256]{1,0:T(8,128)(2,1)S(1)} collective-permute-done((bf16[512,256]{1,0:T(8,128)(2,1)S(1)}, bf16[512,256]{1,0:T(8,128)(2,1)S(1)}, u32[]{:S(2)}, u32[]{:S(2)}) %collective-permute-start.28) | collective-permute-done | bytes 262176 | tf_op jit(solution)/shard_map/ppermute | solution.py:318
  114.6 2.2 %collective-permute-done.30.refs_0_ = bf16[512,256]{1,0:T(8,128)(2,1)S(1)} collective-permute-done((bf16[512,256]{1,0:T(8,128)(2,1)S(1)}, bf16[512,256]{1,0:T(8,128)(2,1)S(1)}, u32[]{:S(2)}, u32[]{:S(2)}) %collective-permute-start.30) | collective-permute-done | bytes 262176 | tf_op jit(solution)/shard_map/ppermute | solution.py:318
  120.3 1.8 %shard_map.98 = (f32[1024,256]{1,0:T(8,128)S(1)}, bf16[512,256]{1,0:T(8,128)(2,1)S(1)}, f32[512,256]{1,0:T(8,128)S(1)}) custom-call(s32[8]{0:T(128)} %copy-done.1, bf16[1024,1536]{1,0:T(8,128)(2,1)S(1)} %get-tuple-element.104.near_op, bf16[1024,256]{1,0:T(8,128)(2,1)S(1)} %get-tuple-element.153.field, bf16[512,256]{1,0:T(8,128)(2,1)S(1)} %collective-permute-done.31.near, ...), custom_call_target="tpu_custom_call" | custom-call | tf_op jit(solution)/shard_map/pallas_call | solution.py:422
  122.2 1.9 %collective-permute-done.32.refs_0_ = bf16[512,256]{1,0:T(8,128)(2,1)S(1)} collective-permute-done((bf16[512,256]{1,0:T(8,128)(2,1)S(1)}, bf16[512,256]{1,0:T(8,128)(2,1)S(1)}, u32[]{:S(2)}, u32[]{:S(2)}) %collective-permute-start.32) | collective-permute-done | bytes 262176 | tf_op jit(solution)/shard_map/ppermute | solution.py:318
  129.2 2.2 %collective-permute-done.34.refs_0_ = bf16[512,256]{1,0:T(8,128)(2,1)S(1)} collective-permute-done((bf16[512,256]{1,0:T(8,128)(2,1)S(1)}, bf16[512,256]{1,0:T(8,128)(2,1)S(1)}, u32[]{:S(2)}, u32[]{:S(2)}) %collective-permute-start.34) | collective-permute-done | bytes 262176 | tf_op jit(solution)/shard_map/ppermute | solution.py:318
  135.9 2.8 %collective-permute-done.36.part = bf16[512,256]{1,0:T(8,128)(2,1)S(1)} collective-permute-done((bf16[512,256]{1,0:T(8,128)(2,1)S(1)}, bf16[512,256]{1,0:T(8,128)(2,1)S(1)}, u32[]{:S(2)}, u32[]{:S(2)}) %collective-permute-start.36) | collective-permute-done | bytes 262176 | tf_op jit(solution)/shard_map/ppermute | solution.py:318
  140.4 2.1 %collective-permute-start.37 = (bf16[256,512]{1,0:T(8,128)(2,1)S(1)}, bf16[256,512]{1,0:T(8,128)(2,1)S(1)}, u32[]{:S(2)}, u32[]{:S(2)}) collective-permute-start(bf16[256,512]{1,0:T(8,128)(2,1)S(1)} %shard_map.105.own), channel_id=1, source_target_pairs={{0,8},{1,4},{2,10},{3,6},{4,1},{5,13},{6,3},{7,15},{8,0},{9,12},{1... | collective-permute-start | bytes 786440 | tf_op jit(solution)/shard_map/ppermute | solution.py:318
  142.5 3.5 %collective-permute-done.38.moved = bf16[256,512]{1,0:T(8,128)(2,1)S(1)} collective-permute-done((bf16[256,512]{1,0:T(8,128)(2,1)S(1)}, bf16[256,512]{1,0:T(8,128)(2,1)S(1)}, u32[]{:S(2)}, u32[]{:S(2)}) %collective-permute-start.38) | collective-permute-done | bytes 262176 | tf_op jit(solution)/shard_map/ppermute | solution.py:318
  146.8 2.0 %collective-permute-done.37.moved = bf16[256,512]{1,0:T(8,128)(2,1)S(1)} collective-permute-done((bf16[256,512]{1,0:T(8,128)(2,1)S(1)}, bf16[256,512]{1,0:T(8,128)(2,1)S(1)}, u32[]{:S(2)}, u32[]{:S(2)}) %collective-permute-start.37) | collective-permute-done | bytes 262176 | tf_op jit(solution)/shard_map/ppermute | solution.py:318
  (108 shorter events, 67.0 us)
Async XLA Ops:
  1.3 15.0 %collective-permute-start.11 = (bf16[256,1024]{1,0:T(8,128)(2,1)S(1)}, bf16[256,1024]{1,0:T(8,128)(2,1)S(1)}, u32[]{:S(2)}, u32[]{:S(2)}) collective-permute-start(bf16[256,1024]{1,0:T(8,128)(2,1)S(1)} %convert_element_type.3.refs_0_), channel_id=1, source_target_pairs={{0,2},{1,3},{2,0},{3,1},{4,6},{5,7},{6,4},{7,5},{8,10},{9,11},{10,... | collective-permute-start | bytes 1572872 | tf_op jit(solution)/shard_map/ppermute | solution.py:333
  4.4 20.4 %collective-permute-start.12 = (bf16[256,1024]{1,0:T(8,128)(2,1)S(1)}, bf16[256,1024]{1,0:T(8,128)(2,1)S(1)}, u32[]{:S(2)}, u32[]{:S(2)}) collective-permute-start(bf16[256,1024]{1,0:T(8,128)(2,1)S(1)} %convert_element_type.3.refs_0_), channel_id=1, source_target_pairs={{0,1},{1,0},{2,3},{3,2},{4,5},{5,4},{6,7},{7,6},{8,9},{9,8},{10,11... | collective-permute-start | bytes 1572872 | tf_op jit(solution)/shard_map/ppermute | solution.py:333
  16.3 8.9 %collective-permute-start.13 = (bf16[256,1024]{1,0:T(8,128)(2,1)S(1)}, bf16[256,1024]{1,0:T(8,128)(2,1)S(1)}, u32[]{:S(2)}, u32[]{:S(2)}) collective-permute-start(bf16[256,1024]{1,0:T(8,128)(2,1)S(1)} %collective-permute-done.11.refs_1_), channel_id=1, source_target_pairs={{0,1},{1,0},{2,3},{3,2},{4,5},{5,4},{6,7},{7,6},{8,9},{9,8},{10,11... | collective-permute-start | bytes 1572872 | tf_op jit(solution)/shard_map/ppermute | solution.py:333
  17.8 22.3 %collective-permute-start.9 = (bf16[1,16,128,128]{3,2,1,0:T(8,128)(2,1)S(1)}, bf16[1,16,128,128]{3,2,1,0:T(8,128)(2,1)S(1)}, u32[]{:S(2)}, u32[]{:S(2)}) collective-permute-start(bf16[1,16,128,128]{3,2,1,0:T(8,128)(2,1)S(1)} %get-tuple-element.95), channel_id=1, source_target_pairs={{0,8},{1,4},{2,10},{3,6},{4,1},{5,13},{6,3},{7,15},{8,0},{9,12},{1... | collective-permute-start | bytes 1572872 | tf_op jit(solution)/shard_map/ppermute | solution.py:318
  20.8 20.1 %collective-permute-start.7 = (bf16[1,16,128,128]{3,2,1,0:T(8,128)(2,1)S(1)}, bf16[1,16,128,128]{3,2,1,0:T(8,128)(2,1)S(1)}, u32[]{:S(2)}, u32[]{:S(2)}) collective-permute-start(bf16[1,16,128,128]{3,2,1,0:T(8,128)(2,1)S(1)} %shard_map.67), channel_id=1, source_target_pairs={{0,8},{1,4},{2,10},{3,6},{4,1},{5,13},{6,3},{7,15},{8,0},{9,12},{1... | collective-permute-start | bytes 1572872 | tf_op jit(solution)/shard_map/ppermute | solution.py:318
  21.1 20.5 %collective-permute-start.4 = (bf16[1,16,128,128]{3,2,1,0:T(8,128)(2,1)S(1)}, bf16[1,16,128,128]{3,2,1,0:T(8,128)(2,1)S(1)}, u32[]{:S(2)}, u32[]{:S(2)}) collective-permute-start(bf16[1,16,128,128]{3,2,1,0:T(8,128)(2,1)S(1)} %get-tuple-element.93), channel_id=1, source_target_pairs={{0,8},{1,4},{2,10},{3,6},{4,1},{5,13},{6,3},{7,15},{8,0},{9,12},{1... | collective-permute-start | bytes 1572872 | tf_op jit(solution)/shard_map/ppermute | solution.py:318
  24.8 13.6 %collective-permute-start = (s32[137]{0:T(256)S(1)}, s32[137]{0:T(256)S(1)}, u32[]{:S(2)}, u32[]{:S(2)}) collective-permute-start(s32[137]{0:T(256)S(1)} %shard_map.64.own), channel_id=1, source_target_pairs={{0,8},{1,4},{2,10},{3,6},{4,1},{5,13},{6,3},{7,15},{8,0},{9,12},{1... | collective-permute-start | bytes 1652 | tf_op jit(solution)/shard_map/ppermute | solution.py:318
  25.1 17.1 %collective-permute-start.2 = (bf16[1,8,128,128]{3,2,1,0:T(8,128)(2,1)S(1)}, bf16[1,8,128,128]{3,2,1,0:T(8,128)(2,1)S(1)}, u32[]{:S(2)}, u32[]{:S(2)}) collective-permute-start(bf16[1,8,128,128]{3,2,1,0:T(8,128)(2,1)S(1)} %get-tuple-element.92), channel_id=1, source_target_pairs={{0,8},{1,4},{2,10},{3,6},{4,1},{5,13},{6,3},{7,15},{8,0},{9,12},{1... | collective-permute-start | bytes 786440 | tf_op jit(solution)/shard_map/ppermute | solution.py:318
  38.4 13.8 %collective-permute-start.14 = (bf16[1024,256]{1,0:T(8,128)(2,1)S(1)}, bf16[1024,256]{1,0:T(8,128)(2,1)S(1)}, u32[]{:S(2)}, u32[]{:S(2)}) collective-permute-start(bf16[1024,256]{1,0:T(8,128)(2,1)S(1)} %shard_map.73.own), channel_id=1, source_target_pairs={{0,8},{1,4},{2,10},{3,6},{4,1},{5,13},{6,3},{7,15},{8,0},{9,12},{1... | collective-permute-start | bytes 1572872 | tf_op jit(solution)/shard_map/ppermute | solution.py:318
  40.2 13.3 %collective-permute-start.10 = (bf16[1,16,128,128]{3,2,1,0:T(8,128)(2,1)S(1)}, bf16[1,16,128,128]{3,2,1,0:T(8,128)(2,1)S(1)}, u32[]{:S(2)}, u32[]{:S(2)}) collective-permute-start(bf16[1,16,128,128]{3,2,1,0:T(8,128)(2,1)S(1)} %collective-permute-done.9.refs_1_), channel_id=1, source_target_pairs={{1,3},{3,1},{4,6},{6,4},{9,11},{11,9},{12,14},{14,12},{17,19},{19,... | collective-permute-start | bytes 1572872 | tf_op jit(solution)/shard_map/ppermute | solution.py:318
  40.9 17.5 %collective-permute-start.8 = (bf16[1,16,128,128]{3,2,1,0:T(8,128)(2,1)S(1)}, bf16[1,16,128,128]{3,2,1,0:T(8,128)(2,1)S(1)}, u32[]{:S(2)}, u32[]{:S(2)}) collective-permute-start(bf16[1,16,128,128]{3,2,1,0:T(8,128)(2,1)S(1)} %collective-permute-done.7.refs_0_), channel_id=1, source_target_pairs={{1,3},{3,1},{4,6},{6,4},{9,11},{11,9},{12,14},{14,12},{17,19},{19,... | collective-permute-start | bytes 1572872 | tf_op jit(solution)/shard_map/ppermute | solution.py:318
  41.6 23.9 %collective-permute-start.5 = (bf16[1,16,128,128]{3,2,1,0:T(8,128)(2,1)S(1)}, bf16[1,16,128,128]{3,2,1,0:T(8,128)(2,1)S(1)}, u32[]{:S(2)}, u32[]{:S(2)}) collective-permute-start(bf16[1,16,128,128]{3,2,1,0:T(8,128)(2,1)S(1)} %collective-permute-done.4.refs_0_), channel_id=1, source_target_pairs={{1,3},{3,1},{4,6},{6,4},{9,11},{11,9},{12,14},{14,12},{17,19},{19,... | collective-permute-start | bytes 1572872 | tf_op jit(solution)/shard_map/ppermute | solution.py:318
  42.3 8.1 %collective-permute-start.6 = (bf16[1,8,128,128]{3,2,1,0:T(8,128)(2,1)S(1)}, bf16[1,8,128,128]{3,2,1,0:T(8,128)(2,1)S(1)}, u32[]{:S(2)}, u32[]{:S(2)}) collective-permute-start(bf16[1,8,128,128]{3,2,1,0:T(8,128)(2,1)S(1)} %get-tuple-element.94), channel_id=1, source_target_pairs={{0,8},{1,4},{2,10},{3,6},{4,1},{5,13},{6,3},{7,15},{8,0},{9,12},{1... | collective-permute-start | bytes 786440 | tf_op jit(solution)/shard_map/ppermute | solution.py:318
  50.4 15.7 %collective-permute-start.1 = (bf16[1,8,128,128]{3,2,1,0:T(8,128)(2,1)S(1)}, bf16[1,8,128,128]{3,2,1,0:T(8,128)(2,1)S(1)}, u32[]{:S(2)}, u32[]{:S(2)}) collective-permute-start(bf16[1,8,128,128]{3,2,1,0:T(8,128)(2,1)S(1)} %get-tuple-element.91), channel_id=1, source_target_pairs={{0,8},{1,4},{2,10},{3,6},{4,1},{5,13},{6,3},{7,15},{8,0},{9,12},{1... | collective-permute-start | bytes 786440 | tf_op jit(solution)/shard_map/ppermute | solution.py:318
  52.2 13.9 %collective-permute-start.3 = (bf16[1,8,128,128]{3,2,1,0:T(8,128)(2,1)S(1)}, bf16[1,8,128,128]{3,2,1,0:T(8,128)(2,1)S(1)}, u32[]{:S(2)}, u32[]{:S(2)}) collective-permute-start(bf16[1,8,128,128]{3,2,1,0:T(8,128)(2,1)S(1)} %collective-permute-done.2.refs_2_), channel_id=1, source_target_pairs={{1,3},{3,1},{4,6},{6,4},{9,11},{11,9},{12,14},{14,12},{17,19},{19,... | collective-permute-start | bytes 786440 | tf_op jit(solution)/shard_map/ppermute | solution.py:318
  53.5 13.4 %collective-permute-start.15 = (bf16[512,256]{1,0:T(8,128)(2,1)S(1)}, bf16[512,256]{1,0:T(8,128)(2,1)S(1)}, u32[]{:S(2)}, u32[]{:S(2)}) collective-permute-start(bf16[512,256]{1,0:T(8,128)(2,1)S(1)} %get-tuple-element.106), channel_id=1, source_target_pairs={{0,1},{1,0},{2,3},{3,2},{4,5},{5,4},{6,7},{7,6},{8,9},{9,8},{10,11... | collective-permute-start | bytes 786440 | tf_op jit(solution)/shard_map/ppermute | solution.py:318
  58.3 9.7 %collective-permute-start.16 = (bf16[512,256]{1,0:T(8,128)(2,1)S(1)}, bf16[512,256]{1,0:T(8,128)(2,1)S(1)}, u32[]{:S(2)}, u32[]{:S(2)}) collective-permute-start(bf16[512,256]{1,0:T(8,128)(2,1)S(1)} %get-tuple-element.109), channel_id=1, source_target_pairs={{0,4},{1,8},{2,6},{3,10},{4,0},{5,12},{6,2},{7,14},{8,1},{9,16},{1... | collective-permute-start | bytes 786440 | tf_op jit(solution)/shard_map/ppermute | solution.py:318
  68.8 6.4 %collective-permute-start.18 = (bf16[512,256]{1,0:T(8,128)(2,1)S(1)}, bf16[512,256]{1,0:T(8,128)(2,1)S(1)}, u32[]{:S(2)}, u32[]{:S(2)}) collective-permute-start(bf16[512,256]{1,0:T(8,128)(2,1)S(1)} %shard_map.79), channel_id=1, source_target_pairs={{0,4},{1,8},{2,6},{3,10},{4,0},{5,12},{6,2},{7,14},{8,1},{9,16},{1... | collective-permute-start | bytes 786440 | tf_op jit(solution)/shard_map/ppermute | solution.py:318
  76.0 6.4 %collective-permute-start.20 = (bf16[512,256]{1,0:T(8,128)(2,1)S(1)}, bf16[512,256]{1,0:T(8,128)(2,1)S(1)}, u32[]{:S(2)}, u32[]{:S(2)}) collective-permute-start(bf16[512,256]{1,0:T(8,128)(2,1)S(1)} %shard_map.83.refs_3_), channel_id=1, source_target_pairs={{0,4},{1,8},{2,6},{3,10},{4,0},{5,12},{6,2},{7,14},{8,1},{9,16},{1... | collective-permute-start | bytes 786440 | tf_op jit(solution)/shard_map/ppermute | solution.py:318
  84.5 7.6 %collective-permute-start.24 = (bf16[256,512]{1,0:T(8,128)(2,1)S(1)}, bf16[256,512]{1,0:T(8,128)(2,1)S(1)}, u32[]{:S(2)}, u32[]{:S(2)}) collective-permute-start(bf16[256,512]{1,0:T(8,128)(2,1)S(1)} %get-tuple-element.116.high), channel_id=1, source_target_pairs={{0,4},{1,8},{2,6},{3,10},{4,0},{5,12},{6,2},{7,14},{8,1},{9,16},{1... | collective-permute-start | bytes 786440 | tf_op jit(solution)/shard_map/ppermute | solution.py:318
  84.9 10.0 %collective-permute-start.22 = (bf16[512,256]{1,0:T(8,128)(2,1)S(1)}, bf16[512,256]{1,0:T(8,128)(2,1)S(1)}, u32[]{:S(2)}, u32[]{:S(2)}) collective-permute-start(bf16[512,256]{1,0:T(8,128)(2,1)S(1)} %get-tuple-element.127), channel_id=1, source_target_pairs={{0,4},{1,8},{2,6},{3,10},{4,0},{5,12},{6,2},{7,14},{8,1},{9,16},{1... | collective-permute-start | bytes 786440 | tf_op jit(solution)/shard_map/ppermute | solution.py:318
  103.1 6.4 %collective-permute-start.28 = (bf16[512,256]{1,0:T(8,128)(2,1)S(1)}, bf16[512,256]{1,0:T(8,128)(2,1)S(1)}, u32[]{:S(2)}, u32[]{:S(2)}) collective-permute-start(bf16[512,256]{1,0:T(8,128)(2,1)S(1)} %get-tuple-element.142), channel_id=1, source_target_pairs={{0,4},{1,8},{2,6},{3,10},{4,0},{5,12},{6,2},{7,14},{8,1},{9,16},{1... | collective-permute-start | bytes 786440 | tf_op jit(solution)/shard_map/ppermute | solution.py:318
  139.5 6.4 %collective-permute-start.38 = (bf16[256,512]{1,0:T(8,128)(2,1)S(1)}, bf16[256,512]{1,0:T(8,128)(2,1)S(1)}, u32[]{:S(2)}, u32[]{:S(2)}) collective-permute-start(bf16[256,512]{1,0:T(8,128)(2,1)S(1)} %shard_map.106.own), channel_id=1, source_target_pairs={{0,8},{1,4},{2,10},{3,6},{4,1},{5,13},{6,3},{7,15},{8,0},{9,12},{1... | collective-permute-start | bytes 786440 | tf_op jit(solution)/shard_map/ppermute | solution.py:318
  140.4 8.4 %collective-permute-start.37 = (bf16[256,512]{1,0:T(8,128)(2,1)S(1)}, bf16[256,512]{1,0:T(8,128)(2,1)S(1)}, u32[]{:S(2)}, u32[]{:S(2)}) collective-permute-start(bf16[256,512]{1,0:T(8,128)(2,1)S(1)} %shard_map.105.own), channel_id=1, source_target_pairs={{0,8},{1,4},{2,10},{3,6},{4,1},{5,13},{6,3},{7,15},{8,0},{9,12},{1... | collective-permute-start | bytes 786440 | tf_op jit(solution)/shard_map/ppermute | solution.py:318
  (19 other events, 103.4 us)

commit v8 on v7

--- a/solution.py
+++ b/solution.py
@@ -145,7 +145,7 @@
             at += 1
 
 
-def tables_kernel(own, moved, info, send_lists):
+def tables_kernel(own, moved, info, send_lists, spread):
     role, keep = here()[:2]
     get = lambda i: jnp.where(keep, own[i], moved[i])
     slots = info.shape[0]
@@ -156,6 +156,8 @@
         up, down = get(slots + i), get(slots + edge + i)
         send_lists[i] = jnp.where(role == 0, up, down)
         send_lists[edge + i] = jnp.where(role == 0, down, up)
+    for i in range(2 * edge):
+        spread[i : i + 1, :] = jnp.full((1, spread.shape[1]), send_lists[i].astype(F32), F32)
 
 
 def row_of(half, step, direct, cap):
@@ -209,15 +211,14 @@
             send[i * width : (i + 1) * width, :] = field[rows, :]
 
 
-def fetch(lists, table, sem):
-    return pltpu.make_async_copy(lists, table, sem)
+def picked(spread, first, edge, width):
+    index = lambda i: jnp.max(spread[i : i + 1, :]).astype(jnp.int32)
+    return [pl.ds(pl.multiple_of(index(first + i) * width, width), width) for i in range(edge)]
 
 
 def local_kernel(width, edge, less, gives, lists, near_op, field, near, *refs):
-    table, sem = refs[-2:]
-    refs = list(refs[:-2])
-    copy = fetch(lists, table, sem)
-    copy.start()
+    refs = list(refs)
+    ats = picked(lists, edge, edge, width), picked(lists, 0, edge, width)
     rows = field.shape[0]
     older = refs.pop(0) if less else None
     far_op = refs.pop(0) if gives == "both" else None
@@ -226,11 +227,9 @@
         near_op[:, rows:], near[...], preferred_element_type=F32
     )
     acc[...] = total - older[...].astype(F32) if less else total
-    copy.wait()
     if not gives:
         return
     part, near_part = refs[:2]
-    ats = pick(table, edge, edge, width), pick(table, 0, edge, width)
     for out, places in zip((part, near_part), ats):
         for i, at in enumerate(places):
             out[i * width : (i + 1) * width, :] = acc[at, :].astype(out.dtype)
@@ -270,19 +269,15 @@
 
 
 def finish_kernel(first, wants, width, edge, lists, acc, far_op, far, *refs):
-    table, sem = refs[-2:]
-    refs = list(refs[:-2])
-    copy = fetch(lists, table, sem)
-    copy.start()
+    refs = list(refs)
     total = result_of(first, acc, far_op, far[...])
     value, part = wants
     if value:
         refs.pop(0)[...] = total
     field = refs[0]
     field[...] = total.astype(BF16)
-    copy.wait()
     if part:
-        for i, rows in enumerate(pick(table, edge, edge, width)):
+        for i, rows in enumerate(picked(lists, edge, edge, width)):
             refs[1][i * width : (i + 1) * width, :] = field[rows, :]
 
 
@@ -355,8 +350,9 @@
 
     n_slots = 1 + cap * nblk
     own = call(gather_kernel, ints(n_slots + 2 * edge), [SMEM] * 3, SMEM)(counts, cols, lists)
-    info, send_lists = call(
-        tables_kernel, (ints(n_slots), ints(2 * edge)), [SMEM] * 2, (SMEM, SMEM)
+    info, send_lists, spread = call(
+        tables_kernel, (ints(n_slots), ints(2 * edge), sds((2 * edge, width), F32)),
+        [SMEM] * 2, (SMEM, SMEM, VMEM),
     )(own, send(own, "trade"))
 
     field = call(
@@ -402,8 +398,6 @@
     older, newer = (), field
     part = lambda kind: sds((edge * width, panel), kind)
     square = sds((edge // 2 * width, edge * width), BF16)
-    table = (pltpu.SMEM((2 * edge,), jnp.int32), pltpu.SemaphoreType.DMA)
-    lists_at = pltpu.with_memory_space_constraint(send_lists, pltpu.HBM)
     moved_part, sent_rows, theirs = None, {}, []
     for step in range(STEPS):
         plain = step <= PLAIN
@@ -418,10 +412,10 @@
         kind = F32 if step < PLAIN else BF16
         outs = (wide(F32),) + ((part(kind), part(F32)) if gives else ())
         outs += (square, square, sds((edge * width, edge * width), BF16)) if first else ()
-        given = (lists_at, near_op, field, near) + older + ((far_op,) if first else ())
+        given = (spread, near_op, field, near) + older + ((far_op,) if first else ())
         mine = call(
             functools.partial(local_kernel, width, edge, not first, gives), outs,
-            [HBM] + [VMEM] * (len(given) - 1), (VMEM,) * len(outs), scratch=table,
+            [VMEM] * len(given), (VMEM,) * len(outs),
         )(*given)
         acc = mine[0]
         if first:
@@ -465,8 +459,8 @@
         outs = ((wide(F32),) if wants[0] else ()) + (wide(BF16),) + ((sent,) if wants[1] else ())
         result = call(
             functools.partial(finish_kernel, first, wants, width, edge), outs,
-            [HBM] + [VMEM] * 3, (VMEM,) * len(outs), scratch=table,
-        )(lists_at, acc, far_op, far)
+            [VMEM] * 4, (VMEM,) * len(outs),
+        )(spread, acc, far_op, far)
         result = list(result)
         older, newer = (newer,), result.pop(0) if wants[0] else None
         field = result[0]

time: 150 us -> 150 us (level)
  Pallas kernels: 47.4 us -> 39 us
  waiting for transfers between devices: 58.3 us -> 66.5 us
    ppermute x36, waiting for transfers between devices: 46.3 us -> 54.6 us  [send(): return lax.ppermute(x, AXES, ways[way])]
    pallas_call x9, Pallas kernels: 8.57 us -> 4.06 us  [body(): call(functools.partial(finish_kernel, first, wants, width, edge), outs, [...]
    pallas_call x10, Pallas kernels: 14.6 us -> 10.7 us  [body(): call(functools.partial(local_kernel, width, edge, not first, gives), outs...]
  transfers between devices with their start and end apart: 39 -> 39, of which waited for: 16 -> 16; matrix products, arithmetic and copies ran while one was open for 0% -> 0% of each run, Pallas kernels for 27% -> 21%
where the time goes in v8:
time: 150 us
  waiting for transfers between devices  66.5 us (44%)
  starting transfers between devices  41.4 us (28%)
  Pallas kernels  39 us (26%)
    ppermute x36, waiting for transfers between devices, send(): return lax.ppermute(x, AXES, ways[way])  54.6 us
    ppermute x36, starting transfers between devices, send(): return lax.ppermute(x, AXES, ways[way])  38.3 us
    ppermute x3, waiting for transfers between devices, body(): lax.ppermute(pieces[place], 'col', [(k, k ^ bit) for k in range(columns)])  11.9 us
    pallas_call x10, Pallas kernels, body(): call(functools.partial(local_kernel, width, edge, not first, gives), outs...  10.7 us
    pallas_call x5, Pallas kernels, body(): call(functools.partial(build_kernel, [(*row[:2], len(row[2])) for row in...  8.01 us
    pallas_call x9, Pallas kernels, body(): call(functools.partial(near_kernel, first, not plain), outs, [VMEM] * (2...  5.31 us
    pallas_call x9, Pallas kernels, body(): call(functools.partial(finish_kernel, first, wants, width, edge), outs, [...  4.06 us
    ppermute x3, starting transfers between devices, body(): lax.ppermute(pieces[place], 'col', [(k, k ^ bit) for k in range(columns)])  3.07 us
  transfers between devices with their start and end apart: 39, of which 16 were waited for; matrix products, arithmetic and copies ran while one was open for 0% of the time, Pallas kernels for 21%

profile of v8, /device:TPU:0, one launch (start us, length us, event | category | flops | bytes accessed | tf_op | source)
XLA Modules:
  0.0 149.7 jit_solution(16477370284271842264)
XLA Ops:
  1.3 3.1 %collective-permute-start.11 = (bf16[256,1024]{1,0:T(8,128)(2,1)S(1)}, bf16[256,1024]{1,0:T(8,128)(2,1)S(1)}, u32[]{:S(2)}, u32[]{:S(2)}) collective-permute-start(bf16[256,1024]{1,0:T(8,128)(2,1)S(1)} %convert_element_type.3.refs_0_), channel_id=1, source_target_pairs={{0,2},{1,3},{2,0},{3,1},{4,6},{5,7},{6,4},{7,5},{8,10},{9,11},{10,... | collective-permute-start | bytes 1572872 | tf_op jit(solution)/shard_map/ppermute | solution.py:328
  4.4 11.9 %collective-permute-done.11.refs_1_ = bf16[256,1024]{1,0:T(8,128)(2,1)S(1)} collective-permute-done((bf16[256,1024]{1,0:T(8,128)(2,1)S(1)}, bf16[256,1024]{1,0:T(8,128)(2,1)S(1)}, u32[]{:S(2)}, u32[]{:S(2)}) %collective-permute-start.11) | collective-permute-done | bytes 524320 | tf_op jit(solution)/shard_map/ppermute | solution.py:328
  17.8 1.9 %collective-permute-start.9 = (bf16[1,16,128,128]{3,2,1,0:T(8,128)(2,1)S(1)}, bf16[1,16,128,128]{3,2,1,0:T(8,128)(2,1)S(1)}, u32[]{:S(2)}, u32[]{:S(2)}) collective-permute-start(bf16[1,16,128,128]{3,2,1,0:T(8,128)(2,1)S(1)} %get-tuple-element.96), channel_id=1, source_target_pairs={{0,8},{1,4},{2,10},{3,6},{4,1},{5,13},{6,3},{7,15},{8,0},{9,12},{1... | collective-permute-start | bytes 1572872 | tf_op jit(solution)/shard_map/ppermute | solution.py:313
  25.1 1.8 %collective-permute-start.2 = (bf16[1,8,128,128]{3,2,1,0:T(8,128)(2,1)S(1)}, bf16[1,8,128,128]{3,2,1,0:T(8,128)(2,1)S(1)}, u32[]{:S(2)}, u32[]{:S(2)}) collective-permute-start(bf16[1,8,128,128]{3,2,1,0:T(8,128)(2,1)S(1)} %get-tuple-element.93), channel_id=1, source_target_pairs={{0,8},{1,4},{2,10},{3,6},{4,1},{5,13},{6,3},{7,15},{8,0},{9,12},{1... | collective-permute-start | bytes 786440 | tf_op jit(solution)/shard_map/ppermute | solution.py:313
  28.2 10.2 %collective-permute-done.moved = s32[137]{0:T(256)S(1)} collective-permute-done((s32[137]{0:T(256)S(1)}, s32[137]{0:T(256)S(1)}, u32[]{:S(2)}, u32[]{:S(2)}) %collective-permute-start) | collective-permute-done | bytes 580 | tf_op jit(solution)/shard_map/ppermute | solution.py:313
  38.4 1.8 %collective-permute-start.14 = (bf16[1024,256]{1,0:T(8,128)(2,1)S(1)}, bf16[1024,256]{1,0:T(8,128)(2,1)S(1)}, u32[]{:S(2)}, u32[]{:S(2)}) collective-permute-start(bf16[1024,256]{1,0:T(8,128)(2,1)S(1)} %shard_map.73.own), channel_id=1, source_target_pairs={{0,8},{1,4},{2,10},{3,6},{4,1},{5,13},{6,3},{7,15},{8,0},{9,12},{1... | collective-permute-start | bytes 1572872 | tf_op jit(solution)/shard_map/ppermute | solution.py:313
  44.3 6.1 %collective-permute-done.6.refs_1_ = bf16[1,8,128,128]{3,2,1,0:T(8,128)(2,1)S(1)} collective-permute-done((bf16[1,8,128,128]{3,2,1,0:T(8,128)(2,1)S(1)}, bf16[1,8,128,128]{3,2,1,0:T(8,128)(2,1)S(1)}, u32[]{:S(2)}, u32[]{:S(2)}) %collective-permute-start.6) | collective-permute-done | bytes 262176 | tf_op jit(solution)/shard_map/ppermute | solution.py:313
  50.4 1.8 %collective-permute-start.1 = (bf16[1,8,128,128]{3,2,1,0:T(8,128)(2,1)S(1)}, bf16[1,8,128,128]{3,2,1,0:T(8,128)(2,1)S(1)}, u32[]{:S(2)}, u32[]{:S(2)}) collective-permute-start(bf16[1,8,128,128]{3,2,1,0:T(8,128)(2,1)S(1)} %get-tuple-element.92), channel_id=1, source_target_pairs={{0,8},{1,4},{2,10},{3,6},{4,1},{5,13},{6,3},{7,15},{8,0},{9,12},{1... | collective-permute-start | bytes 786440 | tf_op jit(solution)/shard_map/ppermute | solution.py:313
  53.5 4.9 %collective-permute-start.15 = (bf16[512,256]{1,0:T(8,128)(2,1)S(1)}, bf16[512,256]{1,0:T(8,128)(2,1)S(1)}, u32[]{:S(2)}, u32[]{:S(2)}) collective-permute-start(bf16[512,256]{1,0:T(8,128)(2,1)S(1)} %get-tuple-element.108), channel_id=1, source_target_pairs={{0,1},{1,0},{2,3},{3,2},{4,5},{5,4},{6,7},{7,6},{8,9},{9,8},{10,11... | collective-permute-start | bytes 786440 | tf_op jit(solution)/shard_map/ppermute | solution.py:313
  58.8 3.0 %shard_map.68 = (bf16[1024,1536]{1,0:T(8,128)(2,1)S(1)}, bf16[1024,512]{1,0:T(8,128)(2,1)S(1)}) custom-call(s32[129]{0:T(256)S(1)} %get-tuple-element.91.info, bf16[8,16,128,128]{3,2,1,0:T(8,128)(2,1)} %blocks.13, bf16[1,16,128,128]{3,2,1,0:T(8,128)(2,1)S(1)} %collective-permute-done.7.refs_0_, bf16[1,16,128,128]{3,2,1,0:T(8,128)(2,1)S(1)} %collective-permute-done.9.refs_1_), custom_call_target="tpu_custom_call" | custom-call | tf_op jit(solution)/shard_map/pallas_call | solution.py:380
  61.8 3.0 %shard_map.69 = (bf16[1024,1536]{1,0:T(8,128)(2,1)S(1)}, bf16[1024,512]{1,0:T(8,128)(2,1)S(1)}) custom-call(s32[129]{0:T(256)S(1)} %get-tuple-element.91.info, bf16[8,16,128,128]{3,2,1,0:T(8,128)(2,1)} %blocks.13, bf16[1,16,128,128]{3,2,1,0:T(8,128)(2,1)S(1)} %collective-permute-done.4.refs_0_, ...), custom_call_target="tpu_custom_call", output_to_operand_aliasing={{0}: (3, {}), {1}: (4, {})} | custom-call | tf_op jit(solution)/shard_map/pallas_call | solution.py:380
  71.9 3.2 %collective-permute-done.18.far.refs_0_ = bf16[512,256]{1,0:T(8,128)(2,1)S(1)} collective-permute-done((bf16[512,256]{1,0:T(8,128)(2,1)S(1)}, bf16[512,256]{1,0:T(8,128)(2,1)S(1)}, u32[]{:S(2)}, u32[]{:S(2)}) %collective-permute-start.18) | collective-permute-done | bytes 262176 | tf_op jit(solution)/shard_map/ppermute | solution.py:313
  79.0 3.3 %collective-permute-done.20.far.refs_0_ = bf16[512,256]{1,0:T(8,128)(2,1)S(1)} collective-permute-done((bf16[512,256]{1,0:T(8,128)(2,1)S(1)}, bf16[512,256]{1,0:T(8,128)(2,1)S(1)}, u32[]{:S(2)}, u32[]{:S(2)}) %collective-permute-start.20) | collective-permute-done | bytes 262176 | tf_op jit(solution)/shard_map/ppermute | solution.py:313
  89.2 2.8 %collective-permute-done.24.refs_2_.high = bf16[256,512]{1,0:T(8,128)(2,1)S(1)} collective-permute-done((bf16[256,512]{1,0:T(8,128)(2,1)S(1)}, bf16[256,512]{1,0:T(8,128)(2,1)S(1)}, u32[]{:S(2)}, u32[]{:S(2)}) %collective-permute-start.24) | collective-permute-done | bytes 262176 | tf_op jit(solution)/shard_map/ppermute | solution.py:313
  92.0 2.8 %collective-permute-done.22.refs_0_ = bf16[512,256]{1,0:T(8,128)(2,1)S(1)} collective-permute-done((bf16[512,256]{1,0:T(8,128)(2,1)S(1)}, bf16[512,256]{1,0:T(8,128)(2,1)S(1)}, u32[]{:S(2)}, u32[]{:S(2)}) %collective-permute-start.22) | collective-permute-done | bytes 262176 | tf_op jit(solution)/shard_map/ppermute | solution.py:313
  98.8 3.3 %collective-permute-done.26.refs_0_ = bf16[512,256]{1,0:T(8,128)(2,1)S(1)} collective-permute-done((bf16[512,256]{1,0:T(8,128)(2,1)S(1)}, bf16[512,256]{1,0:T(8,128)(2,1)S(1)}, u32[]{:S(2)}, u32[]{:S(2)}) %collective-permute-start.26) | collective-permute-done | bytes 262176 | tf_op jit(solution)/shard_map/ppermute | solution.py:313
  106.1 3.3 %collective-permute-done.28.refs_0_ = bf16[512,256]{1,0:T(8,128)(2,1)S(1)} collective-permute-done((bf16[512,256]{1,0:T(8,128)(2,1)S(1)}, bf16[512,256]{1,0:T(8,128)(2,1)S(1)}, u32[]{:S(2)}, u32[]{:S(2)}) %collective-permute-start.28) | collective-permute-done | bytes 262176 | tf_op jit(solution)/shard_map/ppermute | solution.py:313
  113.4 3.3 %collective-permute-done.30.refs_0_ = bf16[512,256]{1,0:T(8,128)(2,1)S(1)} collective-permute-done((bf16[512,256]{1,0:T(8,128)(2,1)S(1)}, bf16[512,256]{1,0:T(8,128)(2,1)S(1)}, u32[]{:S(2)}, u32[]{:S(2)}) %collective-permute-start.30) | collective-permute-done | bytes 262176 | tf_op jit(solution)/shard_map/ppermute | solution.py:313
  120.9 3.1 %collective-permute-done.32.refs_0_ = bf16[512,256]{1,0:T(8,128)(2,1)S(1)} collective-permute-done((bf16[512,256]{1,0:T(8,128)(2,1)S(1)}, bf16[512,256]{1,0:T(8,128)(2,1)S(1)}, u32[]{:S(2)}, u32[]{:S(2)}) %collective-permute-start.32) | collective-permute-done | bytes 262176 | tf_op jit(solution)/shard_map/ppermute | solution.py:313
  128.0 3.3 %collective-permute-done.34.refs_0_ = bf16[512,256]{1,0:T(8,128)(2,1)S(1)} collective-permute-done((bf16[512,256]{1,0:T(8,128)(2,1)S(1)}, bf16[512,256]{1,0:T(8,128)(2,1)S(1)}, u32[]{:S(2)}, u32[]{:S(2)}) %collective-permute-start.34) | collective-permute-done | bytes 262176 | tf_op jit(solution)/shard_map/ppermute | solution.py:313
  135.2 3.4 %collective-permute-done.36.part = bf16[512,256]{1,0:T(8,128)(2,1)S(1)} collective-permute-done((bf16[512,256]{1,0:T(8,128)(2,1)S(1)}, bf16[512,256]{1,0:T(8,128)(2,1)S(1)}, u32[]{:S(2)}, u32[]{:S(2)}) %collective-permute-start.36) | collective-permute-done | bytes 262176 | tf_op jit(solution)/shard_map/ppermute | solution.py:313
  140.3 2.1 %collective-permute-start.37 = (bf16[256,512]{1,0:T(8,128)(2,1)S(1)}, bf16[256,512]{1,0:T(8,128)(2,1)S(1)}, u32[]{:S(2)}, u32[]{:S(2)}) collective-permute-start(bf16[256,512]{1,0:T(8,128)(2,1)S(1)} %shard_map.105.own), channel_id=1, source_target_pairs={{0,8},{1,4},{2,10},{3,6},{4,1},{5,13},{6,3},{7,15},{8,0},{9,12},{1... | collective-permute-start | bytes 786440 | tf_op jit(solution)/shard_map/ppermute | solution.py:313
  142.4 3.5 %collective-permute-done.38.moved = bf16[256,512]{1,0:T(8,128)(2,1)S(1)} collective-permute-done((bf16[256,512]{1,0:T(8,128)(2,1)S(1)}, bf16[256,512]{1,0:T(8,128)(2,1)S(1)}, u32[]{:S(2)}, u32[]{:S(2)}) %collective-permute-start.38) | collective-permute-done | bytes 262176 | tf_op jit(solution)/shard_map/ppermute | solution.py:313
  146.7 2.0 %collective-permute-done.37.moved = bf16[256,512]{1,0:T(8,128)(2,1)S(1)} collective-permute-done((bf16[256,512]{1,0:T(8,128)(2,1)S(1)}, bf16[256,512]{1,0:T(8,128)(2,1)S(1)}, u32[]{:S(2)}, u32[]{:S(2)}) %collective-permute-start.37) | collective-permute-done | bytes 262176 | tf_op jit(solution)/shard_map/ppermute | solution.py:313
  (106 shorter events, 59.8 us)
Async XLA Ops:
  1.3 15.0 %collective-permute-start.11 = (bf16[256,1024]{1,0:T(8,128)(2,1)S(1)}, bf16[256,1024]{1,0:T(8,128)(2,1)S(1)}, u32[]{:S(2)}, u32[]{:S(2)}) collective-permute-start(bf16[256,1024]{1,0:T(8,128)(2,1)S(1)} %convert_element_type.3.refs_0_), channel_id=1, source_target_pairs={{0,2},{1,3},{2,0},{3,1},{4,6},{5,7},{6,4},{7,5},{8,10},{9,11},{10,... | collective-permute-start | bytes 1572872 | tf_op jit(solution)/shard_map/ppermute | solution.py:328
  4.4 20.4 %collective-permute-start.12 = (bf16[256,1024]{1,0:T(8,128)(2,1)S(1)}, bf16[256,1024]{1,0:T(8,128)(2,1)S(1)}, u32[]{:S(2)}, u32[]{:S(2)}) collective-permute-start(bf16[256,1024]{1,0:T(8,128)(2,1)S(1)} %convert_element_type.3.refs_0_), channel_id=1, source_target_pairs={{0,1},{1,0},{2,3},{3,2},{4,5},{5,4},{6,7},{7,6},{8,9},{9,8},{10,11... | collective-permute-start | bytes 1572872 | tf_op jit(solution)/shard_map/ppermute | solution.py:328
  16.3 8.9 %collective-permute-start.13 = (bf16[256,1024]{1,0:T(8,128)(2,1)S(1)}, bf16[256,1024]{1,0:T(8,128)(2,1)S(1)}, u32[]{:S(2)}, u32[]{:S(2)}) collective-permute-start(bf16[256,1024]{1,0:T(8,128)(2,1)S(1)} %collective-permute-done.11.refs_1_), channel_id=1, source_target_pairs={{0,1},{1,0},{2,3},{3,2},{4,5},{5,4},{6,7},{7,6},{8,9},{9,8},{10,11... | collective-permute-start | bytes 1572872 | tf_op jit(solution)/shard_map/ppermute | solution.py:328
  17.8 22.3 %collective-permute-start.9 = (bf16[1,16,128,128]{3,2,1,0:T(8,128)(2,1)S(1)}, bf16[1,16,128,128]{3,2,1,0:T(8,128)(2,1)S(1)}, u32[]{:S(2)}, u32[]{:S(2)}) collective-permute-start(bf16[1,16,128,128]{3,2,1,0:T(8,128)(2,1)S(1)} %get-tuple-element.96), channel_id=1, source_target_pairs={{0,8},{1,4},{2,10},{3,6},{4,1},{5,13},{6,3},{7,15},{8,0},{9,12},{1... | collective-permute-start | bytes 1572872 | tf_op jit(solution)/shard_map/ppermute | solution.py:313
  20.8 20.1 %collective-permute-start.7 = (bf16[1,16,128,128]{3,2,1,0:T(8,128)(2,1)S(1)}, bf16[1,16,128,128]{3,2,1,0:T(8,128)(2,1)S(1)}, u32[]{:S(2)}, u32[]{:S(2)}) collective-permute-start(bf16[1,16,128,128]{3,2,1,0:T(8,128)(2,1)S(1)} %shard_map.67), channel_id=1, source_target_pairs={{0,8},{1,4},{2,10},{3,6},{4,1},{5,13},{6,3},{7,15},{8,0},{9,12},{1... | collective-permute-start | bytes 1572872 | tf_op jit(solution)/shard_map/ppermute | solution.py:313
  21.1 20.5 %collective-permute-start.4 = (bf16[1,16,128,128]{3,2,1,0:T(8,128)(2,1)S(1)}, bf16[1,16,128,128]{3,2,1,0:T(8,128)(2,1)S(1)}, u32[]{:S(2)}, u32[]{:S(2)}) collective-permute-start(bf16[1,16,128,128]{3,2,1,0:T(8,128)(2,1)S(1)} %get-tuple-element.94), channel_id=1, source_target_pairs={{0,8},{1,4},{2,10},{3,6},{4,1},{5,13},{6,3},{7,15},{8,0},{9,12},{1... | collective-permute-start | bytes 1572872 | tf_op jit(solution)/shard_map/ppermute | solution.py:313
  24.8 13.6 %collective-permute-start = (s32[137]{0:T(256)S(1)}, s32[137]{0:T(256)S(1)}, u32[]{:S(2)}, u32[]{:S(2)}) collective-permute-start(s32[137]{0:T(256)S(1)} %shard_map.64.own), channel_id=1, source_target_pairs={{0,8},{1,4},{2,10},{3,6},{4,1},{5,13},{6,3},{7,15},{8,0},{9,12},{1... | collective-permute-start | bytes 1652 | tf_op jit(solution)/shard_map/ppermute | solution.py:313
  25.1 17.1 %collective-permute-start.2 = (bf16[1,8,128,128]{3,2,1,0:T(8,128)(2,1)S(1)}, bf16[1,8,128,128]{3,2,1,0:T(8,128)(2,1)S(1)}, u32[]{:S(2)}, u32[]{:S(2)}) collective-permute-start(bf16[1,8,128,128]{3,2,1,0:T(8,128)(2,1)S(1)} %get-tuple-element.93), channel_id=1, source_target_pairs={{0,8},{1,4},{2,10},{3,6},{4,1},{5,13},{6,3},{7,15},{8,0},{9,12},{1... | collective-permute-start | bytes 786440 | tf_op jit(solution)/shard_map/ppermute | solution.py:313
  38.4 13.8 %collective-permute-start.14 = (bf16[1024,256]{1,0:T(8,128)(2,1)S(1)}, bf16[1024,256]{1,0:T(8,128)(2,1)S(1)}, u32[]{:S(2)}, u32[]{:S(2)}) collective-permute-start(bf16[1024,256]{1,0:T(8,128)(2,1)S(1)} %shard_map.73.own), channel_id=1, source_target_pairs={{0,8},{1,4},{2,10},{3,6},{4,1},{5,13},{6,3},{7,15},{8,0},{9,12},{1... | collective-permute-start | bytes 1572872 | tf_op jit(solution)/shard_map/ppermute | solution.py:313
  40.2 13.3 %collective-permute-start.10 = (bf16[1,16,128,128]{3,2,1,0:T(8,128)(2,1)S(1)}, bf16[1,16,128,128]{3,2,1,0:T(8,128)(2,1)S(1)}, u32[]{:S(2)}, u32[]{:S(2)}) collective-permute-start(bf16[1,16,128,128]{3,2,1,0:T(8,128)(2,1)S(1)} %collective-permute-done.9.refs_1_), channel_id=1, source_target_pairs={{1,3},{3,1},{4,6},{6,4},{9,11},{11,9},{12,14},{14,12},{17,19},{19,... | collective-permute-start | bytes 1572872 | tf_op jit(solution)/shard_map/ppermute | solution.py:313
  40.9 17.5 %collective-permute-start.8 = (bf16[1,16,128,128]{3,2,1,0:T(8,128)(2,1)S(1)}, bf16[1,16,128,128]{3,2,1,0:T(8,128)(2,1)S(1)}, u32[]{:S(2)}, u32[]{:S(2)}) collective-permute-start(bf16[1,16,128,128]{3,2,1,0:T(8,128)(2,1)S(1)} %collective-permute-done.7.refs_0_), channel_id=1, source_target_pairs={{1,3},{3,1},{4,6},{6,4},{9,11},{11,9},{12,14},{14,12},{17,19},{19,... | collective-permute-start | bytes 1572872 | tf_op jit(solution)/shard_map/ppermute | solution.py:313
  41.6 23.9 %collective-permute-start.5 = (bf16[1,16,128,128]{3,2,1,0:T(8,128)(2,1)S(1)}, bf16[1,16,128,128]{3,2,1,0:T(8,128)(2,1)S(1)}, u32[]{:S(2)}, u32[]{:S(2)}) collective-permute-start(bf16[1,16,128,128]{3,2,1,0:T(8,128)(2,1)S(1)} %collective-permute-done.4.refs_0_), channel_id=1, source_target_pairs={{1,3},{3,1},{4,6},{6,4},{9,11},{11,9},{12,14},{14,12},{17,19},{19,... | collective-permute-start | bytes 1572872 | tf_op jit(solution)/shard_map/ppermute | solution.py:313
  42.3 8.1 %collective-permute-start.6 = (bf16[1,8,128,128]{3,2,1,0:T(8,128)(2,1)S(1)}, bf16[1,8,128,128]{3,2,1,0:T(8,128)(2,1)S(1)}, u32[]{:S(2)}, u32[]{:S(2)}) collective-permute-start(bf16[1,8,128,128]{3,2,1,0:T(8,128)(2,1)S(1)} %get-tuple-element.95), channel_id=1, source_target_pairs={{0,8},{1,4},{2,10},{3,6},{4,1},{5,13},{6,3},{7,15},{8,0},{9,12},{1... | collective-permute-start | bytes 786440 | tf_op jit(solution)/shard_map/ppermute | solution.py:313
  50.4 15.7 %collective-permute-start.1 = (bf16[1,8,128,128]{3,2,1,0:T(8,128)(2,1)S(1)}, bf16[1,8,128,128]{3,2,1,0:T(8,128)(2,1)S(1)}, u32[]{:S(2)}, u32[]{:S(2)}) collective-permute-start(bf16[1,8,128,128]{3,2,1,0:T(8,128)(2,1)S(1)} %get-tuple-element.92), channel_id=1, source_target_pairs={{0,8},{1,4},{2,10},{3,6},{4,1},{5,13},{6,3},{7,15},{8,0},{9,12},{1... | collective-permute-start | bytes 786440 | tf_op jit(solution)/shard_map/ppermute | solution.py:313
  52.2 13.9 %collective-permute-start.3 = (bf16[1,8,128,128]{3,2,1,0:T(8,128)(2,1)S(1)}, bf16[1,8,128,128]{3,2,1,0:T(8,128)(2,1)S(1)}, u32[]{:S(2)}, u32[]{:S(2)}) collective-permute-start(bf16[1,8,128,128]{3,2,1,0:T(8,128)(2,1)S(1)} %collective-permute-done.2.refs_2_), channel_id=1, source_target_pairs={{1,3},{3,1},{4,6},{6,4},{9,11},{11,9},{12,14},{14,12},{17,19},{19,... | collective-permute-start | bytes 786440 | tf_op jit(solution)/shard_map/ppermute | solution.py:313
  53.5 13.4 %collective-permute-start.15 = (bf16[512,256]{1,0:T(8,128)(2,1)S(1)}, bf16[512,256]{1,0:T(8,128)(2,1)S(1)}, u32[]{:S(2)}, u32[]{:S(2)}) collective-permute-start(bf16[512,256]{1,0:T(8,128)(2,1)S(1)} %get-tuple-element.108), channel_id=1, source_target_pairs={{0,1},{1,0},{2,3},{3,2},{4,5},{5,4},{6,7},{7,6},{8,9},{9,8},{10,11... | collective-permute-start | bytes 786440 | tf_op jit(solution)/shard_map/ppermute | solution.py:313
  58.3 9.6 %collective-permute-start.16 = (bf16[512,256]{1,0:T(8,128)(2,1)S(1)}, bf16[512,256]{1,0:T(8,128)(2,1)S(1)}, u32[]{:S(2)}, u32[]{:S(2)}) collective-permute-start(bf16[512,256]{1,0:T(8,128)(2,1)S(1)} %get-tuple-element.111), channel_id=1, source_target_pairs={{0,4},{1,8},{2,6},{3,10},{4,0},{5,12},{6,2},{7,14},{8,1},{9,16},{1... | collective-permute-start | bytes 786440 | tf_op jit(solution)/shard_map/ppermute | solution.py:313
  68.7 6.4 %collective-permute-start.18 = (bf16[512,256]{1,0:T(8,128)(2,1)S(1)}, bf16[512,256]{1,0:T(8,128)(2,1)S(1)}, u32[]{:S(2)}, u32[]{:S(2)}) collective-permute-start(bf16[512,256]{1,0:T(8,128)(2,1)S(1)} %shard_map.79), channel_id=1, source_target_pairs={{0,4},{1,8},{2,6},{3,10},{4,0},{5,12},{6,2},{7,14},{8,1},{9,16},{1... | collective-permute-start | bytes 786440 | tf_op jit(solution)/shard_map/ppermute | solution.py:313
  75.9 6.4 %collective-permute-start.20 = (bf16[512,256]{1,0:T(8,128)(2,1)S(1)}, bf16[512,256]{1,0:T(8,128)(2,1)S(1)}, u32[]{:S(2)}, u32[]{:S(2)}) collective-permute-start(bf16[512,256]{1,0:T(8,128)(2,1)S(1)} %shard_map.83.refs_3_), channel_id=1, source_target_pairs={{0,4},{1,8},{2,6},{3,10},{4,0},{5,12},{6,2},{7,14},{8,1},{9,16},{1... | collective-permute-start | bytes 786440 | tf_op jit(solution)/shard_map/ppermute | solution.py:313
  84.4 7.6 %collective-permute-start.24 = (bf16[256,512]{1,0:T(8,128)(2,1)S(1)}, bf16[256,512]{1,0:T(8,128)(2,1)S(1)}, u32[]{:S(2)}, u32[]{:S(2)}) collective-permute-start(bf16[256,512]{1,0:T(8,128)(2,1)S(1)} %get-tuple-element.118.high), channel_id=1, source_target_pairs={{0,4},{1,8},{2,6},{3,10},{4,0},{5,12},{6,2},{7,14},{8,1},{9,16},{1... | collective-permute-start | bytes 786440 | tf_op jit(solution)/shard_map/ppermute | solution.py:313
  84.8 10.0 %collective-permute-start.22 = (bf16[512,256]{1,0:T(8,128)(2,1)S(1)}, bf16[512,256]{1,0:T(8,128)(2,1)S(1)}, u32[]{:S(2)}, u32[]{:S(2)}) collective-permute-start(bf16[512,256]{1,0:T(8,128)(2,1)S(1)} %get-tuple-element.129), channel_id=1, source_target_pairs={{0,4},{1,8},{2,6},{3,10},{4,0},{5,12},{6,2},{7,14},{8,1},{9,16},{1... | collective-permute-start | bytes 786440 | tf_op jit(solution)/shard_map/ppermute | solution.py:313
  124.9 6.4 %collective-permute-start.34 = (bf16[512,256]{1,0:T(8,128)(2,1)S(1)}, bf16[512,256]{1,0:T(8,128)(2,1)S(1)}, u32[]{:S(2)}, u32[]{:S(2)}) collective-permute-start(bf16[512,256]{1,0:T(8,128)(2,1)S(1)} %get-tuple-element.168), channel_id=1, source_target_pairs={{0,4},{1,8},{2,6},{3,10},{4,0},{5,12},{6,2},{7,14},{8,1},{9,16},{1... | collective-permute-start | bytes 786440 | tf_op jit(solution)/shard_map/ppermute | solution.py:313
  139.4 6.4 %collective-permute-start.38 = (bf16[256,512]{1,0:T(8,128)(2,1)S(1)}, bf16[256,512]{1,0:T(8,128)(2,1)S(1)}, u32[]{:S(2)}, u32[]{:S(2)}) collective-permute-start(bf16[256,512]{1,0:T(8,128)(2,1)S(1)} %shard_map.106.own), channel_id=1, source_target_pairs={{0,8},{1,4},{2,10},{3,6},{4,1},{5,13},{6,3},{7,15},{8,0},{9,12},{1... | collective-permute-start | bytes 786440 | tf_op jit(solution)/shard_map/ppermute | solution.py:313
  140.3 8.4 %collective-permute-start.37 = (bf16[256,512]{1,0:T(8,128)(2,1)S(1)}, bf16[256,512]{1,0:T(8,128)(2,1)S(1)}, u32[]{:S(2)}, u32[]{:S(2)}) collective-permute-start(bf16[256,512]{1,0:T(8,128)(2,1)S(1)} %shard_map.105.own), channel_id=1, source_target_pairs={{0,8},{1,4},{2,10},{3,6},{4,1},{5,13},{6,3},{7,15},{8,0},{9,12},{1... | collective-permute-start | bytes 786440 | tf_op jit(solution)/shard_map/ppermute | solution.py:313
  (18 other events, 81.3 us)

commit v9 on v8

--- a/solution.py
+++ b/solution.py
@@ -247,29 +247,45 @@
 
 
 def ahead_kernel(first, acc, low, high, far, out):
-    far_op = jnp.concatenate([low[...], high[...]], axis=0)
-    total = acc[...] + jnp.dot(far_op, far[...], preferred_element_type=F32)
-    out[...] = (0.5 * total if first else total).astype(BF16)
-
-
-def far_rows(part, low, high, sent):
-    op = jnp.concatenate([low[...], high[...]], axis=0)
-    total = part[...].astype(F32) + jnp.dot(op, sent[...], preferred_element_type=F32)
-    return total.astype(BF16)
-
-
-def near_kernel(first, apart, acc, far_op, *refs):
+    half = low.shape[0]
+    for at, op in ((0, low), (half, high)):
+        rows = pl.ds(at, half)
+        total = acc[rows, :] + jnp.dot(op[...], far[...], preferred_element_type=F32)
+        out[rows, :] = (0.5 * total if first else total).astype(BF16)
+
+
+def far_rows(part, low, high, sent, out):
+    half = low.shape[0]
+    for at, op in ((0, low), (half, high)):
+        rows = pl.ds(at, half)
+        total = part[rows, :].astype(F32) + jnp.dot(op[...], sent[...], preferred_element_type=F32)
+        out[rows, :] = total.astype(BF16)
+
+
+def mix_kernel(far_op, low, high, out):
+    half = low.shape[0]
+    total = jnp.dot(far_op[:, :half], low[...], preferred_element_type=F32) + jnp.dot(
+        far_op[:, half:], high[...], preferred_element_type=F32
+    )
+    out[...] = total.astype(BF16)
+
+
+def before_kernel(near_part, mixed, sent, out):
+    out[...] = near_part[...] + jnp.dot(mixed[...], sent[...], preferred_element_type=F32)
+
+
+def near_kernel(first, acc, far_op, far, out):
+    out[...] = result_of(first, acc, far_op, far[...]).astype(BF16)
+
+
+def finish_kernel(first, apart, wants, width, edge, spread, acc, far_op, *refs):
+    refs = list(refs)
     if apart:
-        far = far_rows(*refs[:4])
-        refs[5][...] = far
-        out = refs[4]
+        far = refs.pop()
+        far_rows(*refs[:4], far)
+        refs = refs[4:]
     else:
-        far, out = refs[0][...], refs[1]
-    out[...] = result_of(first, acc, far_op, far).astype(BF16)
-
-
-def finish_kernel(first, wants, width, edge, lists, acc, far_op, far, *refs):
-    refs = list(refs)
+        far = refs.pop(0)
     total = result_of(first, acc, far_op, far[...])
     value, part = wants
     if value:
@@ -277,14 +293,14 @@
     field = refs[0]
     field[...] = total.astype(BF16)
     if part:
-        for i, rows in enumerate(picked(lists, edge, edge, width)):
+        for i, rows in enumerate(picked(spread, edge, edge, width)):
             refs[1][i * width : (i + 1) * width, :] = field[rows, :]
 
 
-def last_kernel(begin, acc, far_op, part, low, high, sent, out):
+def last_kernel(begin, acc, far_op, part, low, high, sent, out, far):
     rows = pl.ds(begin, out.shape[1])
-    far = far_rows(part, low, high, sent)
-    total = acc[rows, :] + jnp.dot(far_op[rows, :], far, preferred_element_type=F32)
+    far_rows(part, low, high, sent, far)
+    total = acc[rows, :] + jnp.dot(far_op[rows, :], far[...], preferred_element_type=F32)
     out[...] = total.T.astype(BF16)
 
 
@@ -398,7 +414,7 @@
     older, newer = (), field
     part = lambda kind: sds((edge * width, panel), kind)
     square = sds((edge // 2 * width, edge * width), BF16)
-    moved_part, sent_rows, theirs = None, {}, []
+    moved_part, sent_rows, theirs, mixed = None, {}, [], None
     for step in range(STEPS):
         plain = step <= PLAIN
         first, last = step == 0, step == STEPS - 1
@@ -427,7 +443,8 @@
             cut = height // 2
             ends = [
                 call(
-                    functools.partial(last_kernel, begin), sds((panel, cut), BF16), [VMEM] * 6, VMEM
+                    functools.partial(last_kernel, begin), sds((panel, cut), BF16), [VMEM] * 6, VMEM,
+                    scratch=(pltpu.VMEM((edge * width, panel), BF16),),
                 )(acc, far_op, arrived_part, *theirs, sent_rows[step - 1])
                 for begin in (0, cut)
             ]
@@ -447,20 +464,26 @@
             far_send = call(
                 functools.partial(ahead_kernel, first), sent, [VMEM] * 4, VMEM
             )(mine[1], *far_part, far)
-        given = (far,) if plain else (arrived_part, *theirs, sent_rows[step - 1])
-        outs = (sent,) if plain else (sent, sent)
-        ready = call(
-            functools.partial(near_kernel, first, not plain), outs,
-            [VMEM] * (2 + len(given)), (VMEM,) * len(outs),
-        )(mine[2], near_far, *given)
-        near_send = ready[0]
-        far = far if plain else ready[1]
+        ready, given, scratch = mine[2], (far,), ()
+        if not plain:
+            if mixed is None:
+                mixed = call(
+                    mix_kernel, sds((edge * width,) * 2, BF16), [VMEM] * 3, VMEM
+                )(near_far, *theirs)
+            ready = call(before_kernel, part(F32), [VMEM] * 3, VMEM)(
+                mine[2], mixed, sent_rows[step - 1]
+            )
+            given = (arrived_part, *theirs, sent_rows[step - 1])
+            scratch = (pltpu.VMEM((edge * width, panel), BF16),)
+        near_send = call(
+            functools.partial(near_kernel, first), sent, [VMEM] * 3, VMEM
+        )(ready, near_far, given[0])
         wants = (step < STEPS - 2, PLAIN <= step < STEPS - 2)
         outs = ((wide(F32),) if wants[0] else ()) + (wide(BF16),) + ((sent,) if wants[1] else ())
         result = call(
-            functools.partial(finish_kernel, first, wants, width, edge), outs,
-            [VMEM] * 4, (VMEM,) * len(outs),
-        )(spread, acc, far_op, far)
+            functools.partial(finish_kernel, first, not plain, wants, width, edge), outs,
+            [VMEM] * (3 + len(given)), (VMEM,) * len(outs), scratch=scratch,
+        )(spread, acc, far_op, *given)
         result = list(result)
         older, newer = (newer,), result.pop(0) if wants[0] else None
         field = result[0]

time: 150 us -> 143 us (0.953)
  waiting for transfers between devices: 66.5 us -> 58.5 us
    ppermute x36, waiting for transfers between devices: 54.6 us -> 46.6 us  [send(): return lax.ppermute(x, AXES, ways[way])]
    pallas_call x18 -> x25, Pallas kernels: 9.37 us -> 10.8 us  [the longest x9 5.93 us: body(): call(functools.partial(finish_kernel, first, not plain, wants, width, edg...]
  transfers between devices with their start and end apart: 39 -> 39, of which waited for: 16 -> 16; matrix products, arithmetic and copies ran while one was open for 0% -> 0% of each run, Pallas kernels for 21% -> 25%
where the time goes in v9:
time: 143 us
  waiting for transfers between devices  58.5 us (41%)
  starting transfers between devices  41.6 us (29%)
  Pallas kernels  39.9 us (28%)
  between operations  1.48 us (1%)
    ppermute x36, waiting for transfers between devices, send(): return lax.ppermute(x, AXES, ways[way])  46.6 us
    ppermute x36, starting transfers between devices, send(): return lax.ppermute(x, AXES, ways[way])  38.5 us
    ppermute x3, waiting for transfers between devices, body(): lax.ppermute(pieces[place], 'col', [(k, k ^ bit) for k in range(columns)])  11.9 us
    pallas_call x10, Pallas kernels, body(): call(functools.partial(local_kernel, width, edge, not first, gives), outs...  10.5 us
    pallas_call x5, Pallas kernels, body(): call(functools.partial(build_kernel, [(*row[:2], len(row[2])) for row in...  8.01 us
    pallas_call x9, Pallas kernels, body(): call(functools.partial(finish_kernel, first, not plain, wants, width, edg...  5.93 us
    ppermute x3, starting transfers between devices, body(): lax.ppermute(pieces[place], 'col', [(k, k ^ bit) for k in range(columns)])  3.07 us
  transfers between devices with their start and end apart: 39, of which 16 were waited for; matrix products, arithmetic and copies ran while one was open for 0% of the time, Pallas kernels for 25%

profile of v9, /device:TPU:0, one launch (start us, length us, event | category | flops | bytes accessed | tf_op | source)
XLA Modules:
  0.0 142.8 jit_solution(10854274918082724356)
XLA Ops:
  1.3 3.1 %collective-permute-start.11 = (bf16[256,1024]{1,0:T(8,128)(2,1)S(1)}, bf16[256,1024]{1,0:T(8,128)(2,1)S(1)}, u32[]{:S(2)}, u32[]{:S(2)}) collective-permute-start(bf16[256,1024]{1,0:T(8,128)(2,1)S(1)} %convert_element_type.3.refs_0_), channel_id=1, source_target_pairs={{0,2},{1,3},{2,0},{3,1},{4,6},{5,7},{6,4},{7,5},{8,10},{9,11},{10,... | collective-permute-start | bytes 1572872 | tf_op jit(solution)/shard_map/ppermute | solution.py:344
  4.4 11.9 %collective-permute-done.11.refs_1_ = bf16[256,1024]{1,0:T(8,128)(2,1)S(1)} collective-permute-done((bf16[256,1024]{1,0:T(8,128)(2,1)S(1)}, bf16[256,1024]{1,0:T(8,128)(2,1)S(1)}, u32[]{:S(2)}, u32[]{:S(2)}) %collective-permute-start.11) | collective-permute-done | bytes 524320 | tf_op jit(solution)/shard_map/ppermute | solution.py:344
  17.8 1.9 %collective-permute-start.9 = (bf16[1,16,128,128]{3,2,1,0:T(8,128)(2,1)S(1)}, bf16[1,16,128,128]{3,2,1,0:T(8,128)(2,1)S(1)}, u32[]{:S(2)}, u32[]{:S(2)}) collective-permute-start(bf16[1,16,128,128]{3,2,1,0:T(8,128)(2,1)S(1)} %get-tuple-element.84), channel_id=1, source_target_pairs={{0,8},{1,4},{2,10},{3,6},{4,1},{5,13},{6,3},{7,15},{8,0},{9,12},{1... | collective-permute-start | bytes 1572872 | tf_op jit(solution)/shard_map/ppermute | solution.py:329
  21.1 1.8 %collective-permute-start.4 = (bf16[1,16,128,128]{3,2,1,0:T(8,128)(2,1)S(1)}, bf16[1,16,128,128]{3,2,1,0:T(8,128)(2,1)S(1)}, u32[]{:S(2)}, u32[]{:S(2)}) collective-permute-start(bf16[1,16,128,128]{3,2,1,0:T(8,128)(2,1)S(1)} %get-tuple-element.82), channel_id=1, source_target_pairs={{0,8},{1,4},{2,10},{3,6},{4,1},{5,13},{6,3},{7,15},{8,0},{9,12},{1... | collective-permute-start | bytes 1572872 | tf_op jit(solution)/shard_map/ppermute | solution.py:329
  25.1 1.8 %collective-permute-start.2 = (bf16[1,8,128,128]{3,2,1,0:T(8,128)(2,1)S(1)}, bf16[1,8,128,128]{3,2,1,0:T(8,128)(2,1)S(1)}, u32[]{:S(2)}, u32[]{:S(2)}) collective-permute-start(bf16[1,8,128,128]{3,2,1,0:T(8,128)(2,1)S(1)} %get-tuple-element.81), channel_id=1, source_target_pairs={{0,8},{1,4},{2,10},{3,6},{4,1},{5,13},{6,3},{7,15},{8,0},{9,12},{1... | collective-permute-start | bytes 786440 | tf_op jit(solution)/shard_map/ppermute | solution.py:329
  28.2 10.2 %collective-permute-done.moved = s32[137]{0:T(256)S(1)} collective-permute-done((s32[137]{0:T(256)S(1)}, s32[137]{0:T(256)S(1)}, u32[]{:S(2)}, u32[]{:S(2)}) %collective-permute-start) | collective-permute-done | bytes 580 | tf_op jit(solution)/shard_map/ppermute | solution.py:329
  38.4 1.8 %collective-permute-start.14 = (bf16[1024,256]{1,0:T(8,128)(2,1)S(1)}, bf16[1024,256]{1,0:T(8,128)(2,1)S(1)}, u32[]{:S(2)}, u32[]{:S(2)}) collective-permute-start(bf16[1024,256]{1,0:T(8,128)(2,1)S(1)} %shard_map.73.own), channel_id=1, source_target_pairs={{0,8},{1,4},{2,10},{3,6},{4,1},{5,13},{6,3},{7,15},{8,0},{9,12},{1... | collective-permute-start | bytes 1572872 | tf_op jit(solution)/shard_map/ppermute | solution.py:329
  44.3 6.1 %collective-permute-done.6.refs_1_ = bf16[1,8,128,128]{3,2,1,0:T(8,128)(2,1)S(1)} collective-permute-done((bf16[1,8,128,128]{3,2,1,0:T(8,128)(2,1)S(1)}, bf16[1,8,128,128]{3,2,1,0:T(8,128)(2,1)S(1)}, u32[]{:S(2)}, u32[]{:S(2)}) %collective-permute-start.6) | collective-permute-done | bytes 262176 | tf_op jit(solution)/shard_map/ppermute | solution.py:329
  50.4 1.8 %collective-permute-start.1 = (bf16[1,8,128,128]{3,2,1,0:T(8,128)(2,1)S(1)}, bf16[1,8,128,128]{3,2,1,0:T(8,128)(2,1)S(1)}, u32[]{:S(2)}, u32[]{:S(2)}) collective-permute-start(bf16[1,8,128,128]{3,2,1,0:T(8,128)(2,1)S(1)} %get-tuple-element.80), channel_id=1, source_target_pairs={{0,8},{1,4},{2,10},{3,6},{4,1},{5,13},{6,3},{7,15},{8,0},{9,12},{1... | collective-permute-start | bytes 786440 | tf_op jit(solution)/shard_map/ppermute | solution.py:329
  53.5 4.9 %collective-permute-start.15 = (bf16[512,256]{1,0:T(8,128)(2,1)S(1)}, bf16[512,256]{1,0:T(8,128)(2,1)S(1)}, u32[]{:S(2)}, u32[]{:S(2)}) collective-permute-start(bf16[512,256]{1,0:T(8,128)(2,1)S(1)} %get-tuple-element.96), channel_id=1, source_target_pairs={{0,1},{1,0},{2,3},{3,2},{4,5},{5,4},{6,7},{7,6},{8,9},{9,8},{10,11... | collective-permute-start | bytes 786440 | tf_op jit(solution)/shard_map/ppermute | solution.py:329
  58.8 3.0 %shard_map.68 = (bf16[1024,1536]{1,0:T(8,128)(2,1)S(1)}, bf16[1024,512]{1,0:T(8,128)(2,1)S(1)}) custom-call(s32[129]{0:T(256)S(1)} %get-tuple-element.79.info, bf16[8,16,128,128]{3,2,1,0:T(8,128)(2,1)} %blocks.13, bf16[1,16,128,128]{3,2,1,0:T(8,128)(2,1)S(1)} %collective-permute-done.7.refs_0_, bf16[1,16,128,128]{3,2,1,0:T(8,128)(2,1)S(1)} %collective-permute-done.9.refs_1_), custom_call_target="tpu_custom_call" | custom-call | tf_op jit(solution)/shard_map/pallas_call | solution.py:396
  61.8 3.0 %shard_map.69 = (bf16[1024,1536]{1,0:T(8,128)(2,1)S(1)}, bf16[1024,512]{1,0:T(8,128)(2,1)S(1)}) custom-call(s32[129]{0:T(256)S(1)} %get-tuple-element.79.info, bf16[8,16,128,128]{3,2,1,0:T(8,128)(2,1)} %blocks.13, bf16[1,16,128,128]{3,2,1,0:T(8,128)(2,1)S(1)} %collective-permute-done.4.refs_0_, ...), custom_call_target="tpu_custom_call", output_to_operand_aliasing={{0}: (3, {}), {1}: (4, {})} | custom-call | tf_op jit(solution)/shard_map/pallas_call | solution.py:396
  68.7 1.7 %collective-permute-start.18 = (bf16[512,256]{1,0:T(8,128)(2,1)S(1)}, bf16[512,256]{1,0:T(8,128)(2,1)S(1)}, u32[]{:S(2)}, u32[]{:S(2)}) collective-permute-start(bf16[512,256]{1,0:T(8,128)(2,1)S(1)} %shard_map.79), channel_id=1, source_target_pairs={{0,4},{1,8},{2,6},{3,10},{4,0},{5,12},{6,2},{7,14},{8,1},{9,16},{1... | collective-permute-start | bytes 786440 | tf_op jit(solution)/shard_map/ppermute | solution.py:329
  71.9 3.2 %collective-permute-done.18.refs_0_.far = bf16[512,256]{1,0:T(8,128)(2,1)S(1)} collective-permute-done((bf16[512,256]{1,0:T(8,128)(2,1)S(1)}, bf16[512,256]{1,0:T(8,128)(2,1)S(1)}, u32[]{:S(2)}, u32[]{:S(2)}) %collective-permute-start.18) | collective-permute-done | bytes 262176 | tf_op jit(solution)/shard_map/ppermute | solution.py:329
  85.2 2.8 %collective-permute-done.24.refs_2_.high = bf16[256,512]{1,0:T(8,128)(2,1)S(1)} collective-permute-done((bf16[256,512]{1,0:T(8,128)(2,1)S(1)}, bf16[256,512]{1,0:T(8,128)(2,1)S(1)}, u32[]{:S(2)}, u32[]{:S(2)}) %collective-permute-start.24) | collective-permute-done | bytes 262176 | tf_op jit(solution)/shard_map/ppermute | solution.py:329
  94.9 2.7 %collective-permute-done.26.refs_0_.far = bf16[512,256]{1,0:T(8,128)(2,1)S(1)} collective-permute-done((bf16[512,256]{1,0:T(8,128)(2,1)S(1)}, bf16[512,256]{1,0:T(8,128)(2,1)S(1)}, u32[]{:S(2)}, u32[]{:S(2)}) %collective-permute-start.26) | collective-permute-done | bytes 262176 | tf_op jit(solution)/shard_map/ppermute | solution.py:329
  101.8 2.7 %collective-permute-done.28.refs_0_.far = bf16[512,256]{1,0:T(8,128)(2,1)S(1)} collective-permute-done((bf16[512,256]{1,0:T(8,128)(2,1)S(1)}, bf16[512,256]{1,0:T(8,128)(2,1)S(1)}, u32[]{:S(2)}, u32[]{:S(2)}) %collective-permute-start.28) | collective-permute-done | bytes 262176 | tf_op jit(solution)/shard_map/ppermute | solution.py:329
  108.7 2.7 %collective-permute-done.30.refs_0_.far = bf16[512,256]{1,0:T(8,128)(2,1)S(1)} collective-permute-done((bf16[512,256]{1,0:T(8,128)(2,1)S(1)}, bf16[512,256]{1,0:T(8,128)(2,1)S(1)}, u32[]{:S(2)}, u32[]{:S(2)}) %collective-permute-start.30) | collective-permute-done | bytes 262176 | tf_op jit(solution)/shard_map/ppermute | solution.py:329
  115.7 2.4 %collective-permute-done.32.refs_0_.far = bf16[512,256]{1,0:T(8,128)(2,1)S(1)} collective-permute-done((bf16[512,256]{1,0:T(8,128)(2,1)S(1)}, bf16[512,256]{1,0:T(8,128)(2,1)S(1)}, u32[]{:S(2)}, u32[]{:S(2)}) %collective-permute-start.32) | collective-permute-done | bytes 262176 | tf_op jit(solution)/shard_map/ppermute | solution.py:329
  122.4 2.7 %collective-permute-done.34.refs_0_.far = bf16[512,256]{1,0:T(8,128)(2,1)S(1)} collective-permute-done((bf16[512,256]{1,0:T(8,128)(2,1)S(1)}, bf16[512,256]{1,0:T(8,128)(2,1)S(1)}, u32[]{:S(2)}, u32[]{:S(2)}) %collective-permute-start.34) | collective-permute-done | bytes 262176 | tf_op jit(solution)/shard_map/ppermute | solution.py:329
  128.8 3.1 %collective-permute-done.36.part = bf16[512,256]{1,0:T(8,128)(2,1)S(1)} collective-permute-done((bf16[512,256]{1,0:T(8,128)(2,1)S(1)}, bf16[512,256]{1,0:T(8,128)(2,1)S(1)}, u32[]{:S(2)}, u32[]{:S(2)}) %collective-permute-start.36) | collective-permute-done | bytes 262176 | tf_op jit(solution)/shard_map/ppermute | solution.py:329
  133.3 2.1 %collective-permute-start.37 = (bf16[256,512]{1,0:T(8,128)(2,1)S(1)}, bf16[256,512]{1,0:T(8,128)(2,1)S(1)}, u32[]{:S(2)}, u32[]{:S(2)}) collective-permute-start(bf16[256,512]{1,0:T(8,128)(2,1)S(1)} %shard_map.112.own), channel_id=1, source_target_pairs={{0,8},{1,4},{2,10},{3,6},{4,1},{5,13},{6,3},{7,15},{8,0},{9,12},{1... | collective-permute-start | bytes 786440 | tf_op jit(solution)/shard_map/ppermute | solution.py:329
  135.3 3.6 %collective-permute-done.38.moved = bf16[256,512]{1,0:T(8,128)(2,1)S(1)} collective-permute-done((bf16[256,512]{1,0:T(8,128)(2,1)S(1)}, bf16[256,512]{1,0:T(8,128)(2,1)S(1)}, u32[]{:S(2)}, u32[]{:S(2)}) %collective-permute-start.38) | collective-permute-done | bytes 262176 | tf_op jit(solution)/shard_map/ppermute | solution.py:329
  139.8 2.0 %collective-permute-done.37.moved = bf16[256,512]{1,0:T(8,128)(2,1)S(1)} collective-permute-done((bf16[256,512]{1,0:T(8,128)(2,1)S(1)}, bf16[256,512]{1,0:T(8,128)(2,1)S(1)}, u32[]{:S(2)}, u32[]{:S(2)}) %collective-permute-start.37) | collective-permute-done | bytes 262176 | tf_op jit(solution)/shard_map/ppermute | solution.py:329
  (113 shorter events, 58.6 us)
Async XLA Ops:
  1.3 15.0 %collective-permute-start.11 = (bf16[256,1024]{1,0:T(8,128)(2,1)S(1)}, bf16[256,1024]{1,0:T(8,128)(2,1)S(1)}, u32[]{:S(2)}, u32[]{:S(2)}) collective-permute-start(bf16[256,1024]{1,0:T(8,128)(2,1)S(1)} %convert_element_type.3.refs_0_), channel_id=1, source_target_pairs={{0,2},{1,3},{2,0},{3,1},{4,6},{5,7},{6,4},{7,5},{8,10},{9,11},{10,... | collective-permute-start | bytes 1572872 | tf_op jit(solution)/shard_map/ppermute | solution.py:344
  4.4 20.4 %collective-permute-start.12 = (bf16[256,1024]{1,0:T(8,128)(2,1)S(1)}, bf16[256,1024]{1,0:T(8,128)(2,1)S(1)}, u32[]{:S(2)}, u32[]{:S(2)}) collective-permute-start(bf16[256,1024]{1,0:T(8,128)(2,1)S(1)} %convert_element_type.3.refs_0_), channel_id=1, source_target_pairs={{0,1},{1,0},{2,3},{3,2},{4,5},{5,4},{6,7},{7,6},{8,9},{9,8},{10,11... | collective-permute-start | bytes 1572872 | tf_op jit(solution)/shard_map/ppermute | solution.py:344
  16.3 8.9 %collective-permute-start.13 = (bf16[256,1024]{1,0:T(8,128)(2,1)S(1)}, bf16[256,1024]{1,0:T(8,128)(2,1)S(1)}, u32[]{:S(2)}, u32[]{:S(2)}) collective-permute-start(bf16[256,1024]{1,0:T(8,128)(2,1)S(1)} %collective-permute-done.11.refs_1_), channel_id=1, source_target_pairs={{0,1},{1,0},{2,3},{3,2},{4,5},{5,4},{6,7},{7,6},{8,9},{9,8},{10,11... | collective-permute-start | bytes 1572872 | tf_op jit(solution)/shard_map/ppermute | solution.py:344
  17.8 22.3 %collective-permute-start.9 = (bf16[1,16,128,128]{3,2,1,0:T(8,128)(2,1)S(1)}, bf16[1,16,128,128]{3,2,1,0:T(8,128)(2,1)S(1)}, u32[]{:S(2)}, u32[]{:S(2)}) collective-permute-start(bf16[1,16,128,128]{3,2,1,0:T(8,128)(2,1)S(1)} %get-tuple-element.84), channel_id=1, source_target_pairs={{0,8},{1,4},{2,10},{3,6},{4,1},{5,13},{6,3},{7,15},{8,0},{9,12},{1... | collective-permute-start | bytes 1572872 | tf_op jit(solution)/shard_map/ppermute | solution.py:329
  20.8 20.1 %collective-permute-start.7 = (bf16[1,16,128,128]{3,2,1,0:T(8,128)(2,1)S(1)}, bf16[1,16,128,128]{3,2,1,0:T(8,128)(2,1)S(1)}, u32[]{:S(2)}, u32[]{:S(2)}) collective-permute-start(bf16[1,16,128,128]{3,2,1,0:T(8,128)(2,1)S(1)} %shard_map.67), channel_id=1, source_target_pairs={{0,8},{1,4},{2,10},{3,6},{4,1},{5,13},{6,3},{7,15},{8,0},{9,12},{1... | collective-permute-start | bytes 1572872 | tf_op jit(solution)/shard_map/ppermute | solution.py:329
  21.1 20.5 %collective-permute-start.4 = (bf16[1,16,128,128]{3,2,1,0:T(8,128)(2,1)S(1)}, bf16[1,16,128,128]{3,2,1,0:T(8,128)(2,1)S(1)}, u32[]{:S(2)}, u32[]{:S(2)}) collective-permute-start(bf16[1,16,128,128]{3,2,1,0:T(8,128)(2,1)S(1)} %get-tuple-element.82), channel_id=1, source_target_pairs={{0,8},{1,4},{2,10},{3,6},{4,1},{5,13},{6,3},{7,15},{8,0},{9,12},{1... | collective-permute-start | bytes 1572872 | tf_op jit(solution)/shard_map/ppermute | solution.py:329
  24.8 13.6 %collective-permute-start = (s32[137]{0:T(256)S(1)}, s32[137]{0:T(256)S(1)}, u32[]{:S(2)}, u32[]{:S(2)}) collective-permute-start(s32[137]{0:T(256)S(1)} %shard_map.64.own), channel_id=1, source_target_pairs={{0,8},{1,4},{2,10},{3,6},{4,1},{5,13},{6,3},{7,15},{8,0},{9,12},{1... | collective-permute-start | bytes 1652 | tf_op jit(solution)/shard_map/ppermute | solution.py:329
  25.1 17.1 %collective-permute-start.2 = (bf16[1,8,128,128]{3,2,1,0:T(8,128)(2,1)S(1)}, bf16[1,8,128,128]{3,2,1,0:T(8,128)(2,1)S(1)}, u32[]{:S(2)}, u32[]{:S(2)}) collective-permute-start(bf16[1,8,128,128]{3,2,1,0:T(8,128)(2,1)S(1)} %get-tuple-element.81), channel_id=1, source_target_pairs={{0,8},{1,4},{2,10},{3,6},{4,1},{5,13},{6,3},{7,15},{8,0},{9,12},{1... | collective-permute-start | bytes 786440 | tf_op jit(solution)/shard_map/ppermute | solution.py:329
  38.4 13.8 %collective-permute-start.14 = (bf16[1024,256]{1,0:T(8,128)(2,1)S(1)}, bf16[1024,256]{1,0:T(8,128)(2,1)S(1)}, u32[]{:S(2)}, u32[]{:S(2)}) collective-permute-start(bf16[1024,256]{1,0:T(8,128)(2,1)S(1)} %shard_map.73.own), channel_id=1, source_target_pairs={{0,8},{1,4},{2,10},{3,6},{4,1},{5,13},{6,3},{7,15},{8,0},{9,12},{1... | collective-permute-start | bytes 1572872 | tf_op jit(solution)/shard_map/ppermute | solution.py:329
  40.2 13.3 %collective-permute-start.10 = (bf16[1,16,128,128]{3,2,1,0:T(8,128)(2,1)S(1)}, bf16[1,16,128,128]{3,2,1,0:T(8,128)(2,1)S(1)}, u32[]{:S(2)}, u32[]{:S(2)}) collective-permute-start(bf16[1,16,128,128]{3,2,1,0:T(8,128)(2,1)S(1)} %collective-permute-done.9.refs_1_), channel_id=1, source_target_pairs={{1,3},{3,1},{4,6},{6,4},{9,11},{11,9},{12,14},{14,12},{17,19},{19,... | collective-permute-start | bytes 1572872 | tf_op jit(solution)/shard_map/ppermute | solution.py:329
  40.9 17.5 %collective-permute-start.8 = (bf16[1,16,128,128]{3,2,1,0:T(8,128)(2,1)S(1)}, bf16[1,16,128,128]{3,2,1,0:T(8,128)(2,1)S(1)}, u32[]{:S(2)}, u32[]{:S(2)}) collective-permute-start(bf16[1,16,128,128]{3,2,1,0:T(8,128)(2,1)S(1)} %collective-permute-done.7.refs_0_), channel_id=1, source_target_pairs={{1,3},{3,1},{4,6},{6,4},{9,11},{11,9},{12,14},{14,12},{17,19},{19,... | collective-permute-start | bytes 1572872 | tf_op jit(solution)/shard_map/ppermute | solution.py:329
  41.6 23.9 %collective-permute-start.5 = (bf16[1,16,128,128]{3,2,1,0:T(8,128)(2,1)S(1)}, bf16[1,16,128,128]{3,2,1,0:T(8,128)(2,1)S(1)}, u32[]{:S(2)}, u32[]{:S(2)}) collective-permute-start(bf16[1,16,128,128]{3,2,1,0:T(8,128)(2,1)S(1)} %collective-permute-done.4.refs_0_), channel_id=1, source_target_pairs={{1,3},{3,1},{4,6},{6,4},{9,11},{11,9},{12,14},{14,12},{17,19},{19,... | collective-permute-start | bytes 1572872 | tf_op jit(solution)/shard_map/ppermute | solution.py:329
  42.3 8.1 %collective-permute-start.6 = (bf16[1,8,128,128]{3,2,1,0:T(8,128)(2,1)S(1)}, bf16[1,8,128,128]{3,2,1,0:T(8,128)(2,1)S(1)}, u32[]{:S(2)}, u32[]{:S(2)}) collective-permute-start(bf16[1,8,128,128]{3,2,1,0:T(8,128)(2,1)S(1)} %get-tuple-element.83), channel_id=1, source_target_pairs={{0,8},{1,4},{2,10},{3,6},{4,1},{5,13},{6,3},{7,15},{8,0},{9,12},{1... | collective-permute-start | bytes 786440 | tf_op jit(solution)/shard_map/ppermute | solution.py:329
  50.4 15.7 %collective-permute-start.1 = (bf16[1,8,128,128]{3,2,1,0:T(8,128)(2,1)S(1)}, bf16[1,8,128,128]{3,2,1,0:T(8,128)(2,1)S(1)}, u32[]{:S(2)}, u32[]{:S(2)}) collective-permute-start(bf16[1,8,128,128]{3,2,1,0:T(8,128)(2,1)S(1)} %get-tuple-element.80), channel_id=1, source_target_pairs={{0,8},{1,4},{2,10},{3,6},{4,1},{5,13},{6,3},{7,15},{8,0},{9,12},{1... | collective-permute-start | bytes 786440 | tf_op jit(solution)/shard_map/ppermute | solution.py:329
  52.2 13.9 %collective-permute-start.3 = (bf16[1,8,128,128]{3,2,1,0:T(8,128)(2,1)S(1)}, bf16[1,8,128,128]{3,2,1,0:T(8,128)(2,1)S(1)}, u32[]{:S(2)}, u32[]{:S(2)}) collective-permute-start(bf16[1,8,128,128]{3,2,1,0:T(8,128)(2,1)S(1)} %collective-permute-done.2.refs_2_), channel_id=1, source_target_pairs={{1,3},{3,1},{4,6},{6,4},{9,11},{11,9},{12,14},{14,12},{17,19},{19,... | collective-permute-start | bytes 786440 | tf_op jit(solution)/shard_map/ppermute | solution.py:329
  53.5 13.4 %collective-permute-start.15 = (bf16[512,256]{1,0:T(8,128)(2,1)S(1)}, bf16[512,256]{1,0:T(8,128)(2,1)S(1)}, u32[]{:S(2)}, u32[]{:S(2)}) collective-permute-start(bf16[512,256]{1,0:T(8,128)(2,1)S(1)} %get-tuple-element.96), channel_id=1, source_target_pairs={{0,1},{1,0},{2,3},{3,2},{4,5},{5,4},{6,7},{7,6},{8,9},{9,8},{10,11... | collective-permute-start | bytes 786440 | tf_op jit(solution)/shard_map/ppermute | solution.py:329
  58.3 9.6 %collective-permute-start.16 = (bf16[512,256]{1,0:T(8,128)(2,1)S(1)}, bf16[512,256]{1,0:T(8,128)(2,1)S(1)}, u32[]{:S(2)}, u32[]{:S(2)}) collective-permute-start(bf16[512,256]{1,0:T(8,128)(2,1)S(1)} %get-tuple-element.99), channel_id=1, source_target_pairs={{0,4},{1,8},{2,6},{3,10},{4,0},{5,12},{6,2},{7,14},{8,1},{9,16},{1... | collective-permute-start | bytes 786440 | tf_op jit(solution)/shard_map/ppermute | solution.py:329
  68.7 6.4 %collective-permute-start.18 = (bf16[512,256]{1,0:T(8,128)(2,1)S(1)}, bf16[512,256]{1,0:T(8,128)(2,1)S(1)}, u32[]{:S(2)}, u32[]{:S(2)}) collective-permute-start(bf16[512,256]{1,0:T(8,128)(2,1)S(1)} %shard_map.79), channel_id=1, source_target_pairs={{0,4},{1,8},{2,6},{3,10},{4,0},{5,12},{6,2},{7,14},{8,1},{9,16},{1... | collective-permute-start | bytes 786440 | tf_op jit(solution)/shard_map/ppermute | solution.py:329
  75.9 6.4 %collective-permute-start.20 = (bf16[512,256]{1,0:T(8,128)(2,1)S(1)}, bf16[512,256]{1,0:T(8,128)(2,1)S(1)}, u32[]{:S(2)}, u32[]{:S(2)}) collective-permute-start(bf16[512,256]{1,0:T(8,128)(2,1)S(1)} %shard_map.83.refs_3_.sent), channel_id=1, source_target_pairs={{0,4},{1,8},{2,6},{3,10},{4,0},{5,12},{6,2},{7,14},{8,1},{9,16},{1... | collective-permute-start | bytes 786440 | tf_op jit(solution)/shard_map/ppermute | solution.py:329
  77.5 7.6 %collective-permute-start.23 = (bf16[256,512]{1,0:T(8,128)(2,1)S(1)}, bf16[256,512]{1,0:T(8,128)(2,1)S(1)}, u32[]{:S(2)}, u32[]{:S(2)}) collective-permute-start(bf16[256,512]{1,0:T(8,128)(2,1)S(1)} %get-tuple-element.105.low), channel_id=1, source_target_pairs={{0,4},{1,8},{2,6},{3,10},{4,0},{5,12},{6,2},{7,14},{8,1},{9,16},{1... | collective-permute-start | bytes 786440 | tf_op jit(solution)/shard_map/ppermute | solution.py:329
  78.0 10.0 %collective-permute-start.24 = (bf16[256,512]{1,0:T(8,128)(2,1)S(1)}, bf16[256,512]{1,0:T(8,128)(2,1)S(1)}, u32[]{:S(2)}, u32[]{:S(2)}) collective-permute-start(bf16[256,512]{1,0:T(8,128)(2,1)S(1)} %get-tuple-element.106.high), channel_id=1, source_target_pairs={{0,4},{1,8},{2,6},{3,10},{4,0},{5,12},{6,2},{7,14},{8,1},{9,16},{1... | collective-permute-start | bytes 786440 | tf_op jit(solution)/shard_map/ppermute | solution.py:329
  82.8 7.9 %collective-permute-start.22 = (bf16[512,256]{1,0:T(8,128)(2,1)S(1)}, bf16[512,256]{1,0:T(8,128)(2,1)S(1)}, u32[]{:S(2)}, u32[]{:S(2)}) collective-permute-start(bf16[512,256]{1,0:T(8,128)(2,1)S(1)} %get-tuple-element.116), channel_id=1, source_target_pairs={{0,4},{1,8},{2,6},{3,10},{4,0},{5,12},{6,2},{7,14},{8,1},{9,16},{1... | collective-permute-start | bytes 786440 | tf_op jit(solution)/shard_map/ppermute | solution.py:329
  132.5 6.4 %collective-permute-start.38 = (bf16[256,512]{1,0:T(8,128)(2,1)S(1)}, bf16[256,512]{1,0:T(8,128)(2,1)S(1)}, u32[]{:S(2)}, u32[]{:S(2)}) collective-permute-start(bf16[256,512]{1,0:T(8,128)(2,1)S(1)} %shard_map.113.own), channel_id=1, source_target_pairs={{0,8},{1,4},{2,10},{3,6},{4,1},{5,13},{6,3},{7,15},{8,0},{9,12},{1... | collective-permute-start | bytes 786440 | tf_op jit(solution)/shard_map/ppermute | solution.py:329
  133.3 8.5 %collective-permute-start.37 = (bf16[256,512]{1,0:T(8,128)(2,1)S(1)}, bf16[256,512]{1,0:T(8,128)(2,1)S(1)}, u32[]{:S(2)}, u32[]{:S(2)}) collective-permute-start(bf16[256,512]{1,0:T(8,128)(2,1)S(1)} %shard_map.112.own), channel_id=1, source_target_pairs={{0,8},{1,4},{2,10},{3,6},{4,1},{5,13},{6,3},{7,15},{8,0},{9,12},{1... | collective-permute-start | bytes 786440 | tf_op jit(solution)/shard_map/ppermute | solution.py:329
  (18 other events, 87.3 us)

commit v10 on v9

--- a/solution.py
+++ b/solution.py
@@ -75,7 +75,7 @@
 
 
 def build_kernel(lot, held, cap, nblk, width, info, blocks, *refs):
-    count = sum(pieces for _, _, pieces in lot)
+    count = 1 + max(which for _, _, sources in lot for which, _ in sources)
     moved, refs = list(refs[:count]), refs[count:]
     near_out, far_out, raw, total, sems = refs[-5:]
     role, keep, half, at_edge, _ = here()
@@ -126,10 +126,14 @@
 
     @pl.when(jnp.logical_not(keep))
     def _():
-        for step, direct, pieces in lot:
-            arrays = [moved.pop(0) for _ in range(pieces)]
-            each = nblk // pieces
-            build(lambda k: arrays[k // each][0, k % each], place(step, direct))
+        for step, direct, sources in lot:
+            each = nblk // len(sources)
+
+            def source(k):
+                which, first = sources[k // each]
+                return moved[which][0, first + k % each]
+
+            build(source, place(step, direct))
 
 
 def gather_kernel(counts, cols, lists, out):
@@ -169,15 +173,12 @@
     outs, sems = refs[:-1], refs[-1]
     half = here()[2]
     copies = []
-    for n, ((step, first, count), out) in enumerate(zip(cuts, outs)):
-        piece = count // 2
-        for p in range(2):
-            copies.append(
-                pltpu.make_async_copy(
-                    blocks.at[row_of(half, step, 1, cap), pl.ds(first + p * piece, piece)],
-                    out.at[0, pl.ds(p * piece, piece)], sems.at[n, p],
-                )
-            )
+    for n, (pieces, out) in enumerate(zip(cuts, outs)):
+        at = 0
+        for p, (step, first, count) in enumerate(pieces):
+            src = blocks.at[row_of(half, step, 1, cap), pl.ds(first, count)]
+            copies.append(pltpu.make_async_copy(src, out.at[0, pl.ds(at, count)], sems.at[n, p]))
+            at += count
     for copy in copies:
         copy.start()
     for copy in copies:
@@ -347,22 +348,24 @@
         bit //= 2
 
     held = pltpu.with_memory_space_constraint(blocks, pltpu.HBM)
-    middle, part_blocks = cap // 2, nblk // 2
+    middle, hb = cap // 2, nblk // 2
     block_rows = lambda count: sds((1, count, width, width), BF16)
 
     def stage(*cuts):
         return call(
-            functools.partial(stage_kernel, cuts, cap), tuple(block_rows(cut[2]) for cut in cuts),
-            [HBM], (VMEM,) * len(cuts), scratch=(pltpu.SemaphoreType.DMA((len(cuts), 2)),),
+            functools.partial(stage_kernel, cuts, cap),
+            tuple(block_rows(sum(count for _, _, count in pieces)) for pieces in cuts),
+            [HBM], (VMEM,) * len(cuts), scratch=(pltpu.SemaphoreType.DMA((len(cuts), 4)),),
         )(held)
 
-    staged = stage((0, 0, nblk))
+    full = lambda k: ((k, 0, hb), (k, hb, hb))
+    staged = stage(full(0))
     staged += stage(
-        *((k, 0, nblk) for k in range(1, middle - 1)),
-        (middle - 1, part_blocks, part_blocks), (middle - 1, 0, part_blocks), (middle, 0, part_blocks),
+        *(full(k) for k in range(1, middle - 2)),
+        full(middle - 2) + ((middle - 1, hb, hb),), ((middle - 1, 0, hb),), ((middle, 0, hb),),
     )
     direct = [send(x, "trade") for x in staged]
-    relayed = [send(x, "across") for x in direct[:middle]]
+    relayed = [send(x, "across") for x in direct[: middle - 1]]
 
     n_slots = 1 + cap * nblk
     own = call(gather_kernel, ints(n_slots + 2 * edge), [SMEM] * 3, SMEM)(counts, cols, lists)
@@ -379,22 +382,21 @@
 
     ops = ()
     op_shapes = (sds((height, height + edge * width), BF16), sds((height, edge * width), BF16))
-    low, high, extra = direct[middle], direct[middle - 1], direct[middle + 1]
-    cut = middle // 2
+    joint, low, extra = direct[middle - 2], direct[middle - 1], direct[middle]
     lots = [
-        [(k, 1, (direct[k],)) for k in range(cut)],
-        [(k, 1, (direct[k],)) for k in range(cut, middle - 1)],
-        [(k, 0, (relayed[k],)) for k in range(middle - 2)],
-        [(middle - 2, 0, (relayed[middle - 2],)), (middle - 1, 1, (low, high))],
-        [(middle, 1, (extra, relayed[middle - 1]))],
+        [(k, 1, ((k, 0),)) for k in range(middle - 2)],
+        [(middle - 2, 1, ((0, 0),))],
+        [(k, 0, ((k, 0),)) for k in range(middle - 2)],
+        [(middle - 1, 1, ((0, 0), (1, nblk)))],
+        [(middle - 2, 0, ((0, 0),)), (middle, 1, ((1, 0), (0, nblk)))],
     ]
+    arrays = [direct[: middle - 2], [joint], relayed[: middle - 2], [low, joint], [relayed[-1], extra]]
     whole = sum([[row[:2] for row in lot] for lot in lots], [])
     holds = [whole[: cap // 2], whole[cap // 2 :], [], [], []]
-    for lot, hold in zip(lots, holds):
-        given = [x for row in lot for x in row[2]]
+    for lot, given, hold in zip(lots, arrays, holds):
         n = len(given)
         ops = call(
-            functools.partial(build_kernel, [(*row[:2], len(row[2])) for row in lot], hold, cap, nblk, width),
+            functools.partial(build_kernel, lot, hold, cap, nblk, width),
             op_shapes, [SMEM, HBM] + [VMEM] * (n + len(ops)), (VMEM, VMEM),
             scratch=(
                 pltpu.VMEM((max(1, len(hold)), nblk, width, width), BF16),

time: 143 us -> 133 us (0.930)
  waiting for transfers between devices: 58.5 us -> 45.3 us
  starting transfers between devices: 41.6 us -> 44.5 us
    ppermute x36 -> x34, waiting for transfers between devices: 46.6 us -> 36.6 us  [send(): return lax.ppermute(x, AXES, ways[way])]
    ppermute x3, waiting for transfers between devices: 11.9 us -> 8.67 us  [body(): lax.ppermute(pieces[place], 'col', [(k, k ^ bit) for k in range(columns)])]
    ppermute x36 -> x34, starting transfers between devices: 38.5 us -> 41.4 us  [send(): return lax.ppermute(x, AXES, ways[way])]
  transfers between devices with their start and end apart: 39 -> 37, of which waited for: 16 -> 17; matrix products, arithmetic and copies ran while one was open for 0% -> 0% of each run, Pallas kernels for 25% -> 27%
where the time goes in v10:
time: 133 us; the launch traced here: 132 us
  waiting for transfers between devices  45.3 us (34%)
  starting transfers between devices  44.5 us (33%)
  Pallas kernels  39.9 us (30%)
  between operations  1.45 us (1%)
    ppermute x34, starting transfers between devices, send(): return lax.ppermute(x, AXES, ways[way])  41.4 us
    ppermute x34, waiting for transfers between devices, send(): return lax.ppermute(x, AXES, ways[way])  36.6 us
    pallas_call x10, Pallas kernels, body(): call(functools.partial(local_kernel, width, edge, not first, gives), outs...  10.5 us
    ppermute x3, waiting for transfers between devices, body(): lax.ppermute(pieces[place], 'col', [(k, k ^ bit) for k in range(columns)])  8.67 us
    pallas_call x5, Pallas kernels, body(): call(functools.partial(build_kernel, lot, hold, cap, nblk, width), op_sha...  8.01 us
    pallas_call x9, Pallas kernels, body(): call(functools.partial(finish_kernel, first, not plain, wants, width, edg...  5.93 us
    ppermute x3, starting transfers between devices, body(): lax.ppermute(pieces[place], 'col', [(k, k ^ bit) for k in range(columns)])  3.09 us
    pallas_call x9, Pallas kernels, body(): call(functools.partial(near_kernel, first), sent, [VMEM] * 3, VMEM)  2.67 us
  transfers between devices with their start and end apart: 37, of which 17 were waited for; matrix products, arithmetic and copies ran while one was open for 0% of the time, Pallas kernels for 27%

profile of v10, /device:TPU:0, one launch (start us, length us, event | category | flops | bytes accessed | tf_op | source)
XLA Modules:
  0.0 132.4 jit_solution(2937631707405026444)
XLA Ops:
  1.3 3.1 %collective-permute-start.9 = (bf16[256,1024]{1,0:T(8,128)(2,1)S(1)}, bf16[256,1024]{1,0:T(8,128)(2,1)S(1)}, u32[]{:S(2)}, u32[]{:S(2)}) collective-permute-start(bf16[256,1024]{1,0:T(8,128)(2,1)S(1)} %convert_element_type.3.refs_0_), channel_id=1, source_target_pairs={{0,2},{1,3},{2,0},{3,1},{4,6},{5,7},{6,4},{7,5},{8,10},{9,11},{10,... | collective-permute-start | bytes 1572872 | tf_op jit(solution)/shard_map/ppermute | solution.py:345
  7.6 8.7 %collective-permute-done.9.refs_1_ = bf16[256,1024]{1,0:T(8,128)(2,1)S(1)} collective-permute-done((bf16[256,1024]{1,0:T(8,128)(2,1)S(1)}, bf16[256,1024]{1,0:T(8,128)(2,1)S(1)}, u32[]{:S(2)}, u32[]{:S(2)}) %collective-permute-start.9) | collective-permute-done | bytes 524320 | tf_op jit(solution)/shard_map/ppermute | solution.py:345
  16.3 1.9 %collective-permute-start.7 = (bf16[1,16,128,128]{3,2,1,0:T(8,128)(2,1)S(1)}, bf16[1,16,128,128]{3,2,1,0:T(8,128)(2,1)S(1)}, u32[]{:S(2)}, u32[]{:S(2)}) collective-permute-start(bf16[1,16,128,128]{3,2,1,0:T(8,128)(2,1)S(1)} %get-tuple-element.82), channel_id=1, source_target_pairs={{0,8},{1,4},{2,10},{3,6},{4,1},{5,13},{6,3},{7,15},{8,0},{9,12},{1... | collective-permute-start | bytes 1572872 | tf_op jit(solution)/shard_map/ppermute | solution.py:330
  21.5 1.9 %collective-permute-start.12 = (bf16[1024,256]{1,0:T(8,128)(2,1)S(1)}, bf16[1024,256]{1,0:T(8,128)(2,1)S(1)}, u32[]{:S(2)}, u32[]{:S(2)}) collective-permute-start(bf16[1024,256]{1,0:T(8,128)(2,1)S(1)} %shard_map.73.own), channel_id=1, source_target_pairs={{0,8},{1,4},{2,10},{3,6},{4,1},{5,13},{6,3},{7,15},{8,0},{9,12},{1... | collective-permute-start | bytes 1572872 | tf_op jit(solution)/shard_map/ppermute | solution.py:330
  26.2 4.9 %collective-permute-done.5.refs_0_ = bf16[1,16,128,128]{3,2,1,0:T(8,128)(2,1)S(1)} collective-permute-done((bf16[1,16,128,128]{3,2,1,0:T(8,128)(2,1)S(1)}, bf16[1,16,128,128]{3,2,1,0:T(8,128)(2,1)S(1)}, u32[]{:S(2)}, u32[]{:S(2)}) %collective-permute-start.5) | collective-permute-done | bytes 524320 | tf_op jit(solution)/shard_map/ppermute | solution.py:330
  33.2 1.9 %collective-permute-start = (s32[137]{0:T(256)S(1)}, s32[137]{0:T(256)S(1)}, u32[]{:S(2)}, u32[]{:S(2)}) collective-permute-start(s32[137]{0:T(256)S(1)} %shard_map.64.own), channel_id=1, source_target_pairs={{0,8},{1,4},{2,10},{3,6},{4,1},{5,13},{6,3},{7,15},{8,0},{9,12},{1... | collective-permute-start | bytes 1652 | tf_op jit(solution)/shard_map/ppermute | solution.py:330
  40.9 2.0 %collective-permute-start.13 = (bf16[512,256]{1,0:T(8,128)(2,1)S(1)}, bf16[512,256]{1,0:T(8,128)(2,1)S(1)}, u32[]{:S(2)}, u32[]{:S(2)}) collective-permute-start(bf16[512,256]{1,0:T(8,128)(2,1)S(1)} %get-tuple-element.94), channel_id=1, source_target_pairs={{0,1},{1,0},{2,3},{3,2},{4,5},{5,4},{6,7},{7,6},{8,9},{9,8},{10,11... | collective-permute-start | bytes 786440 | tf_op jit(solution)/shard_map/ppermute | solution.py:330
  42.9 5.5 %collective-permute-start.14 = (bf16[512,256]{1,0:T(8,128)(2,1)S(1)}, bf16[512,256]{1,0:T(8,128)(2,1)S(1)}, u32[]{:S(2)}, u32[]{:S(2)}) collective-permute-start(bf16[512,256]{1,0:T(8,128)(2,1)S(1)} %get-tuple-element.97), channel_id=1, source_target_pairs={{0,4},{1,8},{2,6},{3,10},{4,0},{5,12},{6,2},{7,14},{8,1},{9,16},{1... | collective-permute-start | bytes 786440 | tf_op jit(solution)/shard_map/ppermute | solution.py:330
  48.4 3.0 %shard_map.68 = (bf16[1024,1536]{1,0:T(8,128)(2,1)S(1)}, bf16[1024,512]{1,0:T(8,128)(2,1)S(1)}) custom-call(s32[129]{0:T(256)S(1)} %get-tuple-element.78.info, bf16[8,16,128,128]{3,2,1,0:T(8,128)(2,1)} %blocks.13, bf16[1,16,128,128]{3,2,1,0:T(8,128)(2,1)S(1)} %collective-permute-done.5.refs_0_, bf16[1,16,128,128]{3,2,1,0:T(8,128)(2,1)S(1)} %collective-permute-done.7.refs_1_), custom_call_target="tpu_custom_call" | custom-call | tf_op jit(solution)/shard_map/pallas_call | solution.py:398
  51.5 3.0 %shard_map.69 = (bf16[1024,1536]{1,0:T(8,128)(2,1)S(1)}, bf16[1024,512]{1,0:T(8,128)(2,1)S(1)}) custom-call(s32[129]{0:T(256)S(1)} %get-tuple-element.78.info, bf16[8,16,128,128]{3,2,1,0:T(8,128)(2,1)} %blocks.13, bf16[1,24,128,128]{3,2,1,0:T(8,128)(2,1)S(1)} %collective-permute-done.1.refs_0_.refs_1_, ...), custom_call_target="tpu_custom_call", output_to_operand_aliasing={{0}: (3, {}), {1}: (4, {})} | custom-call | tf_op jit(solution)/shard_map/pallas_call | solution.py:398
  58.3 2.0 %collective-permute-start.16 = (bf16[512,256]{1,0:T(8,128)(2,1)S(1)}, bf16[512,256]{1,0:T(8,128)(2,1)S(1)}, u32[]{:S(2)}, u32[]{:S(2)}) collective-permute-start(bf16[512,256]{1,0:T(8,128)(2,1)S(1)} %shard_map.79), channel_id=1, source_target_pairs={{0,4},{1,8},{2,6},{3,10},{4,0},{5,12},{6,2},{7,14},{8,1},{9,16},{1... | collective-permute-start | bytes 786440 | tf_op jit(solution)/shard_map/ppermute | solution.py:330
  61.8 3.0 %collective-permute-done.16.refs_0_.far = bf16[512,256]{1,0:T(8,128)(2,1)S(1)} collective-permute-done((bf16[512,256]{1,0:T(8,128)(2,1)S(1)}, bf16[512,256]{1,0:T(8,128)(2,1)S(1)}, u32[]{:S(2)}, u32[]{:S(2)}) %collective-permute-start.16) | collective-permute-done | bytes 262176 | tf_op jit(solution)/shard_map/ppermute | solution.py:330
  65.5 1.9 %collective-permute-start.18 = (bf16[512,256]{1,0:T(8,128)(2,1)S(1)}, bf16[512,256]{1,0:T(8,128)(2,1)S(1)}, u32[]{:S(2)}, u32[]{:S(2)}) collective-permute-start(bf16[512,256]{1,0:T(8,128)(2,1)S(1)} %shard_map.83.refs_3_.sent), channel_id=1, source_target_pairs={{0,4},{1,8},{2,6},{3,10},{4,0},{5,12},{6,2},{7,14},{8,1},{9,16},{1... | collective-permute-start | bytes 786440 | tf_op jit(solution)/shard_map/ppermute | solution.py:330
  72.5 1.9 %collective-permute-start.20 = (bf16[512,256]{1,0:T(8,128)(2,1)S(1)}, bf16[512,256]{1,0:T(8,128)(2,1)S(1)}, u32[]{:S(2)}, u32[]{:S(2)}) collective-permute-start(bf16[512,256]{1,0:T(8,128)(2,1)S(1)} %get-tuple-element.114), channel_id=1, source_target_pairs={{0,4},{1,8},{2,6},{3,10},{4,0},{5,12},{6,2},{7,14},{8,1},{9,16},{1... | collective-permute-start | bytes 786440 | tf_op jit(solution)/shard_map/ppermute | solution.py:330
  74.8 2.8 %collective-permute-done.22.refs_2_.high = bf16[256,512]{1,0:T(8,128)(2,1)S(1)} collective-permute-done((bf16[256,512]{1,0:T(8,128)(2,1)S(1)}, bf16[256,512]{1,0:T(8,128)(2,1)S(1)}, u32[]{:S(2)}, u32[]{:S(2)}) %collective-permute-start.22) | collective-permute-done | bytes 262176 | tf_op jit(solution)/shard_map/ppermute | solution.py:330
  84.8 2.5 %collective-permute-done.24.refs_0_.far = bf16[512,256]{1,0:T(8,128)(2,1)S(1)} collective-permute-done((bf16[512,256]{1,0:T(8,128)(2,1)S(1)}, bf16[512,256]{1,0:T(8,128)(2,1)S(1)}, u32[]{:S(2)}, u32[]{:S(2)}) %collective-permute-start.24) | collective-permute-done | bytes 262176 | tf_op jit(solution)/shard_map/ppermute | solution.py:330
  91.6 2.5 %collective-permute-done.26.refs_0_.far = bf16[512,256]{1,0:T(8,128)(2,1)S(1)} collective-permute-done((bf16[512,256]{1,0:T(8,128)(2,1)S(1)}, bf16[512,256]{1,0:T(8,128)(2,1)S(1)}, u32[]{:S(2)}, u32[]{:S(2)}) %collective-permute-start.26) | collective-permute-done | bytes 262176 | tf_op jit(solution)/shard_map/ppermute | solution.py:330
  98.5 2.5 %collective-permute-done.28.refs_0_.far = bf16[512,256]{1,0:T(8,128)(2,1)S(1)} collective-permute-done((bf16[512,256]{1,0:T(8,128)(2,1)S(1)}, bf16[512,256]{1,0:T(8,128)(2,1)S(1)}, u32[]{:S(2)}, u32[]{:S(2)}) %collective-permute-start.28) | collective-permute-done | bytes 262176 | tf_op jit(solution)/shard_map/ppermute | solution.py:330
  105.6 2.2 %collective-permute-done.30.refs_0_.far = bf16[512,256]{1,0:T(8,128)(2,1)S(1)} collective-permute-done((bf16[512,256]{1,0:T(8,128)(2,1)S(1)}, bf16[512,256]{1,0:T(8,128)(2,1)S(1)}, u32[]{:S(2)}, u32[]{:S(2)}) %collective-permute-start.30) | collective-permute-done | bytes 262176 | tf_op jit(solution)/shard_map/ppermute | solution.py:330
  112.2 2.5 %collective-permute-done.32.refs_0_.far = bf16[512,256]{1,0:T(8,128)(2,1)S(1)} collective-permute-done((bf16[512,256]{1,0:T(8,128)(2,1)S(1)}, bf16[512,256]{1,0:T(8,128)(2,1)S(1)}, u32[]{:S(2)}, u32[]{:S(2)}) %collective-permute-start.32) | collective-permute-done | bytes 262176 | tf_op jit(solution)/shard_map/ppermute | solution.py:330
  118.7 2.9 %collective-permute-done.34.part = bf16[512,256]{1,0:T(8,128)(2,1)S(1)} collective-permute-done((bf16[512,256]{1,0:T(8,128)(2,1)S(1)}, bf16[512,256]{1,0:T(8,128)(2,1)S(1)}, u32[]{:S(2)}, u32[]{:S(2)}) %collective-permute-start.34) | collective-permute-done | bytes 262176 | tf_op jit(solution)/shard_map/ppermute | solution.py:330
  122.9 2.1 %collective-permute-start.35 = (bf16[256,512]{1,0:T(8,128)(2,1)S(1)}, bf16[256,512]{1,0:T(8,128)(2,1)S(1)}, u32[]{:S(2)}, u32[]{:S(2)}) collective-permute-start(bf16[256,512]{1,0:T(8,128)(2,1)S(1)} %shard_map.112.own), channel_id=1, source_target_pairs={{0,8},{1,4},{2,10},{3,6},{4,1},{5,13},{6,3},{7,15},{8,0},{9,12},{1... | collective-permute-start | bytes 786440 | tf_op jit(solution)/shard_map/ppermute | solution.py:330
  125.0 3.6 %collective-permute-done.36.moved = bf16[256,512]{1,0:T(8,128)(2,1)S(1)} collective-permute-done((bf16[256,512]{1,0:T(8,128)(2,1)S(1)}, bf16[256,512]{1,0:T(8,128)(2,1)S(1)}, u32[]{:S(2)}, u32[]{:S(2)}) %collective-permute-start.36) | collective-permute-done | bytes 262176 | tf_op jit(solution)/shard_map/ppermute | solution.py:330
  129.5 2.0 %collective-permute-done.35.moved = bf16[256,512]{1,0:T(8,128)(2,1)S(1)} collective-permute-done((bf16[256,512]{1,0:T(8,128)(2,1)S(1)}, bf16[256,512]{1,0:T(8,128)(2,1)S(1)}, u32[]{:S(2)}, u32[]{:S(2)}) %collective-permute-start.35) | collective-permute-done | bytes 262176 | tf_op jit(solution)/shard_map/ppermute | solution.py:330
  (109 shorter events, 61.1 us)
Async XLA Ops:
  1.3 15.0 %collective-permute-start.9 = (bf16[256,1024]{1,0:T(8,128)(2,1)S(1)}, bf16[256,1024]{1,0:T(8,128)(2,1)S(1)}, u32[]{:S(2)}, u32[]{:S(2)}) collective-permute-start(bf16[256,1024]{1,0:T(8,128)(2,1)S(1)} %convert_element_type.3.refs_0_), channel_id=1, source_target_pairs={{0,2},{1,3},{2,0},{3,1},{4,6},{5,7},{6,4},{7,5},{8,10},{9,11},{10,... | collective-permute-start | bytes 1572872 | tf_op jit(solution)/shard_map/ppermute | solution.py:345
  5.9 17.4 %collective-permute-start.1 = (bf16[1,24,128,128]{3,2,1,0:T(8,128)(2,1)S(1)}, bf16[1,24,128,128]{3,2,1,0:T(8,128)(2,1)S(1)}, u32[]{:S(2)}, u32[]{:S(2)}) collective-permute-start(bf16[1,24,128,128]{3,2,1,0:T(8,128)(2,1)S(1)} %get-tuple-element.79), channel_id=1, source_target_pairs={{0,8},{1,4},{2,10},{3,6},{4,1},{5,13},{6,3},{7,15},{8,0},{9,12},{1... | collective-permute-start | bytes 2359304 | tf_op jit(solution)/shard_map/ppermute | solution.py:330
  7.6 12.6 %collective-permute-start.10 = (bf16[256,1024]{1,0:T(8,128)(2,1)S(1)}, bf16[256,1024]{1,0:T(8,128)(2,1)S(1)}, u32[]{:S(2)}, u32[]{:S(2)}) collective-permute-start(bf16[256,1024]{1,0:T(8,128)(2,1)S(1)} %convert_element_type.3.refs_0_), channel_id=1, source_target_pairs={{0,1},{1,0},{2,3},{3,2},{4,5},{5,4},{6,7},{7,6},{8,9},{9,8},{10,11... | collective-permute-start | bytes 1572872 | tf_op jit(solution)/shard_map/ppermute | solution.py:345
  16.3 9.2 %collective-permute-start.7 = (bf16[1,16,128,128]{3,2,1,0:T(8,128)(2,1)S(1)}, bf16[1,16,128,128]{3,2,1,0:T(8,128)(2,1)S(1)}, u32[]{:S(2)}, u32[]{:S(2)}) collective-permute-start(bf16[1,16,128,128]{3,2,1,0:T(8,128)(2,1)S(1)} %get-tuple-element.82), channel_id=1, source_target_pairs={{0,8},{1,4},{2,10},{3,6},{4,1},{5,13},{6,3},{7,15},{8,0},{9,12},{1... | collective-permute-start | bytes 1572872 | tf_op jit(solution)/shard_map/ppermute | solution.py:330
  19.2 11.9 %collective-permute-start.5 = (bf16[1,16,128,128]{3,2,1,0:T(8,128)(2,1)S(1)}, bf16[1,16,128,128]{3,2,1,0:T(8,128)(2,1)S(1)}, u32[]{:S(2)}, u32[]{:S(2)}) collective-permute-start(bf16[1,16,128,128]{3,2,1,0:T(8,128)(2,1)S(1)} %shard_map.67), channel_id=1, source_target_pairs={{0,8},{1,4},{2,10},{3,6},{4,1},{5,13},{6,3},{7,15},{8,0},{9,12},{1... | collective-permute-start | bytes 1572872 | tf_op jit(solution)/shard_map/ppermute | solution.py:330
  21.5 18.5 %collective-permute-start.12 = (bf16[1024,256]{1,0:T(8,128)(2,1)S(1)}, bf16[1024,256]{1,0:T(8,128)(2,1)S(1)}, u32[]{:S(2)}, u32[]{:S(2)}) collective-permute-start(bf16[1024,256]{1,0:T(8,128)(2,1)S(1)} %shard_map.73.own), channel_id=1, source_target_pairs={{0,8},{1,4},{2,10},{3,6},{4,1},{5,13},{6,3},{7,15},{8,0},{9,12},{1... | collective-permute-start | bytes 1572872 | tf_op jit(solution)/shard_map/ppermute | solution.py:330
  23.3 32.4 %collective-permute-start.2 = (bf16[1,24,128,128]{3,2,1,0:T(8,128)(2,1)S(1)}, bf16[1,24,128,128]{3,2,1,0:T(8,128)(2,1)S(1)}, u32[]{:S(2)}, u32[]{:S(2)}) collective-permute-start(bf16[1,24,128,128]{3,2,1,0:T(8,128)(2,1)S(1)} %collective-permute-done.1.refs_0_.refs_1_), channel_id=1, source_target_pairs={{1,3},{3,1},{4,6},{6,4},{9,11},{11,9},{12,14},{14,12},{17,19},{19,... | collective-permute-start | bytes 2359304 | tf_op jit(solution)/shard_map/ppermute | solution.py:330
  25.5 15.4 %collective-permute-start.8 = (bf16[1,16,128,128]{3,2,1,0:T(8,128)(2,1)S(1)}, bf16[1,16,128,128]{3,2,1,0:T(8,128)(2,1)S(1)}, u32[]{:S(2)}, u32[]{:S(2)}) collective-permute-start(bf16[1,16,128,128]{3,2,1,0:T(8,128)(2,1)S(1)} %collective-permute-done.7.refs_1_), channel_id=1, source_target_pairs={{1,3},{3,1},{4,6},{6,4},{9,11},{11,9},{12,14},{14,12},{17,19},{19,... | collective-permute-start | bytes 1572872 | tf_op jit(solution)/shard_map/ppermute | solution.py:330
  31.2 11.8 %collective-permute-start.6 = (bf16[1,16,128,128]{3,2,1,0:T(8,128)(2,1)S(1)}, bf16[1,16,128,128]{3,2,1,0:T(8,128)(2,1)S(1)}, u32[]{:S(2)}, u32[]{:S(2)}) collective-permute-start(bf16[1,16,128,128]{3,2,1,0:T(8,128)(2,1)S(1)} %collective-permute-done.5.refs_0_), channel_id=1, source_target_pairs={{1,3},{3,1},{4,6},{6,4},{9,11},{11,9},{12,14},{14,12},{17,19},{19,... | collective-permute-start | bytes 1572872 | tf_op jit(solution)/shard_map/ppermute | solution.py:330
  36.8 18.3 %collective-permute-start.4 = (bf16[1,8,128,128]{3,2,1,0:T(8,128)(2,1)S(1)}, bf16[1,8,128,128]{3,2,1,0:T(8,128)(2,1)S(1)}, u32[]{:S(2)}, u32[]{:S(2)}) collective-permute-start(bf16[1,8,128,128]{3,2,1,0:T(8,128)(2,1)S(1)} %get-tuple-element.81), channel_id=1, source_target_pairs={{0,8},{1,4},{2,10},{3,6},{4,1},{5,13},{6,3},{7,15},{8,0},{9,12},{1... | collective-permute-start | bytes 786440 | tf_op jit(solution)/shard_map/ppermute | solution.py:330
  40.0 15.7 %collective-permute-start.3 = (bf16[1,8,128,128]{3,2,1,0:T(8,128)(2,1)S(1)}, bf16[1,8,128,128]{3,2,1,0:T(8,128)(2,1)S(1)}, u32[]{:S(2)}, u32[]{:S(2)}) collective-permute-start(bf16[1,8,128,128]{3,2,1,0:T(8,128)(2,1)S(1)} %get-tuple-element.80), channel_id=1, source_target_pairs={{0,8},{1,4},{2,10},{3,6},{4,1},{5,13},{6,3},{7,15},{8,0},{9,12},{1... | collective-permute-start | bytes 786440 | tf_op jit(solution)/shard_map/ppermute | solution.py:330
  40.9 15.6 %collective-permute-start.13 = (bf16[512,256]{1,0:T(8,128)(2,1)S(1)}, bf16[512,256]{1,0:T(8,128)(2,1)S(1)}, u32[]{:S(2)}, u32[]{:S(2)}) collective-permute-start(bf16[512,256]{1,0:T(8,128)(2,1)S(1)} %get-tuple-element.94), channel_id=1, source_target_pairs={{0,1},{1,0},{2,3},{3,2},{4,5},{5,4},{6,7},{7,6},{8,9},{9,8},{10,11... | collective-permute-start | bytes 786440 | tf_op jit(solution)/shard_map/ppermute | solution.py:330
  42.9 14.7 %collective-permute-start.14 = (bf16[512,256]{1,0:T(8,128)(2,1)S(1)}, bf16[512,256]{1,0:T(8,128)(2,1)S(1)}, u32[]{:S(2)}, u32[]{:S(2)}) collective-permute-start(bf16[512,256]{1,0:T(8,128)(2,1)S(1)} %get-tuple-element.97), channel_id=1, source_target_pairs={{0,4},{1,8},{2,6},{3,10},{4,0},{5,12},{6,2},{7,14},{8,1},{9,16},{1... | collective-permute-start | bytes 786440 | tf_op jit(solution)/shard_map/ppermute | solution.py:330
  58.3 6.4 %collective-permute-start.16 = (bf16[512,256]{1,0:T(8,128)(2,1)S(1)}, bf16[512,256]{1,0:T(8,128)(2,1)S(1)}, u32[]{:S(2)}, u32[]{:S(2)}) collective-permute-start(bf16[512,256]{1,0:T(8,128)(2,1)S(1)} %shard_map.79), channel_id=1, source_target_pairs={{0,4},{1,8},{2,6},{3,10},{4,0},{5,12},{6,2},{7,14},{8,1},{9,16},{1... | collective-permute-start | bytes 786440 | tf_op jit(solution)/shard_map/ppermute | solution.py:330
  65.5 6.4 %collective-permute-start.18 = (bf16[512,256]{1,0:T(8,128)(2,1)S(1)}, bf16[512,256]{1,0:T(8,128)(2,1)S(1)}, u32[]{:S(2)}, u32[]{:S(2)}) collective-permute-start(bf16[512,256]{1,0:T(8,128)(2,1)S(1)} %shard_map.83.refs_3_.sent), channel_id=1, source_target_pairs={{0,4},{1,8},{2,6},{3,10},{4,0},{5,12},{6,2},{7,14},{8,1},{9,16},{1... | collective-permute-start | bytes 786440 | tf_op jit(solution)/shard_map/ppermute | solution.py:330
  67.4 7.4 %collective-permute-start.21 = (bf16[256,512]{1,0:T(8,128)(2,1)S(1)}, bf16[256,512]{1,0:T(8,128)(2,1)S(1)}, u32[]{:S(2)}, u32[]{:S(2)}) collective-permute-start(bf16[256,512]{1,0:T(8,128)(2,1)S(1)} %get-tuple-element.103.low), channel_id=1, source_target_pairs={{0,4},{1,8},{2,6},{3,10},{4,0},{5,12},{6,2},{7,14},{8,1},{9,16},{1... | collective-permute-start | bytes 786440 | tf_op jit(solution)/shard_map/ppermute | solution.py:330
  67.6 10.0 %collective-permute-start.22 = (bf16[256,512]{1,0:T(8,128)(2,1)S(1)}, bf16[256,512]{1,0:T(8,128)(2,1)S(1)}, u32[]{:S(2)}, u32[]{:S(2)}) collective-permute-start(bf16[256,512]{1,0:T(8,128)(2,1)S(1)} %get-tuple-element.104.high), channel_id=1, source_target_pairs={{0,4},{1,8},{2,6},{3,10},{4,0},{5,12},{6,2},{7,14},{8,1},{9,16},{1... | collective-permute-start | bytes 786440 | tf_op jit(solution)/shard_map/ppermute | solution.py:330
  72.5 7.9 %collective-permute-start.20 = (bf16[512,256]{1,0:T(8,128)(2,1)S(1)}, bf16[512,256]{1,0:T(8,128)(2,1)S(1)}, u32[]{:S(2)}, u32[]{:S(2)}) collective-permute-start(bf16[512,256]{1,0:T(8,128)(2,1)S(1)} %get-tuple-element.114), channel_id=1, source_target_pairs={{0,4},{1,8},{2,6},{3,10},{4,0},{5,12},{6,2},{7,14},{8,1},{9,16},{1... | collective-permute-start | bytes 786440 | tf_op jit(solution)/shard_map/ppermute | solution.py:330
  80.9 6.4 %collective-permute-start.24 = (bf16[512,256]{1,0:T(8,128)(2,1)S(1)}, bf16[512,256]{1,0:T(8,128)(2,1)S(1)}, u32[]{:S(2)}, u32[]{:S(2)}) collective-permute-start(bf16[512,256]{1,0:T(8,128)(2,1)S(1)} %get-tuple-element.119), channel_id=1, source_target_pairs={{0,4},{1,8},{2,6},{3,10},{4,0},{5,12},{6,2},{7,14},{8,1},{9,16},{1... | collective-permute-start | bytes 786440 | tf_op jit(solution)/shard_map/ppermute | solution.py:330
  94.6 6.4 %collective-permute-start.28 = (bf16[512,256]{1,0:T(8,128)(2,1)S(1)}, bf16[512,256]{1,0:T(8,128)(2,1)S(1)}, u32[]{:S(2)}, u32[]{:S(2)}) collective-permute-start(bf16[512,256]{1,0:T(8,128)(2,1)S(1)} %get-tuple-element.131), channel_id=1, source_target_pairs={{0,4},{1,8},{2,6},{3,10},{4,0},{5,12},{6,2},{7,14},{8,1},{9,16},{1... | collective-permute-start | bytes 786440 | tf_op jit(solution)/shard_map/ppermute | solution.py:330
  108.3 6.4 %collective-permute-start.32 = (bf16[512,256]{1,0:T(8,128)(2,1)S(1)}, bf16[512,256]{1,0:T(8,128)(2,1)S(1)}, u32[]{:S(2)}, u32[]{:S(2)}) collective-permute-start(bf16[512,256]{1,0:T(8,128)(2,1)S(1)} %get-tuple-element.143), channel_id=1, source_target_pairs={{0,4},{1,8},{2,6},{3,10},{4,0},{5,12},{6,2},{7,14},{8,1},{9,16},{1... | collective-permute-start | bytes 786440 | tf_op jit(solution)/shard_map/ppermute | solution.py:330
  115.2 6.4 %collective-permute-start.34 = (bf16[512,256]{1,0:T(8,128)(2,1)S(1)}, bf16[512,256]{1,0:T(8,128)(2,1)S(1)}, u32[]{:S(2)}, u32[]{:S(2)}) collective-permute-start(bf16[512,256]{1,0:T(8,128)(2,1)S(1)} %get-tuple-element.147), channel_id=1, source_target_pairs={{0,4},{1,8},{2,6},{3,10},{4,0},{5,12},{6,2},{7,14},{8,1},{9,16},{1... | collective-permute-start | bytes 786440 | tf_op jit(solution)/shard_map/ppermute | solution.py:330
  122.2 6.4 %collective-permute-start.36 = (bf16[256,512]{1,0:T(8,128)(2,1)S(1)}, bf16[256,512]{1,0:T(8,128)(2,1)S(1)}, u32[]{:S(2)}, u32[]{:S(2)}) collective-permute-start(bf16[256,512]{1,0:T(8,128)(2,1)S(1)} %shard_map.113.own), channel_id=1, source_target_pairs={{0,8},{1,4},{2,10},{3,6},{4,1},{5,13},{6,3},{7,15},{8,0},{9,12},{1... | collective-permute-start | bytes 786440 | tf_op jit(solution)/shard_map/ppermute | solution.py:330
  122.9 8.5 %collective-permute-start.35 = (bf16[256,512]{1,0:T(8,128)(2,1)S(1)}, bf16[256,512]{1,0:T(8,128)(2,1)S(1)}, u32[]{:S(2)}, u32[]{:S(2)}) collective-permute-start(bf16[256,512]{1,0:T(8,128)(2,1)S(1)} %shard_map.112.own), channel_id=1, source_target_pairs={{0,8},{1,4},{2,10},{3,6},{4,1},{5,13},{6,3},{7,15},{8,0},{9,12},{1... | collective-permute-start | bytes 786440 | tf_op jit(solution)/shard_map/ppermute | solution.py:330
  (16 other events, 96.0 us)

commit v11 on v9

--- a/solution.py
+++ b/solution.py
@@ -305,20 +305,23 @@
 
 
 def merge_kernel(begin, own, moved, *refs):
-    out, wide, sem = refs[-3:]
+    out, wide, sems = refs[-3:]
     keep = here()[1]
-
-    @pl.when(keep)
-    def _():
-        wide[...] = own[...].astype(F32)
-
-    @pl.when(jnp.logical_not(keep))
-    def _():
-        wide[...] = moved[...].astype(F32)
-
-    copy = pltpu.make_async_copy(wide, out.at[:, pl.ds(begin, wide.shape[1])], sem)
-    copy.start()
-    copy.wait()
+    pieces = 4
+    piece = wide.shape[0] // pieces
+    copies = []
+    for n in range(pieces):
+        rows = pl.ds(n * piece, piece)
+        value = jnp.where(keep, own[rows, :], moved[rows, :])
+        wide[rows, :] = value.astype(F32)
+        copies.append(
+            pltpu.make_async_copy(
+                wide.at[rows, :], out.at[rows, pl.ds(begin, wide.shape[1])], sems.at[n]
+            )
+        )
+        copies[-1].start()
+    for copy in copies:
+        copy.wait()
 
 
 def body(vectors, rotation, blocks, cols, lists, counts):
@@ -455,7 +458,7 @@
                     call(
                         functools.partial(merge_kernel, at * cut), sds((panel, height), F32),
                         [VMEM] * 2 + [HBM] * len(out), HBM,
-                        scratch=(pltpu.VMEM((panel, cut), F32), pltpu.SemaphoreType.DMA),
+                        scratch=(pltpu.VMEM((panel, cut), F32), pltpu.SemaphoreType.DMA((4,))),
                         aliases={2: 0} if out else {},
                     )(own, back, *out),
                 )

time: 143 us -> 143 us (level)
  no operation moved by 1% of the time
where the time goes in v11:
time: 143 us
  waiting for transfers between devices  58.5 us (41%)
  starting transfers between devices  41.6 us (29%)
  Pallas kernels  39.9 us (28%)
  between operations  1.48 us (1%)
    ppermute x36, waiting for transfers between devices, send(): return lax.ppermute(x, AXES, ways[way])  46.6 us
    ppermute x36, starting transfers between devices, send(): return lax.ppermute(x, AXES, ways[way])  38.5 us
    ppermute x3, waiting for transfers between devices, body(): lax.ppermute(pieces[place], 'col', [(k, k ^ bit) for k in range(columns)])  11.9 us
    pallas_call x10, Pallas kernels, body(): call(functools.partial(local_kernel, width, edge, not first, gives), outs...  10.5 us
    pallas_call x5, Pallas kernels, body(): call(functools.partial(build_kernel, [(*row[:2], len(row[2])) for row in...  8.01 us
    pallas_call x9, Pallas kernels, body(): call(functools.partial(finish_kernel, first, not plain, wants, width, edg...  5.93 us
    ppermute x3, starting transfers between devices, body(): lax.ppermute(pieces[place], 'col', [(k, k ^ bit) for k in range(columns)])  3.07 us
  transfers between devices with their start and end apart: 39, of which 16 were waited for; matrix products, arithmetic and copies ran while one was open for 0% of the time, Pallas kernels for 25%

profile of v11, /device:TPU:0, one launch (start us, length us, event | category | flops | bytes accessed | tf_op | source)
XLA Modules:
  0.0 142.8 jit_solution(4066427960259631964)
XLA Ops:
  1.3 3.1 %collective-permute-start.11 = (bf16[256,1024]{1,0:T(8,128)(2,1)S(1)}, bf16[256,1024]{1,0:T(8,128)(2,1)S(1)}, u32[]{:S(2)}, u32[]{:S(2)}) collective-permute-start(bf16[256,1024]{1,0:T(8,128)(2,1)S(1)} %convert_element_type.3.refs_0_), channel_id=1, source_target_pairs={{0,2},{1,3},{2,0},{3,1},{4,6},{5,7},{6,4},{7,5},{8,10},{9,11},{10,... | collective-permute-start | bytes 1572872 | tf_op jit(solution)/shard_map/ppermute | solution.py:347
  4.4 11.9 %collective-permute-done.11.refs_1_ = bf16[256,1024]{1,0:T(8,128)(2,1)S(1)} collective-permute-done((bf16[256,1024]{1,0:T(8,128)(2,1)S(1)}, bf16[256,1024]{1,0:T(8,128)(2,1)S(1)}, u32[]{:S(2)}, u32[]{:S(2)}) %collective-permute-start.11) | collective-permute-done | bytes 524320 | tf_op jit(solution)/shard_map/ppermute | solution.py:347
  17.8 1.9 %collective-permute-start.9 = (bf16[1,16,128,128]{3,2,1,0:T(8,128)(2,1)S(1)}, bf16[1,16,128,128]{3,2,1,0:T(8,128)(2,1)S(1)}, u32[]{:S(2)}, u32[]{:S(2)}) collective-permute-start(bf16[1,16,128,128]{3,2,1,0:T(8,128)(2,1)S(1)} %get-tuple-element.84), channel_id=1, source_target_pairs={{0,8},{1,4},{2,10},{3,6},{4,1},{5,13},{6,3},{7,15},{8,0},{9,12},{1... | collective-permute-start | bytes 1572872 | tf_op jit(solution)/shard_map/ppermute | solution.py:332
  21.1 1.8 %collective-permute-start.4 = (bf16[1,16,128,128]{3,2,1,0:T(8,128)(2,1)S(1)}, bf16[1,16,128,128]{3,2,1,0:T(8,128)(2,1)S(1)}, u32[]{:S(2)}, u32[]{:S(2)}) collective-permute-start(bf16[1,16,128,128]{3,2,1,0:T(8,128)(2,1)S(1)} %get-tuple-element.82), channel_id=1, source_target_pairs={{0,8},{1,4},{2,10},{3,6},{4,1},{5,13},{6,3},{7,15},{8,0},{9,12},{1... | collective-permute-start | bytes 1572872 | tf_op jit(solution)/shard_map/ppermute | solution.py:332
  25.1 1.8 %collective-permute-start.2 = (bf16[1,8,128,128]{3,2,1,0:T(8,128)(2,1)S(1)}, bf16[1,8,128,128]{3,2,1,0:T(8,128)(2,1)S(1)}, u32[]{:S(2)}, u32[]{:S(2)}) collective-permute-start(bf16[1,8,128,128]{3,2,1,0:T(8,128)(2,1)S(1)} %get-tuple-element.81), channel_id=1, source_target_pairs={{0,8},{1,4},{2,10},{3,6},{4,1},{5,13},{6,3},{7,15},{8,0},{9,12},{1... | collective-permute-start | bytes 786440 | tf_op jit(solution)/shard_map/ppermute | solution.py:332
  28.2 10.2 %collective-permute-done.moved = s32[137]{0:T(256)S(1)} collective-permute-done((s32[137]{0:T(256)S(1)}, s32[137]{0:T(256)S(1)}, u32[]{:S(2)}, u32[]{:S(2)}) %collective-permute-start) | collective-permute-done | bytes 580 | tf_op jit(solution)/shard_map/ppermute | solution.py:332
  38.4 1.8 %collective-permute-start.14 = (bf16[1024,256]{1,0:T(8,128)(2,1)S(1)}, bf16[1024,256]{1,0:T(8,128)(2,1)S(1)}, u32[]{:S(2)}, u32[]{:S(2)}) collective-permute-start(bf16[1024,256]{1,0:T(8,128)(2,1)S(1)} %shard_map.73.own), channel_id=1, source_target_pairs={{0,8},{1,4},{2,10},{3,6},{4,1},{5,13},{6,3},{7,15},{8,0},{9,12},{1... | collective-permute-start | bytes 1572872 | tf_op jit(solution)/shard_map/ppermute | solution.py:332
  44.3 6.1 %collective-permute-done.6.refs_1_ = bf16[1,8,128,128]{3,2,1,0:T(8,128)(2,1)S(1)} collective-permute-done((bf16[1,8,128,128]{3,2,1,0:T(8,128)(2,1)S(1)}, bf16[1,8,128,128]{3,2,1,0:T(8,128)(2,1)S(1)}, u32[]{:S(2)}, u32[]{:S(2)}) %collective-permute-start.6) | collective-permute-done | bytes 262176 | tf_op jit(solution)/shard_map/ppermute | solution.py:332
  50.4 1.8 %collective-permute-start.1 = (bf16[1,8,128,128]{3,2,1,0:T(8,128)(2,1)S(1)}, bf16[1,8,128,128]{3,2,1,0:T(8,128)(2,1)S(1)}, u32[]{:S(2)}, u32[]{:S(2)}) collective-permute-start(bf16[1,8,128,128]{3,2,1,0:T(8,128)(2,1)S(1)} %get-tuple-element.80), channel_id=1, source_target_pairs={{0,8},{1,4},{2,10},{3,6},{4,1},{5,13},{6,3},{7,15},{8,0},{9,12},{1... | collective-permute-start | bytes 786440 | tf_op jit(solution)/shard_map/ppermute | solution.py:332
  53.5 4.9 %collective-permute-start.15 = (bf16[512,256]{1,0:T(8,128)(2,1)S(1)}, bf16[512,256]{1,0:T(8,128)(2,1)S(1)}, u32[]{:S(2)}, u32[]{:S(2)}) collective-permute-start(bf16[512,256]{1,0:T(8,128)(2,1)S(1)} %get-tuple-element.96), channel_id=1, source_target_pairs={{0,1},{1,0},{2,3},{3,2},{4,5},{5,4},{6,7},{7,6},{8,9},{9,8},{10,11... | collective-permute-start | bytes 786440 | tf_op jit(solution)/shard_map/ppermute | solution.py:332
  58.8 3.0 %shard_map.68 = (bf16[1024,1536]{1,0:T(8,128)(2,1)S(1)}, bf16[1024,512]{1,0:T(8,128)(2,1)S(1)}) custom-call(s32[129]{0:T(256)S(1)} %get-tuple-element.79.info, bf16[8,16,128,128]{3,2,1,0:T(8,128)(2,1)} %blocks.13, bf16[1,16,128,128]{3,2,1,0:T(8,128)(2,1)S(1)} %collective-permute-done.7.refs_0_, bf16[1,16,128,128]{3,2,1,0:T(8,128)(2,1)S(1)} %collective-permute-done.9.refs_1_), custom_call_target="tpu_custom_call" | custom-call | tf_op jit(solution)/shard_map/pallas_call | solution.py:399
  61.8 3.0 %shard_map.69 = (bf16[1024,1536]{1,0:T(8,128)(2,1)S(1)}, bf16[1024,512]{1,0:T(8,128)(2,1)S(1)}) custom-call(s32[129]{0:T(256)S(1)} %get-tuple-element.79.info, bf16[8,16,128,128]{3,2,1,0:T(8,128)(2,1)} %blocks.13, bf16[1,16,128,128]{3,2,1,0:T(8,128)(2,1)S(1)} %collective-permute-done.4.refs_0_, ...), custom_call_target="tpu_custom_call", output_to_operand_aliasing={{0}: (3, {}), {1}: (4, {})} | custom-call | tf_op jit(solution)/shard_map/pallas_call | solution.py:399
  68.7 1.7 %collective-permute-start.18 = (bf16[512,256]{1,0:T(8,128)(2,1)S(1)}, bf16[512,256]{1,0:T(8,128)(2,1)S(1)}, u32[]{:S(2)}, u32[]{:S(2)}) collective-permute-start(bf16[512,256]{1,0:T(8,128)(2,1)S(1)} %shard_map.79), channel_id=1, source_target_pairs={{0,4},{1,8},{2,6},{3,10},{4,0},{5,12},{6,2},{7,14},{8,1},{9,16},{1... | collective-permute-start | bytes 786440 | tf_op jit(solution)/shard_map/ppermute | solution.py:332
  71.9 3.2 %collective-permute-done.18.refs_0_.far = bf16[512,256]{1,0:T(8,128)(2,1)S(1)} collective-permute-done((bf16[512,256]{1,0:T(8,128)(2,1)S(1)}, bf16[512,256]{1,0:T(8,128)(2,1)S(1)}, u32[]{:S(2)}, u32[]{:S(2)}) %collective-permute-start.18) | collective-permute-done | bytes 262176 | tf_op jit(solution)/shard_map/ppermute | solution.py:332
  85.2 2.8 %collective-permute-done.24.refs_2_.high = bf16[256,512]{1,0:T(8,128)(2,1)S(1)} collective-permute-done((bf16[256,512]{1,0:T(8,128)(2,1)S(1)}, bf16[256,512]{1,0:T(8,128)(2,1)S(1)}, u32[]{:S(2)}, u32[]{:S(2)}) %collective-permute-start.24) | collective-permute-done | bytes 262176 | tf_op jit(solution)/shard_map/ppermute | solution.py:332
  94.9 2.7 %collective-permute-done.26.refs_0_.far = bf16[512,256]{1,0:T(8,128)(2,1)S(1)} collective-permute-done((bf16[512,256]{1,0:T(8,128)(2,1)S(1)}, bf16[512,256]{1,0:T(8,128)(2,1)S(1)}, u32[]{:S(2)}, u32[]{:S(2)}) %collective-permute-start.26) | collective-permute-done | bytes 262176 | tf_op jit(solution)/shard_map/ppermute | solution.py:332
  101.8 2.7 %collective-permute-done.28.refs_0_.far = bf16[512,256]{1,0:T(8,128)(2,1)S(1)} collective-permute-done((bf16[512,256]{1,0:T(8,128)(2,1)S(1)}, bf16[512,256]{1,0:T(8,128)(2,1)S(1)}, u32[]{:S(2)}, u32[]{:S(2)}) %collective-permute-start.28) | collective-permute-done | bytes 262176 | tf_op jit(solution)/shard_map/ppermute | solution.py:332
  108.7 2.7 %collective-permute-done.30.refs_0_.far = bf16[512,256]{1,0:T(8,128)(2,1)S(1)} collective-permute-done((bf16[512,256]{1,0:T(8,128)(2,1)S(1)}, bf16[512,256]{1,0:T(8,128)(2,1)S(1)}, u32[]{:S(2)}, u32[]{:S(2)}) %collective-permute-start.30) | collective-permute-done | bytes 262176 | tf_op jit(solution)/shard_map/ppermute | solution.py:332
  115.7 2.4 %collective-permute-done.32.refs_0_.far = bf16[512,256]{1,0:T(8,128)(2,1)S(1)} collective-permute-done((bf16[512,256]{1,0:T(8,128)(2,1)S(1)}, bf16[512,256]{1,0:T(8,128)(2,1)S(1)}, u32[]{:S(2)}, u32[]{:S(2)}) %collective-permute-start.32) | collective-permute-done | bytes 262176 | tf_op jit(solution)/shard_map/ppermute | solution.py:332
  122.4 2.7 %collective-permute-done.34.refs_0_.far = bf16[512,256]{1,0:T(8,128)(2,1)S(1)} collective-permute-done((bf16[512,256]{1,0:T(8,128)(2,1)S(1)}, bf16[512,256]{1,0:T(8,128)(2,1)S(1)}, u32[]{:S(2)}, u32[]{:S(2)}) %collective-permute-start.34) | collective-permute-done | bytes 262176 | tf_op jit(solution)/shard_map/ppermute | solution.py:332
  128.8 3.1 %collective-permute-done.36.part = bf16[512,256]{1,0:T(8,128)(2,1)S(1)} collective-permute-done((bf16[512,256]{1,0:T(8,128)(2,1)S(1)}, bf16[512,256]{1,0:T(8,128)(2,1)S(1)}, u32[]{:S(2)}, u32[]{:S(2)}) %collective-permute-start.36) | collective-permute-done | bytes 262176 | tf_op jit(solution)/shard_map/ppermute | solution.py:332
  133.3 2.1 %collective-permute-start.37 = (bf16[256,512]{1,0:T(8,128)(2,1)S(1)}, bf16[256,512]{1,0:T(8,128)(2,1)S(1)}, u32[]{:S(2)}, u32[]{:S(2)}) collective-permute-start(bf16[256,512]{1,0:T(8,128)(2,1)S(1)} %shard_map.112.own), channel_id=1, source_target_pairs={{0,8},{1,4},{2,10},{3,6},{4,1},{5,13},{6,3},{7,15},{8,0},{9,12},{1... | collective-permute-start | bytes 786440 | tf_op jit(solution)/shard_map/ppermute | solution.py:332
  135.3 3.6 %collective-permute-done.38.moved = bf16[256,512]{1,0:T(8,128)(2,1)S(1)} collective-permute-done((bf16[256,512]{1,0:T(8,128)(2,1)S(1)}, bf16[256,512]{1,0:T(8,128)(2,1)S(1)}, u32[]{:S(2)}, u32[]{:S(2)}) %collective-permute-start.38) | collective-permute-done | bytes 262176 | tf_op jit(solution)/shard_map/ppermute | solution.py:332
  139.8 2.0 %collective-permute-done.37.moved = bf16[256,512]{1,0:T(8,128)(2,1)S(1)} collective-permute-done((bf16[256,512]{1,0:T(8,128)(2,1)S(1)}, bf16[256,512]{1,0:T(8,128)(2,1)S(1)}, u32[]{:S(2)}, u32[]{:S(2)}) %collective-permute-start.37) | collective-permute-done | bytes 262176 | tf_op jit(solution)/shard_map/ppermute | solution.py:332
  (113 shorter events, 58.5 us)
Async XLA Ops:
  1.3 15.0 %collective-permute-start.11 = (bf16[256,1024]{1,0:T(8,128)(2,1)S(1)}, bf16[256,1024]{1,0:T(8,128)(2,1)S(1)}, u32[]{:S(2)}, u32[]{:S(2)}) collective-permute-start(bf16[256,1024]{1,0:T(8,128)(2,1)S(1)} %convert_element_type.3.refs_0_), channel_id=1, source_target_pairs={{0,2},{1,3},{2,0},{3,1},{4,6},{5,7},{6,4},{7,5},{8,10},{9,11},{10,... | collective-permute-start | bytes 1572872 | tf_op jit(solution)/shard_map/ppermute | solution.py:347
  4.4 20.4 %collective-permute-start.12 = (bf16[256,1024]{1,0:T(8,128)(2,1)S(1)}, bf16[256,1024]{1,0:T(8,128)(2,1)S(1)}, u32[]{:S(2)}, u32[]{:S(2)}) collective-permute-start(bf16[256,1024]{1,0:T(8,128)(2,1)S(1)} %convert_element_type.3.refs_0_), channel_id=1, source_target_pairs={{0,1},{1,0},{2,3},{3,2},{4,5},{5,4},{6,7},{7,6},{8,9},{9,8},{10,11... | collective-permute-start | bytes 1572872 | tf_op jit(solution)/shard_map/ppermute | solution.py:347
  16.3 8.9 %collective-permute-start.13 = (bf16[256,1024]{1,0:T(8,128)(2,1)S(1)}, bf16[256,1024]{1,0:T(8,128)(2,1)S(1)}, u32[]{:S(2)}, u32[]{:S(2)}) collective-permute-start(bf16[256,1024]{1,0:T(8,128)(2,1)S(1)} %collective-permute-done.11.refs_1_), channel_id=1, source_target_pairs={{0,1},{1,0},{2,3},{3,2},{4,5},{5,4},{6,7},{7,6},{8,9},{9,8},{10,11... | collective-permute-start | bytes 1572872 | tf_op jit(solution)/shard_map/ppermute | solution.py:347
  17.8 22.3 %collective-permute-start.9 = (bf16[1,16,128,128]{3,2,1,0:T(8,128)(2,1)S(1)}, bf16[1,16,128,128]{3,2,1,0:T(8,128)(2,1)S(1)}, u32[]{:S(2)}, u32[]{:S(2)}) collective-permute-start(bf16[1,16,128,128]{3,2,1,0:T(8,128)(2,1)S(1)} %get-tuple-element.84), channel_id=1, source_target_pairs={{0,8},{1,4},{2,10},{3,6},{4,1},{5,13},{6,3},{7,15},{8,0},{9,12},{1... | collective-permute-start | bytes 1572872 | tf_op jit(solution)/shard_map/ppermute | solution.py:332
  20.8 20.1 %collective-permute-start.7 = (bf16[1,16,128,128]{3,2,1,0:T(8,128)(2,1)S(1)}, bf16[1,16,128,128]{3,2,1,0:T(8,128)(2,1)S(1)}, u32[]{:S(2)}, u32[]{:S(2)}) collective-permute-start(bf16[1,16,128,128]{3,2,1,0:T(8,128)(2,1)S(1)} %shard_map.67), channel_id=1, source_target_pairs={{0,8},{1,4},{2,10},{3,6},{4,1},{5,13},{6,3},{7,15},{8,0},{9,12},{1... | collective-permute-start | bytes 1572872 | tf_op jit(solution)/shard_map/ppermute | solution.py:332
  21.1 20.5 %collective-permute-start.4 = (bf16[1,16,128,128]{3,2,1,0:T(8,128)(2,1)S(1)}, bf16[1,16,128,128]{3,2,1,0:T(8,128)(2,1)S(1)}, u32[]{:S(2)}, u32[]{:S(2)}) collective-permute-start(bf16[1,16,128,128]{3,2,1,0:T(8,128)(2,1)S(1)} %get-tuple-element.82), channel_id=1, source_target_pairs={{0,8},{1,4},{2,10},{3,6},{4,1},{5,13},{6,3},{7,15},{8,0},{9,12},{1... | collective-permute-start | bytes 1572872 | tf_op jit(solution)/shard_map/ppermute | solution.py:332
  24.8 13.6 %collective-permute-start = (s32[137]{0:T(256)S(1)}, s32[137]{0:T(256)S(1)}, u32[]{:S(2)}, u32[]{:S(2)}) collective-permute-start(s32[137]{0:T(256)S(1)} %shard_map.64.own), channel_id=1, source_target_pairs={{0,8},{1,4},{2,10},{3,6},{4,1},{5,13},{6,3},{7,15},{8,0},{9,12},{1... | collective-permute-start | bytes 1652 | tf_op jit(solution)/shard_map/ppermute | solution.py:332
  25.1 17.1 %collective-permute-start.2 = (bf16[1,8,128,128]{3,2,1,0:T(8,128)(2,1)S(1)}, bf16[1,8,128,128]{3,2,1,0:T(8,128)(2,1)S(1)}, u32[]{:S(2)}, u32[]{:S(2)}) collective-permute-start(bf16[1,8,128,128]{3,2,1,0:T(8,128)(2,1)S(1)} %get-tuple-element.81), channel_id=1, source_target_pairs={{0,8},{1,4},{2,10},{3,6},{4,1},{5,13},{6,3},{7,15},{8,0},{9,12},{1... | collective-permute-start | bytes 786440 | tf_op jit(solution)/shard_map/ppermute | solution.py:332
  38.4 13.8 %collective-permute-start.14 = (bf16[1024,256]{1,0:T(8,128)(2,1)S(1)}, bf16[1024,256]{1,0:T(8,128)(2,1)S(1)}, u32[]{:S(2)}, u32[]{:S(2)}) collective-permute-start(bf16[1024,256]{1,0:T(8,128)(2,1)S(1)} %shard_map.73.own), channel_id=1, source_target_pairs={{0,8},{1,4},{2,10},{3,6},{4,1},{5,13},{6,3},{7,15},{8,0},{9,12},{1... | collective-permute-start | bytes 1572872 | tf_op jit(solution)/shard_map/ppermute | solution.py:332
  40.2 13.3 %collective-permute-start.10 = (bf16[1,16,128,128]{3,2,1,0:T(8,128)(2,1)S(1)}, bf16[1,16,128,128]{3,2,1,0:T(8,128)(2,1)S(1)}, u32[]{:S(2)}, u32[]{:S(2)}) collective-permute-start(bf16[1,16,128,128]{3,2,1,0:T(8,128)(2,1)S(1)} %collective-permute-done.9.refs_1_), channel_id=1, source_target_pairs={{1,3},{3,1},{4,6},{6,4},{9,11},{11,9},{12,14},{14,12},{17,19},{19,... | collective-permute-start | bytes 1572872 | tf_op jit(solution)/shard_map/ppermute | solution.py:332
  40.9 17.5 %collective-permute-start.8 = (bf16[1,16,128,128]{3,2,1,0:T(8,128)(2,1)S(1)}, bf16[1,16,128,128]{3,2,1,0:T(8,128)(2,1)S(1)}, u32[]{:S(2)}, u32[]{:S(2)}) collective-permute-start(bf16[1,16,128,128]{3,2,1,0:T(8,128)(2,1)S(1)} %collective-permute-done.7.refs_0_), channel_id=1, source_target_pairs={{1,3},{3,1},{4,6},{6,4},{9,11},{11,9},{12,14},{14,12},{17,19},{19,... | collective-permute-start | bytes 1572872 | tf_op jit(solution)/shard_map/ppermute | solution.py:332
  41.6 23.9 %collective-permute-start.5 = (bf16[1,16,128,128]{3,2,1,0:T(8,128)(2,1)S(1)}, bf16[1,16,128,128]{3,2,1,0:T(8,128)(2,1)S(1)}, u32[]{:S(2)}, u32[]{:S(2)}) collective-permute-start(bf16[1,16,128,128]{3,2,1,0:T(8,128)(2,1)S(1)} %collective-permute-done.4.refs_0_), channel_id=1, source_target_pairs={{1,3},{3,1},{4,6},{6,4},{9,11},{11,9},{12,14},{14,12},{17,19},{19,... | collective-permute-start | bytes 1572872 | tf_op jit(solution)/shard_map/ppermute | solution.py:332
  42.3 8.1 %collective-permute-start.6 = (bf16[1,8,128,128]{3,2,1,0:T(8,128)(2,1)S(1)}, bf16[1,8,128,128]{3,2,1,0:T(8,128)(2,1)S(1)}, u32[]{:S(2)}, u32[]{:S(2)}) collective-permute-start(bf16[1,8,128,128]{3,2,1,0:T(8,128)(2,1)S(1)} %get-tuple-element.83), channel_id=1, source_target_pairs={{0,8},{1,4},{2,10},{3,6},{4,1},{5,13},{6,3},{7,15},{8,0},{9,12},{1... | collective-permute-start | bytes 786440 | tf_op jit(solution)/shard_map/ppermute | solution.py:332
  50.4 15.7 %collective-permute-start.1 = (bf16[1,8,128,128]{3,2,1,0:T(8,128)(2,1)S(1)}, bf16[1,8,128,128]{3,2,1,0:T(8,128)(2,1)S(1)}, u32[]{:S(2)}, u32[]{:S(2)}) collective-permute-start(bf16[1,8,128,128]{3,2,1,0:T(8,128)(2,1)S(1)} %get-tuple-element.80), channel_id=1, source_target_pairs={{0,8},{1,4},{2,10},{3,6},{4,1},{5,13},{6,3},{7,15},{8,0},{9,12},{1... | collective-permute-start | bytes 786440 | tf_op jit(solution)/shard_map/ppermute | solution.py:332
  52.2 13.9 %collective-permute-start.3 = (bf16[1,8,128,128]{3,2,1,0:T(8,128)(2,1)S(1)}, bf16[1,8,128,128]{3,2,1,0:T(8,128)(2,1)S(1)}, u32[]{:S(2)}, u32[]{:S(2)}) collective-permute-start(bf16[1,8,128,128]{3,2,1,0:T(8,128)(2,1)S(1)} %collective-permute-done.2.refs_2_), channel_id=1, source_target_pairs={{1,3},{3,1},{4,6},{6,4},{9,11},{11,9},{12,14},{14,12},{17,19},{19,... | collective-permute-start | bytes 786440 | tf_op jit(solution)/shard_map/ppermute | solution.py:332
  53.5 13.4 %collective-permute-start.15 = (bf16[512,256]{1,0:T(8,128)(2,1)S(1)}, bf16[512,256]{1,0:T(8,128)(2,1)S(1)}, u32[]{:S(2)}, u32[]{:S(2)}) collective-permute-start(bf16[512,256]{1,0:T(8,128)(2,1)S(1)} %get-tuple-element.96), channel_id=1, source_target_pairs={{0,1},{1,0},{2,3},{3,2},{4,5},{5,4},{6,7},{7,6},{8,9},{9,8},{10,11... | collective-permute-start | bytes 786440 | tf_op jit(solution)/shard_map/ppermute | solution.py:332
  58.3 9.6 %collective-permute-start.16 = (bf16[512,256]{1,0:T(8,128)(2,1)S(1)}, bf16[512,256]{1,0:T(8,128)(2,1)S(1)}, u32[]{:S(2)}, u32[]{:S(2)}) collective-permute-start(bf16[512,256]{1,0:T(8,128)(2,1)S(1)} %get-tuple-element.99), channel_id=1, source_target_pairs={{0,4},{1,8},{2,6},{3,10},{4,0},{5,12},{6,2},{7,14},{8,1},{9,16},{1... | collective-permute-start | bytes 786440 | tf_op jit(solution)/shard_map/ppermute | solution.py:332
  68.7 6.4 %collective-permute-start.18 = (bf16[512,256]{1,0:T(8,128)(2,1)S(1)}, bf16[512,256]{1,0:T(8,128)(2,1)S(1)}, u32[]{:S(2)}, u32[]{:S(2)}) collective-permute-start(bf16[512,256]{1,0:T(8,128)(2,1)S(1)} %shard_map.79), channel_id=1, source_target_pairs={{0,4},{1,8},{2,6},{3,10},{4,0},{5,12},{6,2},{7,14},{8,1},{9,16},{1... | collective-permute-start | bytes 786440 | tf_op jit(solution)/shard_map/ppermute | solution.py:332
  75.9 6.4 %collective-permute-start.20 = (bf16[512,256]{1,0:T(8,128)(2,1)S(1)}, bf16[512,256]{1,0:T(8,128)(2,1)S(1)}, u32[]{:S(2)}, u32[]{:S(2)}) collective-permute-start(bf16[512,256]{1,0:T(8,128)(2,1)S(1)} %shard_map.83.refs_3_.sent), channel_id=1, source_target_pairs={{0,4},{1,8},{2,6},{3,10},{4,0},{5,12},{6,2},{7,14},{8,1},{9,16},{1... | collective-permute-start | bytes 786440 | tf_op jit(solution)/shard_map/ppermute | solution.py:332
  77.5 7.6 %collective-permute-start.23 = (bf16[256,512]{1,0:T(8,128)(2,1)S(1)}, bf16[256,512]{1,0:T(8,128)(2,1)S(1)}, u32[]{:S(2)}, u32[]{:S(2)}) collective-permute-start(bf16[256,512]{1,0:T(8,128)(2,1)S(1)} %get-tuple-element.105.low), channel_id=1, source_target_pairs={{0,4},{1,8},{2,6},{3,10},{4,0},{5,12},{6,2},{7,14},{8,1},{9,16},{1... | collective-permute-start | bytes 786440 | tf_op jit(solution)/shard_map/ppermute | solution.py:332
  78.0 10.0 %collective-permute-start.24 = (bf16[256,512]{1,0:T(8,128)(2,1)S(1)}, bf16[256,512]{1,0:T(8,128)(2,1)S(1)}, u32[]{:S(2)}, u32[]{:S(2)}) collective-permute-start(bf16[256,512]{1,0:T(8,128)(2,1)S(1)} %get-tuple-element.106.high), channel_id=1, source_target_pairs={{0,4},{1,8},{2,6},{3,10},{4,0},{5,12},{6,2},{7,14},{8,1},{9,16},{1... | collective-permute-start | bytes 786440 | tf_op jit(solution)/shard_map/ppermute | solution.py:332
  82.8 7.9 %collective-permute-start.22 = (bf16[512,256]{1,0:T(8,128)(2,1)S(1)}, bf16[512,256]{1,0:T(8,128)(2,1)S(1)}, u32[]{:S(2)}, u32[]{:S(2)}) collective-permute-start(bf16[512,256]{1,0:T(8,128)(2,1)S(1)} %get-tuple-element.116), channel_id=1, source_target_pairs={{0,4},{1,8},{2,6},{3,10},{4,0},{5,12},{6,2},{7,14},{8,1},{9,16},{1... | collective-permute-start | bytes 786440 | tf_op jit(solution)/shard_map/ppermute | solution.py:332
  132.5 6.4 %collective-permute-start.38 = (bf16[256,512]{1,0:T(8,128)(2,1)S(1)}, bf16[256,512]{1,0:T(8,128)(2,1)S(1)}, u32[]{:S(2)}, u32[]{:S(2)}) collective-permute-start(bf16[256,512]{1,0:T(8,128)(2,1)S(1)} %shard_map.113.own), channel_id=1, source_target_pairs={{0,8},{1,4},{2,10},{3,6},{4,1},{5,13},{6,3},{7,15},{8,0},{9,12},{1... | collective-permute-start | bytes 786440 | tf_op jit(solution)/shard_map/ppermute | solution.py:332
  133.3 8.5 %collective-permute-start.37 = (bf16[256,512]{1,0:T(8,128)(2,1)S(1)}, bf16[256,512]{1,0:T(8,128)(2,1)S(1)}, u32[]{:S(2)}, u32[]{:S(2)}) collective-permute-start(bf16[256,512]{1,0:T(8,128)(2,1)S(1)} %shard_map.112.own), channel_id=1, source_target_pairs={{0,8},{1,4},{2,10},{3,6},{4,1},{5,13},{6,3},{7,15},{8,0},{9,12},{1... | collective-permute-start | bytes 786440 | tf_op jit(solution)/shard_map/ppermute | solution.py:332
  (18 other events, 87.3 us)
